TPU v7x, 128 devices: a whole 4x4x4 slice. The times are simulated.
128 devices in a mesh: member: 16 (over z, x_lo, core), tensor: 8 (over y, x_hi).
Axes of the slice: x: 4 (x_hi: 2, x_lo: 2; x = x_hi * 2 + x_lo), y: 4, z: 4, core: 2. Of those that a mesh axis runs over, the one named last changes fastest.
Arguments:
- query: bfloat16 [8192, 8192], P('member', 'tensor'), may hold values from -100 to 100
- keys: bfloat16 [8192, 1024], P('member', 'tensor'), may hold values from -6 to 6
- values: bfloat16 [8192, 1024], P('member', 'tensor'), may hold values from -12 to 12
- residual: bfloat16 [8192, 8192], P('member', 'tensor'), may hold values from -6 to 6
- out_weight: bfloat16 [8192, 8192], P('tensor', 'member'), may hold values from -0.0625 to 0.0625
- norm_gain: float32 [8192], replicated, may hold values from 0.1 to 1.9
- cand_len: int32 [64], P('member'), may hold values from 32 to 128, as said below
- head_w1: bfloat16 [16, 8192, 4096], P('member', None, 'tensor'), may hold values from -0.0625 to 0.0625
- head_b1: float32 [16, 4096], P('member', 'tensor'), may hold values from -3 to 3
- head_w2: bfloat16 [16, 4096, 4096], P('member', 'tensor'), may hold values from -0.09375 to 0.09375
- head_b2: float32 [16, 4096], P('member'), may hold values from -3 to 3
- head_w3: bfloat16 [16, 4096], P('member'), may hold values from -0.09375 to 0.09375
- head_b3: float32 [16], P('member'), may hold values from -4 to 4
Outputs:
- trunk_out: bfloat16 [8192, 8192], P('member', 'tensor')
- scores: float32 [16, 64], P('member')
Inputs may be any that keep to these rules, and one draw needn't show every extreme that they name: Token slots of candidate c at places cand_len[c] and beyond are padding: excluded as keys, and the slot at place cand_len[c] - 1 is the one that is scored.
All inputs are finite; a program needn't handle non-finite values.
Results may differ from a plain program's by a relative error of at most 0.014.
Values may be sent and summed in bfloat16 or wider, within the bound.
No kernel may reach another device: no remote copies, remote signals or barrier semaphores. Data moves between devices by JAX's collectives and lax.ppermute only.
A program may use at most 192 MiB of HBM per device.

v0:
```python
import jax
import jax.numpy as jnp
from jax import lax
from jax.sharding import PartitionSpec as P

HEAD_WIDTH = 128
SEQUENCE_SLOTS = 128


def local(
    query,
    keys,
    values,
    residual,
    out_weight,
    norm_gain,
    cand_len,
    head_w1,
    head_b1,
    head_w2,
    head_b2,
    head_w3,
    head_b3,
):
    row_count = query.shape[0]
    cand_count = row_count // SEQUENCE_SLOTS
    heads_here = query.shape[1] // HEAD_WIDTH
    kv_here = keys.shape[1] // HEAD_WIDTH
    group_width = heads_here // kv_here
    query_tiles = query.reshape(cand_count, SEQUENCE_SLOTS, kv_here, group_width, HEAD_WIDTH)
    key_tiles = keys.reshape(cand_count, SEQUENCE_SLOTS, kv_here, HEAD_WIDTH)
    value_tiles = values.reshape(cand_count, SEQUENCE_SLOTS, kv_here, HEAD_WIDTH)
    logits = jnp.einsum(
        "cskgd,ctkd->ckgst", query_tiles, key_tiles, preferred_element_type=jnp.float32
    ) * HEAD_WIDTH ** (-0.5)
    places = jnp.arange(SEQUENCE_SLOTS, dtype=jnp.int32)
    allowed = (places[None, :, None] >= places[None, None, :]) & (
        places[None, None, :] < cand_len[:, None, None]
    )
    allowed = allowed[:, None, None]
    logits = jnp.where(allowed, logits, jnp.float32(-1e30))
    row_max = jnp.max(logits, axis=-1, keepdims=True)
    probs = jnp.where(allowed, jnp.exp(logits - row_max), jnp.float32(0.0))
    totals = jnp.sum(probs, axis=-1, keepdims=True)
    attn_weights = (probs / totals).astype(jnp.bfloat16)
    attn_out = jnp.einsum(
        "ckgst,ctkd->cskgd", attn_weights, value_tiles, preferred_element_type=jnp.float32
    )
    attn_out = attn_out.astype(jnp.bfloat16).reshape(row_count, heads_here * HEAD_WIDTH)
    projected = jnp.dot(
        attn_out,
        lax.all_gather(out_weight, "member", axis=1, tiled=True),
        preferred_element_type=jnp.float32,
    )
    summed = lax.psum_scatter(
        projected.astype(jnp.bfloat16), "tensor", scatter_dimension=1, tiled=True
    ).astype(jnp.float32)
    trunk_out = (summed + residual.astype(jnp.float32)).astype(jnp.bfloat16)
    last_rows = jnp.arange(cand_count, dtype=jnp.int32) * SEQUENCE_SLOTS + cand_len - 1
    picked = jnp.take(trunk_out, last_rows, axis=0)
    full_rows = lax.all_gather(picked, "tensor", axis=1, tiled=True).astype(jnp.float32)
    mean_square = jnp.mean(full_rows * full_rows, axis=-1, keepdims=True) + 1e-05
    features = (full_rows * lax.rsqrt(mean_square) * norm_gain).astype(jnp.bfloat16)
    all_features = lax.all_gather(features, "member", axis=0, tiled=True)
    first = jax.nn.silu(
        jnp.dot(all_features, head_w1[0], preferred_element_type=jnp.float32) + head_b1[0]
    ).astype(jnp.bfloat16)
    hidden_terms = jnp.dot(first, head_w2[0], preferred_element_type=jnp.float32)
    second = jax.nn.silu(
        lax.psum(hidden_terms.astype(jnp.bfloat16), "tensor").astype(jnp.float32) + head_b2[0]
    )
    scores = jnp.sum(second * head_w3[0].astype(jnp.float32), axis=-1) + head_b3[0]
    return (trunk_out, scores[None, :])


def solution(mesh):
    in_specs = (
        P("member", "tensor"),
        P("member", "tensor"),
        P("member", "tensor"),
        P("member", "tensor"),
        P("tensor", "member"),
        P(),
        P("member"),
        P("member", None, "tensor"),
        P("member", "tensor"),
        P("member", "tensor", None),
        P("member", None),
        P("member", None),
        P("member"),
    )
    out_specs = (P("member", "tensor"), P("member", None))
    return jax.shard_map(local, mesh=mesh, in_specs=in_specs, out_specs=out_specs, check_vma=False)
```

profile of v0, /device:TPU:0, one launch (start us, length us, event | category | flops | bytes accessed | tf_op | source)
XLA Modules:
  0.0 407.6 jit_solution(14648535822901284644)
XLA Ops:
  7.2 0.7 all-gather.4.cloned.1.call-update
  8.0 1.5 copy.26
  9.5 0.1 iota_compare_fusion.1
  9.6 0.1 broadcast_and_fusion
  9.7 0.5 fusion.3
  10.2 0.6 fusion.4
  10.8 0.9 fusion.5
  11.7 0.7 copy.22
  12.4 91.4 %all-gather.4.cloned.1.call-done = bf16[1024,8192]{1,0:T(8,128)(2,1)} async-done(((bf16[1024,512]{1,0:T(8,128)(2,1)}), bf16[1024,8192]{1,0:T(8,128)(2,1)}) %all-gather.4.cloned.1.call-update) | async-done | bytes 16777232 | tf_op jit(solution)/shard_map/all_gather | solution.py:52
  103.8 16.8 %convolution_convert_fusion = bf16[512,8192]{1,0:T(8,128)(2,1)} fusion(bf16[1024,8192]{1,0:T(8,128)(2,1)} %all-gather.4.cloned.1.call-done, bf16[64,8,8,128]{3,2,1,0:T(8,128)(2,1)S(1)} %bitcast.71), kind=kOutput, calls=%fused_computation.1 | convolution fusion | flops 8594128896 | bytes 26214400 | tf_op jit(solution)/shard_map/dot_general | solution.py:50
  120.6 0.0 all-gather.6.cloned.1.call-start
  120.7 115.5 %reduce-scatter.2.cloned.1.call-done = bf16[512,1024]{1,0:T(8,128)(2,1)} async-done(((bf16[512,8192]{1,0:T(8,128)(2,1)}), bf16[512,1024]{1,0:T(8,128)(2,1)}) %reduce-scatter.2.cloned.1.call-update) | async-done | bytes 1048592 | tf_op jit(solution)/shard_map/reduce_scatter | solution.py:55
  236.2 1.6 add_convert_fusion
  237.8 0.6 gather_fusion
  238.4 0.1 broadcast_select_fusion
  238.5 34.2 %all_gather.10 = bf16[4,8192]{1,0:T(4,128)(2,1)S(1)} all-gather(bf16[4,1024]{1,0:T(4,128)(2,1)S(1)} %broadcast_select_fusion), channel_id=1, replica_groups=mesh['member'=16,'tensor'=8] {'tensor'}, dimensions={1}, use_global_device_ids=true | all-gather | bytes 73728 | tf_op jit(solution)/shard_map/all_gather | solution.py:61
  272.7 0.2 fusion.15
  272.9 0.7 fusion.22
  273.7 30.1 %all-gather.6.cloned.1.call-done = bf16[16,4,8192]{2,1,0:T(4,128)(2,1)} async-done(((bf16[1,4,8192]{2,1,0:T(4,128)(2,1)}), bf16[16,4,8192]{2,1,0:T(4,128)(2,1)}) %all-gather.6.cloned.1.call-update) | async-done | bytes 1048592 | tf_op jit(solution)/shard_map/all_gather | solution.py:64
  303.8 1.3 reshape.118
  305.2 7.8 %convolution_convert_fusion.1 = bf16[64,4096]{1,0:T(8,128)(2,1)} fusion(bf16[1,512,4096]{2,1,0:T(8,128)(2,1)} %param.22, bf16[64,8192]{1,0:T(8,128)(2,1)S(1)} %reshape.118, bf16[1,8192,512]{2,1,0:T(8,128)(2,1)} %param.20, f32[512]{0:T(512)S(1)} %bitcast.74), kind=kOutput, calls=%fused_computation.4 | convolution fusion | flops 805765120 | bytes 14157824 | tf_op jit(solution)/shard_map/dot_general | solution.py:68
  313.6 85.4 %all-reduce.2.cloned.1.call-done = bf16[64,4096]{1,0:T(8,128)(2,1)} async-done(((bf16[64,4096]{1,0:T(8,128)(2,1)}), bf16[64,4096]{1,0:T(8,128)(2,1)}) %all-reduce.2.cloned.1.call-update) | async-done | bytes 524304 | tf_op jit(solution)/shard_map/psum | solution.py:70
  399.1 1.5 multiply_reduce_fusion
  400.5 0.5 add_bitcast_fusion
  (29 shorter events, 0.3 us)
Async XLA Ops:
  7.2 2.6 copy-start
  7.2 2.3 copy-start.8
  7.2 96.6 %all-gather.4.cloned.1.call-start = ((), (), s32[]{:S(2)}) async-start(), calls=%async_computation.1 | async-start | bytes 17825792 | tf_op jit(solution)/shard_map/all_gather | solution.py:52
  7.9 228.3 %reduce-scatter.2.cloned.1.call-start = ((), (), s32[]{:S(2)}) async-start(), calls=%async_computation.2 | async-start | bytes 9437184 | tf_op jit(solution)/shard_map/reduce_scatter | solution.py:55
  9.7 1.1 copy-start.7
  120.6 115.6 %copy-start.2 = (bf16[512,1024]{1,0:T(8,128)(2,1)S(1)}, bf16[512,1024]{1,0:T(8,128)(2,1)}, u32[]{:S(2)}) copy-start(bf16[512,1024]{1,0:T(8,128)(2,1)} %param.16) | copy-start | bytes 3145732
  120.6 152.3 %copy-start.3 = (f32[8192]{0:T(1024)S(1)}, f32[8192]{0:T(1024)}, u32[]{:S(2)}) copy-start(f32[8192]{0:T(1024)} %param.18) | copy-start | bytes 98308
  120.6 183.2 %all-gather.6.cloned.1.call-start = ((), (), s32[]{:S(2)}) async-start(), calls=%async_computation.4 | async-start | bytes 1114112 | tf_op jit(solution)/shard_map/all_gather | solution.py:64
  120.7 184.4 %copy-start.6 = (f32[1,512]{1,0:T(1,128)S(1)}, f32[1,512]{1,0:T(1,128)}, u32[]{:S(2)}) copy-start(f32[1,512]{1,0:T(1,128)} %param.21) | copy-start | bytes 6148
  237.8 75.1 %copy-start.1 = (bf16[512,1024]{1,0:T(8,128)(2,1)}, bf16[512,1024]{1,0:T(8,128)(2,1)S(1)}, u32[]{:S(2)}) copy-start(bf16[512,1024]{1,0:T(8,128)(2,1)S(1)} %add_convert_fusion) | copy-start | bytes 3145732
  273.7 125.4 %all-reduce.2.cloned.1.call-start = ((), (), s32[]{:S(2)}) async-start(), calls=%async_computation.3 | async-start | bytes 1048576 | tf_op jit(solution)/shard_map/psum | solution.py:70
  305.2 7.8 %copy-start.5 = (bf16[1,4096]{1,0:T(2,128)(2,1)S(1)}, bf16[1,4096]{1,0:T(2,128)(2,1)}, u32[]{:S(2)}) copy-start(bf16[1,4096]{1,0:T(2,128)(2,1)} %param.24) | copy-start | bytes 24580
  305.2 93.9 %copy-start.4 = (f32[1,4096]{1,0:T(1,128)S(1)}, f32[1,4096]{1,0:T(1,128)}, u32[]{:S(2)}) copy-start(f32[1,4096]{1,0:T(1,128)} %param.23) | copy-start | bytes 49156
Sparse Core Ops, SparseCore 0:
  9.7 94.0 all-gather.3
  120.8 115.3 reduce-scatter.1
  273.8 29.9 all-gather.5
  313.1 85.9 all-reduce.1
where the time goes:
time: 408 us
  waiting for transfers between devices  323 us (79%)
  blocking collectives  34.2 us (8%)
  matrix products  25.9 us (6%)
  between operations  14.6 us (4%)
  other arithmetic  5.43 us (1%)
  local copies, waits for them, and re-layouts  4.13 us (1%)
    reduce_scatter x1, waiting for transfers between devices, local(): lax.psum_scatter(projected.astype(jnp.bfloat16), 'tensor', scatter_dimens...  115 us
    all_gather x1, waiting for transfers between devices, local(): lax.all_gather(out_weight, 'member', axis=1, tiled=True)  91.4 us
    psum x1, waiting for transfers between devices, local(): lax.psum(hidden_terms.astype(jnp.bfloat16), 'tensor').astype(jnp.float32)  85.4 us
    all_gather x1, blocking collectives, local(): lax.all_gather(picked, 'tensor', axis=1, tiled=True).astype(jnp.float32)  34.2 us
    all_gather x1, waiting for transfers between devices, local(): all_features = lax.all_gather(features, 'member', axis=0, tiled=True)  30.1 us
    dot_general x1, matrix products, local(): jnp.dot(attn_out, lax.all_gather(out_weight, 'member', axis=1, tiled=True...  16.8 us
  transfers between devices with their start and end apart: 4, of which 4 were waited for; matrix products, arithmetic and copies ran while one was open for 1% of the time, Pallas kernels for 0%

commit v1 on v0

v1 whole, which is shorter than its diff:
```python
import functools

import jax
import jax.numpy as jnp
from jax import lax
from jax.experimental import pallas as pl
from jax.experimental.pallas import tpu as pltpu
from jax.sharding import Mesh, PartitionSpec as P

HEAD_WIDTH = 128
SEQUENCE_SLOTS = 128
Z, XL, CORE, Y, XH = 4, 2, 2, 4, 2
MEMBER = ("z", "xl", "core")
TENSOR = ("y", "xh")
ALL = MEMBER + TENSOR


def flat(z, xl, core, y, xh):
    return (((z % Z) * XL + xl % XL) * CORE + core) * Y * XH + (y % Y) * XH + xh % XH


def weight_moves():
    return [
        (flat(z, xl, core, y, xh), flat(y - z, xh - xl, core, z, xl))
        for z in range(Z)
        for xl in range(XL)
        for core in range(CORE)
        for y in range(Y)
        for xh in range(XH)
    ]


def from_ahead(x, axis, size, step):
    return lax.ppermute(x, axis, [(i, (i - step) % size) for i in range(size)])


def attention(query, keys, values, cand_len):
    row_count = query.shape[0]
    cand_count = row_count // SEQUENCE_SLOTS
    heads_here = query.shape[1] // HEAD_WIDTH
    kv_here = keys.shape[1] // HEAD_WIDTH
    group_width = heads_here // kv_here
    query_tiles = query.reshape(cand_count, SEQUENCE_SLOTS, kv_here, group_width, HEAD_WIDTH)
    key_tiles = keys.reshape(cand_count, SEQUENCE_SLOTS, kv_here, HEAD_WIDTH)
    value_tiles = values.reshape(cand_count, SEQUENCE_SLOTS, kv_here, HEAD_WIDTH)
    logits = jnp.einsum(
        "cskgd,ctkd->ckgst", query_tiles, key_tiles, preferred_element_type=jnp.float32
    ) * HEAD_WIDTH ** (-0.5)
    places = jnp.arange(SEQUENCE_SLOTS, dtype=jnp.int32)
    allowed = (places[None, :, None] >= places[None, None, :]) & (
        places[None, None, :] < cand_len[:, None, None]
    )
    allowed = allowed[:, None, None]
    logits = jnp.where(allowed, logits, jnp.float32(-1e30))
    row_max = jnp.max(logits, axis=-1, keepdims=True)
    probs = jnp.where(allowed, jnp.exp(logits - row_max), jnp.float32(0.0))
    totals = jnp.sum(probs, axis=-1, keepdims=True)
    attn_weights = (probs / totals).astype(jnp.bfloat16)
    attn_out = jnp.einsum(
        "ckgst,ctkd->cskgd", attn_weights, value_tiles, preferred_element_type=jnp.float32
    )
    return attn_out.astype(jnp.bfloat16).reshape(row_count, heads_here * HEAD_WIDTH)


def trunk_kernel(*refs):
    acts, w_ref, residual_ref, out_ref = refs[:8], refs[8], refs[9], refs[10]
    total = residual_ref[...].astype(jnp.float32)
    for slot in range(8):
        total = total + jnp.dot(
            acts[slot][...], w_ref[slot, 0], preferred_element_type=jnp.float32
        )
    out_ref[...] = total.astype(jnp.bfloat16)


def trunk_matmul(acts, weights, residual):
    rows, depth = acts[0].shape
    half = weights.shape[-1]
    width = 256
    per = half // width
    whole = pl.BlockSpec((rows, depth), lambda j: (0, 0), pipeline_mode=pl.Buffered(1))
    tile = pl.BlockSpec((rows, width), lambda j: (0, j))
    return pl.pallas_call(
        trunk_kernel,
        grid=(CORE * per,),
        in_specs=[whole] * 8
        + [pl.BlockSpec((8, 1, depth, width), lambda j: (0, j // per, 0, j % per)), tile],
        out_specs=tile,
        out_shape=jax.ShapeDtypeStruct(residual.shape, jnp.bfloat16),
        compiler_params=pltpu.CompilerParams(vmem_limit_bytes=40 * 2**20),
        cost_estimate=pl.CostEstimate(
            flops=2 * rows * 8 * depth * CORE * half,
            bytes_accessed=2 * (8 * rows * depth + 8 * depth * CORE * half),
            transcendentals=0,
        ),
        name="trunk_matmul",
    )(*acts, weights, residual)


def norm_kernel(place_ref, p0, p1, p2, p3, gain_ref, out_ref):
    pieces = (p0, p1, p2, p3)
    z = place_ref[0]
    group = p0.shape[1] // Z
    width = p0.shape[2]
    per_z = p0.shape[0]
    scales = []
    for r in range(Z):
        square = jnp.zeros((group, 1), jnp.float32)
        for s in range(Z):
            for q in range(per_z):
                rows = pieces[s][q, pl.ds(((r - s) % Z) * group, group), :].astype(jnp.float32)
                square = square + jnp.sum(rows * rows, axis=-1, keepdims=True)
        scales.append(lax.rsqrt(square / (Z * per_z * width) + 1e-05))
    for s in range(Z):
        for q in range(per_z):
            start = pl.multiple_of((lax.rem(z + s, Z) * per_z + q) * width, width)
            gain = gain_ref[:, pl.ds(start, width)]
            for r in range(Z):
                rows = pieces[s][q, pl.ds(((r - s) % Z) * group, group), :].astype(jnp.float32)
                out_ref[pl.ds(r * group, group), pl.ds(start, width)] = (
                    rows * scales[r] * gain
                ).astype(jnp.bfloat16)


def normalize(pieces, gain, z):
    per_z, rows, width = pieces[0].shape
    total = Z * per_z * width
    return pl.pallas_call(
        norm_kernel,
        in_specs=[pl.BlockSpec(memory_space=pltpu.SMEM)]
        + [pl.BlockSpec(memory_space=pltpu.VMEM)] * 5,
        out_specs=pl.BlockSpec(memory_space=pltpu.VMEM),
        out_shape=jax.ShapeDtypeStruct((rows, total), jnp.bfloat16),
        cost_estimate=pl.CostEstimate(
            flops=8 * rows * total, bytes_accessed=4 * rows * total, transcendentals=rows
        ),
        name="normalize",
    )(z[None], *pieces, gain[None, :])


def local(
    query,
    keys,
    values,
    residual,
    out_weight,
    norm_gain,
    cand_len,
    head_w1,
    head_b1,
    head_w2,
    head_b2,
    head_w3,
    head_b3,
):
    z = lax.axis_index("z")
    xl = lax.axis_index("xl")
    core = lax.axis_index("core")
    y = lax.axis_index("y")
    xh = lax.axis_index("xh")
    cand_count = cand_len.shape[0]

    moved = lax.ppermute(out_weight, ALL, weight_moves())
    attn_out = attention(query, keys, values, cand_len)

    last_rows = jnp.arange(cand_count, dtype=jnp.int32) * SEQUENCE_SLOTS + cand_len - 1
    picked = jnp.concatenate(
        [jnp.take(attn_out, last_rows, axis=0), jnp.take(residual, last_rows, axis=0)], axis=1
    )
    near = lax.all_gather(picked, ("xl", "core"), axis=0, tiled=True)
    rows = jnp.concatenate([near] + [from_ahead(near, "z", Z, s) for s in (1, 2, 3)], axis=0)
    width = out_weight.shape[1]
    own = jnp.dot(rows[:, : attn_out.shape[1]], out_weight, preferred_element_type=jnp.float32)
    res = rows[:, attn_out.shape[1] :]
    res = jnp.where(core == 0, res[:, :width], res[:, width:]).astype(jnp.float32)
    own = jnp.where((y == z) & (xh == xl), own + res, own).astype(jnp.bfloat16)
    pair = jnp.stack([own, from_ahead(own, "xh", XH, 1)])
    parts = [pair] + [from_ahead(pair, "y", Y, s) for s in (1, 2, 3)]
    pooled = sum(jnp.sum(p.astype(jnp.float32), axis=0) for p in parts).astype(jnp.bfloat16)
    moved, bulk, _ = lax.optimization_barrier((moved, attn_out, pooled))
    near = lax.all_gather(pooled, ("xl", "core"), axis=0, tiled=False)
    pieces = [near] + [from_ahead(near, "z", Z, s) for s in (1, 2, 3)]
    features = normalize(pieces, norm_gain, z)
    first = jax.nn.silu(
        jnp.dot(features, head_w1[0], preferred_element_type=jnp.float32) + head_b1[0]
    ).astype(jnp.bfloat16)
    terms = jnp.dot(first, head_w2[0], preferred_element_type=jnp.float32).astype(jnp.bfloat16)
    count = terms.shape[0] // Y
    terms = lax.all_to_all(
        terms.reshape(Y, count, terms.shape[1]), "y", split_axis=0, concat_axis=0, tiled=True
    )
    half = jnp.sum(terms.astype(jnp.float32), axis=0).astype(jnp.bfloat16)
    other = from_ahead(half, "xh", XH, 1)
    second = jax.nn.silu(half.astype(jnp.float32) + other.astype(jnp.float32) + head_b2[0])
    mine = jnp.sum(second * head_w3[0].astype(jnp.float32), axis=-1) + head_b3[0]
    scores = lax.all_gather(mine, "y", axis=0, tiled=False)
    scores = jnp.roll(scores, z, axis=0).reshape(1, Y * count)

    weights = lax.all_gather(moved, MEMBER, axis=0, tiled=False)
    weights = weights.reshape((Z * XL, CORE) + out_weight.shape)
    acts = {}
    for e in range(XH):
        base = bulk if e == 0 else from_ahead(bulk, "xh", XH, 1)
        acts[0, e] = base
        for s in (1, 3, 2):
            acts[s, e] = from_ahead(base, "y", Y, s)
    ordered = [acts[s, e] for s in range(Y) for e in range(XH)]
    trunk_out = trunk_matmul(ordered, weights, residual)
    return (trunk_out, scores)


def solution(mesh):
    fine = Mesh(mesh.devices.reshape(Z, XL, CORE, Y, XH), ALL)
    in_specs = (
        P(MEMBER, TENSOR),
        P(MEMBER, TENSOR),
        P(MEMBER, TENSOR),
        P(MEMBER, TENSOR),
        P(TENSOR, MEMBER),
        P(),
        P(MEMBER),
        P(MEMBER, None, TENSOR),
        P(MEMBER, TENSOR),
        P(MEMBER, TENSOR, None),
        P(MEMBER, None),
        P(MEMBER, None),
        P(MEMBER),
    )
    out_specs = (P(MEMBER, TENSOR), P(MEMBER, None))
    return jax.shard_map(local, mesh=fine, in_specs=in_specs, out_specs=out_specs, check_vma=False)
```

time: 408 us -> 287 us (0.70)
  waiting for transfers between devices: 323 us -> 47.9 us
  blocking collectives: 34.2 us -> 113 us
  starting transfers between devices: 0.16 us -> 67.3 us
  Pallas kernels: 0 us -> 17.2 us
  matrix products: 25.9 us -> 10.9 us
  local copies, waits for them, and re-layouts: 4.13 us -> 9.12 us
    all_gather x2 -> x1, waiting for transfers between devices: 122 us -> 0.02 us  [local(): weights = lax.all_gather(moved, MEMBER, axis=0, tiled=False)]
    reduce_scatter x1 -> x0, waiting for transfers between devices: 115 us -> none  [local(): lax.psum_scatter(projected.astype(jnp.bfloat16), 'tensor', scatter_dimens...]
    psum x1 -> x0, waiting for transfers between devices: 85.4 us -> none  [local(): lax.psum(hidden_terms.astype(jnp.bfloat16), 'tensor').astype(jnp.float32)]
    unnamed x0 -> x1, blocking collectives: none -> 69.2 us
    ppermute x0 -> x19, starting transfers between devices: none -> 67.3 us  [the longest x18 57.8 us: from_ahead(): return lax.ppermute(x, axis, [(i, (i - step) % size) for i in range(size)])]
    ppermute x0 -> x19, waiting for transfers between devices: none -> 47.9 us  [the longest x18 47.9 us: from_ahead(): return lax.ppermute(x, axis, [(i, (i - step) % size) for i in range(size)])]
    all_to_all x0 -> x1, blocking collectives: none -> 19.1 us  [local(): lax.all_to_all(terms.reshape(Y, count, terms.shape[1]), 'y', split_axis=0...]
    pallas_call x0 -> x2, Pallas kernels: none -> 17.2 us  [the longest x1 14.3 us: trunk_matmul(): pl.pallas_call(trunk_kernel, grid=(CORE * per,), in_specs=[whole] * 8 + [...]
  transfers between devices with their start and end apart: 4 -> 20, of which waited for: 4 -> 10; matrix products, arithmetic and copies ran while one was open for 1% -> 8% of each run, Pallas kernels for 0% -> 1%
where the time goes in v1:
time: 287 us; the launch traced here: 285 us
  blocking collectives  113 us (39%)
  starting transfers between devices  67.3 us (23%)
  waiting for transfers between devices  47.9 us (17%)
  Pallas kernels  17.2 us (6%)
  between operations  15.6 us (5%)
  matrix products  10.9 us (4%)
  local copies, waits for them, and re-layouts  9.12 us (3%)
  other arithmetic  4.59 us (2%)
    unnamed x1, blocking collectives  69.2 us
    ppermute x18, starting transfers between devices, from_ahead(): return lax.ppermute(x, axis, [(i, (i - step) % size) for i in range(size)])  57.8 us
    ppermute x18, waiting for transfers between devices, from_ahead(): return lax.ppermute(x, axis, [(i, (i - step) % size) for i in range(size)])  47.9 us
    all_to_all x1, blocking collectives, local(): lax.all_to_all(terms.reshape(Y, count, terms.shape[1]), 'y', split_axis=0...  19.1 us
    all_gather x1, blocking collectives, local(): near = lax.all_gather(picked, ('xl', 'core'), axis=0, tiled=True)  16.7 us
    pallas_call x1, Pallas kernels, trunk_matmul(): pl.pallas_call(trunk_kernel, grid=(CORE * per,), in_specs=[whole] * 8 + [...  14.3 us
    ppermute x1, starting transfers between devices, local(): moved = lax.ppermute(out_weight, ALL, weight_moves())  9.51 us
    dot_general x1, matrix products, local(): jnp.dot(first, head_w2[0], preferred_element_type=jnp.float32)  8.3 us
  transfers between devices with their start and end apart: 20, of which 10 were waited for; matrix products, arithmetic and copies ran while one was open for 8% of the time, Pallas kernels for 1%

profile of v1, /device:TPU:0, one launch (start us, length us, event | category | flops | bytes accessed | tf_op | source)
XLA Modules:
  0.0 285.4 jit_solution(16696715335925065270)
XLA Ops:
  7.2 9.5 %collective-permute-start = (bf16[1024,512]{1,0:T(8,128)(2,1)}, bf16[1024,512]{1,0:T(8,128)(2,1)}, u32[]{:S(2)}, u32[]{:S(2)}) collective-permute-start(bf16[1024,512]{1,0:T(8,128)(2,1)} %param.19), channel_id=1, source_target_pairs={{0,0},{1,16},{2,32},{3,48},{4,64},{5,80},{6,96},{7,112},{8,8},{9,2... | collective-permute-start | bytes 3145736 | tf_op jit(solution)/shard_map/ppermute | solution.py:162
  23.7 16.7 %all-gather.3 = bf16[4,4,2048]{2,1,0:T(4,128)(2,1)S(1)} all-gather(bf16[1,4,2048]{2,1,0:T(4,128)(2,1)S(1)} %maximum_bitcast_fusion), channel_id=1, replica_groups=mesh['z'=4,'xl'=2,'core'=2,'y'=4,'xh'=2] {'xl','core'}, dimensions={0}, use_global_device_ids=true | all-gather | bytes 81920 | tf_op jit(solution)/shard_map/all_gather | solution.py:169
  40.5 30.8 %collective-permute-start.8 = (bf16[16,2048]{1,0:T(8,128)(2,1)S(1)}, bf16[16,2048]{1,0:T(8,128)(2,1)S(1)}, u32[]{:S(2)}, u32[]{:S(2)}) collective-permute-start(bf16[16,2048]{1,0:T(8,128)(2,1)S(1)} %reshape.169), channel_id=1, source_target_pairs={{0,96},{32,0},{64,32},{96,64},{1,97},{33,1},{65,33},{97,65},{2,98}... | collective-permute-start | bytes 196616 | tf_op jit(solution)/shard_map/ppermute | solution.py:34
  75.2 3.7 %collective-permute-done.9 = bf16[16,2048]{1,0:T(8,128)(2,1)S(1)} collective-permute-done((bf16[16,2048]{1,0:T(8,128)(2,1)S(1)}, bf16[16,2048]{1,0:T(8,128)(2,1)S(1)}, u32[]{:S(2)}, u32[]{:S(2)}) %collective-permute-start.9) | collective-permute-done | bytes 65568 | tf_op jit(solution)/shard_map/ppermute | solution.py:34
  81.4 3.3 %collective-permute-start.11 = (bf16[64,512]{1,0:T(8,128)(2,1)S(1)}, bf16[64,512]{1,0:T(8,128)(2,1)S(1)}, u32[]{:S(2)}, u32[]{:S(2)}) collective-permute-start(bf16[64,512]{1,0:T(8,128)(2,1)S(1)} %fusion.13), channel_id=1, source_target_pairs={{0,1},{1,0},{2,3},{3,2},{4,5},{5,4},{6,7},{7,6},{8,9},{9,8},{10,11... | collective-permute-start | bytes 196616 | tf_op jit(solution)/shard_map/ppermute | solution.py:34
  84.7 4.0 %collective-permute-done.11 = bf16[64,512]{1,0:T(8,128)(2,1)S(1)} collective-permute-done((bf16[64,512]{1,0:T(8,128)(2,1)S(1)}, bf16[64,512]{1,0:T(8,128)(2,1)S(1)}, u32[]{:S(2)}, u32[]{:S(2)}) %collective-permute-start.11) | collective-permute-done | bytes 65568 | tf_op jit(solution)/shard_map/ppermute | solution.py:34
  88.8 2.7 collective-permute-start.13
  92.1 4.9 %collective-permute-done.14 = bf16[2,64,512]{2,1,0:T(8,128)(2,1)S(1)} collective-permute-done((bf16[2,64,512]{2,1,0:T(8,128)(2,1)S(1)}, bf16[2,64,512]{2,1,0:T(8,128)(2,1)S(1)}, u32[]{:S(2)}, u32[]{:S(2)}) %collective-permute-start.14) | collective-permute-done | bytes 131104 | tf_op jit(solution)/shard_map/ppermute | solution.py:34
  97.3 7.7 %all-gather.1 = bf16[256,512]{1,0:T(8,128)(2,1)S(1)} all-gather(bf16[64,512]{1,0:T(8,128)(2,1)S(1)} %add_convert_fusion), channel_id=3, replica_groups=mesh['z'=4,'xl'=2,'core'=2,'y'=4,'xh'=2] {'xl','core'}, dimensions={0}, use_global_device_ids=true | all-gather | bytes 327680 | tf_op jit(solution)/shard_map/all_gather | solution.py:180
  105.0 2.7 collective-permute-start.15
  108.6 11.2 %collective-permute-done.15.p1 = bf16[4,64,512]{2,1,0:T(8,128)(2,1)S(1)} collective-permute-done((bf16[4,64,512]{2,1,0:T(8,128)(2,1)S(1)}, bf16[4,64,512]{2,1,0:T(8,128)(2,1)S(1)}, u32[]{:S(2)}, u32[]{:S(2)}) %collective-permute-start.15) | collective-permute-done | bytes 262176 | tf_op jit(solution)/shard_map/ppermute | solution.py:34
  119.8 4.2 %collective-permute-done.16.p2 = bf16[4,64,512]{2,1,0:T(8,128)(2,1)S(1)} collective-permute-done((bf16[4,64,512]{2,1,0:T(8,128)(2,1)S(1)}, bf16[4,64,512]{2,1,0:T(8,128)(2,1)S(1)}, u32[]{:S(2)}, u32[]{:S(2)}) %collective-permute-start.16) | collective-permute-done | bytes 262176 | tf_op jit(solution)/shard_map/ppermute | solution.py:34
  124.0 7.0 %collective-permute-done.17.p3 = bf16[4,64,512]{2,1,0:T(8,128)(2,1)S(1)} collective-permute-done((bf16[4,64,512]{2,1,0:T(8,128)(2,1)S(1)}, bf16[4,64,512]{2,1,0:T(8,128)(2,1)S(1)}, u32[]{:S(2)}, u32[]{:S(2)}) %collective-permute-start.17) | collective-permute-done | bytes 262176 | tf_op jit(solution)/shard_map/ppermute | solution.py:34
  131.7 2.8 normalize.1
  134.6 3.4 %collective-permute-start.1 = (bf16[512,1024]{1,0:T(8,128)(2,1)S(1)}, bf16[512,1024]{1,0:T(8,128)(2,1)S(1)}, u32[]{:S(2)}, u32[]{:S(2)}) collective-permute-start(bf16[512,1024]{1,0:T(8,128)(2,1)S(1)} %bitcast.76), channel_id=1, source_target_pairs={{0,1},{1,0},{2,3},{3,2},{4,5},{5,4},{6,7},{7,6},{8,9},{9,8},{10,11... | collective-permute-start | bytes 3145736 | tf_op jit(solution)/shard_map/ppermute | solution.py:34
  138.0 2.4 collective-permute-start.2
  140.4 8.3 %convolution_convert_fusion = bf16[64,4096]{1,0:T(8,128)(2,1)} fusion(bf16[1,512,4096]{2,1,0:T(8,128)(2,1)} %param.24, bf16[64,8192]{1,0:T(8,128)(2,1)} %normalize.1, bf16[1,8192,512]{2,1,0:T(8,128)(2,1)} %param.22, f32[512]{0:T(512)S(1)} %bitcast.96), kind=kOutput, calls=%fused_computation.4 | convolution fusion | flops 805765120 | bytes 14157824 | tf_op jit(solution)/shard_map/dot_general | solution.py:186
  148.7 19.1 %all_to_all.5 = bf16[4,16,4096]{2,1,0:T(8,128)(2,1)} all-to-all(bf16[4,16,4096]{2,1,0:T(8,128)(2,1)} %bitcast.83), channel_id=1, replica_groups=mesh['z'=4,'xl'=2,'core'=2,'y'=4,'xh'=2] {'y'}, dimensions={0} | all-to-all | bytes 1048576 | tf_op jit(solution)/shard_map/all_to_all | solution.py:188
  169.4 1.8 collective-permute-start.4
  171.2 2.7 collective-permute-start.6
  173.9 10.3 %collective-permute-done.1.refs_1_ = bf16[512,1024]{1,0:T(8,128)(2,1)S(1)} collective-permute-done((bf16[512,1024]{1,0:T(8,128)(2,1)S(1)}, bf16[512,1024]{1,0:T(8,128)(2,1)S(1)}, u32[]{:S(2)}, u32[]{:S(2)}) %collective-permute-start.1) | collective-permute-done | bytes 1048608 | tf_op jit(solution)/shard_map/ppermute | solution.py:34
  184.1 2.3 collective-permute-start.3
  194.2 69.2 %all-reduce = f32[64]{0:T(128)S(1)} all-reduce(f32[64]{0:T(128)S(1)} %add_dynamic-update-slice_fusion), channel_id=4, replica_groups=mesh['z'=4,'xl'=2,'core'=2,'y'=4,'xh'=2] {'y'}, use_global_device_ids=true, to_apply=%add | all-reduce | flops 64 | bytes 512
  264.2 14.3 %trunk_matmul.1 = bf16[512,1024]{1,0:T(8,128)(2,1)} custom-call(bf16[512,1024]{1,0:T(8,128)(2,1)S(1)} %bitcast.80, bf16[512,1024]{1,0:T(8,128)(2,1)S(1)} %collective-permute-done.1.refs_1_, bf16[512,1024]{1,0:T(8,128)(2,1)} %collective-permute-done.2.refs_2_, bf16[512,1024]{1,0:T(8,128)(2,1)} %collective-permute-done.3.refs_3_, ...), custom_call_target="tpu_custom_call" | custom-call | flops 8589934592 | bytes 25165824 | tf_op jit(solution)/shard_map/trunk_matmul/pallas_call | solution.py:82
  (81 shorter events, 24.5 us)
Async XLA Ops:
  7.2 12.0 %copy-start = (bf16[512,128]{1,0:T(8,128)(2,1)S(1)}, bf16[512,128]{1,0:T(8,128)(2,1)}, u32[]{:S(2)}) copy-start(bf16[512,128]{1,0:T(8,128)(2,1)} %param.16) | copy-start | bytes 393220
  7.2 257.0 %all-gather.6.cloned.1.call-start = ((), (), s32[]{:S(2)}) async-start(), calls=%async_computation.1 | async-start | bytes 17825792 | tf_op jit(solution)/shard_map/all_gather | solution.py:198
  7.2 14.9 %collective-permute-start = (bf16[1024,512]{1,0:T(8,128)(2,1)}, bf16[1024,512]{1,0:T(8,128)(2,1)}, u32[]{:S(2)}, u32[]{:S(2)}) collective-permute-start(bf16[1024,512]{1,0:T(8,128)(2,1)} %param.19), channel_id=1, source_target_pairs={{0,0},{1,16},{2,32},{3,48},{4,64},{5,80},{6,96},{7,112},{8,8},{9,2... | collective-permute-start | bytes 3145736 | tf_op jit(solution)/shard_map/ppermute | solution.py:162
  21.8 58.4 %copy-start.3 = (bf16[1024,512]{1,0:T(8,128)(2,1)S(1)}, bf16[1024,512]{1,0:T(8,128)(2,1)}, u32[]{:S(2)}) copy-start(bf16[1024,512]{1,0:T(8,128)(2,1)} %param.19) | copy-start | bytes 3145732
  40.5 34.1 %collective-permute-start.8 = (bf16[16,2048]{1,0:T(8,128)(2,1)S(1)}, bf16[16,2048]{1,0:T(8,128)(2,1)S(1)}, u32[]{:S(2)}, u32[]{:S(2)}) collective-permute-start(bf16[16,2048]{1,0:T(8,128)(2,1)S(1)} %reshape.169), channel_id=1, source_target_pairs={{0,96},{32,0},{64,32},{96,64},{1,97},{33,1},{65,33},{97,65},{2,98}... | collective-permute-start | bytes 196616 | tf_op jit(solution)/shard_map/ppermute | solution.py:34
  71.3 7.7 %collective-permute-start.9 = (bf16[16,2048]{1,0:T(8,128)(2,1)S(1)}, bf16[16,2048]{1,0:T(8,128)(2,1)S(1)}, u32[]{:S(2)}, u32[]{:S(2)}) collective-permute-start(bf16[16,2048]{1,0:T(8,128)(2,1)S(1)} %reshape.169), channel_id=1, source_target_pairs={{0,64},{32,96},{64,0},{96,32},{1,65},{33,97},{65,1},{97,33},{2,66}... | collective-permute-start | bytes 196616 | tf_op jit(solution)/shard_map/ppermute | solution.py:34
  71.3 8.3 %collective-permute-start.10 = (bf16[16,2048]{1,0:T(8,128)(2,1)S(1)}, bf16[16,2048]{1,0:T(8,128)(2,1)S(1)}, u32[]{:S(2)}, u32[]{:S(2)}) collective-permute-start(bf16[16,2048]{1,0:T(8,128)(2,1)S(1)} %reshape.169), channel_id=1, source_target_pairs={{0,32},{32,64},{64,96},{96,0},{1,33},{33,65},{65,97},{97,1},{2,34}... | collective-permute-start | bytes 196616 | tf_op jit(solution)/shard_map/ppermute | solution.py:34
  81.4 7.3 %collective-permute-start.11 = (bf16[64,512]{1,0:T(8,128)(2,1)S(1)}, bf16[64,512]{1,0:T(8,128)(2,1)S(1)}, u32[]{:S(2)}, u32[]{:S(2)}) collective-permute-start(bf16[64,512]{1,0:T(8,128)(2,1)S(1)} %fusion.13), channel_id=1, source_target_pairs={{0,1},{1,0},{2,3},{3,2},{4,5},{5,4},{6,7},{7,6},{8,9},{9,8},{10,11... | collective-permute-start | bytes 196616 | tf_op jit(solution)/shard_map/ppermute | solution.py:34
  88.7 51.7 %copy-start.7 = (f32[1,512]{1,0:T(1,128)S(1)}, f32[1,512]{1,0:T(1,128)}, u32[]{:S(2)}) copy-start(f32[1,512]{1,0:T(1,128)} %param.23) | copy-start | bytes 6148
  88.7 8.2 %collective-permute-start.14 = (bf16[2,64,512]{2,1,0:T(8,128)(2,1)S(1)}, bf16[2,64,512]{2,1,0:T(8,128)(2,1)S(1)}, u32[]{:S(2)}, u32[]{:S(2)}) collective-permute-start(bf16[2,64,512]{2,1,0:T(8,128)(2,1)S(1)} %pad_maximum_fusion), channel_id=1, source_target_pairs={{0,2},{2,4},{4,6},{6,0},{1,3},{3,5},{5,7},{7,1},{8,10},{10,12},{12... | collective-permute-start | bytes 393224 | tf_op jit(solution)/shard_map/ppermute | solution.py:34
  88.8 8.2 %collective-permute-start.13 = (bf16[2,64,512]{2,1,0:T(8,128)(2,1)S(1)}, bf16[2,64,512]{2,1,0:T(8,128)(2,1)S(1)}, u32[]{:S(2)}, u32[]{:S(2)}) collective-permute-start(bf16[2,64,512]{2,1,0:T(8,128)(2,1)S(1)} %pad_maximum_fusion), channel_id=1, source_target_pairs={{0,4},{2,6},{4,0},{6,2},{1,5},{3,7},{5,1},{7,3},{8,12},{10,14},{12... | collective-permute-start | bytes 393224 | tf_op jit(solution)/shard_map/ppermute | solution.py:34
  91.5 5.8 %collective-permute-start.12 = (bf16[2,64,512]{2,1,0:T(8,128)(2,1)S(1)}, bf16[2,64,512]{2,1,0:T(8,128)(2,1)S(1)}, u32[]{:S(2)}, u32[]{:S(2)}) collective-permute-start(bf16[2,64,512]{2,1,0:T(8,128)(2,1)S(1)} %pad_maximum_fusion), channel_id=1, source_target_pairs={{0,6},{2,0},{4,2},{6,4},{1,7},{3,1},{5,3},{7,5},{8,14},{10,8},{12,... | collective-permute-start | bytes 393224 | tf_op jit(solution)/shard_map/ppermute | solution.py:34
  105.0 26.1 %copy-start.2 = (bf16[256,512]{1,0:T(8,128)(2,1)}, bf16[256,512]{1,0:T(8,128)(2,1)S(1)}, u32[]{:S(2)}) copy-start(bf16[256,512]{1,0:T(8,128)(2,1)S(1)} %all-gather.1) | copy-start | bytes 786436
  105.0 14.8 %collective-permute-start.15 = (bf16[4,64,512]{2,1,0:T(8,128)(2,1)S(1)}, bf16[4,64,512]{2,1,0:T(8,128)(2,1)S(1)}, u32[]{:S(2)}, u32[]{:S(2)}) collective-permute-start(bf16[4,64,512]{2,1,0:T(8,128)(2,1)S(1)} %bitcast.84), channel_id=1, source_target_pairs={{0,96},{32,0},{64,32},{96,64},{1,97},{33,1},{65,33},{97,65},{2,98}... | collective-permute-start | bytes 786440 | tf_op jit(solution)/shard_map/ppermute | solution.py:34
  107.7 16.3 %collective-permute-start.16 = (bf16[4,64,512]{2,1,0:T(8,128)(2,1)S(1)}, bf16[4,64,512]{2,1,0:T(8,128)(2,1)S(1)}, u32[]{:S(2)}, u32[]{:S(2)}) collective-permute-start(bf16[4,64,512]{2,1,0:T(8,128)(2,1)S(1)} %bitcast.85), channel_id=1, source_target_pairs={{0,64},{32,96},{64,0},{96,32},{1,65},{33,97},{65,1},{97,33},{2,66}... | collective-permute-start | bytes 786440 | tf_op jit(solution)/shard_map/ppermute | solution.py:34
  107.7 23.3 %collective-permute-start.17 = (bf16[4,64,512]{2,1,0:T(8,128)(2,1)S(1)}, bf16[4,64,512]{2,1,0:T(8,128)(2,1)S(1)}, u32[]{:S(2)}, u32[]{:S(2)}) collective-permute-start(bf16[4,64,512]{2,1,0:T(8,128)(2,1)S(1)} %bitcast.86), channel_id=1, source_target_pairs={{0,32},{32,64},{64,96},{96,0},{1,33},{33,65},{65,97},{97,1},{2,34}... | collective-permute-start | bytes 786440 | tf_op jit(solution)/shard_map/ppermute | solution.py:34
  134.6 49.6 %collective-permute-start.1 = (bf16[512,1024]{1,0:T(8,128)(2,1)S(1)}, bf16[512,1024]{1,0:T(8,128)(2,1)S(1)}, u32[]{:S(2)}, u32[]{:S(2)}) collective-permute-start(bf16[512,1024]{1,0:T(8,128)(2,1)S(1)} %bitcast.76), channel_id=1, source_target_pairs={{0,1},{1,0},{2,3},{3,2},{4,5},{5,4},{6,7},{7,6},{8,9},{9,8},{10,11... | collective-permute-start | bytes 3145736 | tf_op jit(solution)/shard_map/ppermute | solution.py:34
  138.0 50.4 %collective-permute-start.2 = (bf16[512,1024]{1,0:T(8,128)(2,1)S(1)}, bf16[512,1024]{1,0:T(8,128)(2,1)}, u32[]{:S(2)}, u32[]{:S(2)}) collective-permute-start(bf16[512,1024]{1,0:T(8,128)(2,1)S(1)} %bitcast.77), channel_id=1, source_target_pairs={{0,6},{2,0},{4,2},{6,4},{1,7},{3,1},{5,3},{7,5},{8,14},{10,8},{12,... | collective-permute-start | bytes 3145736 | tf_op jit(solution)/shard_map/ppermute | solution.py:34
  169.0 18.0 %collective-permute-start.18 = (bf16[16,4096]{1,0:T(8,128)(2,1)S(1)}, bf16[16,4096]{1,0:T(8,128)(2,1)S(1)}, u32[]{:S(2)}, u32[]{:S(2)}) collective-permute-start(bf16[16,4096]{1,0:T(8,128)(2,1)S(1)} %reduce_sum.71), channel_id=1, source_target_pairs={{0,1},{1,0},{2,3},{3,2},{4,5},{5,4},{6,7},{7,6},{8,9},{9,8},{10,11... | collective-permute-start | bytes 393224 | tf_op jit(solution)/shard_map/ppermute | solution.py:34
  169.4 94.7 %collective-permute-start.4 = (bf16[512,1024]{1,0:T(8,128)(2,1)S(1)}, bf16[512,1024]{1,0:T(8,128)(2,1)}, u32[]{:S(2)}, u32[]{:S(2)}) collective-permute-start(bf16[512,1024]{1,0:T(8,128)(2,1)S(1)} %bitcast.78), channel_id=1, source_target_pairs={{0,4},{2,6},{4,0},{6,2},{1,5},{3,7},{5,1},{7,3},{8,12},{10,14},{12... | collective-permute-start | bytes 3145736 | tf_op jit(solution)/shard_map/ppermute | solution.py:34
  171.2 92.9 %collective-permute-start.6 = (bf16[512,1024]{1,0:T(8,128)(2,1)S(1)}, bf16[512,1024]{1,0:T(8,128)(2,1)}, u32[]{:S(2)}, u32[]{:S(2)}) collective-permute-start(bf16[512,1024]{1,0:T(8,128)(2,1)S(1)} %bitcast.79), channel_id=1, source_target_pairs={{0,2},{2,4},{4,6},{6,0},{1,3},{3,5},{5,7},{7,1},{8,10},{10,12},{12... | collective-permute-start | bytes 3145736 | tf_op jit(solution)/shard_map/ppermute | solution.py:34
  184.1 80.0 %collective-permute-start.3 = (bf16[512,1024]{1,0:T(8,128)(2,1)S(1)}, bf16[512,1024]{1,0:T(8,128)(2,1)}, u32[]{:S(2)}, u32[]{:S(2)}) collective-permute-start(bf16[512,1024]{1,0:T(8,128)(2,1)S(1)} %collective-permute-done.1.refs_1_), channel_id=1, source_target_pairs={{0,6},{2,0},{4,2},{6,4},{1,7},{3,1},{5,3},{7,5},{8,14},{10,8},{12,... | collective-permute-start | bytes 3145736 | tf_op jit(solution)/shard_map/ppermute | solution.py:34
  187.0 77.1 %collective-permute-start.5 = (bf16[512,1024]{1,0:T(8,128)(2,1)S(1)}, bf16[512,1024]{1,0:T(8,128)(2,1)}, u32[]{:S(2)}, u32[]{:S(2)}) collective-permute-start(bf16[512,1024]{1,0:T(8,128)(2,1)S(1)} %collective-permute-done.1.refs_1_), channel_id=1, source_target_pairs={{0,4},{2,6},{4,0},{6,2},{1,5},{3,7},{5,1},{7,3},{8,12},{10,14},{12... | collective-permute-start | bytes 3145736 | tf_op jit(solution)/shard_map/ppermute | solution.py:34
  188.4 75.7 %collective-permute-start.7 = (bf16[512,1024]{1,0:T(8,128)(2,1)S(1)}, bf16[512,1024]{1,0:T(8,128)(2,1)}, u32[]{:S(2)}, u32[]{:S(2)}) collective-permute-start(bf16[512,1024]{1,0:T(8,128)(2,1)S(1)} %collective-permute-done.1.refs_1_), channel_id=1, source_target_pairs={{0,2},{2,4},{4,6},{6,0},{1,3},{3,5},{5,7},{7,1},{8,10},{10,12},{12... | collective-permute-start | bytes 3145736 | tf_op jit(solution)/shard_map/ppermute | solution.py:34
  (6 other events, 22.1 us)
Sparse Core Ops, SparseCore 0:
  22.2 159.3 all-gather.5

commit v2 on v1

--- a/solution.py
+++ b/solution.py
@@ -63,7 +63,7 @@
 
 
 def trunk_kernel(*refs):
-    acts, w_ref, residual_ref, out_ref = refs[:8], refs[8], refs[9], refs[10]
+    acts, w_ref, residual_ref, out_ref = refs[:8], refs[8], refs[9], refs[11]
     total = residual_ref[...].astype(jnp.float32)
     for slot in range(8):
         total = total + jnp.dot(
@@ -72,7 +72,7 @@
     out_ref[...] = total.astype(jnp.bfloat16)
 
 
-def trunk_matmul(acts, weights, residual):
+def trunk_matmul(acts, weights, residual, token):
     rows, depth = acts[0].shape
     half = weights.shape[-1]
     width = 256
@@ -83,7 +83,8 @@
         trunk_kernel,
         grid=(CORE * per,),
         in_specs=[whole] * 8
-        + [pl.BlockSpec((8, 1, depth, width), lambda j: (0, j // per, 0, j % per)), tile],
+        + [pl.BlockSpec((8, 1, depth, width), lambda j: (0, j // per, 0, j % per)), tile]
+        + [pl.BlockSpec(memory_space=pl.ANY)],
         out_specs=tile,
         out_shape=jax.ShapeDtypeStruct(residual.shape, jnp.bfloat16),
         compiler_params=pltpu.CompilerParams(vmem_limit_bytes=40 * 2**20),
@@ -93,7 +94,7 @@
             transcendentals=0,
         ),
         name="trunk_matmul",
-    )(*acts, weights, residual)
+    )(*acts, weights, residual, token)
 
 
 def norm_kernel(place_ref, p0, p1, p2, p3, gain_ref, out_ref):
@@ -168,6 +169,13 @@
     )
     near = lax.all_gather(picked, ("xl", "core"), axis=0, tiled=True)
     rows = jnp.concatenate([near] + [from_ahead(near, "z", Z, s) for s in (1, 2, 3)], axis=0)
+    acts = {}
+    moved, acts[0, 0], token = lax.optimization_barrier((moved, attn_out, rows))
+    weights = lax.all_gather(moved, MEMBER, axis=0, tiled=False)
+    weights = weights.reshape((Z * XL, CORE) + out_weight.shape)
+    acts[1, 0] = from_ahead(acts[0, 0], "y", Y, 1)
+    acts[3, 0] = from_ahead(acts[0, 0], "y", Y, 3)
+    acts[0, 1] = from_ahead(acts[0, 0], "xh", XH, 1)
     width = out_weight.shape[1]
     own = jnp.dot(rows[:, : attn_out.shape[1]], out_weight, preferred_element_type=jnp.float32)
     res = rows[:, attn_out.shape[1] :]
@@ -176,10 +184,19 @@
     pair = jnp.stack([own, from_ahead(own, "xh", XH, 1)])
     parts = [pair] + [from_ahead(pair, "y", Y, s) for s in (1, 2, 3)]
     pooled = sum(jnp.sum(p.astype(jnp.float32), axis=0) for p in parts).astype(jnp.bfloat16)
-    moved, bulk, _ = lax.optimization_barrier((moved, attn_out, pooled))
+    pooled, acts[1, 0], acts[3, 0], acts[0, 1], acts[0, 0] = lax.optimization_barrier(
+        (pooled, acts[1, 0], acts[3, 0], acts[0, 1], acts[0, 0])
+    )
+    acts[1, 1] = from_ahead(acts[0, 1], "y", Y, 1)
+    acts[3, 1] = from_ahead(acts[0, 1], "y", Y, 3)
     near = lax.all_gather(pooled, ("xl", "core"), axis=0, tiled=False)
     pieces = [near] + [from_ahead(near, "z", Z, s) for s in (1, 2, 3)]
     features = normalize(pieces, norm_gain, z)
+    features, acts[1, 1], acts[3, 1], acts[0, 0], acts[0, 1] = lax.optimization_barrier(
+        (features, acts[1, 1], acts[3, 1], acts[0, 0], acts[0, 1])
+    )
+    acts[2, 0] = from_ahead(acts[0, 0], "y", Y, 2)
+    acts[2, 1] = from_ahead(acts[0, 1], "y", Y, 2)
     first = jax.nn.silu(
         jnp.dot(features, head_w1[0], preferred_element_type=jnp.float32) + head_b1[0]
     ).astype(jnp.bfloat16)
@@ -195,16 +212,8 @@
     scores = lax.all_gather(mine, "y", axis=0, tiled=False)
     scores = jnp.roll(scores, z, axis=0).reshape(1, Y * count)
 
-    weights = lax.all_gather(moved, MEMBER, axis=0, tiled=False)
-    weights = weights.reshape((Z * XL, CORE) + out_weight.shape)
-    acts = {}
-    for e in range(XH):
-        base = bulk if e == 0 else from_ahead(bulk, "xh", XH, 1)
-        acts[0, e] = base
-        for s in (1, 3, 2):
-            acts[s, e] = from_ahead(base, "y", Y, s)
     ordered = [acts[s, e] for s in range(Y) for e in range(XH)]
-    trunk_out = trunk_matmul(ordered, weights, residual)
+    trunk_out = trunk_matmul(ordered, weights, residual, token)
     return (trunk_out, scores)
 
 

time: 287 us -> 283 us (0.986)
  waiting for transfers between devices: 47.9 us -> 86.1 us
  blocking collectives: 113 us -> 76.8 us
  starting transfers between devices: 67.3 us -> 56.4 us
  local copies, waits for them, and re-layouts: 9.12 us -> 13.4 us
    ppermute x18, waiting for transfers between devices: 47.9 us -> 78.6 us  [from_ahead(): return lax.ppermute(x, axis, [(i, (i - step) % size) for i in range(size)])]
    unnamed x1, blocking collectives: 69.2 us -> 49.1 us
    all_to_all x1 -> x0, blocking collectives: 19.1 us -> none  [local(): lax.all_to_all(terms.reshape(Y, count, terms.shape[1]), 'y', split_axis=0...]
    ppermute x18, starting transfers between devices: 57.8 us -> 50.1 us  [from_ahead(): return lax.ppermute(x, axis, [(i, (i - step) % size) for i in range(size)])]
    ppermute x1, starting transfers between devices: 9.51 us -> 1.88 us  [local(): moved = lax.ppermute(out_weight, ALL, weight_moves())]
    all_to_all x0 -> x1, waiting for transfers between devices: none -> 7.39 us  [local(): lax.all_to_all(terms.reshape(Y, count, terms.shape[1]), 'y', split_axis=0...]
    unnamed x28 -> x34, local copies, waits for them, and re-layouts: 5.97 us -> 10.9 us
    all_to_all x0 -> x1, starting transfers between devices: none -> 4.31 us  [local(): lax.all_to_all(terms.reshape(Y, count, terms.shape[1]), 'y', split_axis=0...]
  transfers between devices with their start and end apart: 20 -> 21, of which waited for: 10 -> 9; matrix products, arithmetic and copies ran while one was open for 8% -> 9% of each run, Pallas kernels for 1% -> 1%
where the time goes in v2:
time: 283 us; the launch traced here: 282 us
  waiting for transfers between devices  86.1 us (30%)
  blocking collectives  76.8 us (27%)
  starting transfers between devices  56.4 us (20%)
  Pallas kernels  16.5 us (6%)
  between operations  15.6 us (6%)
  local copies, waits for them, and re-layouts  13.4 us (5%)
  matrix products  10.9 us (4%)
  other arithmetic  6.14 us (2%)
    ppermute x18, waiting for transfers between devices, from_ahead(): return lax.ppermute(x, axis, [(i, (i - step) % size) for i in range(size)])  78.6 us
    ppermute x18, starting transfers between devices, from_ahead(): return lax.ppermute(x, axis, [(i, (i - step) % size) for i in range(size)])  50.1 us
    unnamed x1, blocking collectives  49.1 us
    all_gather x1, blocking collectives, local(): near = lax.all_gather(picked, ('xl', 'core'), axis=0, tiled=True)  20.5 us
    pallas_call x1, Pallas kernels, trunk_matmul(): pl.pallas_call(trunk_kernel, grid=(CORE * per,), in_specs=[whole] * 8 + [...  13.7 us
    unnamed x34, local copies, waits for them, and re-layouts  10.9 us
    dot_general x1, matrix products, local(): jnp.dot(first, head_w2[0], preferred_element_type=jnp.float32)  8.08 us
    all_to_all x1, waiting for transfers between devices, local(): lax.all_to_all(terms.reshape(Y, count, terms.shape[1]), 'y', split_axis=0...  7.39 us
  transfers between devices with their start and end apart: 21, of which 9 were waited for; matrix products, arithmetic and copies ran while one was open for 9% of the time, Pallas kernels for 1%

profile of v2, /device:TPU:0, one launch (start us, length us, event | category | flops | bytes accessed | tf_op | source)
XLA Modules:
  0.0 281.8 jit_solution(1331903631037326357)
XLA Ops:
  7.2 1.9 collective-permute-start.7
  16.6 20.5 %all-gather.3 = bf16[4,4,2048]{2,1,0:T(4,128)(2,1)S(1)} all-gather(bf16[1,4,2048]{2,1,0:T(4,128)(2,1)S(1)} %maximum_bitcast_fusion), channel_id=1, replica_groups=mesh['z'=4,'xl'=2,'core'=2,'y'=4,'xh'=2] {'xl','core'}, dimensions={0}, use_global_device_ids=true | all-gather | bytes 81920 | tf_op jit(solution)/shard_map/all_gather | solution.py:170
  37.7 23.7 %collective-permute-start.2 = (bf16[16,2048]{1,0:T(8,128)(2,1)}, bf16[16,2048]{1,0:T(8,128)(2,1)S(1)}, u32[]{:S(2)}, u32[]{:S(2)}) collective-permute-start(bf16[16,2048]{1,0:T(8,128)(2,1)} %reshape.137), channel_id=1, source_target_pairs={{0,32},{32,64},{64,96},{96,0},{1,33},{33,65},{65,97},{97,1},{2,34}... | collective-permute-start | bytes 196616 | tf_op jit(solution)/shard_map/ppermute | solution.py:34
  61.4 2.5 collective-permute-start.1
  65.4 3.0 %collective-permute-done = bf16[16,2048]{1,0:T(8,128)(2,1)S(1)} collective-permute-done((bf16[16,2048]{1,0:T(8,128)(2,1)}, bf16[16,2048]{1,0:T(8,128)(2,1)S(1)}, u32[]{:S(2)}, u32[]{:S(2)}) %collective-permute-start) | collective-permute-done | bytes 65568 | tf_op jit(solution)/shard_map/ppermute | solution.py:34
  69.5 5.7 %collective-permute-start.10 = (bf16[512,1024]{1,0:T(8,128)(2,1)S(1)}, bf16[512,1024]{1,0:T(8,128)(2,1)S(1)}, u32[]{:S(2)}, u32[]{:S(2)}) collective-permute-start(bf16[512,1024]{1,0:T(8,128)(2,1)S(1)} %bitcast.76), channel_id=1, source_target_pairs={{0,1},{1,0},{2,3},{3,2},{4,5},{5,4},{6,7},{7,6},{8,9},{9,8},{10,11... | collective-permute-start | bytes 3145736 | tf_op jit(solution)/shard_map/ppermute | solution.py:34
  75.2 3.2 %collective-permute-start.8 = (bf16[512,1024]{1,0:T(8,128)(2,1)S(1)}, bf16[512,1024]{1,0:T(8,128)(2,1)S(1)}, u32[]{:S(2)}, u32[]{:S(2)}) collective-permute-start(bf16[512,1024]{1,0:T(8,128)(2,1)S(1)} %bitcast.78), channel_id=1, source_target_pairs={{0,6},{2,0},{4,2},{6,4},{1,7},{3,1},{5,3},{7,5},{8,14},{10,8},{12,... | collective-permute-start | bytes 3145736 | tf_op jit(solution)/shard_map/ppermute | solution.py:34
  80.1 38.0 %collective-permute-done.3 = bf16[64,512]{1,0:T(8,128)(2,1)S(1)} collective-permute-done((bf16[64,512]{1,0:T(8,128)(2,1)S(1)}, bf16[64,512]{1,0:T(8,128)(2,1)S(1)}, u32[]{:S(2)}, u32[]{:S(2)}) %collective-permute-start.3) | collective-permute-done | bytes 65568 | tf_op jit(solution)/shard_map/ppermute | solution.py:34
  119.4 5.3 %collective-permute-done.5 = bf16[2,64,512]{2,1,0:T(8,128)(2,1)S(1)} collective-permute-done((bf16[2,64,512]{2,1,0:T(8,128)(2,1)S(1)}, bf16[2,64,512]{2,1,0:T(8,128)(2,1)S(1)}, u32[]{:S(2)}, u32[]{:S(2)}) %collective-permute-start.5) | collective-permute-done | bytes 131104 | tf_op jit(solution)/shard_map/ppermute | solution.py:34
  124.7 7.5 %collective-permute-done.6 = bf16[2,64,512]{2,1,0:T(8,128)(2,1)S(1)} collective-permute-done((bf16[2,64,512]{2,1,0:T(8,128)(2,1)S(1)}, bf16[2,64,512]{2,1,0:T(8,128)(2,1)S(1)}, u32[]{:S(2)}, u32[]{:S(2)}) %collective-permute-start.6) | collective-permute-done | bytes 131104 | tf_op jit(solution)/shard_map/ppermute | solution.py:34
  134.3 3.2 %collective-permute-start.14 = (bf16[512,1024]{1,0:T(8,128)(2,1)S(1)}, bf16[512,1024]{1,0:T(8,128)(2,1)}, u32[]{:S(2)}, u32[]{:S(2)}) collective-permute-start(bf16[512,1024]{1,0:T(8,128)(2,1)S(1)} %collective-permute-done.10.refs_1_), channel_id=1, source_target_pairs={{0,6},{2,0},{4,2},{6,4},{1,7},{3,1},{5,3},{7,5},{8,14},{10,8},{12,... | collective-permute-start | bytes 3145736 | tf_op jit(solution)/shard_map/ppermute | solution.py:34
  137.6 7.1 %all-gather = bf16[256,512]{1,0:T(8,128)(2,1)S(1)} all-gather(bf16[64,512]{1,0:T(8,128)(2,1)S(1)} %add_convert_fusion), channel_id=2, replica_groups=mesh['z'=4,'xl'=2,'core'=2,'y'=4,'xh'=2] {'xl','core'}, dimensions={0}, use_global_device_ids=true | all-gather | bytes 327680 | tf_op jit(solution)/shard_map/all_gather | solution.py:192
  146.0 1.9 collective-permute-start.11
  147.9 9.0 %collective-permute-done.13.p3 = bf16[4,64,512]{2,1,0:T(8,128)(2,1)S(1)} collective-permute-done((bf16[4,64,512]{2,1,0:T(8,128)(2,1)S(1)}, bf16[4,64,512]{2,1,0:T(8,128)(2,1)S(1)}, u32[]{:S(2)}, u32[]{:S(2)}) %collective-permute-start.13) | collective-permute-done | bytes 262176 | tf_op jit(solution)/shard_map/ppermute | solution.py:34
  156.9 12.6 %collective-permute-done.12.p2 = bf16[4,64,512]{2,1,0:T(8,128)(2,1)S(1)} collective-permute-done((bf16[4,64,512]{2,1,0:T(8,128)(2,1)S(1)}, bf16[4,64,512]{2,1,0:T(8,128)(2,1)S(1)}, u32[]{:S(2)}, u32[]{:S(2)}) %collective-permute-start.12) | collective-permute-done | bytes 262176 | tf_op jit(solution)/shard_map/ppermute | solution.py:34
  169.5 2.7 collective-permute-done.11.p1
  172.9 2.8 normalize.1
  175.7 8.1 %convolution_convert_fusion = bf16[64,4096]{1,0:T(8,128)(2,1)} fusion(bf16[1,512,4096]{2,1,0:T(8,128)(2,1)} %param.24, bf16[64,8192]{1,0:T(8,128)(2,1)} %normalize.1, bf16[1,8192,512]{2,1,0:T(8,128)(2,1)} %param.22, f32[512]{0:T(512)S(1)} %bitcast.96), kind=kOutput, calls=%fused_computation.4 | convolution fusion | flops 805765120 | bytes 14157824 | tf_op jit(solution)/shard_map/dot_general | solution.py:203
  183.8 4.3 %all-to-all-start = ((bf16[4,16,4096]{2,1,0:T(8,128)(2,1)}), bf16[4,16,4096]{2,1,0:T(8,128)(2,1)}, u32[]{:S(2)}, u32[]{:S(2)}) async-start(bf16[4,16,4096]{2,1,0:T(8,128)(2,1)} %bitcast.83), calls=%async_computation | async-start | bytes 1048576 | tf_op jit(solution)/shard_map/all_to_all | solution.py:205
  188.1 3.5 %collective-permute-start.16 = (bf16[512,1024]{1,0:T(8,128)(2,1)S(1)}, bf16[512,1024]{1,0:T(8,128)(2,1)}, u32[]{:S(2)}, u32[]{:S(2)}) collective-permute-start(bf16[512,1024]{1,0:T(8,128)(2,1)S(1)} %bitcast.79), channel_id=1, source_target_pairs={{0,4},{2,6},{4,0},{6,2},{1,5},{3,7},{5,1},{7,3},{8,12},{10,14},{12... | collective-permute-start | bytes 3145736 | tf_op jit(solution)/shard_map/ppermute | solution.py:34
  191.7 7.4 %all-to-all-done = bf16[4,16,4096]{2,1,0:T(8,128)(2,1)} async-done(((bf16[4,16,4096]{2,1,0:T(8,128)(2,1)}), bf16[4,16,4096]{2,1,0:T(8,128)(2,1)}, u32[]{:S(2)}, u32[]{:S(2)}) %all-to-all-start) | async-done | bytes 524320 | tf_op jit(solution)/shard_map/all_to_all | solution.py:205
  200.9 2.9 %collective-permute-start.18 = (bf16[16,4096]{1,0:T(8,128)(2,1)}, bf16[16,4096]{1,0:T(8,128)(2,1)}, u32[]{:S(2)}, u32[]{:S(2)}) collective-permute-start(bf16[16,4096]{1,0:T(8,128)(2,1)} %reduce_sum.71), channel_id=1, source_target_pairs={{0,1},{1,0},{2,3},{3,2},{4,5},{5,4},{6,7},{7,6},{8,9},{9,8},{10,11... | collective-permute-start | bytes 393224 | tf_op jit(solution)/shard_map/ppermute | solution.py:34
  209.0 49.1 %all-reduce = f32[64]{0:T(128)S(1)} all-reduce(f32[64]{0:T(128)S(1)} %add_dynamic-update-slice_fusion), channel_id=4, replica_groups=mesh['z'=4,'xl'=2,'core'=2,'y'=4,'xh'=2] {'y'}, use_global_device_ids=true, to_apply=%add | all-reduce | flops 64 | bytes 512
  261.3 13.7 %trunk_matmul.1 = bf16[512,1024]{1,0:T(8,128)(2,1)} custom-call(bf16[512,1024]{1,0:T(8,128)(2,1)S(1)} %bitcast.80, bf16[512,1024]{1,0:T(8,128)(2,1)S(1)} %collective-permute-done.10.refs_1_, bf16[512,1024]{1,0:T(8,128)(2,1)S(1)} %copy-done.5, bf16[512,1024]{1,0:T(8,128)(2,1)} %collective-permute-done.14.refs_3_, ...), custom_call_target="tpu_custom_call" | custom-call | flops 8589934592 | bytes 25165824 | tf_op jit(solution)/shard_map/trunk_matmul/pallas_call | solution.py:82
  (88 shorter events, 26.6 us)
Async XLA Ops:
  7.2 5.0 %copy-start = (bf16[512,128]{1,0:T(8,128)(2,1)S(1)}, bf16[512,128]{1,0:T(8,128)(2,1)}, u32[]{:S(2)}) copy-start(bf16[512,128]{1,0:T(8,128)(2,1)} %param.16) | copy-start | bytes 393220
  7.2 251.7 %all-gather.6.cloned.1.call-start = ((), (), s32[]{:S(2)}) async-start(), calls=%async_computation.1 | async-start | bytes 17825792 | tf_op jit(solution)/shard_map/all_gather | solution.py:174
  7.2 61.2 %collective-permute-start.7 = (bf16[1024,512]{1,0:T(8,128)(2,1)}, bf16[1024,512]{1,0:T(8,128)(2,1)S(1)}, u32[]{:S(2)}, u32[]{:S(2)}) collective-permute-start(bf16[1024,512]{1,0:T(8,128)(2,1)} %param.19), channel_id=1, source_target_pairs={{0,0},{1,16},{2,32},{3,48},{4,64},{5,80},{6,96},{7,112},{8,8},{9,2... | collective-permute-start | bytes 3145736 | tf_op jit(solution)/shard_map/ppermute | solution.py:163
  37.7 30.7 %collective-permute-start.2 = (bf16[16,2048]{1,0:T(8,128)(2,1)}, bf16[16,2048]{1,0:T(8,128)(2,1)S(1)}, u32[]{:S(2)}, u32[]{:S(2)}) collective-permute-start(bf16[16,2048]{1,0:T(8,128)(2,1)} %reshape.137), channel_id=1, source_target_pairs={{0,32},{32,64},{64,96},{96,0},{1,33},{33,65},{65,97},{97,1},{2,34}... | collective-permute-start | bytes 196616 | tf_op jit(solution)/shard_map/ppermute | solution.py:34
  61.4 7.0 %collective-permute-start.1 = (bf16[16,2048]{1,0:T(8,128)(2,1)}, bf16[16,2048]{1,0:T(8,128)(2,1)S(1)}, u32[]{:S(2)}, u32[]{:S(2)}) collective-permute-start(bf16[16,2048]{1,0:T(8,128)(2,1)} %reshape.137), channel_id=1, source_target_pairs={{0,64},{32,96},{64,0},{96,32},{1,65},{33,97},{65,1},{97,33},{2,66}... | collective-permute-start | bytes 196616 | tf_op jit(solution)/shard_map/ppermute | solution.py:34
  63.9 4.5 %collective-permute-start = (bf16[16,2048]{1,0:T(8,128)(2,1)}, bf16[16,2048]{1,0:T(8,128)(2,1)S(1)}, u32[]{:S(2)}, u32[]{:S(2)}) collective-permute-start(bf16[16,2048]{1,0:T(8,128)(2,1)} %reshape.137), channel_id=1, source_target_pairs={{0,96},{32,0},{64,32},{96,64},{1,97},{33,1},{65,33},{97,65},{2,98}... | collective-permute-start | bytes 196616 | tf_op jit(solution)/shard_map/ppermute | solution.py:34
  69.5 62.9 %collective-permute-start.10 = (bf16[512,1024]{1,0:T(8,128)(2,1)S(1)}, bf16[512,1024]{1,0:T(8,128)(2,1)S(1)}, u32[]{:S(2)}, u32[]{:S(2)}) collective-permute-start(bf16[512,1024]{1,0:T(8,128)(2,1)S(1)} %bitcast.76), channel_id=1, source_target_pairs={{0,1},{1,0},{2,3},{3,2},{4,5},{5,4},{6,7},{7,6},{8,9},{9,8},{10,11... | collective-permute-start | bytes 3145736 | tf_op jit(solution)/shard_map/ppermute | solution.py:34
  75.2 57.2 %collective-permute-start.9 = (bf16[512,1024]{1,0:T(8,128)(2,1)S(1)}, bf16[512,1024]{1,0:T(8,128)(2,1)S(1)}, u32[]{:S(2)}, u32[]{:S(2)}) collective-permute-start(bf16[512,1024]{1,0:T(8,128)(2,1)S(1)} %bitcast.77), channel_id=1, source_target_pairs={{0,2},{2,4},{4,6},{6,0},{1,3},{3,5},{5,7},{7,1},{8,10},{10,12},{12... | collective-permute-start | bytes 3145736 | tf_op jit(solution)/shard_map/ppermute | solution.py:34
  75.2 58.2 %collective-permute-start.8 = (bf16[512,1024]{1,0:T(8,128)(2,1)S(1)}, bf16[512,1024]{1,0:T(8,128)(2,1)S(1)}, u32[]{:S(2)}, u32[]{:S(2)}) collective-permute-start(bf16[512,1024]{1,0:T(8,128)(2,1)S(1)} %bitcast.78), channel_id=1, source_target_pairs={{0,6},{2,0},{4,2},{6,4},{1,7},{3,1},{5,3},{7,5},{8,14},{10,8},{12,... | collective-permute-start | bytes 3145736 | tf_op jit(solution)/shard_map/ppermute | solution.py:34
  79.9 38.2 %collective-permute-start.3 = (bf16[64,512]{1,0:T(8,128)(2,1)S(1)}, bf16[64,512]{1,0:T(8,128)(2,1)S(1)}, u32[]{:S(2)}, u32[]{:S(2)}) collective-permute-start(bf16[64,512]{1,0:T(8,128)(2,1)S(1)} %fusion.13), channel_id=1, source_target_pairs={{0,1},{1,0},{2,3},{3,2},{4,5},{5,4},{6,7},{7,6},{8,9},{9,8},{10,11... | collective-permute-start | bytes 196616 | tf_op jit(solution)/shard_map/ppermute | solution.py:34
  118.1 57.6 %copy-start.11 = (f32[1,512]{1,0:T(1,128)S(1)}, f32[1,512]{1,0:T(1,128)}, u32[]{:S(2)}) copy-start(f32[1,512]{1,0:T(1,128)} %param.23) | copy-start | bytes 6148
  118.1 6.6 %collective-permute-start.5 = (bf16[2,64,512]{2,1,0:T(8,128)(2,1)S(1)}, bf16[2,64,512]{2,1,0:T(8,128)(2,1)S(1)}, u32[]{:S(2)}, u32[]{:S(2)}) collective-permute-start(bf16[2,64,512]{2,1,0:T(8,128)(2,1)S(1)} %pad_maximum_fusion), channel_id=1, source_target_pairs={{0,4},{2,6},{4,0},{6,2},{1,5},{3,7},{5,1},{7,3},{8,12},{10,14},{12... | collective-permute-start | bytes 393224 | tf_op jit(solution)/shard_map/ppermute | solution.py:34
  118.2 6.5 %collective-permute-start.4 = (bf16[2,64,512]{2,1,0:T(8,128)(2,1)S(1)}, bf16[2,64,512]{2,1,0:T(8,128)(2,1)S(1)}, u32[]{:S(2)}, u32[]{:S(2)}) collective-permute-start(bf16[2,64,512]{2,1,0:T(8,128)(2,1)S(1)} %pad_maximum_fusion), channel_id=1, source_target_pairs={{0,6},{2,0},{4,2},{6,4},{1,7},{3,1},{5,3},{7,5},{8,14},{10,8},{12,... | collective-permute-start | bytes 393224 | tf_op jit(solution)/shard_map/ppermute | solution.py:34
  124.7 7.6 %collective-permute-start.6 = (bf16[2,64,512]{2,1,0:T(8,128)(2,1)S(1)}, bf16[2,64,512]{2,1,0:T(8,128)(2,1)S(1)}, u32[]{:S(2)}, u32[]{:S(2)}) collective-permute-start(bf16[2,64,512]{2,1,0:T(8,128)(2,1)S(1)} %pad_maximum_fusion), channel_id=1, source_target_pairs={{0,2},{2,4},{4,6},{6,0},{1,3},{3,5},{5,7},{7,1},{8,10},{10,12},{12... | collective-permute-start | bytes 393224 | tf_op jit(solution)/shard_map/ppermute | solution.py:34
  134.3 41.4 %collective-permute-start.15 = (bf16[512,1024]{1,0:T(8,128)(2,1)S(1)}, bf16[512,1024]{1,0:T(8,128)(2,1)}, u32[]{:S(2)}, u32[]{:S(2)}) collective-permute-start(bf16[512,1024]{1,0:T(8,128)(2,1)S(1)} %collective-permute-done.10.refs_1_), channel_id=1, source_target_pairs={{0,2},{2,4},{4,6},{6,0},{1,3},{3,5},{5,7},{7,1},{8,10},{10,12},{12... | collective-permute-start | bytes 3145736 | tf_op jit(solution)/shard_map/ppermute | solution.py:34
  134.3 41.4 %collective-permute-start.14 = (bf16[512,1024]{1,0:T(8,128)(2,1)S(1)}, bf16[512,1024]{1,0:T(8,128)(2,1)}, u32[]{:S(2)}, u32[]{:S(2)}) collective-permute-start(bf16[512,1024]{1,0:T(8,128)(2,1)S(1)} %collective-permute-done.10.refs_1_), channel_id=1, source_target_pairs={{0,6},{2,0},{4,2},{6,4},{1,7},{3,1},{5,3},{7,5},{8,14},{10,8},{12,... | collective-permute-start | bytes 3145736 | tf_op jit(solution)/shard_map/ppermute | solution.py:34
  144.7 12.2 %collective-permute-start.13 = (bf16[4,64,512]{2,1,0:T(8,128)(2,1)S(1)}, bf16[4,64,512]{2,1,0:T(8,128)(2,1)S(1)}, u32[]{:S(2)}, u32[]{:S(2)}) collective-permute-start(bf16[4,64,512]{2,1,0:T(8,128)(2,1)S(1)} %bitcast.84), channel_id=1, source_target_pairs={{0,32},{32,64},{64,96},{96,0},{1,33},{33,65},{65,97},{97,1},{2,34}... | collective-permute-start | bytes 786440 | tf_op jit(solution)/shard_map/ppermute | solution.py:34
  144.7 24.8 %collective-permute-start.12 = (bf16[4,64,512]{2,1,0:T(8,128)(2,1)S(1)}, bf16[4,64,512]{2,1,0:T(8,128)(2,1)S(1)}, u32[]{:S(2)}, u32[]{:S(2)}) collective-permute-start(bf16[4,64,512]{2,1,0:T(8,128)(2,1)S(1)} %bitcast.85), channel_id=1, source_target_pairs={{0,64},{32,96},{64,0},{96,32},{1,65},{33,97},{65,1},{97,33},{2,66}... | collective-permute-start | bytes 786440 | tf_op jit(solution)/shard_map/ppermute | solution.py:34
  146.0 26.1 %collective-permute-start.11 = (bf16[4,64,512]{2,1,0:T(8,128)(2,1)S(1)}, bf16[4,64,512]{2,1,0:T(8,128)(2,1)S(1)}, u32[]{:S(2)}, u32[]{:S(2)}) collective-permute-start(bf16[4,64,512]{2,1,0:T(8,128)(2,1)S(1)} %bitcast.86), channel_id=1, source_target_pairs={{0,96},{32,0},{64,32},{96,64},{1,97},{33,1},{65,33},{97,65},{2,98}... | collective-permute-start | bytes 786440 | tf_op jit(solution)/shard_map/ppermute | solution.py:34
  156.9 15.3 %copy-start.8 = (bf16[4,64,512]{2,1,0:T(8,128)(2,1)}, bf16[4,64,512]{2,1,0:T(8,128)(2,1)S(1)}, u32[]{:S(2)}) copy-start(bf16[4,64,512]{2,1,0:T(8,128)(2,1)S(1)} %collective-permute-done.13.p3) | copy-start | bytes 786436
  183.8 15.3 %all-to-all-start = ((bf16[4,16,4096]{2,1,0:T(8,128)(2,1)}), bf16[4,16,4096]{2,1,0:T(8,128)(2,1)}, u32[]{:S(2)}, u32[]{:S(2)}) async-start(bf16[4,16,4096]{2,1,0:T(8,128)(2,1)} %bitcast.83), calls=%async_computation | async-start | bytes 1048576 | tf_op jit(solution)/shard_map/all_to_all | solution.py:205
  188.1 70.7 %collective-permute-start.16 = (bf16[512,1024]{1,0:T(8,128)(2,1)S(1)}, bf16[512,1024]{1,0:T(8,128)(2,1)}, u32[]{:S(2)}, u32[]{:S(2)}) collective-permute-start(bf16[512,1024]{1,0:T(8,128)(2,1)S(1)} %bitcast.79), channel_id=1, source_target_pairs={{0,4},{2,6},{4,0},{6,2},{1,5},{3,7},{5,1},{7,3},{8,12},{10,14},{12... | collective-permute-start | bytes 3145736 | tf_op jit(solution)/shard_map/ppermute | solution.py:34
  191.6 67.2 %collective-permute-start.17 = (bf16[512,1024]{1,0:T(8,128)(2,1)S(1)}, bf16[512,1024]{1,0:T(8,128)(2,1)}, u32[]{:S(2)}, u32[]{:S(2)}) collective-permute-start(bf16[512,1024]{1,0:T(8,128)(2,1)S(1)} %collective-permute-done.10.refs_1_), channel_id=1, source_target_pairs={{0,4},{2,6},{4,0},{6,2},{1,5},{3,7},{5,1},{7,3},{8,12},{10,14},{12... | collective-permute-start | bytes 3145736 | tf_op jit(solution)/shard_map/ppermute | solution.py:34
  200.9 6.8 %collective-permute-start.18 = (bf16[16,4096]{1,0:T(8,128)(2,1)}, bf16[16,4096]{1,0:T(8,128)(2,1)}, u32[]{:S(2)}, u32[]{:S(2)}) collective-permute-start(bf16[16,4096]{1,0:T(8,128)(2,1)} %reduce_sum.71), channel_id=1, source_target_pairs={{0,1},{1,0},{2,3},{3,2},{4,5},{5,4},{6,7},{7,6},{8,9},{9,8},{10,11... | collective-permute-start | bytes 393224 | tf_op jit(solution)/shard_map/ppermute | solution.py:34
  (10 other events, 12.5 us)
Sparse Core Ops, SparseCore 0:
  69.6 109.6 all-gather.5

commit v3 on v1

--- a/solution.py
+++ b/solution.py
@@ -1,4 +1,4 @@
-import functools
+import itertools
 
 import jax
 import jax.numpy as jnp
@@ -19,14 +19,20 @@
     return (((z % Z) * XL + xl % XL) * CORE + core) * Y * XH + (y % Y) * XH + xh % XH
 
 
-def weight_moves():
+def places():
+    return itertools.product(range(Z), range(XL), range(CORE), range(Y), range(XH))
+
+
+def spread_moves(v):
     return [
-        (flat(z, xl, core, y, xh), flat(y - z, xh - xl, core, z, xl))
-        for z in range(Z)
-        for xl in range(XL)
-        for core in range(CORE)
-        for y in range(Y)
-        for xh in range(XH)
+        (flat(z, xl, core, y, xh), flat(z - y - v, xl, core, y, xh)) for z, xl, core, y, xh in places()
+    ]
+
+
+def column_moves(v):
+    return [
+        (flat(z, xl, core, y, xh), flat(z, xh - xl, core, y + z + v, xl))
+        for z, xl, core, y, xh in places()
     ]
 
 
@@ -63,16 +69,20 @@
 
 
 def trunk_kernel(*refs):
-    acts, w_ref, residual_ref, out_ref = refs[:8], refs[8], refs[9], refs[10]
+    acts, w_ref, residual_ref, out_ref = refs[:8], refs[8], refs[9], refs[-1]
     total = residual_ref[...].astype(jnp.float32)
-    for slot in range(8):
-        total = total + jnp.dot(
-            acts[slot][...], w_ref[slot, 0], preferred_element_type=jnp.float32
-        )
+    for a in range(Y):
+        for e in range(XH):
+            block = jnp.concatenate(
+                [w_ref[((-a - v) % Z) * XL + e, 0, v] for v in range(Z)], axis=0
+            )
+            total = total + jnp.dot(
+                acts[a * XH + e][...], block, preferred_element_type=jnp.float32
+            )
     out_ref[...] = total.astype(jnp.bfloat16)
 
 
-def trunk_matmul(acts, weights, residual):
+def trunk_matmul(acts, weights, residual, tokens):
     rows, depth = acts[0].shape
     half = weights.shape[-1]
     width = 256
@@ -83,7 +93,13 @@
         trunk_kernel,
         grid=(CORE * per,),
         in_specs=[whole] * 8
-        + [pl.BlockSpec((8, 1, depth, width), lambda j: (0, j // per, 0, j % per)), tile],
+        + [
+            pl.BlockSpec(
+                (Z * XL, 1, Z, depth // Z, width), lambda j: (0, j // per, 0, 0, j % per)
+            ),
+            tile,
+        ]
+        + [pl.BlockSpec(memory_space=pl.ANY)] * len(tokens),
         out_specs=tile,
         out_shape=jax.ShapeDtypeStruct(residual.shape, jnp.bfloat16),
         compiler_params=pltpu.CompilerParams(vmem_limit_bytes=40 * 2**20),
@@ -93,7 +109,7 @@
             transcendentals=0,
         ),
         name="trunk_matmul",
-    )(*acts, weights, residual)
+    )(*acts, weights, residual, *tokens)
 
 
 def norm_kernel(place_ref, p0, p1, p2, p3, gain_ref, out_ref):
@@ -159,25 +175,43 @@
     xh = lax.axis_index("xh")
     cand_count = cand_len.shape[0]
 
-    moved = lax.ppermute(out_weight, ALL, weight_moves())
-    attn_out = attention(query, keys, values, cand_len)
+    quarter = out_weight.shape[0] // Z
+    moved = [
+        lax.ppermute(out_weight[v * quarter : (v + 1) * quarter], ALL, spread_moves(v))
+        for v in range(Z)
+    ]
+    acts = {}
+    acts[0, 0] = attention(query, keys, values, cand_len)
 
     last_rows = jnp.arange(cand_count, dtype=jnp.int32) * SEQUENCE_SLOTS + cand_len - 1
     picked = jnp.concatenate(
-        [jnp.take(attn_out, last_rows, axis=0), jnp.take(residual, last_rows, axis=0)], axis=1
-    )
+        [jnp.take(acts[0, 0], last_rows, axis=0), jnp.take(residual, last_rows, axis=0)], axis=1
+    )
+    depth = acts[0, 0].shape[1]
     near = lax.all_gather(picked, ("xl", "core"), axis=0, tiled=True)
+    *moved, near = lax.optimization_barrier((*moved, near))
+    moved = [lax.ppermute(m, ALL, column_moves(v)) for v, m in enumerate(moved)]
     rows = jnp.concatenate([near] + [from_ahead(near, "z", Z, s) for s in (1, 2, 3)], axis=0)
     width = out_weight.shape[1]
-    own = jnp.dot(rows[:, : attn_out.shape[1]], out_weight, preferred_element_type=jnp.float32)
-    res = rows[:, attn_out.shape[1] :]
+    own = jnp.dot(rows[:, :depth], out_weight, preferred_element_type=jnp.float32)
+    res = rows[:, depth:]
     res = jnp.where(core == 0, res[:, :width], res[:, width:]).astype(jnp.float32)
     own = jnp.where((y == z) & (xh == xl), own + res, own).astype(jnp.bfloat16)
     pair = jnp.stack([own, from_ahead(own, "xh", XH, 1)])
+    *moved, acts[0, 0], pair = lax.optimization_barrier((*moved, acts[0, 0], pair))
+    weights = lax.all_gather(jnp.stack(moved), MEMBER, axis=0, tiled=False)
+    weights = weights.reshape((Z * XL, CORE, Z, quarter, width))
+    acts[0, 1] = from_ahead(acts[0, 0], "xh", XH, 1)
     parts = [pair] + [from_ahead(pair, "y", Y, s) for s in (1, 2, 3)]
     pooled = sum(jnp.sum(p.astype(jnp.float32), axis=0) for p in parts).astype(jnp.bfloat16)
-    moved, bulk, _ = lax.optimization_barrier((moved, attn_out, pooled))
+    acts[0, 0], token = lax.optimization_barrier((acts[0, 0], pooled))
+    acts[1, 0] = from_ahead(acts[0, 0], "y", Y, 1)
+    acts[3, 0] = from_ahead(acts[0, 0], "y", Y, 3)
     near = lax.all_gather(pooled, ("xl", "core"), axis=0, tiled=False)
+    acts[0, 0], acts[0, 1], near = lax.optimization_barrier((acts[0, 0], acts[0, 1], near))
+    acts[1, 1] = from_ahead(acts[0, 1], "y", Y, 1)
+    acts[3, 1] = from_ahead(acts[0, 1], "y", Y, 3)
+    acts[2, 0] = from_ahead(acts[0, 0], "y", Y, 2)
     pieces = [near] + [from_ahead(near, "z", Z, s) for s in (1, 2, 3)]
     features = normalize(pieces, norm_gain, z)
     first = jax.nn.silu(
@@ -188,6 +222,10 @@
     terms = lax.all_to_all(
         terms.reshape(Y, count, terms.shape[1]), "y", split_axis=0, concat_axis=0, tiled=True
     )
+    terms, acts[0, 1], acts[1, 0], acts[3, 0], acts[1, 1], acts[3, 1] = lax.optimization_barrier(
+        (terms, acts[0, 1], acts[1, 0], acts[3, 0], acts[1, 1], acts[3, 1])
+    )
+    acts[2, 1] = from_ahead(acts[0, 1], "y", Y, 2)
     half = jnp.sum(terms.astype(jnp.float32), axis=0).astype(jnp.bfloat16)
     other = from_ahead(half, "xh", XH, 1)
     second = jax.nn.silu(half.astype(jnp.float32) + other.astype(jnp.float32) + head_b2[0])
@@ -195,16 +233,8 @@
     scores = lax.all_gather(mine, "y", axis=0, tiled=False)
     scores = jnp.roll(scores, z, axis=0).reshape(1, Y * count)
 
-    weights = lax.all_gather(moved, MEMBER, axis=0, tiled=False)
-    weights = weights.reshape((Z * XL, CORE) + out_weight.shape)
-    acts = {}
-    for e in range(XH):
-        base = bulk if e == 0 else from_ahead(bulk, "xh", XH, 1)
-        acts[0, e] = base
-        for s in (1, 3, 2):
-            acts[s, e] = from_ahead(base, "y", Y, s)
-    ordered = [acts[s, e] for s in range(Y) for e in range(XH)]
-    trunk_out = trunk_matmul(ordered, weights, residual)
+    ordered = [acts[a, e] for a in range(Y) for e in range(XH)]
+    trunk_out = trunk_matmul(ordered, weights, residual, (token,))
     return (trunk_out, scores)
 
 

time: 287 us -> 252 us (0.88)
  blocking collectives: 113 us -> 51.3 us
  waiting for transfers between devices: 47.9 us -> 74 us
  starting transfers between devices: 67.3 us -> 71.8 us
    unnamed x1, blocking collectives: 69.2 us -> 10.4 us
    all_to_all x0 -> x1, waiting for transfers between devices: none -> 45.1 us  [local(): lax.all_to_all(terms.reshape(Y, count, terms.shape[1]), 'y', split_axis=0...]
    all_gather x1, blocking collectives: 7.65 us -> 35.7 us  [local(): near = lax.all_gather(pooled, ('xl', 'core'), axis=0, tiled=False)]
    ppermute x1 -> x8, starting transfers between devices: 9.51 us -> 29.7 us  [the longest x4 15.9 us: local(): lax.ppermute(out_weight[v * quarter:(v + 1) * quarter], ALL, spread_moves...]
    ppermute x18, starting transfers between devices: 57.8 us -> 37.9 us  [from_ahead(): return lax.ppermute(x, axis, [(i, (i - step) % size) for i in range(size)])]
    all_to_all x1 -> x0, blocking collectives: 19.1 us -> none  [local(): lax.all_to_all(terms.reshape(Y, count, terms.shape[1]), 'y', split_axis=0...]
    ppermute x18, waiting for transfers between devices: 47.9 us -> 28.9 us  [from_ahead(): return lax.ppermute(x, axis, [(i, (i - step) % size) for i in range(size)])]
    all_gather x1, blocking collectives: 16.7 us -> 5.25 us  [local(): near = lax.all_gather(picked, ('xl', 'core'), axis=0, tiled=True)]
  transfers between devices with their start and end apart: 20 -> 28, of which waited for: 10 -> 9; matrix products, arithmetic and copies ran while one was open for 8% -> 7% of each run, Pallas kernels for 1% -> 1%
where the time goes in v3:
time: 252 us; the launch traced here: 251 us
  waiting for transfers between devices  74 us (29%)
  starting transfers between devices  71.8 us (28%)
  blocking collectives  51.3 us (20%)
  Pallas kernels  17.2 us (7%)
  between operations  15.8 us (6%)
  matrix products  9.96 us (4%)
  local copies, waits for them, and re-layouts  6.93 us (3%)
  other arithmetic  4.5 us (2%)
    all_to_all x1, waiting for transfers between devices, local(): lax.all_to_all(terms.reshape(Y, count, terms.shape[1]), 'y', split_axis=0...  45.1 us
    ppermute x18, starting transfers between devices, from_ahead(): return lax.ppermute(x, axis, [(i, (i - step) % size) for i in range(size)])  37.9 us
    all_gather x1, blocking collectives, local(): near = lax.all_gather(pooled, ('xl', 'core'), axis=0, tiled=False)  35.7 us
    ppermute x18, waiting for transfers between devices, from_ahead(): return lax.ppermute(x, axis, [(i, (i - step) % size) for i in range(size)])  28.9 us
    ppermute x4, starting transfers between devices, local(): lax.ppermute(out_weight[v * quarter:(v + 1) * quarter], ALL, spread_moves...  15.9 us
    pallas_call x1, Pallas kernels, trunk_matmul(): pl.pallas_call(trunk_kernel, grid=(CORE * per,), in_specs=[whole] * 8 + [...  14.3 us
    ppermute x4, starting transfers between devices, local(): moved = [lax.ppermute(m, ALL, column_moves(v)) for v, m in enumerate(moved)]  13.7 us
    unnamed x1, blocking collectives  10.4 us
  transfers between devices with their start and end apart: 28, of which 9 were waited for; matrix products, arithmetic and copies ran while one was open for 7% of the time, Pallas kernels for 1%

profile of v3, /device:TPU:0, one launch (start us, length us, event | category | flops | bytes accessed | tf_op | source)
XLA Modules:
  0.0 251.4 jit_solution(2175378229827164758)
XLA Ops:
  7.2 2.3 fusion.28
  9.5 3.9 %collective-permute-start.3 = (bf16[256,512]{1,0:T(8,128)(2,1)}, bf16[256,512]{1,0:T(8,128)(2,1)}, u32[]{:S(2)}, u32[]{:S(2)}) collective-permute-start(bf16[256,512]{1,0:T(8,128)(2,1)} %get-tuple-element.49), channel_id=1, source_target_pairs={{0,32},{1,33},{2,2},{3,3},{4,100},{5,101},{6,70},{7,71},{8,40},{9,... | collective-permute-start | bytes 786440 | tf_op jit(solution)/shard_map/ppermute | solution.py:180
  13.4 5.5 %collective-permute-start.2 = (bf16[256,512]{1,0:T(8,128)(2,1)}, bf16[256,512]{1,0:T(8,128)(2,1)}, u32[]{:S(2)}, u32[]{:S(2)}) collective-permute-start(bf16[256,512]{1,0:T(8,128)(2,1)} %get-tuple-element.50), channel_id=1, source_target_pairs={{0,64},{1,65},{2,34},{3,35},{4,4},{5,5},{6,102},{7,103},{8,72},{9,... | collective-permute-start | bytes 786440 | tf_op jit(solution)/shard_map/ppermute | solution.py:180
  18.9 2.9 %collective-permute-start.1 = (bf16[256,512]{1,0:T(8,128)(2,1)}, bf16[256,512]{1,0:T(8,128)(2,1)}, u32[]{:S(2)}, u32[]{:S(2)}) collective-permute-start(bf16[256,512]{1,0:T(8,128)(2,1)} %get-tuple-element.51), channel_id=1, source_target_pairs={{0,96},{1,97},{2,66},{3,67},{4,36},{5,37},{6,6},{7,7},{8,104},{9,1... | collective-permute-start | bytes 786440 | tf_op jit(solution)/shard_map/ppermute | solution.py:180
  21.8 3.6 %collective-permute-start = (bf16[256,512]{1,0:T(8,128)(2,1)}, bf16[256,512]{1,0:T(8,128)(2,1)}, u32[]{:S(2)}, u32[]{:S(2)}) collective-permute-start(bf16[256,512]{1,0:T(8,128)(2,1)} %get-tuple-element.52), channel_id=1, source_target_pairs={{0,0},{1,1},{2,98},{3,99},{4,68},{5,69},{6,38},{7,39},{8,8},{9,9},... | collective-permute-start | bytes 786440 | tf_op jit(solution)/shard_map/ppermute | solution.py:180
  30.4 5.2 %all-gather.3 = bf16[4,4,2048]{2,1,0:T(4,128)(2,1)S(1)} all-gather(bf16[1,4,2048]{2,1,0:T(4,128)(2,1)S(1)} %maximum_bitcast_fusion), channel_id=1, replica_groups=mesh['z'=4,'xl'=2,'core'=2,'y'=4,'xh'=2] {'xl','core'}, dimensions={0}, use_global_device_ids=true | all-gather | bytes 81920 | tf_op jit(solution)/shard_map/all_gather | solution.py:191
  37.3 2.3 collective-permute-start.8
  41.2 3.5 %collective-permute-start.5 = (bf16[256,512]{1,0:T(8,128)(2,1)}, bf16[256,512]{1,0:T(8,128)(2,1)S(1)}, u32[]{:S(2)}, u32[]{:S(2)}) collective-permute-start(bf16[256,512]{1,0:T(8,128)(2,1)} %collective-permute-done.1), channel_id=1, source_target_pairs={{0,2},{1,18},{2,4},{3,20},{4,6},{5,22},{6,0},{7,16},{8,10},{9,26},... | collective-permute-start | bytes 786440 | tf_op jit(solution)/shard_map/ppermute | solution.py:193
  44.7 4.2 %collective-permute-start.6 = (bf16[256,512]{1,0:T(8,128)(2,1)}, bf16[256,512]{1,0:T(8,128)(2,1)S(1)}, u32[]{:S(2)}, u32[]{:S(2)}) collective-permute-start(bf16[256,512]{1,0:T(8,128)(2,1)} %collective-permute-done.2), channel_id=1, source_target_pairs={{0,4},{1,20},{2,6},{3,22},{4,0},{5,16},{6,2},{7,18},{8,12},{9,28},... | collective-permute-start | bytes 786440 | tf_op jit(solution)/shard_map/ppermute | solution.py:193
  48.9 4.5 %collective-permute-start.7 = (bf16[256,512]{1,0:T(8,128)(2,1)}, bf16[256,512]{1,0:T(8,128)(2,1)S(1)}, u32[]{:S(2)}, u32[]{:S(2)}) collective-permute-start(bf16[256,512]{1,0:T(8,128)(2,1)} %collective-permute-done.3), channel_id=1, source_target_pairs={{0,6},{1,22},{2,0},{3,16},{4,2},{5,18},{6,4},{7,20},{8,14},{9,30},... | collective-permute-start | bytes 786440 | tf_op jit(solution)/shard_map/ppermute | solution.py:193
  53.8 5.8 %collective-permute-start.11 = (bf16[64,512]{1,0:T(8,128)(2,1)S(1)}, bf16[64,512]{1,0:T(8,128)(2,1)S(1)}, u32[]{:S(2)}, u32[]{:S(2)}) collective-permute-start(bf16[64,512]{1,0:T(8,128)(2,1)S(1)} %fusion.13), channel_id=1, source_target_pairs={{0,1},{1,0},{2,3},{3,2},{4,5},{5,4},{6,7},{7,6},{8,9},{9,8},{10,11... | collective-permute-start | bytes 196616 | tf_op jit(solution)/shard_map/ppermute | solution.py:40
  63.0 9.5 %collective-permute-start.15 = (bf16[512,1024]{1,0:T(8,128)(2,1)S(1)}, bf16[512,1024]{1,0:T(8,128)(2,1)S(1)}, u32[]{:S(2)}, u32[]{:S(2)}) collective-permute-start(bf16[512,1024]{1,0:T(8,128)(2,1)S(1)} %bitcast.80), channel_id=1, source_target_pairs={{0,1},{1,0},{2,3},{3,2},{4,5},{5,4},{6,7},{7,6},{8,9},{9,8},{10,11... | collective-permute-start | bytes 3145736 | tf_op jit(solution)/shard_map/ppermute | solution.py:40
  81.7 35.7 %all-gather = bf16[256,512]{1,0:T(8,128)(2,1)S(1)} all-gather(bf16[64,512]{1,0:T(8,128)(2,1)S(1)} %add_convert_fusion.refs_10_), channel_id=2, replica_groups=mesh['z'=4,'xl'=2,'core'=2,'y'=4,'xh'=2] {'xl','core'}, dimensions={0}, use_global_device_ids=true | all-gather | bytes 327680 | tf_op jit(solution)/shard_map/all_gather | solution.py:210
  121.4 2.4 collective-permute-start.19
  123.8 5.7 %collective-permute-done.18.p3 = bf16[4,64,512]{2,1,0:T(8,128)(2,1)S(1)} collective-permute-done((bf16[4,64,512]{2,1,0:T(8,128)(2,1)S(1)}, bf16[4,64,512]{2,1,0:T(8,128)(2,1)S(1)}, u32[]{:S(2)}, u32[]{:S(2)}) %collective-permute-start.18) | collective-permute-done | bytes 262176 | tf_op jit(solution)/shard_map/ppermute | solution.py:40
  130.3 12.2 %collective-permute-done.17.p2 = bf16[4,64,512]{2,1,0:T(8,128)(2,1)S(1)} collective-permute-done((bf16[4,64,512]{2,1,0:T(8,128)(2,1)S(1)}, bf16[4,64,512]{2,1,0:T(8,128)(2,1)S(1)}, u32[]{:S(2)}, u32[]{:S(2)}) %collective-permute-start.17) | collective-permute-done | bytes 262176 | tf_op jit(solution)/shard_map/ppermute | solution.py:40
  144.7 2.9 %normalize.1 = bf16[64,8192]{1,0:T(8,128)(2,1)} custom-call(s32[1]{0:T(128)} %bitcast.16.place_ref, bf16[4,64,512]{2,1,0:T(8,128)(2,1)} %bitcast.91, bf16[4,64,512]{2,1,0:T(8,128)(2,1)} %copy-done.7, bf16[4,64,512]{2,1,0:T(8,128)(2,1)} %copy-done.6, bf16[4,64,512]{2,1,0:T(8,128)(2,1)} %copy-done.5, f32[1,8192]{1,0:T(1,128)} %bitcast.100), custom_call_target="tpu_custom_call" | custom-call | flops 4194304 | bytes 2097152 | tf_op jit(solution)/shard_map/normalize/pallas_call | solution.py:143
  147.5 8.3 %convolution_convert_fusion = bf16[64,4096]{1,0:T(8,128)(2,1)} fusion(bf16[1,512,4096]{2,1,0:T(8,128)(2,1)} %param.24, bf16[64,8192]{1,0:T(8,128)(2,1)} %normalize.1, bf16[1,8192,512]{2,1,0:T(8,128)(2,1)} %param.22, f32[512]{0:T(512)S(1)} %bitcast.102), kind=kOutput, calls=%fused_computation.4 | convolution fusion | flops 805765120 | bytes 14157824 | tf_op jit(solution)/shard_map/dot_general | solution.py:220
  155.8 4.1 %all-to-all-start = ((bf16[4,16,4096]{2,1,0:T(8,128)(2,1)}), bf16[4,16,4096]{2,1,0:T(8,128)(2,1)}, u32[]{:S(2)}, u32[]{:S(2)}) async-start(bf16[4,16,4096]{2,1,0:T(8,128)(2,1)} %bitcast.87), calls=%async_computation | async-start | bytes 1048576 | tf_op jit(solution)/shard_map/all_to_all | solution.py:222
  160.0 3.5 %collective-permute-start.23 = (bf16[512,1024]{1,0:T(8,128)(2,1)S(1)}, bf16[512,1024]{1,0:T(8,128)(2,1)}, u32[]{:S(2)}, u32[]{:S(2)}) collective-permute-start(bf16[512,1024]{1,0:T(8,128)(2,1)S(1)} %bitcast.83), channel_id=1, source_target_pairs={{0,4},{2,6},{4,0},{6,2},{1,5},{3,7},{5,1},{7,3},{8,12},{10,14},{12... | collective-permute-start | bytes 3145736 | tf_op jit(solution)/shard_map/ppermute | solution.py:40
  163.5 45.1 %all-to-all-done = bf16[4,16,4096]{2,1,0:T(8,128)(2,1)} async-done(((bf16[4,16,4096]{2,1,0:T(8,128)(2,1)}), bf16[4,16,4096]{2,1,0:T(8,128)(2,1)}, u32[]{:S(2)}, u32[]{:S(2)}) %all-to-all-start) | async-done | bytes 524320 | tf_op jit(solution)/shard_map/all_to_all | solution.py:222
  213.3 4.6 %collective-permute-done.25 = bf16[16,4096]{1,0:T(8,128)(2,1)} collective-permute-done((bf16[16,4096]{1,0:T(8,128)(2,1)S(1)}, bf16[16,4096]{1,0:T(8,128)(2,1)}, u32[]{:S(2)}, u32[]{:S(2)}) %collective-permute-start.25) | collective-permute-done | bytes 131104 | tf_op jit(solution)/shard_map/ppermute | solution.py:40
  219.2 10.4 %all-reduce = f32[64]{0:T(128)S(1)} all-reduce(f32[64]{0:T(128)S(1)} %add_dynamic-update-slice_fusion), channel_id=4, replica_groups=mesh['z'=4,'xl'=2,'core'=2,'y'=4,'xh'=2] {'y'}, use_global_device_ids=true, to_apply=%add | all-reduce | flops 64 | bytes 512
  230.2 14.3 %trunk_matmul.1 = bf16[512,1024]{1,0:T(8,128)(2,1)} custom-call(bf16[512,1024]{1,0:T(8,128)(2,1)S(1)} %bitcast.84, bf16[512,1024]{1,0:T(8,128)(2,1)S(1)} %collective-permute-done.15.refs_1_, bf16[512,1024]{1,0:T(8,128)(2,1)} %collective-permute-done.19.refs_2_, bf16[512,1024]{1,0:T(8,128)(2,1)} %collective-permute-done.21.refs_3_, ...), custom_call_target="tpu_custom_call" | custom-call | flops 8589934592 | bytes 25165824 | tf_op jit(solution)/shard_map/trunk_matmul/pallas_call | solution.py:92
  (106 shorter events, 33.5 us)
Async XLA Ops:
  7.2 223.0 %all-gather.6.cloned.1.call-start = ((), (), s32[]{:S(2)}) async-start(), calls=%async_computation.1 | async-start | bytes 17825792 | tf_op jit(solution)/shard_map/all_gather | solution.py:202
  9.5 26.2 %collective-permute-start.3 = (bf16[256,512]{1,0:T(8,128)(2,1)}, bf16[256,512]{1,0:T(8,128)(2,1)}, u32[]{:S(2)}, u32[]{:S(2)}) collective-permute-start(bf16[256,512]{1,0:T(8,128)(2,1)} %get-tuple-element.49), channel_id=1, source_target_pairs={{0,32},{1,33},{2,2},{3,3},{4,100},{5,101},{6,70},{7,71},{8,40},{9,... | collective-permute-start | bytes 786440 | tf_op jit(solution)/shard_map/ppermute | solution.py:180
  13.4 22.3 %collective-permute-start.2 = (bf16[256,512]{1,0:T(8,128)(2,1)}, bf16[256,512]{1,0:T(8,128)(2,1)}, u32[]{:S(2)}, u32[]{:S(2)}) collective-permute-start(bf16[256,512]{1,0:T(8,128)(2,1)} %get-tuple-element.50), channel_id=1, source_target_pairs={{0,64},{1,65},{2,34},{3,35},{4,4},{5,5},{6,102},{7,103},{8,72},{9,... | collective-permute-start | bytes 786440 | tf_op jit(solution)/shard_map/ppermute | solution.py:180
  18.9 16.8 %collective-permute-start.1 = (bf16[256,512]{1,0:T(8,128)(2,1)}, bf16[256,512]{1,0:T(8,128)(2,1)}, u32[]{:S(2)}, u32[]{:S(2)}) collective-permute-start(bf16[256,512]{1,0:T(8,128)(2,1)} %get-tuple-element.51), channel_id=1, source_target_pairs={{0,96},{1,97},{2,66},{3,67},{4,36},{5,37},{6,6},{7,7},{8,104},{9,1... | collective-permute-start | bytes 786440 | tf_op jit(solution)/shard_map/ppermute | solution.py:180
  21.8 13.9 %collective-permute-start = (bf16[256,512]{1,0:T(8,128)(2,1)}, bf16[256,512]{1,0:T(8,128)(2,1)}, u32[]{:S(2)}, u32[]{:S(2)}) collective-permute-start(bf16[256,512]{1,0:T(8,128)(2,1)} %get-tuple-element.52), channel_id=1, source_target_pairs={{0,0},{1,1},{2,98},{3,99},{4,68},{5,69},{6,38},{7,39},{8,8},{9,9},... | collective-permute-start | bytes 786440 | tf_op jit(solution)/shard_map/ppermute | solution.py:180
  35.8 17.7 %collective-permute-start.10 = (bf16[16,2048]{1,0:T(8,128)(2,1)S(1)}, bf16[16,2048]{1,0:T(8,128)(2,1)S(1)}, u32[]{:S(2)}, u32[]{:S(2)}) collective-permute-start(bf16[16,2048]{1,0:T(8,128)(2,1)S(1)} %reshape.169), channel_id=1, source_target_pairs={{0,32},{32,64},{64,96},{96,0},{1,33},{33,65},{65,97},{97,1},{2,34}... | collective-permute-start | bytes 196616 | tf_op jit(solution)/shard_map/ppermute | solution.py:40
  36.8 12.1 %collective-permute-start.9 = (bf16[16,2048]{1,0:T(8,128)(2,1)S(1)}, bf16[16,2048]{1,0:T(8,128)(2,1)S(1)}, u32[]{:S(2)}, u32[]{:S(2)}) collective-permute-start(bf16[16,2048]{1,0:T(8,128)(2,1)S(1)} %reshape.169), channel_id=1, source_target_pairs={{0,64},{32,96},{64,0},{96,32},{1,65},{33,97},{65,1},{97,33},{2,66}... | collective-permute-start | bytes 196616 | tf_op jit(solution)/shard_map/ppermute | solution.py:40
  37.3 7.4 %collective-permute-start.8 = (bf16[16,2048]{1,0:T(8,128)(2,1)S(1)}, bf16[16,2048]{1,0:T(8,128)(2,1)S(1)}, u32[]{:S(2)}, u32[]{:S(2)}) collective-permute-start(bf16[16,2048]{1,0:T(8,128)(2,1)S(1)} %reshape.169), channel_id=1, source_target_pairs={{0,96},{32,0},{64,32},{96,64},{1,97},{33,1},{65,33},{97,65},{2,98}... | collective-permute-start | bytes 196616 | tf_op jit(solution)/shard_map/ppermute | solution.py:40
  39.6 22.2 %collective-permute-start.4 = (bf16[256,512]{1,0:T(8,128)(2,1)}, bf16[256,512]{1,0:T(8,128)(2,1)S(1)}, u32[]{:S(2)}, u32[]{:S(2)}) collective-permute-start(bf16[256,512]{1,0:T(8,128)(2,1)} %collective-permute-done), channel_id=1, source_target_pairs={{0,0},{1,16},{2,2},{3,18},{4,4},{5,20},{6,6},{7,22},{8,8},{9,24},{... | collective-permute-start | bytes 786440 | tf_op jit(solution)/shard_map/ppermute | solution.py:193
  41.2 20.6 %collective-permute-start.5 = (bf16[256,512]{1,0:T(8,128)(2,1)}, bf16[256,512]{1,0:T(8,128)(2,1)S(1)}, u32[]{:S(2)}, u32[]{:S(2)}) collective-permute-start(bf16[256,512]{1,0:T(8,128)(2,1)} %collective-permute-done.1), channel_id=1, source_target_pairs={{0,2},{1,18},{2,4},{3,20},{4,6},{5,22},{6,0},{7,16},{8,10},{9,26},... | collective-permute-start | bytes 786440 | tf_op jit(solution)/shard_map/ppermute | solution.py:193
  44.7 17.1 %collective-permute-start.6 = (bf16[256,512]{1,0:T(8,128)(2,1)}, bf16[256,512]{1,0:T(8,128)(2,1)S(1)}, u32[]{:S(2)}, u32[]{:S(2)}) collective-permute-start(bf16[256,512]{1,0:T(8,128)(2,1)} %collective-permute-done.2), channel_id=1, source_target_pairs={{0,4},{1,20},{2,6},{3,22},{4,0},{5,16},{6,2},{7,18},{8,12},{9,28},... | collective-permute-start | bytes 786440 | tf_op jit(solution)/shard_map/ppermute | solution.py:193
  48.9 12.9 %collective-permute-start.7 = (bf16[256,512]{1,0:T(8,128)(2,1)}, bf16[256,512]{1,0:T(8,128)(2,1)S(1)}, u32[]{:S(2)}, u32[]{:S(2)}) collective-permute-start(bf16[256,512]{1,0:T(8,128)(2,1)} %collective-permute-done.3), channel_id=1, source_target_pairs={{0,6},{1,22},{2,0},{3,16},{4,2},{5,18},{6,4},{7,20},{8,14},{9,30},... | collective-permute-start | bytes 786440 | tf_op jit(solution)/shard_map/ppermute | solution.py:193
  53.8 8.0 %collective-permute-start.11 = (bf16[64,512]{1,0:T(8,128)(2,1)S(1)}, bf16[64,512]{1,0:T(8,128)(2,1)S(1)}, u32[]{:S(2)}, u32[]{:S(2)}) collective-permute-start(bf16[64,512]{1,0:T(8,128)(2,1)S(1)} %fusion.13), channel_id=1, source_target_pairs={{0,1},{1,0},{2,3},{3,2},{4,5},{5,4},{6,7},{7,6},{8,9},{9,8},{10,11... | collective-permute-start | bytes 196616 | tf_op jit(solution)/shard_map/ppermute | solution.py:40
  63.0 54.4 %collective-permute-start.15 = (bf16[512,1024]{1,0:T(8,128)(2,1)S(1)}, bf16[512,1024]{1,0:T(8,128)(2,1)S(1)}, u32[]{:S(2)}, u32[]{:S(2)}) collective-permute-start(bf16[512,1024]{1,0:T(8,128)(2,1)S(1)} %bitcast.80), channel_id=1, source_target_pairs={{0,1},{1,0},{2,3},{3,2},{4,5},{5,4},{6,7},{7,6},{8,9},{9,8},{10,11... | collective-permute-start | bytes 3145736 | tf_op jit(solution)/shard_map/ppermute | solution.py:40
  117.4 12.1 %collective-permute-start.18 = (bf16[4,64,512]{2,1,0:T(8,128)(2,1)S(1)}, bf16[4,64,512]{2,1,0:T(8,128)(2,1)S(1)}, u32[]{:S(2)}, u32[]{:S(2)}) collective-permute-start(bf16[4,64,512]{2,1,0:T(8,128)(2,1)S(1)} %bitcast.88), channel_id=1, source_target_pairs={{0,32},{32,64},{64,96},{96,0},{1,33},{33,65},{65,97},{97,1},{2,34}... | collective-permute-start | bytes 786440 | tf_op jit(solution)/shard_map/ppermute | solution.py:40
  117.4 25.2 %collective-permute-start.17 = (bf16[4,64,512]{2,1,0:T(8,128)(2,1)S(1)}, bf16[4,64,512]{2,1,0:T(8,128)(2,1)S(1)}, u32[]{:S(2)}, u32[]{:S(2)}) collective-permute-start(bf16[4,64,512]{2,1,0:T(8,128)(2,1)S(1)} %bitcast.89), channel_id=1, source_target_pairs={{0,64},{32,96},{64,0},{96,32},{1,65},{33,97},{65,1},{97,33},{2,66}... | collective-permute-start | bytes 786440 | tf_op jit(solution)/shard_map/ppermute | solution.py:40
  119.5 24.5 %collective-permute-start.16 = (bf16[4,64,512]{2,1,0:T(8,128)(2,1)S(1)}, bf16[4,64,512]{2,1,0:T(8,128)(2,1)S(1)}, u32[]{:S(2)}, u32[]{:S(2)}) collective-permute-start(bf16[4,64,512]{2,1,0:T(8,128)(2,1)S(1)} %bitcast.90), channel_id=1, source_target_pairs={{0,96},{32,0},{64,32},{96,64},{1,97},{33,1},{65,33},{97,65},{2,98}... | collective-permute-start | bytes 786440 | tf_op jit(solution)/shard_map/ppermute | solution.py:40
  120.6 42.9 %collective-permute-start.20 = (bf16[512,1024]{1,0:T(8,128)(2,1)S(1)}, bf16[512,1024]{1,0:T(8,128)(2,1)}, u32[]{:S(2)}, u32[]{:S(2)}) collective-permute-start(bf16[512,1024]{1,0:T(8,128)(2,1)S(1)} %bitcast.81), channel_id=1, source_target_pairs={{0,2},{2,4},{4,6},{6,0},{1,3},{3,5},{5,7},{7,1},{8,10},{10,12},{12... | collective-permute-start | bytes 3145736 | tf_op jit(solution)/shard_map/ppermute | solution.py:40
  121.4 42.0 %collective-permute-start.19 = (bf16[512,1024]{1,0:T(8,128)(2,1)S(1)}, bf16[512,1024]{1,0:T(8,128)(2,1)}, u32[]{:S(2)}, u32[]{:S(2)}) collective-permute-start(bf16[512,1024]{1,0:T(8,128)(2,1)S(1)} %bitcast.82), channel_id=1, source_target_pairs={{0,6},{2,0},{4,2},{6,4},{1,7},{3,1},{5,3},{7,5},{8,14},{10,8},{12,... | collective-permute-start | bytes 3145736 | tf_op jit(solution)/shard_map/ppermute | solution.py:40
  129.5 79.1 %collective-permute-start.22 = (bf16[512,1024]{1,0:T(8,128)(2,1)S(1)}, bf16[512,1024]{1,0:T(8,128)(2,1)}, u32[]{:S(2)}, u32[]{:S(2)}) collective-permute-start(bf16[512,1024]{1,0:T(8,128)(2,1)S(1)} %collective-permute-done.15.refs_1_), channel_id=1, source_target_pairs={{0,2},{2,4},{4,6},{6,0},{1,3},{3,5},{5,7},{7,1},{8,10},{10,12},{12... | collective-permute-start | bytes 3145736 | tf_op jit(solution)/shard_map/ppermute | solution.py:40
  142.5 66.1 %collective-permute-start.21 = (bf16[512,1024]{1,0:T(8,128)(2,1)S(1)}, bf16[512,1024]{1,0:T(8,128)(2,1)}, u32[]{:S(2)}, u32[]{:S(2)}) collective-permute-start(bf16[512,1024]{1,0:T(8,128)(2,1)S(1)} %collective-permute-done.15.refs_1_), channel_id=1, source_target_pairs={{0,6},{2,0},{4,2},{6,4},{1,7},{3,1},{5,3},{7,5},{8,14},{10,8},{12,... | collective-permute-start | bytes 3145736 | tf_op jit(solution)/shard_map/ppermute | solution.py:40
  155.8 52.7 %all-to-all-start = ((bf16[4,16,4096]{2,1,0:T(8,128)(2,1)}), bf16[4,16,4096]{2,1,0:T(8,128)(2,1)}, u32[]{:S(2)}, u32[]{:S(2)}) async-start(bf16[4,16,4096]{2,1,0:T(8,128)(2,1)} %bitcast.87), calls=%async_computation | async-start | bytes 1048576 | tf_op jit(solution)/shard_map/all_to_all | solution.py:222
  160.0 70.2 %collective-permute-start.23 = (bf16[512,1024]{1,0:T(8,128)(2,1)S(1)}, bf16[512,1024]{1,0:T(8,128)(2,1)}, u32[]{:S(2)}, u32[]{:S(2)}) collective-permute-start(bf16[512,1024]{1,0:T(8,128)(2,1)S(1)} %bitcast.83), channel_id=1, source_target_pairs={{0,4},{2,6},{4,0},{6,2},{1,5},{3,7},{5,1},{7,3},{8,12},{10,14},{12... | collective-permute-start | bytes 3145736 | tf_op jit(solution)/shard_map/ppermute | solution.py:40
  208.6 21.6 %collective-permute-start.24 = (bf16[512,1024]{1,0:T(8,128)(2,1)S(1)}, bf16[512,1024]{1,0:T(8,128)(2,1)}, u32[]{:S(2)}, u32[]{:S(2)}) collective-permute-start(bf16[512,1024]{1,0:T(8,128)(2,1)S(1)} %collective-permute-done.15.refs_1_), channel_id=1, source_target_pairs={{0,4},{2,6},{4,0},{6,2},{1,5},{3,7},{5,1},{7,3},{8,12},{10,14},{12... | collective-permute-start | bytes 3145736 | tf_op jit(solution)/shard_map/ppermute | solution.py:40
  (18 other events, 421.9 us)
Sparse Core Ops, SparseCore 0:
  63.1 117.3 all-gather.5

commit v4 on v1

--- a/solution.py
+++ b/solution.py
@@ -1,4 +1,4 @@
-import functools
+import itertools
 
 import jax
 import jax.numpy as jnp
@@ -19,14 +19,21 @@
     return (((z % Z) * XL + xl % XL) * CORE + core) * Y * XH + (y % Y) * XH + xh % XH
 
 
-def weight_moves():
+def places():
+    return itertools.product(range(Z), range(XL), range(CORE), range(Y), range(XH))
+
+
+def spread_moves(v):
     return [
-        (flat(z, xl, core, y, xh), flat(y - z, xh - xl, core, z, xl))
-        for z in range(Z)
-        for xl in range(XL)
-        for core in range(CORE)
-        for y in range(Y)
-        for xh in range(XH)
+        (flat(z, xl, core, y, xh), flat(z - y - 2 * v, xl, core, y, xh))
+        for z, xl, core, y, xh in places()
+    ]
+
+
+def column_moves(v):
+    return [
+        (flat(z, xl, core, y, xh), flat(z, xh - xl, core, y + z + 2 * v, xl))
+        for z, xl, core, y, xh in places()
     ]
 
 
@@ -62,38 +69,73 @@
     return attn_out.astype(jnp.bfloat16).reshape(row_count, heads_here * HEAD_WIDTH)
 
 
-def trunk_kernel(*refs):
-    acts, w_ref, residual_ref, out_ref = refs[:8], refs[8], refs[9], refs[10]
-    total = residual_ref[...].astype(jnp.float32)
-    for slot in range(8):
-        total = total + jnp.dot(
-            acts[slot][...], w_ref[slot, 0], preferred_element_type=jnp.float32
-        )
-    out_ref[...] = total.astype(jnp.bfloat16)
-
-
-def trunk_matmul(acts, weights, residual):
-    rows, depth = acts[0].shape
-    half = weights.shape[-1]
-    width = 256
-    per = half // width
-    whole = pl.BlockSpec((rows, depth), lambda j: (0, 0), pipeline_mode=pl.Buffered(1))
-    tile = pl.BlockSpec((rows, width), lambda j: (0, j))
+def trunk_kernel(place_ref, acts_ref, *refs):
+    residual_ref, out_ref = refs[20], refs[21]
+    j = pl.program_id(0)
+
+    def tile(blocks):
+        total = residual_ref[...].astype(jnp.float32)
+        for e in range(XL):
+            for s in range(Z):
+                for v in range(2):
+                    if s == 2:
+                        block = blocks[5 * e + 3 + v][...]
+                    else:
+                        block = blocks[5 * e + min(s, 2)][v]
+                    depth = block.shape[0]
+                    group = lax.rem(place_ref[0] + 2 * Y - s - 2 * v, Y) * XH + lax.rem(
+                        place_ref[1] + e, XH
+                    )
+                    total = total + jnp.dot(
+                        acts_ref[group, :, v * depth : (v + 1) * depth],
+                        block,
+                        preferred_element_type=jnp.float32,
+                    )
+        out_ref[...] = total.astype(jnp.bfloat16)
+
+    @pl.when(j < 2)
+    def _():
+        tile(refs[:10])
+
+    @pl.when(j >= 2)
+    def _():
+        tile(refs[10:20])
+
+
+def trunk_matmul(place, acts, own, other, residual):
+    groups, rows, depth = acts.shape
+    half = residual.shape[1] // CORE
+    width = half // 2
+
+    def spec(w, index):
+        shape = w.shape[:-1] + (width,)
+        return pl.BlockSpec(shape, lambda j, p: (0,) * (len(shape) - 1) + (index(j),))
+
+    tile = pl.BlockSpec(
+        (rows, width), lambda j, p: (0, jnp.where(j < 2, p[2], 1 - p[2]) * 2 + lax.rem(j, 2))
+    )
     return pl.pallas_call(
         trunk_kernel,
-        grid=(CORE * per,),
-        in_specs=[whole] * 8
-        + [pl.BlockSpec((8, 1, depth, width), lambda j: (0, j // per, 0, j % per)), tile],
-        out_specs=tile,
+        grid_spec=pltpu.PrefetchScalarGridSpec(
+            num_scalar_prefetch=1,
+            grid=(4,),
+            in_specs=[
+                pl.BlockSpec(acts.shape, lambda j, p: (0, 0, 0), pipeline_mode=pl.Buffered(1))
+            ]
+            + [spec(w, lambda j: jnp.minimum(j, 1)) for w in own]
+            + [spec(w, lambda j: jnp.maximum(j - 2, 0)) for w in other]
+            + [tile],
+            out_specs=tile,
+        ),
         out_shape=jax.ShapeDtypeStruct(residual.shape, jnp.bfloat16),
-        compiler_params=pltpu.CompilerParams(vmem_limit_bytes=40 * 2**20),
+        compiler_params=pltpu.CompilerParams(vmem_limit_bytes=44 * 2**20),
         cost_estimate=pl.CostEstimate(
-            flops=2 * rows * 8 * depth * CORE * half,
-            bytes_accessed=2 * (8 * rows * depth + 8 * depth * CORE * half),
+            flops=2 * rows * groups * depth * CORE * half,
+            bytes_accessed=2 * (groups * rows * depth + groups * depth * CORE * half),
             transcendentals=0,
         ),
         name="trunk_matmul",
-    )(*acts, weights, residual)
+    )(place, acts, *own, *other, residual)
 
 
 def norm_kernel(place_ref, p0, p1, p2, p3, gain_ref, out_ref):
@@ -159,52 +201,84 @@
     xh = lax.axis_index("xh")
     cand_count = cand_len.shape[0]
 
-    moved = lax.ppermute(out_weight, ALL, weight_moves())
+    lock = lax.optimization_barrier
+    rows_half = out_weight.shape[0] // 2
+    moved = [
+        lax.ppermute(out_weight[v * rows_half : (v + 1) * rows_half], ALL, spread_moves(v))
+        for v in range(2)
+    ]
     attn_out = attention(query, keys, values, cand_len)
+    acts = lax.all_gather(attn_out, TENSOR, axis=0, tiled=False)
 
     last_rows = jnp.arange(cand_count, dtype=jnp.int32) * SEQUENCE_SLOTS + cand_len - 1
     picked = jnp.concatenate(
         [jnp.take(attn_out, last_rows, axis=0), jnp.take(residual, last_rows, axis=0)], axis=1
     )
+    depth = attn_out.shape[1]
+    width = out_weight.shape[1]
     near = lax.all_gather(picked, ("xl", "core"), axis=0, tiled=True)
+    near, *moved = lock((near, *moved))
+    moved = [lax.ppermute(m, ALL, column_moves(v)) for v, m in enumerate(moved)]
     rows = jnp.concatenate([near] + [from_ahead(near, "z", Z, s) for s in (1, 2, 3)], axis=0)
-    width = out_weight.shape[1]
-    own = jnp.dot(rows[:, : attn_out.shape[1]], out_weight, preferred_element_type=jnp.float32)
-    res = rows[:, attn_out.shape[1] :]
+    own = jnp.dot(rows[:, :depth], out_weight, preferred_element_type=jnp.float32)
+    res = rows[:, depth:]
     res = jnp.where(core == 0, res[:, :width], res[:, width:]).astype(jnp.float32)
     own = jnp.where((y == z) & (xh == xl), own + res, own).astype(jnp.bfloat16)
     pair = jnp.stack([own, from_ahead(own, "xh", XH, 1)])
+    pair, *moved = lock((pair, *moved))
+    w, swapped = {}, {}
+    w[0, 0] = jnp.stack(moved)
+    w[1, 0] = from_ahead(w[0, 0], "z", Z, 1)
+    w[3, 0] = from_ahead(w[0, 0], "z", Z, 3)
+    swapped[0, 0] = from_ahead(w[0, 0], "core", CORE, 1)
     parts = [pair] + [from_ahead(pair, "y", Y, s) for s in (1, 2, 3)]
     pooled = sum(jnp.sum(p.astype(jnp.float32), axis=0) for p in parts).astype(jnp.bfloat16)
-    moved, bulk, _ = lax.optimization_barrier((moved, attn_out, pooled))
     near = lax.all_gather(pooled, ("xl", "core"), axis=0, tiled=False)
+    near, w[0, 0], w[1, 0], w[3, 0], swapped[0, 0] = lock(
+        (near, w[0, 0], w[1, 0], w[3, 0], swapped[0, 0])
+    )
+    w[0, 1] = from_ahead(w[0, 0], "xl", XL, 1)
     pieces = [near] + [from_ahead(near, "z", Z, s) for s in (1, 2, 3)]
     features = normalize(pieces, norm_gain, z)
+    w[2, 0, 0] = from_ahead(w[1, 0][0], "z", Z, 1)
+    w[2, 0, 1] = from_ahead(w[3, 0][1], "z", Z, 3)
+    swapped[1, 0] = from_ahead(w[1, 0], "core", CORE, 1)
+    swapped[3, 0] = from_ahead(w[3, 0], "core", CORE, 1)
     first = jax.nn.silu(
         jnp.dot(features, head_w1[0], preferred_element_type=jnp.float32) + head_b1[0]
     ).astype(jnp.bfloat16)
     terms = jnp.dot(first, head_w2[0], preferred_element_type=jnp.float32).astype(jnp.bfloat16)
+    names = [(0, 1), (2, 0, 0), (2, 0, 1)]
+    terms, swapped[1, 0], swapped[3, 0], *late = lock(
+        (terms, swapped[1, 0], swapped[3, 0], *[w[n] for n in names])
+    )
+    w.update(zip(names, late))
+    w[1, 1] = from_ahead(w[0, 1], "z", Z, 1)
+    w[3, 1] = from_ahead(w[0, 1], "z", Z, 3)
+    for n in names:
+        swapped[n] = from_ahead(w[n], "core", CORE, 1)
     count = terms.shape[0] // Y
     terms = lax.all_to_all(
         terms.reshape(Y, count, terms.shape[1]), "y", split_axis=0, concat_axis=0, tiled=True
     )
     half = jnp.sum(terms.astype(jnp.float32), axis=0).astype(jnp.bfloat16)
     other = from_ahead(half, "xh", XH, 1)
+    other, w[1, 1], w[3, 1], *late = lock((other, w[1, 1], w[3, 1], *[swapped[n] for n in names]))
+    swapped.update(zip(names, late))
+    w[2, 1, 0] = from_ahead(w[1, 1][0], "z", Z, 1)
+    w[2, 1, 1] = from_ahead(w[3, 1][1], "z", Z, 3)
+    for n in ((1, 1), (3, 1), (2, 1, 0), (2, 1, 1)):
+        swapped[n] = from_ahead(w[n], "core", CORE, 1)
     second = jax.nn.silu(half.astype(jnp.float32) + other.astype(jnp.float32) + head_b2[0])
     mine = jnp.sum(second * head_w3[0].astype(jnp.float32), axis=-1) + head_b3[0]
     scores = lax.all_gather(mine, "y", axis=0, tiled=False)
     scores = jnp.roll(scores, z, axis=0).reshape(1, Y * count)
 
-    weights = lax.all_gather(moved, MEMBER, axis=0, tiled=False)
-    weights = weights.reshape((Z * XL, CORE) + out_weight.shape)
-    acts = {}
-    for e in range(XH):
-        base = bulk if e == 0 else from_ahead(bulk, "xh", XH, 1)
-        acts[0, e] = base
-        for s in (1, 3, 2):
-            acts[s, e] = from_ahead(base, "y", Y, s)
-    ordered = [acts[s, e] for s in range(Y) for e in range(XH)]
-    trunk_out = trunk_matmul(ordered, weights, residual)
+    order = [n for e in range(XL) for n in ((0, e), (1, e), (3, e), (2, e, 0), (2, e, 1))]
+    place = jnp.stack([lax.rem(y - z + Y, Y), lax.rem(xh + xl, XH), core])
+    trunk_out = trunk_matmul(
+        place, acts, [w[n] for n in order], [swapped[n] for n in order], residual
+    )
     return (trunk_out, scores)
 
 

time: 287 us -> 227 us (0.79)
  blocking collectives: 113 us -> 32.7 us
  waiting for transfers between devices: 47.9 us -> 63.3 us
  local copies, waits for them, and re-layouts: 9.12 us -> 16.6 us
  starting transfers between devices: 67.3 us -> 63.1 us
    unnamed x1, blocking collectives: 69.2 us -> 10.4 us
    ppermute x18 -> x30, starting transfers between devices: 57.8 us -> 35.5 us  [from_ahead(): return lax.ppermute(x, axis, [(i, (i - step) % size) for i in range(size)])]
    all_to_all x1 -> x0, blocking collectives: 19.1 us -> none  [local(): lax.all_to_all(terms.reshape(Y, count, terms.shape[1]), 'y', split_axis=0...]
    ppermute x1 -> x4, starting transfers between devices: 9.51 us -> 23.3 us  [the longest x2 12.1 us: local(): moved = [lax.ppermute(m, ALL, column_moves(v)) for v, m in enumerate(moved)]]
    all_gather x1, blocking collectives: 16.7 us -> 5.57 us  [local(): near = lax.all_gather(picked, ('xl', 'core'), axis=0, tiled=True)]
    all_to_all x0 -> x1, waiting for transfers between devices: none -> 9.9 us  [local(): lax.all_to_all(terms.reshape(Y, count, terms.shape[1]), 'y', split_axis=0...]
    all_gather x1, blocking collectives: 7.65 us -> 16.7 us  [local(): near = lax.all_gather(pooled, ('xl', 'core'), axis=0, tiled=False)]
    ppermute x1 -> x4, waiting for transfers between devices: 0.01 us -> 5.87 us  [the longest x2 5.87 us: local(): moved = [lax.ppermute(m, ALL, column_moves(v)) for v, m in enumerate(moved)]]
  transfers between devices with their start and end apart: 20 -> 36, of which waited for: 10 -> 13; matrix products, arithmetic and copies ran while one was open for 8% -> 10% of each run, Pallas kernels for 1% -> 1%
where the time goes in v4:
time: 227 us; the launch traced here: 226 us
  waiting for transfers between devices  63.3 us (28%)
  starting transfers between devices  63.1 us (28%)
  blocking collectives  32.7 us (14%)
  Pallas kernels  19.6 us (9%)
  local copies, waits for them, and re-layouts  16.6 us (7%)
  between operations  15.6 us (7%)
  matrix products  9.72 us (4%)
  other arithmetic  5.39 us (2%)
    ppermute x30, waiting for transfers between devices, from_ahead(): return lax.ppermute(x, axis, [(i, (i - step) % size) for i in range(size)])  47.5 us
    ppermute x30, starting transfers between devices, from_ahead(): return lax.ppermute(x, axis, [(i, (i - step) % size) for i in range(size)])  35.5 us
    all_gather x1, blocking collectives, local(): near = lax.all_gather(pooled, ('xl', 'core'), axis=0, tiled=False)  16.7 us
    pallas_call x1, Pallas kernels, trunk_matmul(): pl.pallas_call(trunk_kernel, grid_spec=pltpu.PrefetchScalarGridSpec(num_s...  16.7 us
    ppermute x2, starting transfers between devices, local(): moved = [lax.ppermute(m, ALL, column_moves(v)) for v, m in enumerate(moved)]  12.1 us
    ppermute x2, starting transfers between devices, local(): lax.ppermute(out_weight[v * rows_half:(v + 1) * rows_half], ALL, spread_m...  11.2 us
    unnamed x1, blocking collectives  10.4 us
    all_to_all x1, waiting for transfers between devices, local(): lax.all_to_all(terms.reshape(Y, count, terms.shape[1]), 'y', split_axis=0...  9.9 us
  transfers between devices with their start and end apart: 36, of which 13 were waited for; matrix products, arithmetic and copies ran while one was open for 10% of the time, Pallas kernels for 1%

profile of v4, /device:TPU:0, one launch (start us, length us, event | category | flops | bytes accessed | tf_op | source)
XLA Modules:
  0.0 226.1 jit_solution(4329486818535742348)
XLA Ops:
  14.7 5.9 %collective-permute-start.1 = (bf16[512,512]{1,0:T(8,128)(2,1)}, bf16[512,512]{1,0:T(8,128)(2,1)}, u32[]{:S(2)}, u32[]{:S(2)}) collective-permute-start(bf16[512,512]{1,0:T(8,128)(2,1)} %get-tuple-element.51), channel_id=1, source_target_pairs={{0,64},{1,65},{2,34},{3,35},{4,4},{5,5},{6,102},{7,103},{8,72},{9,... | collective-permute-start | bytes 1572872 | tf_op jit(solution)/shard_map/ppermute | solution.py:207
  20.5 5.4 %collective-permute-start = (bf16[512,512]{1,0:T(8,128)(2,1)}, bf16[512,512]{1,0:T(8,128)(2,1)}, u32[]{:S(2)}, u32[]{:S(2)}) collective-permute-start(bf16[512,512]{1,0:T(8,128)(2,1)} %get-tuple-element.52), channel_id=1, source_target_pairs={{0,0},{1,1},{2,98},{3,99},{4,68},{5,69},{6,38},{7,39},{8,8},{9,9},... | collective-permute-start | bytes 1572872 | tf_op jit(solution)/shard_map/ppermute | solution.py:207
  28.9 5.6 %all-gather.2 = bf16[4,4,2048]{2,1,0:T(4,128)(2,1)S(1)} all-gather(bf16[1,4,2048]{2,1,0:T(4,128)(2,1)S(1)} %maximum_bitcast_fusion), channel_id=1, replica_groups=mesh['z'=4,'xl'=2,'core'=2,'y'=4,'xh'=2] {'xl','core'}, dimensions={0}, use_global_device_ids=true | all-gather | bytes 81920 | tf_op jit(solution)/shard_map/all_gather | solution.py:219
  40.3 10.4 %collective-permute-start.7 = (bf16[512,512]{1,0:T(8,128)(2,1)}, bf16[512,512]{1,0:T(8,128)(2,1)S(1)}, u32[]{:S(2)}, u32[]{:S(2)}) collective-permute-start(bf16[512,512]{1,0:T(8,128)(2,1)} %collective-permute-done.1), channel_id=1, source_target_pairs={{0,4},{1,20},{2,6},{3,22},{4,0},{5,16},{6,2},{7,18},{8,12},{9,28},... | collective-permute-start | bytes 1572872 | tf_op jit(solution)/shard_map/ppermute | solution.py:221
  51.1 5.4 %collective-permute-start.5 = (bf16[64,512]{1,0:T(8,128)(2,1)S(1)}, bf16[64,512]{1,0:T(8,128)(2,1)S(1)}, u32[]{:S(2)}, u32[]{:S(2)}) collective-permute-start(bf16[64,512]{1,0:T(8,128)(2,1)S(1)} %fusion.13), channel_id=1, source_target_pairs={{0,1},{1,0},{2,3},{3,2},{4,5},{5,4},{6,7},{7,6},{8,9},{9,8},{10,11... | collective-permute-start | bytes 196616 | tf_op jit(solution)/shard_map/ppermute | solution.py:41
  58.8 5.9 %collective-permute-done.7 = bf16[512,512]{1,0:T(8,128)(2,1)S(1)} collective-permute-done((bf16[512,512]{1,0:T(8,128)(2,1)}, bf16[512,512]{1,0:T(8,128)(2,1)S(1)}, u32[]{:S(2)}, u32[]{:S(2)}) %collective-permute-start.7) | collective-permute-done | bytes 524320 | tf_op jit(solution)/shard_map/ppermute | solution.py:221
  65.0 3.2 %collective-permute-start.11 = (bf16[2,512,512]{2,1,0:T(8,128)(2,1)S(1)}, bf16[2,512,512]{2,1,0:T(8,128)(2,1)S(1)}, u32[]{:S(2)}, u32[]{:S(2)}) collective-permute-start(bf16[2,512,512]{2,1,0:T(8,128)(2,1)S(1)} %pad_maximum_fusion.refs_0_), channel_id=1, source_target_pairs={{0,96},{32,0},{64,32},{96,64},{1,97},{33,1},{65,33},{97,65},{2,98}... | collective-permute-start | bytes 3145736 | tf_op jit(solution)/shard_map/ppermute | solution.py:41
  70.9 7.3 %collective-permute-done.10 = bf16[2,64,512]{2,1,0:T(8,128)(2,1)S(1)} collective-permute-done((bf16[2,64,512]{2,1,0:T(8,128)(2,1)S(1)}, bf16[2,64,512]{2,1,0:T(8,128)(2,1)S(1)}, u32[]{:S(2)}, u32[]{:S(2)}) %collective-permute-start.10) | collective-permute-done | bytes 131104 | tf_op jit(solution)/shard_map/ppermute | solution.py:41
  78.3 7.7 %collective-permute-done.8 = bf16[2,64,512]{2,1,0:T(8,128)(2,1)S(1)} collective-permute-done((bf16[2,64,512]{2,1,0:T(8,128)(2,1)S(1)}, bf16[2,64,512]{2,1,0:T(8,128)(2,1)S(1)}, u32[]{:S(2)}, u32[]{:S(2)}) %collective-permute-start.8) | collective-permute-done | bytes 131104 | tf_op jit(solution)/shard_map/ppermute | solution.py:41
  86.0 16.7 %all-gather = bf16[256,512]{1,0:T(8,128)(2,1)S(1)} all-gather(bf16[64,512]{1,0:T(8,128)(2,1)S(1)} %add_convert_fusion), channel_id=2, replica_groups=mesh['z'=4,'xl'=2,'core'=2,'y'=4,'xh'=2] {'xl','core'}, dimensions={0}, use_global_device_ids=true | all-gather | bytes 327680 | tf_op jit(solution)/shard_map/all_gather | solution.py:236
  103.8 2.8 %collective-permute-start.15 = (bf16[4,64,512]{2,1,0:T(8,128)(2,1)S(1)}, bf16[4,64,512]{2,1,0:T(8,128)(2,1)S(1)}, u32[]{:S(2)}, u32[]{:S(2)}) collective-permute-start(bf16[4,64,512]{2,1,0:T(8,128)(2,1)S(1)} %bitcast.96), channel_id=1, source_target_pairs={{0,64},{32,96},{64,0},{96,32},{1,65},{33,97},{65,1},{97,33},{2,66}... | collective-permute-start | bytes 786440 | tf_op jit(solution)/shard_map/ppermute | solution.py:41
  106.6 2.6 %collective-permute-start.14 = (bf16[4,64,512]{2,1,0:T(8,128)(2,1)S(1)}, bf16[4,64,512]{2,1,0:T(8,128)(2,1)S(1)}, u32[]{:S(2)}, u32[]{:S(2)}) collective-permute-start(bf16[4,64,512]{2,1,0:T(8,128)(2,1)S(1)} %bitcast.97), channel_id=1, source_target_pairs={{0,96},{32,0},{64,32},{96,64},{1,97},{33,1},{65,33},{97,65},{2,98}... | collective-permute-start | bytes 786440 | tf_op jit(solution)/shard_map/ppermute | solution.py:41
  110.6 8.5 %collective-permute-done.16.p3 = bf16[4,64,512]{2,1,0:T(8,128)(2,1)S(1)} collective-permute-done((bf16[4,64,512]{2,1,0:T(8,128)(2,1)S(1)}, bf16[4,64,512]{2,1,0:T(8,128)(2,1)S(1)}, u32[]{:S(2)}, u32[]{:S(2)}) %collective-permute-start.16) | collective-permute-done | bytes 262176 | tf_op jit(solution)/shard_map/ppermute | solution.py:41
  122.3 2.8 %collective-permute-start.20 = (bf16[512,512]{1,0:T(8,128)(2,1)}, bf16[512,512]{1,0:T(8,128)(2,1)}, u32[]{:S(2)}, u32[]{:S(2)}) collective-permute-start(bf16[512,512]{1,0:T(8,128)(2,1)} %slice_bitcast_fusion.3), channel_id=1, source_target_pairs={{0,96},{32,0},{64,32},{96,64},{1,97},{33,1},{65,33},{97,65},{2,98}... | collective-permute-start | bytes 1572872 | tf_op jit(solution)/shard_map/ppermute | solution.py:41
  125.1 2.9 %normalize.1 = bf16[64,8192]{1,0:T(8,128)(2,1)} custom-call(s32[1]{0:T(128)} %bitcast.23.place_ref, bf16[4,64,512]{2,1,0:T(8,128)(2,1)} %bitcast.98, bf16[4,64,512]{2,1,0:T(8,128)(2,1)} %copy-done.5, bf16[4,64,512]{2,1,0:T(8,128)(2,1)} %copy-done.4, bf16[4,64,512]{2,1,0:T(8,128)(2,1)} %copy-done.3, f32[1,8192]{1,0:T(1,128)} %bitcast.105), custom_call_target="tpu_custom_call" | custom-call | flops 4194304 | bytes 2097152 | tf_op jit(solution)/shard_map/normalize/pallas_call | solution.py:169
  127.9 8.1 %convolution_convert_fusion = bf16[64,4096]{1,0:T(8,128)(2,1)} fusion(bf16[1,512,4096]{2,1,0:T(8,128)(2,1)} %param.24, bf16[64,8192]{1,0:T(8,128)(2,1)} %normalize.1, bf16[1,8192,512]{2,1,0:T(8,128)(2,1)} %param.22, f32[512]{0:T(512)S(1)} %bitcast.107), kind=kOutput, calls=%fused_computation.4 | convolution fusion | flops 805765120 | bytes 14157824 | tf_op jit(solution)/shard_map/dot_general | solution.py:250
  137.4 7.1 %collective-permute-done.19.refs_5_ = bf16[2,512,512]{2,1,0:T(8,128)(2,1)} collective-permute-done((bf16[2,512,512]{2,1,0:T(8,128)(2,1)S(1)}, bf16[2,512,512]{2,1,0:T(8,128)(2,1)}, u32[]{:S(2)}, u32[]{:S(2)}) %collective-permute-start.19) | collective-permute-done | bytes 1048608 | tf_op jit(solution)/shard_map/ppermute | solution.py:41
  147.9 4.3 %all-to-all-start = ((bf16[4,16,4096]{2,1,0:T(8,128)(2,1)}), bf16[4,16,4096]{2,1,0:T(8,128)(2,1)}, u32[]{:S(2)}, u32[]{:S(2)}) async-start(bf16[4,16,4096]{2,1,0:T(8,128)(2,1)} %bitcast.93), calls=%async_computation | async-start | bytes 1048576 | tf_op jit(solution)/shard_map/all_to_all | solution.py:261
  152.6 9.9 %all-to-all-done = bf16[4,16,4096]{2,1,0:T(8,128)(2,1)} async-done(((bf16[4,16,4096]{2,1,0:T(8,128)(2,1)}), bf16[4,16,4096]{2,1,0:T(8,128)(2,1)}, u32[]{:S(2)}, u32[]{:S(2)}) %all-to-all-start) | async-done | bytes 524320 | tf_op jit(solution)/shard_map/all_to_all | solution.py:261
  163.7 2.8 %collective-permute-start.22 = (bf16[16,4096]{1,0:T(8,128)(2,1)S(1)}, bf16[16,4096]{1,0:T(8,128)(2,1)S(1)}, u32[]{:S(2)}, u32[]{:S(2)}) collective-permute-start(bf16[16,4096]{1,0:T(8,128)(2,1)S(1)} %reduce_sum.71), channel_id=1, source_target_pairs={{0,1},{1,0},{2,3},{3,2},{4,5},{5,4},{6,7},{7,6},{8,9},{9,8},{10,11... | collective-permute-start | bytes 393224 | tf_op jit(solution)/shard_map/ppermute | solution.py:41
  166.4 3.8 %collective-permute-done.22 = bf16[16,4096]{1,0:T(8,128)(2,1)S(1)} collective-permute-done((bf16[16,4096]{1,0:T(8,128)(2,1)S(1)}, bf16[16,4096]{1,0:T(8,128)(2,1)S(1)}, u32[]{:S(2)}, u32[]{:S(2)}) %collective-permute-start.22) | collective-permute-done | bytes 131104 | tf_op jit(solution)/shard_map/ppermute | solution.py:41
  182.5 6.1 %collective-permute-done.29.refs_9_ = bf16[512,512]{1,0:T(8,128)(2,1)} collective-permute-done((bf16[512,512]{1,0:T(8,128)(2,1)}, bf16[512,512]{1,0:T(8,128)(2,1)}, u32[]{:S(2)}, u32[]{:S(2)}) %collective-permute-start.29) | collective-permute-done | bytes 524320 | tf_op jit(solution)/shard_map/ppermute | solution.py:41
  191.3 10.4 %all-reduce = f32[64]{0:T(128)S(1)} all-reduce(f32[64]{0:T(128)S(1)} %add_dynamic-update-slice_fusion), channel_id=3, replica_groups=mesh['z'=4,'xl'=2,'core'=2,'y'=4,'xh'=2] {'y'}, use_global_device_ids=true, to_apply=%add | all-reduce | flops 64 | bytes 512
  202.5 16.7 %trunk_matmul.1 = bf16[512,1024]{1,0:T(8,128)(2,1)} custom-call(s32[3]{0:T(128)S(1)} %pad_add_fusion.place_ref, bf16[8,512,1024]{2,1,0:T(8,128)(2,1)} %all-gather.5.cloned.1.call-done.acts_ref, bf16[2,512,512]{2,1,0:T(8,128)(2,1)S(1)} %pad_maximum_fusion.refs_0_, bf16[2,512,512]{2,1,0:T(8,128)(2,1)S(1)} %collective-permute-done.11.refs_1_, ...), custom_call_target="tpu_custom_call" | custom-call | flops 8589934592 | bytes 25165824 | tf_op jit(solution)/shard_map/trunk_matmul/pallas_call | solution.py:117
  (122 shorter events, 48.2 us)
Async XLA Ops:
  7.2 195.3 %all-gather.5.cloned.1.call-start = ((), (), s32[]{:S(2)}) async-start(), calls=%async_computation.1 | async-start | bytes 9437184 | tf_op jit(solution)/shard_map/all_gather | solution.py:211
  14.7 19.9 %collective-permute-start.1 = (bf16[512,512]{1,0:T(8,128)(2,1)}, bf16[512,512]{1,0:T(8,128)(2,1)}, u32[]{:S(2)}, u32[]{:S(2)}) collective-permute-start(bf16[512,512]{1,0:T(8,128)(2,1)} %get-tuple-element.51), channel_id=1, source_target_pairs={{0,64},{1,65},{2,34},{3,35},{4,4},{5,5},{6,102},{7,103},{8,72},{9,... | collective-permute-start | bytes 1572872 | tf_op jit(solution)/shard_map/ppermute | solution.py:207
  34.6 16.2 %collective-permute-start.4 = (bf16[16,2048]{1,0:T(8,128)(2,1)S(1)}, bf16[16,2048]{1,0:T(8,128)(2,1)S(1)}, u32[]{:S(2)}, u32[]{:S(2)}) collective-permute-start(bf16[16,2048]{1,0:T(8,128)(2,1)S(1)} %reshape.163), channel_id=1, source_target_pairs={{0,32},{32,64},{64,96},{96,0},{1,33},{33,65},{65,97},{97,1},{2,34}... | collective-permute-start | bytes 196616 | tf_op jit(solution)/shard_map/ppermute | solution.py:41
  35.7 15.1 %collective-permute-start.3 = (bf16[16,2048]{1,0:T(8,128)(2,1)S(1)}, bf16[16,2048]{1,0:T(8,128)(2,1)S(1)}, u32[]{:S(2)}, u32[]{:S(2)}) collective-permute-start(bf16[16,2048]{1,0:T(8,128)(2,1)S(1)} %reshape.163), channel_id=1, source_target_pairs={{0,64},{32,96},{64,0},{96,32},{1,65},{33,97},{65,1},{97,33},{2,66}... | collective-permute-start | bytes 196616 | tf_op jit(solution)/shard_map/ppermute | solution.py:41
  38.6 20.2 %collective-permute-start.6 = (bf16[512,512]{1,0:T(8,128)(2,1)}, bf16[512,512]{1,0:T(8,128)(2,1)S(1)}, u32[]{:S(2)}, u32[]{:S(2)}) collective-permute-start(bf16[512,512]{1,0:T(8,128)(2,1)} %collective-permute-done), channel_id=1, source_target_pairs={{0,0},{1,16},{2,2},{3,18},{4,4},{5,20},{6,6},{7,22},{8,8},{9,24},{... | collective-permute-start | bytes 1572872 | tf_op jit(solution)/shard_map/ppermute | solution.py:221
  40.3 24.4 %collective-permute-start.7 = (bf16[512,512]{1,0:T(8,128)(2,1)}, bf16[512,512]{1,0:T(8,128)(2,1)S(1)}, u32[]{:S(2)}, u32[]{:S(2)}) collective-permute-start(bf16[512,512]{1,0:T(8,128)(2,1)} %collective-permute-done.1), channel_id=1, source_target_pairs={{0,4},{1,20},{2,6},{3,22},{4,0},{5,16},{6,2},{7,18},{8,12},{9,28},... | collective-permute-start | bytes 1572872 | tf_op jit(solution)/shard_map/ppermute | solution.py:221
  64.8 38.0 %collective-permute-start.13 = (bf16[2,512,512]{2,1,0:T(8,128)(2,1)S(1)}, bf16[2,512,512]{2,1,0:T(8,128)(2,1)S(1)}, u32[]{:S(2)}, u32[]{:S(2)}) collective-permute-start(bf16[2,512,512]{2,1,0:T(8,128)(2,1)S(1)} %pad_maximum_fusion.refs_0_), channel_id=1, source_target_pairs={{0,8},{8,0},{1,9},{9,1},{2,10},{10,2},{3,11},{11,3},{4,12},{12,4},... | collective-permute-start | bytes 3145736 | tf_op jit(solution)/shard_map/ppermute | solution.py:41
  64.9 37.9 %collective-permute-start.12 = (bf16[2,512,512]{2,1,0:T(8,128)(2,1)S(1)}, bf16[2,512,512]{2,1,0:T(8,128)(2,1)S(1)}, u32[]{:S(2)}, u32[]{:S(2)}) collective-permute-start(bf16[2,512,512]{2,1,0:T(8,128)(2,1)S(1)} %pad_maximum_fusion.refs_0_), channel_id=1, source_target_pairs={{0,32},{32,64},{64,96},{96,0},{1,33},{33,65},{65,97},{97,1},{2,34}... | collective-permute-start | bytes 3145736 | tf_op jit(solution)/shard_map/ppermute | solution.py:41
  65.0 37.8 %collective-permute-start.11 = (bf16[2,512,512]{2,1,0:T(8,128)(2,1)S(1)}, bf16[2,512,512]{2,1,0:T(8,128)(2,1)S(1)}, u32[]{:S(2)}, u32[]{:S(2)}) collective-permute-start(bf16[2,512,512]{2,1,0:T(8,128)(2,1)S(1)} %pad_maximum_fusion.refs_0_), channel_id=1, source_target_pairs={{0,96},{32,0},{64,32},{96,64},{1,97},{33,1},{65,33},{97,65},{2,98}... | collective-permute-start | bytes 3145736 | tf_op jit(solution)/shard_map/ppermute | solution.py:41
  103.8 15.4 %collective-permute-start.16 = (bf16[4,64,512]{2,1,0:T(8,128)(2,1)S(1)}, bf16[4,64,512]{2,1,0:T(8,128)(2,1)S(1)}, u32[]{:S(2)}, u32[]{:S(2)}) collective-permute-start(bf16[4,64,512]{2,1,0:T(8,128)(2,1)S(1)} %bitcast.95), channel_id=1, source_target_pairs={{0,32},{32,64},{64,96},{96,0},{1,33},{33,65},{65,97},{97,1},{2,34}... | collective-permute-start | bytes 786440 | tf_op jit(solution)/shard_map/ppermute | solution.py:41
  103.8 17.8 %collective-permute-start.15 = (bf16[4,64,512]{2,1,0:T(8,128)(2,1)S(1)}, bf16[4,64,512]{2,1,0:T(8,128)(2,1)S(1)}, u32[]{:S(2)}, u32[]{:S(2)}) collective-permute-start(bf16[4,64,512]{2,1,0:T(8,128)(2,1)S(1)} %bitcast.96), channel_id=1, source_target_pairs={{0,64},{32,96},{64,0},{96,32},{1,65},{33,97},{65,1},{97,33},{2,66}... | collective-permute-start | bytes 786440 | tf_op jit(solution)/shard_map/ppermute | solution.py:41
  106.6 15.0 %collective-permute-start.14 = (bf16[4,64,512]{2,1,0:T(8,128)(2,1)S(1)}, bf16[4,64,512]{2,1,0:T(8,128)(2,1)S(1)}, u32[]{:S(2)}, u32[]{:S(2)}) collective-permute-start(bf16[4,64,512]{2,1,0:T(8,128)(2,1)S(1)} %bitcast.97), channel_id=1, source_target_pairs={{0,96},{32,0},{64,32},{96,64},{1,97},{33,1},{65,33},{97,65},{2,98}... | collective-permute-start | bytes 786440 | tf_op jit(solution)/shard_map/ppermute | solution.py:41
  109.2 35.3 %collective-permute-start.19 = (bf16[2,512,512]{2,1,0:T(8,128)(2,1)S(1)}, bf16[2,512,512]{2,1,0:T(8,128)(2,1)}, u32[]{:S(2)}, u32[]{:S(2)}) collective-permute-start(bf16[2,512,512]{2,1,0:T(8,128)(2,1)S(1)} %pad_maximum_fusion.refs_0_), channel_id=1, source_target_pairs={{0,16},{16,0},{1,17},{17,1},{2,18},{18,2},{3,19},{19,3},{4,20},{20... | collective-permute-start | bytes 3145736 | tf_op jit(solution)/shard_map/ppermute | solution.py:41
  110.6 33.9 %collective-permute-start.17 = (bf16[2,512,512]{2,1,0:T(8,128)(2,1)S(1)}, bf16[2,512,512]{2,1,0:T(8,128)(2,1)}, u32[]{:S(2)}, u32[]{:S(2)}) collective-permute-start(bf16[2,512,512]{2,1,0:T(8,128)(2,1)S(1)} %collective-permute-done.11.refs_1_), channel_id=1, source_target_pairs={{0,8},{8,0},{1,9},{9,1},{2,10},{10,2},{3,11},{11,3},{4,12},{12,4},... | collective-permute-start | bytes 3145736 | tf_op jit(solution)/shard_map/ppermute | solution.py:41
  119.9 24.7 %collective-permute-start.18 = (bf16[2,512,512]{2,1,0:T(8,128)(2,1)S(1)}, bf16[2,512,512]{2,1,0:T(8,128)(2,1)}, u32[]{:S(2)}, u32[]{:S(2)}) collective-permute-start(bf16[2,512,512]{2,1,0:T(8,128)(2,1)S(1)} %collective-permute-done.12.refs_2_), channel_id=1, source_target_pairs={{0,8},{8,0},{1,9},{9,1},{2,10},{10,2},{3,11},{11,3},{4,12},{12,4},... | collective-permute-start | bytes 3145736 | tf_op jit(solution)/shard_map/ppermute | solution.py:41
  121.6 15.9 %collective-permute-start.21 = (bf16[512,512]{1,0:T(8,128)(2,1)}, bf16[512,512]{1,0:T(8,128)(2,1)}, u32[]{:S(2)}, u32[]{:S(2)}) collective-permute-start(bf16[512,512]{1,0:T(8,128)(2,1)} %slice_bitcast_fusion.2), channel_id=1, source_target_pairs={{0,32},{32,64},{64,96},{96,0},{1,33},{33,65},{65,97},{97,1},{2,34}... | collective-permute-start | bytes 1572872 | tf_op jit(solution)/shard_map/ppermute | solution.py:41
  122.3 15.2 %collective-permute-start.20 = (bf16[512,512]{1,0:T(8,128)(2,1)}, bf16[512,512]{1,0:T(8,128)(2,1)}, u32[]{:S(2)}, u32[]{:S(2)}) collective-permute-start(bf16[512,512]{1,0:T(8,128)(2,1)} %slice_bitcast_fusion.3), channel_id=1, source_target_pairs={{0,96},{32,0},{64,32},{96,64},{1,97},{33,1},{65,33},{97,65},{2,98}... | collective-permute-start | bytes 1572872 | tf_op jit(solution)/shard_map/ppermute | solution.py:41
  144.6 25.6 %collective-permute-start.25 = (bf16[2,512,512]{2,1,0:T(8,128)(2,1)}, bf16[2,512,512]{2,1,0:T(8,128)(2,1)}, u32[]{:S(2)}, u32[]{:S(2)}) collective-permute-start(bf16[2,512,512]{2,1,0:T(8,128)(2,1)} %collective-permute-done.19.refs_5_), channel_id=1, source_target_pairs={{0,8},{8,0},{1,9},{9,1},{2,10},{10,2},{3,11},{11,3},{4,12},{12,4},... | collective-permute-start | bytes 3145736 | tf_op jit(solution)/shard_map/ppermute | solution.py:41
  144.6 27.1 %collective-permute-start.24 = (bf16[2,512,512]{2,1,0:T(8,128)(2,1)}, bf16[2,512,512]{2,1,0:T(8,128)(2,1)}, u32[]{:S(2)}, u32[]{:S(2)}) collective-permute-start(bf16[2,512,512]{2,1,0:T(8,128)(2,1)} %collective-permute-done.19.refs_5_), channel_id=1, source_target_pairs={{0,32},{32,64},{64,96},{96,0},{1,33},{33,65},{65,97},{97,1},{2,34}... | collective-permute-start | bytes 3145736 | tf_op jit(solution)/shard_map/ppermute | solution.py:41
  146.2 25.5 %collective-permute-start.23 = (bf16[2,512,512]{2,1,0:T(8,128)(2,1)}, bf16[2,512,512]{2,1,0:T(8,128)(2,1)}, u32[]{:S(2)}, u32[]{:S(2)}) collective-permute-start(bf16[2,512,512]{2,1,0:T(8,128)(2,1)} %collective-permute-done.19.refs_5_), channel_id=1, source_target_pairs={{0,96},{32,0},{64,32},{96,64},{1,97},{33,1},{65,33},{97,65},{2,98}... | collective-permute-start | bytes 3145736 | tf_op jit(solution)/shard_map/ppermute | solution.py:41
  147.9 15.8 %collective-permute-start.26 = (bf16[512,512]{1,0:T(8,128)(2,1)}, bf16[512,512]{1,0:T(8,128)(2,1)}, u32[]{:S(2)}, u32[]{:S(2)}) collective-permute-start(bf16[512,512]{1,0:T(8,128)(2,1)} %collective-permute-done.20.refs_3_), channel_id=1, source_target_pairs={{0,8},{8,0},{1,9},{9,1},{2,10},{10,2},{3,11},{11,3},{4,12},{12,4},... | collective-permute-start | bytes 1572872 | tf_op jit(solution)/shard_map/ppermute | solution.py:41
  173.6 15.0 %collective-permute-start.29 = (bf16[512,512]{1,0:T(8,128)(2,1)}, bf16[512,512]{1,0:T(8,128)(2,1)}, u32[]{:S(2)}, u32[]{:S(2)}) collective-permute-start(bf16[512,512]{1,0:T(8,128)(2,1)} %slice_bitcast_fusion), channel_id=1, source_target_pairs={{0,32},{32,64},{64,96},{96,0},{1,33},{33,65},{65,97},{97,1},{2,34}... | collective-permute-start | bytes 1572872 | tf_op jit(solution)/shard_map/ppermute | solution.py:41
  178.7 23.7 %collective-permute-start.30 = (bf16[2,512,512]{2,1,0:T(8,128)(2,1)}, bf16[2,512,512]{2,1,0:T(8,128)(2,1)}, u32[]{:S(2)}, u32[]{:S(2)}) collective-permute-start(bf16[2,512,512]{2,1,0:T(8,128)(2,1)} %collective-permute-done.23.refs_6_), channel_id=1, source_target_pairs={{0,8},{8,0},{1,9},{9,1},{2,10},{10,2},{3,11},{11,3},{4,12},{12,4},... | collective-permute-start | bytes 3145736 | tf_op jit(solution)/shard_map/ppermute | solution.py:41
  178.7 23.7 %collective-permute-start.31 = (bf16[2,512,512]{2,1,0:T(8,128)(2,1)}, bf16[2,512,512]{2,1,0:T(8,128)(2,1)}, u32[]{:S(2)}, u32[]{:S(2)}) collective-permute-start(bf16[2,512,512]{2,1,0:T(8,128)(2,1)} %collective-permute-done.24.refs_7_), channel_id=1, source_target_pairs={{0,8},{8,0},{1,9},{9,1},{2,10},{10,2},{3,11},{11,3},{4,12},{12,4},... | collective-permute-start | bytes 3145736 | tf_op jit(solution)/shard_map/ppermute | solution.py:41
  (23 other events, 250.7 us)
Sparse Core Ops, SparseCore 0:
  13.7 135.6 all-gather.4

commit v5 on v4

--- a/solution.py
+++ b/solution.py
@@ -1,3 +1,4 @@
+import functools
 import itertools
 
 import jax
@@ -69,73 +70,67 @@
     return attn_out.astype(jnp.bfloat16).reshape(row_count, heads_here * HEAD_WIDTH)
 
 
-def trunk_kernel(place_ref, acts_ref, *refs):
-    residual_ref, out_ref = refs[20], refs[21]
-    j = pl.program_id(0)
+def trunk_kernel(count, place_ref, *refs):
+    acts, own, other = refs[:count], refs[count : 2 * count], refs[2 * count : 3 * count]
+    base_ref, out_ref = refs[3 * count], refs[3 * count + 1]
 
     def tile(blocks):
-        total = residual_ref[...].astype(jnp.float32)
-        for e in range(XL):
-            for s in range(Z):
-                for v in range(2):
-                    if s == 2:
-                        block = blocks[5 * e + 3 + v][...]
-                    else:
-                        block = blocks[5 * e + min(s, 2)][v]
-                    depth = block.shape[0]
-                    group = lax.rem(place_ref[0] + 2 * Y - s - 2 * v, Y) * XH + lax.rem(
-                        place_ref[1] + e, XH
-                    )
-                    total = total + jnp.dot(
-                        acts_ref[group, :, v * depth : (v + 1) * depth],
-                        block,
-                        preferred_element_type=jnp.float32,
-                    )
-        out_ref[...] = total.astype(jnp.bfloat16)
-
-    @pl.when(j < 2)
+        total = base_ref[...].astype(jnp.float32)
+        for a, b in zip(acts, blocks):
+            total = total + jnp.dot(a[...], b[...], preferred_element_type=jnp.float32)
+        out_ref[...] = total.astype(out_ref.dtype)
+
+    @pl.when(pl.program_id(0) < 2)
     def _():
-        tile(refs[:10])
-
-    @pl.when(j >= 2)
+        tile(own)
+
+    @pl.when(pl.program_id(0) >= 2)
     def _():
-        tile(refs[10:20])
-
-
-def trunk_matmul(place, acts, own, other, residual):
-    groups, rows, depth = acts.shape
-    half = residual.shape[1] // CORE
+        tile(other)
+
+
+def trunk_part(place, acts, terms, base, dtype):
+    rows = acts.shape[1]
+    half = base.shape[1] // CORE
     width = half // 2
-
-    def spec(w, index):
-        shape = w.shape[:-1] + (width,)
-        return pl.BlockSpec(shape, lambda j, p: (0,) * (len(shape) - 1) + (index(j),))
+    depth = acts.shape[2] // 2
+
+    def act_spec(s, e, v):
+        def index(j, p):
+            group = lax.rem(p[0] + 2 * Y - s - 2 * v, Y) * XH + lax.rem(p[1] + e, XH)
+            return (group, 0, v)
+
+        return pl.BlockSpec((None, rows, depth), index, pipeline_mode=pl.Buffered(1))
+
+    def weight_spec(w, v, index):
+        if w.ndim == 3:
+            return pl.BlockSpec((None, depth, width), lambda j, p: (v, 0, index(j)))
+        return pl.BlockSpec((depth, width), lambda j, p: (0, index(j)))
 
     tile = pl.BlockSpec(
         (rows, width), lambda j, p: (0, jnp.where(j < 2, p[2], 1 - p[2]) * 2 + lax.rem(j, 2))
     )
+    count = len(terms)
     return pl.pallas_call(
-        trunk_kernel,
+        functools.partial(trunk_kernel, count),
         grid_spec=pltpu.PrefetchScalarGridSpec(
             num_scalar_prefetch=1,
             grid=(4,),
-            in_specs=[
-                pl.BlockSpec(acts.shape, lambda j, p: (0, 0, 0), pipeline_mode=pl.Buffered(1))
-            ]
-            + [spec(w, lambda j: jnp.minimum(j, 1)) for w in own]
-            + [spec(w, lambda j: jnp.maximum(j - 2, 0)) for w in other]
+            in_specs=[act_spec(s, e, v) for s, e, v, _, _ in terms]
+            + [weight_spec(w, v, lambda j: jnp.minimum(j, 1)) for _, _, v, w, _ in terms]
+            + [weight_spec(w, v, lambda j: jnp.maximum(j - 2, 0)) for _, _, v, _, w in terms]
             + [tile],
             out_specs=tile,
         ),
-        out_shape=jax.ShapeDtypeStruct(residual.shape, jnp.bfloat16),
-        compiler_params=pltpu.CompilerParams(vmem_limit_bytes=44 * 2**20),
+        out_shape=jax.ShapeDtypeStruct(base.shape, dtype),
+        compiler_params=pltpu.CompilerParams(vmem_limit_bytes=40 * 2**20),
         cost_estimate=pl.CostEstimate(
-            flops=2 * rows * groups * depth * CORE * half,
-            bytes_accessed=2 * (groups * rows * depth + groups * depth * CORE * half),
+            flops=2 * rows * count * depth * CORE * half,
+            bytes_accessed=2 * count * depth * (rows + CORE * half) + 8 * rows * CORE * half,
             transcendentals=0,
         ),
-        name="trunk_matmul",
-    )(place, acts, *own, *other, residual)
+        name="trunk_part",
+    )(place, *[pltpu.with_memory_space_constraint(acts, pltpu.HBM)] * count, *[t[3] for t in terms], *[t[4] for t in terms], base)
 
 
 def norm_kernel(place_ref, p0, p1, p2, p3, gain_ref, out_ref):
@@ -202,6 +197,7 @@
     cand_count = cand_len.shape[0]
 
     lock = lax.optimization_barrier
+    place = jnp.stack([lax.rem(y - z + Y, Y), lax.rem(xh + xl, XH), core])
     rows_half = out_weight.shape[0] // 2
     moved = [
         lax.ppermute(out_weight[v * rows_half : (v + 1) * rows_half], ALL, spread_moves(v))
@@ -210,6 +206,8 @@
     attn_out = attention(query, keys, values, cand_len)
     acts = lax.all_gather(attn_out, TENSOR, axis=0, tiled=False)
 
+    attn_out, *moved = lock((attn_out, *moved))
+    moved = [lax.ppermute(m, ALL, column_moves(v)) for v, m in enumerate(moved)]
     last_rows = jnp.arange(cand_count, dtype=jnp.int32) * SEQUENCE_SLOTS + cand_len - 1
     picked = jnp.concatenate(
         [jnp.take(attn_out, last_rows, axis=0), jnp.take(residual, last_rows, axis=0)], axis=1
@@ -217,67 +215,71 @@
     depth = attn_out.shape[1]
     width = out_weight.shape[1]
     near = lax.all_gather(picked, ("xl", "core"), axis=0, tiled=True)
-    near, *moved = lock((near, *moved))
-    moved = [lax.ppermute(m, ALL, column_moves(v)) for v, m in enumerate(moved)]
     rows = jnp.concatenate([near] + [from_ahead(near, "z", Z, s) for s in (1, 2, 3)], axis=0)
+    rows, *moved = lock((rows, *moved))
+    w, swapped = {}, {}
+    w[0, 0] = jnp.stack(moved)
+    w[1, 0] = from_ahead(w[0, 0], "z", Z, 1)
+    w[3, 0] = from_ahead(w[0, 0], "z", Z, 3)
     own = jnp.dot(rows[:, :depth], out_weight, preferred_element_type=jnp.float32)
     res = rows[:, depth:]
     res = jnp.where(core == 0, res[:, :width], res[:, width:]).astype(jnp.float32)
     own = jnp.where((y == z) & (xh == xl), own + res, own).astype(jnp.bfloat16)
     pair = jnp.stack([own, from_ahead(own, "xh", XH, 1)])
-    pair, *moved = lock((pair, *moved))
-    w, swapped = {}, {}
-    w[0, 0] = jnp.stack(moved)
-    w[1, 0] = from_ahead(w[0, 0], "z", Z, 1)
-    w[3, 0] = from_ahead(w[0, 0], "z", Z, 3)
-    swapped[0, 0] = from_ahead(w[0, 0], "core", CORE, 1)
     parts = [pair] + [from_ahead(pair, "y", Y, s) for s in (1, 2, 3)]
     pooled = sum(jnp.sum(p.astype(jnp.float32), axis=0) for p in parts).astype(jnp.bfloat16)
     near = lax.all_gather(pooled, ("xl", "core"), axis=0, tiled=False)
-    near, w[0, 0], w[1, 0], w[3, 0], swapped[0, 0] = lock(
-        (near, w[0, 0], w[1, 0], w[3, 0], swapped[0, 0])
-    )
+    near, w[1, 0], w[3, 0], w[0, 0] = lock((near, w[1, 0], w[3, 0], w[0, 0]))
+    pieces = [near] + [from_ahead(near, "z", Z, s) for s in (1, 2, 3)]
     w[0, 1] = from_ahead(w[0, 0], "xl", XL, 1)
-    pieces = [near] + [from_ahead(near, "z", Z, s) for s in (1, 2, 3)]
-    features = normalize(pieces, norm_gain, z)
+    swapped[0, 0] = from_ahead(w[0, 0], "core", CORE, 1)
     w[2, 0, 0] = from_ahead(w[1, 0][0], "z", Z, 1)
     w[2, 0, 1] = from_ahead(w[3, 0][1], "z", Z, 3)
-    swapped[1, 0] = from_ahead(w[1, 0], "core", CORE, 1)
-    swapped[3, 0] = from_ahead(w[3, 0], "core", CORE, 1)
+    features = normalize(pieces, norm_gain, z)
+    features, w[0, 1], swapped[0, 0] = lock((features, w[0, 1], swapped[0, 0]))
+    w[1, 1] = from_ahead(w[0, 1], "z", Z, 1)
+    w[3, 1] = from_ahead(w[0, 1], "z", Z, 3)
+    for n in ((1, 0), (3, 0)):
+        swapped[n] = from_ahead(w[n], "core", CORE, 1)
     first = jax.nn.silu(
         jnp.dot(features, head_w1[0], preferred_element_type=jnp.float32) + head_b1[0]
     ).astype(jnp.bfloat16)
     terms = jnp.dot(first, head_w2[0], preferred_element_type=jnp.float32).astype(jnp.bfloat16)
-    names = [(0, 1), (2, 0, 0), (2, 0, 1)]
-    terms, swapped[1, 0], swapped[3, 0], *late = lock(
-        (terms, swapped[1, 0], swapped[3, 0], *[w[n] for n in names])
-    )
-    w.update(zip(names, late))
-    w[1, 1] = from_ahead(w[0, 1], "z", Z, 1)
-    w[3, 1] = from_ahead(w[0, 1], "z", Z, 3)
-    for n in names:
+    terms, w[2, 0, 0], w[2, 0, 1], swapped[1, 0], swapped[3, 0] = lock(
+        (terms, w[2, 0, 0], w[2, 0, 1], swapped[1, 0], swapped[3, 0])
+    )
+    for n in ((2, 0, 0), (2, 0, 1), (0, 1)):
         swapped[n] = from_ahead(w[n], "core", CORE, 1)
     count = terms.shape[0] // Y
     terms = lax.all_to_all(
         terms.reshape(Y, count, terms.shape[1]), "y", split_axis=0, concat_axis=0, tiled=True
     )
+
+    def products(*names):
+        for n in names:
+            for v in (0, 1) if len(n) == 2 else n[2:]:
+                yield (n[0], n[1], v, w[n], swapped[n])
+
+    first_names = ((0, 0), (1, 0), (3, 0), (2, 0, 0), (2, 0, 1), (0, 1))
+    trunk = trunk_part(place, acts, list(products(*first_names)), residual, jnp.float32)
+    terms, w[1, 1], w[3, 1], trunk = lock((terms, w[1, 1], w[3, 1], trunk))
+    w[2, 1, 0] = from_ahead(w[1, 1][0], "z", Z, 1)
+    w[2, 1, 1] = from_ahead(w[3, 1][1], "z", Z, 3)
+    for n in ((1, 1), (3, 1)):
+        swapped[n] = from_ahead(w[n], "core", CORE, 1)
     half = jnp.sum(terms.astype(jnp.float32), axis=0).astype(jnp.bfloat16)
     other = from_ahead(half, "xh", XH, 1)
-    other, w[1, 1], w[3, 1], *late = lock((other, w[1, 1], w[3, 1], *[swapped[n] for n in names]))
-    swapped.update(zip(names, late))
-    w[2, 1, 0] = from_ahead(w[1, 1][0], "z", Z, 1)
-    w[2, 1, 1] = from_ahead(w[3, 1][1], "z", Z, 3)
-    for n in ((1, 1), (3, 1), (2, 1, 0), (2, 1, 1)):
-        swapped[n] = from_ahead(w[n], "core", CORE, 1)
+    trunk = trunk_part(place, acts, list(products((1, 1), (3, 1))), trunk, jnp.float32)
+    other, trunk = lock((other, trunk))
     second = jax.nn.silu(half.astype(jnp.float32) + other.astype(jnp.float32) + head_b2[0])
     mine = jnp.sum(second * head_w3[0].astype(jnp.float32), axis=-1) + head_b3[0]
     scores = lax.all_gather(mine, "y", axis=0, tiled=False)
+    scores, w[2, 1, 0], w[2, 1, 1] = lock((scores, w[2, 1, 0], w[2, 1, 1]))
+    for n in ((2, 1, 0), (2, 1, 1)):
+        swapped[n] = from_ahead(w[n], "core", CORE, 1)
     scores = jnp.roll(scores, z, axis=0).reshape(1, Y * count)
-
-    order = [n for e in range(XL) for n in ((0, e), (1, e), (3, e), (2, e, 0), (2, e, 1))]
-    place = jnp.stack([lax.rem(y - z + Y, Y), lax.rem(xh + xl, XH), core])
-    trunk_out = trunk_matmul(
-        place, acts, [w[n] for n in order], [swapped[n] for n in order], residual
+    trunk_out = trunk_part(
+        place, acts, list(products((2, 1, 0), (2, 1, 1))), trunk, jnp.bfloat16
     )
     return (trunk_out, scores)
 

time: 227 us -> 232 us (1.022)
  starting transfers between devices: 63.1 us -> 50.3 us
  blocking collectives: 32.7 us -> 43.1 us
  Pallas kernels: 19.6 us -> 25.1 us
  local copies, waits for them, and re-layouts: 16.6 us -> 21.6 us
  waiting for transfers between devices: 63.3 us -> 59.5 us
    all_gather x1, blocking collectives: 5.57 us -> 25 us  [local(): near = lax.all_gather(picked, ('xl', 'core'), axis=0, tiled=True)]
    all_to_all x1, waiting for transfers between devices: 9.9 us -> 0.01 us  [local(): lax.all_to_all(terms.reshape(Y, count, terms.shape[1]), 'y', split_axis=0...]
    ppermute x2, waiting for transfers between devices: 0.01 us -> 9.75 us  [local(): lax.ppermute(out_weight[v * rows_half:(v + 1) * rows_half], ALL, spread_m...]
    all_gather x1, blocking collectives: 16.7 us -> 7.16 us  [local(): near = lax.all_gather(pooled, ('xl', 'core'), axis=0, tiled=False)]
    ppermute x2, starting transfers between devices: 12.1 us -> 5.37 us  [local(): moved = [lax.ppermute(m, ALL, column_moves(v)) for v, m in enumerate(moved)]]
    unnamed x29 -> x43, local copies, waits for them, and re-layouts: 4.82 us -> 11 us
    ppermute x2, waiting for transfers between devices: 5.87 us -> 0.01 us  [local(): moved = [lax.ppermute(m, ALL, column_moves(v)) for v, m in enumerate(moved)]]
    pallas_call x1 -> x3, Pallas kernels: 16.7 us -> 22.3 us  [trunk_part(): pl.pallas_call(functools.partial(trunk_kernel, count), grid_spec=pltpu.Pr...]
  transfers between devices with their start and end apart: 36 -> 36, of which waited for: 13 -> 11; matrix products, arithmetic and copies ran while one was open for 10% -> 9% of each run, Pallas kernels for 1% -> 9%
where the time goes in v5:
time: 232 us; the launch traced here: 230 us
  waiting for transfers between devices  59.5 us (26%)
  starting transfers between devices  50.3 us (22%)
  blocking collectives  43.1 us (19%)
  Pallas kernels  25.1 us (11%)
  local copies, waits for them, and re-layouts  21.6 us (9%)
  between operations  15.7 us (7%)
  matrix products  10.9 us (5%)
  other arithmetic  3.35 us (1%)
    ppermute x30, waiting for transfers between devices, from_ahead(): return lax.ppermute(x, axis, [(i, (i - step) % size) for i in range(size)])  49.7 us
    ppermute x30, starting transfers between devices, from_ahead(): return lax.ppermute(x, axis, [(i, (i - step) % size) for i in range(size)])  32.6 us
    all_gather x1, blocking collectives, local(): near = lax.all_gather(picked, ('xl', 'core'), axis=0, tiled=True)  25 us
    pallas_call x3, Pallas kernels, trunk_part(): pl.pallas_call(functools.partial(trunk_kernel, count), grid_spec=pltpu.Pr...  22.3 us
    unnamed x43, local copies, waits for them, and re-layouts  11 us
    unnamed x1, blocking collectives  10.9 us
    ppermute x2, waiting for transfers between devices, local(): lax.ppermute(out_weight[v * rows_half:(v + 1) * rows_half], ALL, spread_m...  9.75 us
    dot_general x1, matrix products, local(): jnp.dot(first, head_w2[0], preferred_element_type=jnp.float32)  8.05 us
  transfers between devices with their start and end apart: 36, of which 11 were waited for; matrix products, arithmetic and copies ran while one was open for 9% of the time, Pallas kernels for 9%

profile of v5, /device:TPU:0, one launch (start us, length us, event | category | flops | bytes accessed | tf_op | source)
XLA Modules:
  0.0 229.7 jit_solution(14002387057378166288)
XLA Ops:
  15.1 5.9 %collective-permute-start.1 = (bf16[512,512]{1,0:T(8,128)(2,1)S(1)}, bf16[512,512]{1,0:T(8,128)(2,1)}, u32[]{:S(2)}, u32[]{:S(2)}) collective-permute-start(bf16[512,512]{1,0:T(8,128)(2,1)S(1)} %get-tuple-element.59), channel_id=1, source_target_pairs={{0,64},{1,65},{2,34},{3,35},{4,4},{5,5},{6,102},{7,103},{8,72},{9,... | collective-permute-start | bytes 1572872 | tf_op jit(solution)/shard_map/ppermute | solution.py:203
  23.3 9.8 %collective-permute-done.1 = bf16[512,512]{1,0:T(8,128)(2,1)} collective-permute-done((bf16[512,512]{1,0:T(8,128)(2,1)S(1)}, bf16[512,512]{1,0:T(8,128)(2,1)}, u32[]{:S(2)}, u32[]{:S(2)}) %collective-permute-start.1) | collective-permute-done | bytes 524320 | tf_op jit(solution)/shard_map/ppermute | solution.py:203
  35.3 3.7 %collective-permute-start.6 = (bf16[512,512]{1,0:T(8,128)(2,1)}, bf16[512,512]{1,0:T(8,128)(2,1)S(1)}, u32[]{:S(2)}, u32[]{:S(2)}) collective-permute-start(bf16[512,512]{1,0:T(8,128)(2,1)} %collective-permute-done.1), channel_id=1, source_target_pairs={{0,4},{1,20},{2,6},{3,22},{4,0},{5,16},{6,2},{7,18},{8,12},{9,28},... | collective-permute-start | bytes 1572872 | tf_op jit(solution)/shard_map/ppermute | solution.py:210
  39.1 25.0 %all-gather.2 = bf16[4,4,2048]{2,1,0:T(4,128)(2,1)S(1)} all-gather(bf16[1,4,2048]{2,1,0:T(4,128)(2,1)S(1)} %maximum_bitcast_fusion), channel_id=1, replica_groups=mesh['z'=4,'xl'=2,'core'=2,'y'=4,'xh'=2] {'xl','core'}, dimensions={0}, use_global_device_ids=true | all-gather | bytes 81920 | tf_op jit(solution)/shard_map/all_gather | solution.py:217
  64.1 4.6 %collective-permute-start.2 = (bf16[16,2048]{1,0:T(8,128)(2,1)S(1)}, bf16[16,2048]{1,0:T(8,128)(2,1)S(1)}, u32[]{:S(2)}, u32[]{:S(2)}) collective-permute-start(bf16[16,2048]{1,0:T(8,128)(2,1)S(1)} %reshape.163), channel_id=1, source_target_pairs={{0,96},{32,0},{64,32},{96,64},{1,97},{33,1},{65,33},{97,65},{2,98}... | collective-permute-start | bytes 196616 | tf_op jit(solution)/shard_map/ppermute | solution.py:42
  69.6 2.3 %collective-permute-done.2 = bf16[16,2048]{1,0:T(8,128)(2,1)S(1)} collective-permute-done((bf16[16,2048]{1,0:T(8,128)(2,1)S(1)}, bf16[16,2048]{1,0:T(8,128)(2,1)S(1)}, u32[]{:S(2)}, u32[]{:S(2)}) %collective-permute-start.2) | collective-permute-done | bytes 65568 | tf_op jit(solution)/shard_map/ppermute | solution.py:42
  72.0 3.0 %collective-permute-done.3 = bf16[16,2048]{1,0:T(8,128)(2,1)S(1)} collective-permute-done((bf16[16,2048]{1,0:T(8,128)(2,1)S(1)}, bf16[16,2048]{1,0:T(8,128)(2,1)S(1)}, u32[]{:S(2)}, u32[]{:S(2)}) %collective-permute-start.3) | collective-permute-done | bytes 65568 | tf_op jit(solution)/shard_map/ppermute | solution.py:42
  80.8 5.6 %collective-permute-done.7 = bf16[64,512]{1,0:T(8,128)(2,1)S(1)} collective-permute-done((bf16[64,512]{1,0:T(8,128)(2,1)S(1)}, bf16[64,512]{1,0:T(8,128)(2,1)S(1)}, u32[]{:S(2)}, u32[]{:S(2)}) %collective-permute-start.7) | collective-permute-done | bytes 65568 | tf_op jit(solution)/shard_map/ppermute | solution.py:42
  86.8 2.7 %collective-permute-start.9 = (bf16[2,64,512]{2,1,0:T(8,128)(2,1)S(1)}, bf16[2,64,512]{2,1,0:T(8,128)(2,1)S(1)}, u32[]{:S(2)}, u32[]{:S(2)}) collective-permute-start(bf16[2,64,512]{2,1,0:T(8,128)(2,1)S(1)} %pad_maximum_fusion.2), channel_id=1, source_target_pairs={{0,4},{2,6},{4,0},{6,2},{1,5},{3,7},{5,1},{7,3},{8,12},{10,14},{12... | collective-permute-start | bytes 393224 | tf_op jit(solution)/shard_map/ppermute | solution.py:42
  91.0 3.4 %collective-permute-done.10 = bf16[2,64,512]{2,1,0:T(8,128)(2,1)S(1)} collective-permute-done((bf16[2,64,512]{2,1,0:T(8,128)(2,1)S(1)}, bf16[2,64,512]{2,1,0:T(8,128)(2,1)S(1)}, u32[]{:S(2)}, u32[]{:S(2)}) %collective-permute-start.10) | collective-permute-done | bytes 131104 | tf_op jit(solution)/shard_map/ppermute | solution.py:42
  94.3 5.0 %collective-permute-done.9 = bf16[2,64,512]{2,1,0:T(8,128)(2,1)S(1)} collective-permute-done((bf16[2,64,512]{2,1,0:T(8,128)(2,1)S(1)}, bf16[2,64,512]{2,1,0:T(8,128)(2,1)S(1)}, u32[]{:S(2)}, u32[]{:S(2)}) %collective-permute-start.9) | collective-permute-done | bytes 131104 | tf_op jit(solution)/shard_map/ppermute | solution.py:42
  99.4 7.2 %all-gather = bf16[256,512]{1,0:T(8,128)(2,1)S(1)} all-gather(bf16[64,512]{1,0:T(8,128)(2,1)S(1)} %add_convert_fusion), channel_id=2, replica_groups=mesh['z'=4,'xl'=2,'core'=2,'y'=4,'xh'=2] {'xl','core'}, dimensions={0}, use_global_device_ids=true | all-gather | bytes 327680 | tf_op jit(solution)/shard_map/all_gather | solution.py:231
  107.4 3.0 %collective-permute-start.13 = (bf16[4,64,512]{2,1,0:T(8,128)(2,1)S(1)}, bf16[4,64,512]{2,1,0:T(8,128)(2,1)S(1)}, u32[]{:S(2)}, u32[]{:S(2)}) collective-permute-start(bf16[4,64,512]{2,1,0:T(8,128)(2,1)S(1)} %bitcast.95), channel_id=1, source_target_pairs={{0,96},{32,0},{64,32},{96,64},{1,97},{33,1},{65,33},{97,65},{2,98}... | collective-permute-start | bytes 786440 | tf_op jit(solution)/shard_map/ppermute | solution.py:42
  113.5 8.6 %collective-permute-done.13.p1 = bf16[4,64,512]{2,1,0:T(8,128)(2,1)S(1)} collective-permute-done((bf16[4,64,512]{2,1,0:T(8,128)(2,1)S(1)}, bf16[4,64,512]{2,1,0:T(8,128)(2,1)S(1)}, u32[]{:S(2)}, u32[]{:S(2)}) %collective-permute-start.13) | collective-permute-done | bytes 262176 | tf_op jit(solution)/shard_map/ppermute | solution.py:42
  122.1 3.7 %collective-permute-start.18 = (bf16[512,512]{1,0:T(8,128)(2,1)}, bf16[512,512]{1,0:T(8,128)(2,1)}, u32[]{:S(2)}, u32[]{:S(2)}) collective-permute-start(bf16[512,512]{1,0:T(8,128)(2,1)} %slice_bitcast_fusion.3), channel_id=1, source_target_pairs={{0,96},{32,0},{64,32},{96,64},{1,97},{33,1},{65,33},{97,65},{2,98}... | collective-permute-start | bytes 1572872 | tf_op jit(solution)/shard_map/ppermute | solution.py:42
  126.0 19.6 %collective-permute-done.16.refs_18_.refs_19_ = bf16[2,512,512]{2,1,0:T(8,128)(2,1)S(1)} collective-permute-done((bf16[2,512,512]{2,1,0:T(8,128)(2,1)S(1)}, bf16[2,512,512]{2,1,0:T(8,128)(2,1)S(1)}, u32[]{:S(2)}, u32[]{:S(2)}) %collective-permute-start.16) | collective-permute-done | bytes 1048608 | tf_op jit(solution)/shard_map/ppermute | solution.py:42
  146.6 2.8 %normalize.1 = bf16[64,8192]{1,0:T(8,128)(2,1)} custom-call(s32[1]{0:T(128)} %bitcast.15.place_ref, bf16[4,64,512]{2,1,0:T(8,128)(2,1)} %bitcast.98, bf16[4,64,512]{2,1,0:T(8,128)(2,1)} %copy-done.10, bf16[4,64,512]{2,1,0:T(8,128)(2,1)} %copy-done.11, bf16[4,64,512]{2,1,0:T(8,128)(2,1)} %copy-done.12, f32[1,8192]{1,0:T(1,128)} %bitcast.107), custom_call_target="tpu_custom_call" | custom-call | flops 4194304 | bytes 2097152 | tf_op jit(solution)/shard_map/normalize/pallas_call | solution.py:164
  152.1 8.1 %convolution_convert_fusion = bf16[64,4096]{1,0:T(8,128)(2,1)} fusion(bf16[1,512,4096]{2,1,0:T(8,128)(2,1)} %param.24, bf16[64,8192]{1,0:T(8,128)(2,1)} %normalize.1, bf16[1,8192,512]{2,1,0:T(8,128)(2,1)} %param.22, f32[512]{0:T(512)S(1)} %bitcast.109), kind=kOutput, calls=%fused_computation.4 | convolution fusion | flops 805765120 | bytes 14157824 | tf_op jit(solution)/shard_map/dot_general | solution.py:247
  160.8 5.1 %all-to-all-start = ((bf16[4,16,4096]{2,1,0:T(8,128)(2,1)}), bf16[4,16,4096]{2,1,0:T(8,128)(2,1)}, u32[]{:S(2)}, u32[]{:S(2)}) async-start(bf16[4,16,4096]{2,1,0:T(8,128)(2,1)} %bitcast.93), calls=%async_computation | async-start | bytes 1048576 | tf_op jit(solution)/shard_map/all_to_all | solution.py:254
  168.3 11.3 %trunk_part.3.refs_12_ = f32[512,1024]{1,0:T(8,128)S(1)} custom-call(s32[3]{0:T(128)S(1)} %pad_add_fusion.place_ref, bf16[8,512,1024]{2,1,0:T(8,128)(2,1)} %all-gather.5.cloned.1.call-done.refs_0_.refs_1_.refs_2_.refs_3_.refs_4_.refs_5_.refs_6_.refs_7_.refs_8_.refs_9_, ...), custom_call_target="tpu_custom_call" | custom-call | flops 5368709120 | bytes 19922944 | tf_op jit(solution)/shard_map/trunk_part/pallas_call | solution.py:114
  188.7 3.2 %collective-permute-start.30 = (bf16[512,512]{1,0:T(8,128)(2,1)}, bf16[512,512]{1,0:T(8,128)(2,1)}, u32[]{:S(2)}, u32[]{:S(2)}) collective-permute-start(bf16[512,512]{1,0:T(8,128)(2,1)} %slice_bitcast_fusion.1), channel_id=1, source_target_pairs={{0,96},{32,0},{64,32},{96,64},{1,97},{33,1},{65,33},{97,65},{2,98}... | collective-permute-start | bytes 1572872 | tf_op jit(solution)/shard_map/ppermute | solution.py:42
  197.6 6.0 %trunk_part.4.refs_6_ = f32[512,1024]{1,0:T(8,128)S(1)} custom-call(s32[3]{0:T(128)S(1)} %pad_add_fusion.place_ref, bf16[8,512,1024]{2,1,0:T(8,128)(2,1)} %all-gather.5.cloned.1.call-done.refs_0_.refs_1_.refs_2_.refs_3_.refs_4_.refs_5_.refs_6_.refs_7_.refs_8_.refs_9_, ...), custom_call_target="tpu_custom_call" | custom-call | flops 2147483648 | bytes 10485760 | tf_op jit(solution)/shard_map/trunk_part/pallas_call | solution.py:114
  204.0 10.9 %all-reduce = f32[64]{0:T(128)S(1)} all-reduce(f32[64]{0:T(128)S(1)} %add_dynamic-update-slice_fusion), channel_id=3, replica_groups=mesh['z'=4,'xl'=2,'core'=2,'y'=4,'xh'=2] {'y'}, use_global_device_ids=true, to_apply=%add | all-reduce | flops 64 | bytes 512
  218.0 4.9 %trunk_part.5 = bf16[512,1024]{1,0:T(8,128)(2,1)} custom-call(s32[3]{0:T(128)S(1)} %pad_add_fusion.place_ref, bf16[8,512,1024]{2,1,0:T(8,128)(2,1)} %all-gather.5.cloned.1.call-done.refs_0_.refs_1_.refs_2_.refs_3_.refs_4_.refs_5_.refs_6_.refs_7_.refs_8_.refs_9_, ...), custom_call_target="tpu_custom_call" | custom-call | flops 1073741824 | bytes 7340032 | tf_op jit(solution)/shard_map/trunk_part/pallas_call | solution.py:114
  (137 shorter events, 48.7 us)
Async XLA Ops:
  7.2 158.7 %all-gather.5.cloned.1.call-start = ((), (), s32[]{:S(2)}) async-start(), calls=%async_computation.1 | async-start | bytes 9437184 | tf_op jit(solution)/shard_map/all_gather | solution.py:207
  15.1 17.9 %collective-permute-start.1 = (bf16[512,512]{1,0:T(8,128)(2,1)S(1)}, bf16[512,512]{1,0:T(8,128)(2,1)}, u32[]{:S(2)}, u32[]{:S(2)}) collective-permute-start(bf16[512,512]{1,0:T(8,128)(2,1)S(1)} %get-tuple-element.59), channel_id=1, source_target_pairs={{0,64},{1,65},{2,34},{3,35},{4,4},{5,5},{6,102},{7,103},{8,72},{9,... | collective-permute-start | bytes 1572872 | tf_op jit(solution)/shard_map/ppermute | solution.py:203
  33.6 41.8 %collective-permute-start.5 = (bf16[512,512]{1,0:T(8,128)(2,1)}, bf16[512,512]{1,0:T(8,128)(2,1)S(1)}, u32[]{:S(2)}, u32[]{:S(2)}) collective-permute-start(bf16[512,512]{1,0:T(8,128)(2,1)} %collective-permute-done), channel_id=1, source_target_pairs={{0,0},{1,16},{2,2},{3,18},{4,4},{5,20},{6,6},{7,22},{8,8},{9,24},{... | collective-permute-start | bytes 1572872 | tf_op jit(solution)/shard_map/ppermute | solution.py:210
  35.3 40.1 %collective-permute-start.6 = (bf16[512,512]{1,0:T(8,128)(2,1)}, bf16[512,512]{1,0:T(8,128)(2,1)S(1)}, u32[]{:S(2)}, u32[]{:S(2)}) collective-permute-start(bf16[512,512]{1,0:T(8,128)(2,1)} %collective-permute-done.1), channel_id=1, source_target_pairs={{0,4},{1,20},{2,6},{3,22},{4,0},{5,16},{6,2},{7,18},{8,12},{9,28},... | collective-permute-start | bytes 1572872 | tf_op jit(solution)/shard_map/ppermute | solution.py:210
  75.5 31.1 %collective-permute-start.11 = (bf16[2,512,512]{2,1,0:T(8,128)(2,1)S(1)}, bf16[2,512,512]{2,1,0:T(8,128)(2,1)S(1)}, u32[]{:S(2)}, u32[]{:S(2)}) collective-permute-start(bf16[2,512,512]{2,1,0:T(8,128)(2,1)S(1)} %pad_maximum_fusion.refs_10_.refs_11_), channel_id=1, source_target_pairs={{0,96},{32,0},{64,32},{96,64},{1,97},{33,1},{65,33},{97,65},{2,98}... | collective-permute-start | bytes 3145736 | tf_op jit(solution)/shard_map/ppermute | solution.py:42
  76.4 30.2 %collective-permute-start.12 = (bf16[2,512,512]{2,1,0:T(8,128)(2,1)S(1)}, bf16[2,512,512]{2,1,0:T(8,128)(2,1)S(1)}, u32[]{:S(2)}, u32[]{:S(2)}) collective-permute-start(bf16[2,512,512]{2,1,0:T(8,128)(2,1)S(1)} %pad_maximum_fusion.refs_10_.refs_11_), channel_id=1, source_target_pairs={{0,32},{32,64},{64,96},{96,0},{1,33},{33,65},{65,97},{97,1},{2,34}... | collective-permute-start | bytes 3145736 | tf_op jit(solution)/shard_map/ppermute | solution.py:42
  106.6 38.9 %collective-permute-start.16 = (bf16[2,512,512]{2,1,0:T(8,128)(2,1)S(1)}, bf16[2,512,512]{2,1,0:T(8,128)(2,1)S(1)}, u32[]{:S(2)}, u32[]{:S(2)}) collective-permute-start(bf16[2,512,512]{2,1,0:T(8,128)(2,1)S(1)} %pad_maximum_fusion.refs_10_.refs_11_), channel_id=1, source_target_pairs={{0,16},{16,0},{1,17},{17,1},{2,18},{18,2},{3,19},{19,3},{4,20},{20... | collective-permute-start | bytes 3145736 | tf_op jit(solution)/shard_map/ppermute | solution.py:42
  107.3 42.1 %collective-permute-start.17 = (bf16[2,512,512]{2,1,0:T(8,128)(2,1)S(1)}, bf16[2,512,512]{2,1,0:T(8,128)(2,1)}, u32[]{:S(2)}, u32[]{:S(2)}) collective-permute-start(bf16[2,512,512]{2,1,0:T(8,128)(2,1)S(1)} %pad_maximum_fusion.refs_10_.refs_11_), channel_id=1, source_target_pairs={{0,8},{8,0},{1,9},{9,1},{2,10},{10,2},{3,11},{11,3},{4,12},{12,4},... | collective-permute-start | bytes 3145736 | tf_op jit(solution)/shard_map/ppermute | solution.py:42
  107.4 14.7 %collective-permute-start.13 = (bf16[4,64,512]{2,1,0:T(8,128)(2,1)S(1)}, bf16[4,64,512]{2,1,0:T(8,128)(2,1)S(1)}, u32[]{:S(2)}, u32[]{:S(2)}) collective-permute-start(bf16[4,64,512]{2,1,0:T(8,128)(2,1)S(1)} %bitcast.95), channel_id=1, source_target_pairs={{0,96},{32,0},{64,32},{96,64},{1,97},{33,1},{65,33},{97,65},{2,98}... | collective-permute-start | bytes 786440 | tf_op jit(solution)/shard_map/ppermute | solution.py:42
  110.3 15.5 %collective-permute-start.14 = (bf16[4,64,512]{2,1,0:T(8,128)(2,1)S(1)}, bf16[4,64,512]{2,1,0:T(8,128)(2,1)S(1)}, u32[]{:S(2)}, u32[]{:S(2)}) collective-permute-start(bf16[4,64,512]{2,1,0:T(8,128)(2,1)S(1)} %bitcast.96), channel_id=1, source_target_pairs={{0,64},{32,96},{64,0},{96,32},{1,65},{33,97},{65,1},{97,33},{2,66}... | collective-permute-start | bytes 786440 | tf_op jit(solution)/shard_map/ppermute | solution.py:42
  111.0 14.8 %collective-permute-start.15 = (bf16[4,64,512]{2,1,0:T(8,128)(2,1)S(1)}, bf16[4,64,512]{2,1,0:T(8,128)(2,1)S(1)}, u32[]{:S(2)}, u32[]{:S(2)}) collective-permute-start(bf16[4,64,512]{2,1,0:T(8,128)(2,1)S(1)} %bitcast.97), channel_id=1, source_target_pairs={{0,32},{32,64},{64,96},{96,0},{1,33},{33,65},{65,97},{97,1},{2,34}... | collective-permute-start | bytes 786440 | tf_op jit(solution)/shard_map/ppermute | solution.py:42
  122.1 27.7 %collective-permute-start.18 = (bf16[512,512]{1,0:T(8,128)(2,1)}, bf16[512,512]{1,0:T(8,128)(2,1)}, u32[]{:S(2)}, u32[]{:S(2)}) collective-permute-start(bf16[512,512]{1,0:T(8,128)(2,1)} %slice_bitcast_fusion.3), channel_id=1, source_target_pairs={{0,96},{32,0},{64,32},{96,64},{1,97},{33,1},{65,33},{97,65},{2,98}... | collective-permute-start | bytes 1572872 | tf_op jit(solution)/shard_map/ppermute | solution.py:42
  125.8 26.3 %collective-permute-start.19 = (bf16[512,512]{1,0:T(8,128)(2,1)}, bf16[512,512]{1,0:T(8,128)(2,1)}, u32[]{:S(2)}, u32[]{:S(2)}) collective-permute-start(bf16[512,512]{1,0:T(8,128)(2,1)} %slice_bitcast_fusion.2), channel_id=1, source_target_pairs={{0,32},{32,64},{64,96},{96,0},{1,33},{33,65},{65,97},{97,1},{2,34}... | collective-permute-start | bytes 1572872 | tf_op jit(solution)/shard_map/ppermute | solution.py:42
  125.9 34.3 %collective-permute-start.20 = (bf16[2,512,512]{2,1,0:T(8,128)(2,1)S(1)}, bf16[2,512,512]{2,1,0:T(8,128)(2,1)}, u32[]{:S(2)}, u32[]{:S(2)}) collective-permute-start(bf16[2,512,512]{2,1,0:T(8,128)(2,1)S(1)} %collective-permute-done.11.refs_12_.refs_13_), channel_id=1, source_target_pairs={{0,8},{8,0},{1,9},{9,1},{2,10},{10,2},{3,11},{11,3},{4,12},{12,4},... | collective-permute-start | bytes 3145736 | tf_op jit(solution)/shard_map/ppermute | solution.py:42
  146.5 13.7 %collective-permute-start.21 = (bf16[2,512,512]{2,1,0:T(8,128)(2,1)S(1)}, bf16[2,512,512]{2,1,0:T(8,128)(2,1)}, u32[]{:S(2)}, u32[]{:S(2)}) collective-permute-start(bf16[2,512,512]{2,1,0:T(8,128)(2,1)S(1)} %collective-permute-done.12.refs_14_.refs_15_), channel_id=1, source_target_pairs={{0,8},{8,0},{1,9},{9,1},{2,10},{10,2},{3,11},{11,3},{4,12},{12,4},... | collective-permute-start | bytes 3145736 | tf_op jit(solution)/shard_map/ppermute | solution.py:42
  149.4 16.5 %collective-permute-start.26 = (bf16[2,512,512]{2,1,0:T(8,128)(2,1)}, bf16[2,512,512]{2,1,0:T(8,128)(2,1)}, u32[]{:S(2)}, u32[]{:S(2)}) collective-permute-start(bf16[2,512,512]{2,1,0:T(8,128)(2,1)} %copy-done.3), channel_id=1, source_target_pairs={{0,8},{8,0},{1,9},{9,1},{2,10},{10,2},{3,11},{11,3},{4,12},{12,4},... | collective-permute-start | bytes 3145736 | tf_op jit(solution)/shard_map/ppermute | solution.py:42
  149.9 31.2 %collective-permute-start.22 = (bf16[2,512,512]{2,1,0:T(8,128)(2,1)}, bf16[2,512,512]{2,1,0:T(8,128)(2,1)}, u32[]{:S(2)}, u32[]{:S(2)}) collective-permute-start(bf16[2,512,512]{2,1,0:T(8,128)(2,1)} %copy-done.3), channel_id=1, source_target_pairs={{0,96},{32,0},{64,32},{96,64},{1,97},{33,1},{65,33},{97,65},{2,98}... | collective-permute-start | bytes 3145736 | tf_op jit(solution)/shard_map/ppermute | solution.py:42
  152.1 28.9 %collective-permute-start.23 = (bf16[2,512,512]{2,1,0:T(8,128)(2,1)}, bf16[2,512,512]{2,1,0:T(8,128)(2,1)}, u32[]{:S(2)}, u32[]{:S(2)}) collective-permute-start(bf16[2,512,512]{2,1,0:T(8,128)(2,1)} %copy-done.3), channel_id=1, source_target_pairs={{0,32},{32,64},{64,96},{96,0},{1,33},{33,65},{65,97},{97,1},{2,34}... | collective-permute-start | bytes 3145736 | tf_op jit(solution)/shard_map/ppermute | solution.py:42
  160.8 20.3 %all-to-all-start = ((bf16[4,16,4096]{2,1,0:T(8,128)(2,1)}), bf16[4,16,4096]{2,1,0:T(8,128)(2,1)}, u32[]{:S(2)}, u32[]{:S(2)}) async-start(bf16[4,16,4096]{2,1,0:T(8,128)(2,1)} %bitcast.93), calls=%async_computation | async-start | bytes 1048576 | tf_op jit(solution)/shard_map/all_to_all | solution.py:254
  181.1 12.8 %collective-permute-start.28 = (bf16[2,512,512]{2,1,0:T(8,128)(2,1)}, bf16[2,512,512]{2,1,0:T(8,128)(2,1)S(1)}, u32[]{:S(2)}, u32[]{:S(2)}) collective-permute-start(bf16[2,512,512]{2,1,0:T(8,128)(2,1)} %collective-permute-done.22.refs_4_.refs_5_), channel_id=1, source_target_pairs={{0,8},{8,0},{1,9},{9,1},{2,10},{10,2},{3,11},{11,3},{4,12},{12,4},... | collective-permute-start | bytes 3145736 | tf_op jit(solution)/shard_map/ppermute | solution.py:42
  181.2 12.7 %collective-permute-start.29 = (bf16[2,512,512]{2,1,0:T(8,128)(2,1)}, bf16[2,512,512]{2,1,0:T(8,128)(2,1)S(1)}, u32[]{:S(2)}, u32[]{:S(2)}) collective-permute-start(bf16[2,512,512]{2,1,0:T(8,128)(2,1)} %collective-permute-done.23.refs_6_.refs_7_), channel_id=1, source_target_pairs={{0,8},{8,0},{1,9},{9,1},{2,10},{10,2},{3,11},{11,3},{4,12},{12,4},... | collective-permute-start | bytes 3145736 | tf_op jit(solution)/shard_map/ppermute | solution.py:42
  184.7 19.0 %collective-permute-start.27 = (bf16[16,4096]{1,0:T(8,128)(2,1)S(1)}, bf16[16,4096]{1,0:T(8,128)(2,1)S(1)}, u32[]{:S(2)}, u32[]{:S(2)}) collective-permute-start(bf16[16,4096]{1,0:T(8,128)(2,1)S(1)} %reduce_sum.71), channel_id=1, source_target_pairs={{0,1},{1,0},{2,3},{3,2},{4,5},{5,4},{6,7},{7,6},{8,9},{9,8},{10,11... | collective-permute-start | bytes 393224 | tf_op jit(solution)/shard_map/ppermute | solution.py:42
  188.7 26.3 %collective-permute-start.30 = (bf16[512,512]{1,0:T(8,128)(2,1)}, bf16[512,512]{1,0:T(8,128)(2,1)}, u32[]{:S(2)}, u32[]{:S(2)}) collective-permute-start(bf16[512,512]{1,0:T(8,128)(2,1)} %slice_bitcast_fusion.1), channel_id=1, source_target_pairs={{0,96},{32,0},{64,32},{96,64},{1,97},{33,1},{65,33},{97,65},{2,98}... | collective-permute-start | bytes 1572872 | tf_op jit(solution)/shard_map/ppermute | solution.py:42
  193.8 21.2 %collective-permute-start.31 = (bf16[512,512]{1,0:T(8,128)(2,1)}, bf16[512,512]{1,0:T(8,128)(2,1)}, u32[]{:S(2)}, u32[]{:S(2)}) collective-permute-start(bf16[512,512]{1,0:T(8,128)(2,1)} %slice_bitcast_fusion), channel_id=1, source_target_pairs={{0,32},{32,64},{64,96},{96,0},{1,33},{33,65},{65,97},{97,1},{2,34}... | collective-permute-start | bytes 1572872 | tf_op jit(solution)/shard_map/ppermute | solution.py:42
  (31 other events, 310.9 us)
Sparse Core Ops, SparseCore 0:
  13.7 141.9 all-gather.4

commit v6 on v5

--- a/solution.py
+++ b/solution.py
@@ -70,37 +70,55 @@
     return attn_out.astype(jnp.bfloat16).reshape(row_count, heads_here * HEAD_WIDTH)
 
 
-def trunk_kernel(count, place_ref, *refs):
-    acts, own, other = refs[:count], refs[count : 2 * count], refs[2 * count : 3 * count]
-    base_ref, out_ref = refs[3 * count], refs[3 * count + 1]
+def trunk_kernel(picks, place_ref, here_ref, there_ref, *refs):
+    count = len(picks)
+    own, other = refs[:count], refs[count : 2 * count]
+    base_ref, out_ref, acts, sems = refs[2 * count :]
+    j = pl.program_id(0)
+
+    def copies(source):
+        for i, (s, v) in enumerate(picks):
+            depth = acts.shape[2]
+            group = lax.rem(place_ref[0] + 2 * Y - s - 2 * v, Y)
+            yield pltpu.make_async_copy(
+                source.at[group, :, pl.ds(v * depth, depth)], acts.at[i], sems.at[i]
+            )
+
+    @pl.when(j == 0)
+    def _():
+        @pl.when(place_ref[1] == 0)
+        def _():
+            for copy in copies(here_ref):
+                copy.start()
+
+        @pl.when(place_ref[1] == 1)
+        def _():
+            for copy in copies(there_ref):
+                copy.start()
+
+        for copy in copies(here_ref):
+            copy.wait()
 
     def tile(blocks):
         total = base_ref[...].astype(jnp.float32)
-        for a, b in zip(acts, blocks):
-            total = total + jnp.dot(a[...], b[...], preferred_element_type=jnp.float32)
+        for i, block in enumerate(blocks):
+            total = total + jnp.dot(acts[i], block[...], preferred_element_type=jnp.float32)
         out_ref[...] = total.astype(out_ref.dtype)
 
-    @pl.when(pl.program_id(0) < 2)
+    @pl.when(j < 2)
     def _():
         tile(own)
 
-    @pl.when(pl.program_id(0) >= 2)
+    @pl.when(j >= 2)
     def _():
         tile(other)
 
 
-def trunk_part(place, acts, terms, base, dtype):
-    rows = acts.shape[1]
+def trunk_part(place, here, there, terms, base, dtype):
+    rows = here.shape[1]
     half = base.shape[1] // CORE
     width = half // 2
-    depth = acts.shape[2] // 2
-
-    def act_spec(s, e, v):
-        def index(j, p):
-            group = lax.rem(p[0] + 2 * Y - s - 2 * v, Y) * XH + lax.rem(p[1] + e, XH)
-            return (group, 0, v)
-
-        return pl.BlockSpec((None, rows, depth), index, pipeline_mode=pl.Buffered(1))
+    depth = here.shape[2] // 2
 
     def weight_spec(w, v, index):
         if w.ndim == 3:
@@ -111,26 +129,38 @@
         (rows, width), lambda j, p: (0, jnp.where(j < 2, p[2], 1 - p[2]) * 2 + lax.rem(j, 2))
     )
     count = len(terms)
+    in_hbm = pltpu.with_memory_space_constraint
     return pl.pallas_call(
-        functools.partial(trunk_kernel, count),
+        functools.partial(trunk_kernel, [(s, v) for s, v, _, _ in terms]),
         grid_spec=pltpu.PrefetchScalarGridSpec(
             num_scalar_prefetch=1,
             grid=(4,),
-            in_specs=[act_spec(s, e, v) for s, e, v, _, _ in terms]
-            + [weight_spec(w, v, lambda j: jnp.minimum(j, 1)) for _, _, v, w, _ in terms]
-            + [weight_spec(w, v, lambda j: jnp.maximum(j - 2, 0)) for _, _, v, _, w in terms]
+            in_specs=[pl.BlockSpec(memory_space=pltpu.HBM)] * 2
+            + [weight_spec(w, v, lambda j: jnp.minimum(j, 1)) for _, v, w, _ in terms]
+            + [weight_spec(w, v, lambda j: jnp.maximum(j - 2, 0)) for _, v, _, w in terms]
             + [tile],
             out_specs=tile,
+            scratch_shapes=[
+                pltpu.VMEM((count, rows, depth), here.dtype),
+                pltpu.SemaphoreType.DMA((count,)),
+            ],
         ),
         out_shape=jax.ShapeDtypeStruct(base.shape, dtype),
-        compiler_params=pltpu.CompilerParams(vmem_limit_bytes=40 * 2**20),
+        compiler_params=pltpu.CompilerParams(vmem_limit_bytes=32 * 2**20),
         cost_estimate=pl.CostEstimate(
             flops=2 * rows * count * depth * CORE * half,
             bytes_accessed=2 * count * depth * (rows + CORE * half) + 8 * rows * CORE * half,
             transcendentals=0,
         ),
         name="trunk_part",
-    )(place, *[pltpu.with_memory_space_constraint(acts, pltpu.HBM)] * count, *[t[3] for t in terms], *[t[4] for t in terms], base)
+    )(
+        place,
+        in_hbm(here, pltpu.HBM),
+        in_hbm(there, pltpu.HBM),
+        *[t[2] for t in terms],
+        *[t[3] for t in terms],
+        base,
+    )
 
 
 def norm_kernel(place_ref, p0, p1, p2, p3, gain_ref, out_ref):
@@ -197,17 +227,14 @@
     cand_count = cand_len.shape[0]
 
     lock = lax.optimization_barrier
-    place = jnp.stack([lax.rem(y - z + Y, Y), lax.rem(xh + xl, XH), core])
     rows_half = out_weight.shape[0] // 2
     moved = [
         lax.ppermute(out_weight[v * rows_half : (v + 1) * rows_half], ALL, spread_moves(v))
         for v in range(2)
     ]
     attn_out = attention(query, keys, values, cand_len)
-    acts = lax.all_gather(attn_out, TENSOR, axis=0, tiled=False)
-
-    attn_out, *moved = lock((attn_out, *moved))
-    moved = [lax.ppermute(m, ALL, column_moves(v)) for v, m in enumerate(moved)]
+    here = lax.all_gather(attn_out, "y", axis=0, tiled=False)
+
     last_rows = jnp.arange(cand_count, dtype=jnp.int32) * SEQUENCE_SLOTS + cand_len - 1
     picked = jnp.concatenate(
         [jnp.take(attn_out, last_rows, axis=0), jnp.take(residual, last_rows, axis=0)], axis=1
@@ -215,72 +242,80 @@
     depth = attn_out.shape[1]
     width = out_weight.shape[1]
     near = lax.all_gather(picked, ("xl", "core"), axis=0, tiled=True)
+    near, held, *moved = lock((near, attn_out, *moved))
+    across = from_ahead(held, "xh", XH, 1)
+    moved = [lax.ppermute(m, ALL, column_moves(v)) for v, m in enumerate(moved)]
     rows = jnp.concatenate([near] + [from_ahead(near, "z", Z, s) for s in (1, 2, 3)], axis=0)
-    rows, *moved = lock((rows, *moved))
-    w, swapped = {}, {}
-    w[0, 0] = jnp.stack(moved)
-    w[1, 0] = from_ahead(w[0, 0], "z", Z, 1)
-    w[3, 0] = from_ahead(w[0, 0], "z", Z, 3)
     own = jnp.dot(rows[:, :depth], out_weight, preferred_element_type=jnp.float32)
     res = rows[:, depth:]
     res = jnp.where(core == 0, res[:, :width], res[:, width:]).astype(jnp.float32)
     own = jnp.where((y == z) & (xh == xl), own + res, own).astype(jnp.bfloat16)
     pair = jnp.stack([own, from_ahead(own, "xh", XH, 1)])
+    pair, across, *moved = lock((pair, across, *moved))
+    there = lax.all_gather(across, "y", axis=0, tiled=False)
+    w, swapped = {}, {}
+    w[0, 0] = jnp.stack(moved)
+    w[1, 0] = from_ahead(w[0, 0], "z", Z, 1)
+    w[3, 0] = from_ahead(w[0, 0], "z", Z, 3)
+    w[0, 1] = from_ahead(w[0, 0], "xl", XL, 1)
     parts = [pair] + [from_ahead(pair, "y", Y, s) for s in (1, 2, 3)]
     pooled = sum(jnp.sum(p.astype(jnp.float32), axis=0) for p in parts).astype(jnp.bfloat16)
     near = lax.all_gather(pooled, ("xl", "core"), axis=0, tiled=False)
-    near, w[1, 0], w[3, 0], w[0, 0] = lock((near, w[1, 0], w[3, 0], w[0, 0]))
+    near, w[1, 0], w[3, 0], w[0, 1] = lock((near, w[1, 0], w[3, 0], w[0, 1]))
     pieces = [near] + [from_ahead(near, "z", Z, s) for s in (1, 2, 3)]
-    w[0, 1] = from_ahead(w[0, 0], "xl", XL, 1)
     swapped[0, 0] = from_ahead(w[0, 0], "core", CORE, 1)
     w[2, 0, 0] = from_ahead(w[1, 0][0], "z", Z, 1)
     w[2, 0, 1] = from_ahead(w[3, 0][1], "z", Z, 3)
+    for n in ((1, 0), (3, 0)):
+        swapped[n] = from_ahead(w[n], "core", CORE, 1)
     features = normalize(pieces, norm_gain, z)
-    features, w[0, 1], swapped[0, 0] = lock((features, w[0, 1], swapped[0, 0]))
+    features, w[2, 0, 0], w[2, 0, 1], swapped[0, 0], w[0, 1] = lock(
+        (features, w[2, 0, 0], w[2, 0, 1], swapped[0, 0], w[0, 1])
+    )
     w[1, 1] = from_ahead(w[0, 1], "z", Z, 1)
     w[3, 1] = from_ahead(w[0, 1], "z", Z, 3)
-    for n in ((1, 0), (3, 0)):
+    for n in ((2, 0, 0), (2, 0, 1), (0, 1)):
         swapped[n] = from_ahead(w[n], "core", CORE, 1)
     first = jax.nn.silu(
         jnp.dot(features, head_w1[0], preferred_element_type=jnp.float32) + head_b1[0]
     ).astype(jnp.bfloat16)
     terms = jnp.dot(first, head_w2[0], preferred_element_type=jnp.float32).astype(jnp.bfloat16)
-    terms, w[2, 0, 0], w[2, 0, 1], swapped[1, 0], swapped[3, 0] = lock(
-        (terms, w[2, 0, 0], w[2, 0, 1], swapped[1, 0], swapped[3, 0])
-    )
-    for n in ((2, 0, 0), (2, 0, 1), (0, 1)):
-        swapped[n] = from_ahead(w[n], "core", CORE, 1)
+    names = [(1, 0), (3, 0), (2, 0, 0), (2, 0, 1)]
+    terms, *early = lock((terms, *[swapped[n] for n in names]))
+    swapped.update(zip(names, early))
     count = terms.shape[0] // Y
     terms = lax.all_to_all(
         terms.reshape(Y, count, terms.shape[1]), "y", split_axis=0, concat_axis=0, tiled=True
     )
 
-    def products(*names):
-        for n in names:
-            for v in (0, 1) if len(n) == 2 else n[2:]:
-                yield (n[0], n[1], v, w[n], swapped[n])
-
-    first_names = ((0, 0), (1, 0), (3, 0), (2, 0, 0), (2, 0, 1), (0, 1))
-    trunk = trunk_part(place, acts, list(products(*first_names)), residual, jnp.float32)
-    terms, w[1, 1], w[3, 1], trunk = lock((terms, w[1, 1], w[3, 1], trunk))
+    def product(e, trunk, dtype, *names):
+        items = [
+            (n[0], v, w[n], swapped[n])
+            for n in names
+            for v in ((0, 1) if len(n) == 2 else n[2:])
+        ]
+        place = jnp.stack([lax.rem(y - z + Y, Y), lax.rem(xl + e, XH), core])
+        return trunk_part(place, here, there, items, trunk, dtype)
+
+    trunk = product(0, residual, jnp.float32, (0, 0), (1, 0), (3, 0), (2, 0, 0), (2, 0, 1))
+    terms, w[1, 1], w[3, 1], swapped[0, 1], trunk = lock(
+        (terms, w[1, 1], w[3, 1], swapped[0, 1], trunk)
+    )
     w[2, 1, 0] = from_ahead(w[1, 1][0], "z", Z, 1)
     w[2, 1, 1] = from_ahead(w[3, 1][1], "z", Z, 3)
     for n in ((1, 1), (3, 1)):
         swapped[n] = from_ahead(w[n], "core", CORE, 1)
     half = jnp.sum(terms.astype(jnp.float32), axis=0).astype(jnp.bfloat16)
     other = from_ahead(half, "xh", XH, 1)
-    trunk = trunk_part(place, acts, list(products((1, 1), (3, 1))), trunk, jnp.float32)
-    other, trunk = lock((other, trunk))
+    trunk = product(1, trunk, jnp.float32, (0, 1), (1, 1), (3, 1))
+    other, w[2, 1, 0], w[2, 1, 1], trunk = lock((other, w[2, 1, 0], w[2, 1, 1], trunk))
     second = jax.nn.silu(half.astype(jnp.float32) + other.astype(jnp.float32) + head_b2[0])
     mine = jnp.sum(second * head_w3[0].astype(jnp.float32), axis=-1) + head_b3[0]
-    scores = lax.all_gather(mine, "y", axis=0, tiled=False)
-    scores, w[2, 1, 0], w[2, 1, 1] = lock((scores, w[2, 1, 0], w[2, 1, 1]))
     for n in ((2, 1, 0), (2, 1, 1)):
         swapped[n] = from_ahead(w[n], "core", CORE, 1)
-    scores = jnp.roll(scores, z, axis=0).reshape(1, Y * count)
-    trunk_out = trunk_part(
-        place, acts, list(products((2, 1, 0), (2, 1, 1))), trunk, jnp.bfloat16
-    )
+    scores = jnp.stack([mine] + [from_ahead(mine, "y", Y, s) for s in (1, 2, 3)])
+    scores = jnp.roll(scores, lax.rem(y + z, Y), axis=0).reshape(1, Y * count)
+    trunk_out = product(1, trunk, jnp.bfloat16, (2, 1, 0), (2, 1, 1))
     return (trunk_out, scores)
 
 

time: 232 us -> 236 us (1.017)
  blocking collectives: 43.1 us -> 11.6 us
  starting transfers between devices: 50.3 us -> 70.6 us
  waiting for transfers between devices: 59.5 us -> 70.8 us
  Pallas kernels: 25.1 us -> 27.8 us
  local copies, waits for them, and re-layouts: 21.6 us -> 24.3 us
    all_gather x1, blocking collectives: 25 us -> 5.25 us  [local(): near = lax.all_gather(picked, ('xl', 'core'), axis=0, tiled=True)]
    ppermute x30 -> x34, starting transfers between devices: 32.6 us -> 51.6 us  [from_ahead(): return lax.ppermute(x, axis, [(i, (i - step) % size) for i in range(size)])]
    ppermute x30 -> x34, waiting for transfers between devices: 49.7 us -> 61 us  [from_ahead(): return lax.ppermute(x, axis, [(i, (i - step) % size) for i in range(size)])]
    unnamed x1 -> x0, blocking collectives: 10.9 us -> none
    ppermute x2, waiting for transfers between devices: 0.01 us -> 5.82 us  [local(): moved = [lax.ppermute(m, ALL, column_moves(v)) for v, m in enumerate(moved)]]
    ppermute x2, waiting for transfers between devices: 9.75 us -> 3.99 us  [local(): lax.ppermute(out_weight[v * rows_half:(v + 1) * rows_half], ALL, spread_m...]
    ppermute x2, starting transfers between devices: 7.29 us -> 11.2 us  [local(): lax.ppermute(out_weight[v * rows_half:(v + 1) * rows_half], ALL, spread_m...]
    pallas_call x3, Pallas kernels: 22.3 us -> 25 us  [trunk_part(): pl.pallas_call(functools.partial(trunk_kernel, [(s, v) for s, v, _, _ in...]
  transfers between devices with their start and end apart: 36 -> 41, of which waited for: 11 -> 14; matrix products, arithmetic and copies ran while one was open for 9% -> 9% of each run, Pallas kernels for 9% -> 9%
where the time goes in v6:
time: 236 us; the launch traced here: 235 us
  waiting for transfers between devices  70.8 us (30%)
  starting transfers between devices  70.6 us (30%)
  Pallas kernels  27.8 us (12%)
  local copies, waits for them, and re-layouts  24.3 us (10%)
  between operations  15.2 us (6%)
  blocking collectives  11.6 us (5%)
  matrix products  9.72 us (4%)
  other arithmetic  4.5 us (2%)
    ppermute x34, waiting for transfers between devices, from_ahead(): return lax.ppermute(x, axis, [(i, (i - step) % size) for i in range(size)])  61 us
    ppermute x34, starting transfers between devices, from_ahead(): return lax.ppermute(x, axis, [(i, (i - step) % size) for i in range(size)])  51.6 us
    pallas_call x3, Pallas kernels, trunk_part(): pl.pallas_call(functools.partial(trunk_kernel, [(s, v) for s, v, _, _ in...  25 us
    unnamed x51, local copies, waits for them, and re-layouts  12.7 us
    ppermute x2, starting transfers between devices, local(): lax.ppermute(out_weight[v * rows_half:(v + 1) * rows_half], ALL, spread_m...  11.2 us
    dot_general x1, matrix products, local(): jnp.dot(first, head_w2[0], preferred_element_type=jnp.float32)  8.06 us
    all_gather x1, blocking collectives, local(): near = lax.all_gather(pooled, ('xl', 'core'), axis=0, tiled=False)  6.32 us
    ppermute x2, waiting for transfers between devices, local(): moved = [lax.ppermute(m, ALL, column_moves(v)) for v, m in enumerate(moved)]  5.82 us
  transfers between devices with their start and end apart: 41, of which 14 were waited for; matrix products, arithmetic and copies ran while one was open for 9% of the time, Pallas kernels for 9%

profile of v6, /device:TPU:0, one launch (start us, length us, event | category | flops | bytes accessed | tf_op | source)
XLA Modules:
  0.0 234.5 jit_solution(6587746590105233370)
XLA Ops:
  14.7 5.4 %collective-permute-start = (bf16[512,512]{1,0:T(8,128)(2,1)}, bf16[512,512]{1,0:T(8,128)(2,1)}, u32[]{:S(2)}, u32[]{:S(2)}) collective-permute-start(bf16[512,512]{1,0:T(8,128)(2,1)} %get-tuple-element.68), channel_id=1, source_target_pairs={{0,0},{1,1},{2,98},{3,99},{4,68},{5,69},{6,38},{7,39},{8,8},{9,9},... | collective-permute-start | bytes 1572872 | tf_op jit(solution)/shard_map/ppermute | solution.py:232
  20.1 5.9 %collective-permute-start.1 = (bf16[512,512]{1,0:T(8,128)(2,1)}, bf16[512,512]{1,0:T(8,128)(2,1)}, u32[]{:S(2)}, u32[]{:S(2)}) collective-permute-start(bf16[512,512]{1,0:T(8,128)(2,1)} %get-tuple-element.67), channel_id=1, source_target_pairs={{0,64},{1,65},{2,34},{3,35},{4,4},{5,5},{6,102},{7,103},{8,72},{9,... | collective-permute-start | bytes 1572872 | tf_op jit(solution)/shard_map/ppermute | solution.py:232
  28.9 5.2 %all-gather.2 = bf16[4,4,2048]{2,1,0:T(4,128)(2,1)S(1)} all-gather(bf16[1,4,2048]{2,1,0:T(4,128)(2,1)S(1)} %maximum_bitcast_fusion), channel_id=1, replica_groups=mesh['z'=4,'xl'=2,'core'=2,'y'=4,'xh'=2] {'xl','core'}, dimensions={0}, use_global_device_ids=true | all-gather | bytes 81920 | tf_op jit(solution)/shard_map/all_gather | solution.py:244
  34.2 4.0 %collective-permute-done.1 = bf16[512,512]{1,0:T(8,128)(2,1)} collective-permute-done((bf16[512,512]{1,0:T(8,128)(2,1)}, bf16[512,512]{1,0:T(8,128)(2,1)}, u32[]{:S(2)}, u32[]{:S(2)}) %collective-permute-start.1) | collective-permute-done | bytes 524320 | tf_op jit(solution)/shard_map/ppermute | solution.py:232
  38.2 3.4 %collective-permute-start.2 = (bf16[16,2048]{1,0:T(8,128)(2,1)S(1)}, bf16[16,2048]{1,0:T(8,128)(2,1)S(1)}, u32[]{:S(2)}, u32[]{:S(2)}) collective-permute-start(bf16[16,2048]{1,0:T(8,128)(2,1)S(1)} %reshape.160), channel_id=1, source_target_pairs={{0,96},{32,0},{64,32},{96,64},{1,97},{33,1},{65,33},{97,65},{2,98}... | collective-permute-start | bytes 196616 | tf_op jit(solution)/shard_map/ppermute | solution.py:42
  42.8 3.0 %collective-permute-start.6 = (bf16[512,1024]{1,0:T(8,128)(2,1)S(1)}, bf16[512,1024]{1,0:T(8,128)(2,1)S(1)}, u32[]{:S(2)}, u32[]{:S(2)}) collective-permute-start(bf16[512,1024]{1,0:T(8,128)(2,1)S(1)} %bitcast.105), channel_id=1, source_target_pairs={{0,1},{1,0},{2,3},{3,2},{4,5},{5,4},{6,7},{7,6},{8,9},{9,8},{10,11... | collective-permute-start | bytes 3145736 | tf_op jit(solution)/shard_map/ppermute | solution.py:42
  49.9 3.0 %collective-permute-start.5 = (bf16[64,512]{1,0:T(8,128)(2,1)S(1)}, bf16[64,512]{1,0:T(8,128)(2,1)S(1)}, u32[]{:S(2)}, u32[]{:S(2)}) collective-permute-start(bf16[64,512]{1,0:T(8,128)(2,1)S(1)} %fusion.13), channel_id=1, source_target_pairs={{0,1},{1,0},{2,3},{3,2},{4,5},{5,4},{6,7},{7,6},{8,9},{9,8},{10,11... | collective-permute-start | bytes 196616 | tf_op jit(solution)/shard_map/ppermute | solution.py:42
  52.8 16.1 %collective-permute-done.5 = bf16[64,512]{1,0:T(8,128)(2,1)S(1)} collective-permute-done((bf16[64,512]{1,0:T(8,128)(2,1)S(1)}, bf16[64,512]{1,0:T(8,128)(2,1)S(1)}, u32[]{:S(2)}, u32[]{:S(2)}) %collective-permute-start.5) | collective-permute-done | bytes 65568 | tf_op jit(solution)/shard_map/ppermute | solution.py:42
  69.8 5.8 %collective-permute-done.8 = bf16[512,512]{1,0:T(8,128)(2,1)S(1)} collective-permute-done((bf16[512,512]{1,0:T(8,128)(2,1)}, bf16[512,512]{1,0:T(8,128)(2,1)S(1)}, u32[]{:S(2)}, u32[]{:S(2)}) %collective-permute-start.8) | collective-permute-done | bytes 524320 | tf_op jit(solution)/shard_map/ppermute | solution.py:247
  81.3 18.0 %collective-permute-start.14 = (bf16[2,512,512]{2,1,0:T(8,128)(2,1)S(1)}, bf16[2,512,512]{2,1,0:T(8,128)(2,1)S(1)}, u32[]{:S(2)}, u32[]{:S(2)}) collective-permute-start(bf16[2,512,512]{2,1,0:T(8,128)(2,1)S(1)} %pad_maximum_fusion.refs_0_.refs_1_), channel_id=1, source_target_pairs={{0,16},{16,0},{1,17},{17,1},{2,18},{18,2},{3,19},{19,3},{4,20},{20... | collective-permute-start | bytes 3145736 | tf_op jit(solution)/shard_map/ppermute | solution.py:42
  101.8 6.1 %collective-permute-done.11 = bf16[2,64,512]{2,1,0:T(8,128)(2,1)S(1)} collective-permute-done((bf16[2,64,512]{2,1,0:T(8,128)(2,1)S(1)}, bf16[2,64,512]{2,1,0:T(8,128)(2,1)S(1)}, u32[]{:S(2)}, u32[]{:S(2)}) %collective-permute-start.11) | collective-permute-done | bytes 131104 | tf_op jit(solution)/shard_map/ppermute | solution.py:42
  108.5 7.2 %collective-permute-done.9 = bf16[2,64,512]{2,1,0:T(8,128)(2,1)S(1)} collective-permute-done((bf16[2,64,512]{2,1,0:T(8,128)(2,1)S(1)}, bf16[2,64,512]{2,1,0:T(8,128)(2,1)S(1)}, u32[]{:S(2)}, u32[]{:S(2)}) %collective-permute-start.9) | collective-permute-done | bytes 131104 | tf_op jit(solution)/shard_map/ppermute | solution.py:42
  115.8 6.3 %all-gather.1 = bf16[256,512]{1,0:T(8,128)(2,1)S(1)} all-gather(bf16[64,512]{1,0:T(8,128)(2,1)S(1)} %add_convert_fusion), channel_id=3, replica_groups=mesh['z'=4,'xl'=2,'core'=2,'y'=4,'xh'=2] {'xl','core'}, dimensions={0}, use_global_device_ids=true | all-gather | bytes 327680 | tf_op jit(solution)/shard_map/all_gather | solution.py:263
  123.1 3.5 %collective-permute-start.15 = (bf16[4,64,512]{2,1,0:T(8,128)(2,1)S(1)}, bf16[4,64,512]{2,1,0:T(8,128)(2,1)S(1)}, u32[]{:S(2)}, u32[]{:S(2)}) collective-permute-start(bf16[4,64,512]{2,1,0:T(8,128)(2,1)S(1)} %bitcast.106), channel_id=1, source_target_pairs={{0,96},{32,0},{64,32},{96,64},{1,97},{33,1},{65,33},{97,65},{2,98}... | collective-permute-start | bytes 786440 | tf_op jit(solution)/shard_map/ppermute | solution.py:42
  130.4 2.9 %collective-permute-done.15.p1 = bf16[4,64,512]{2,1,0:T(8,128)(2,1)S(1)} collective-permute-done((bf16[4,64,512]{2,1,0:T(8,128)(2,1)S(1)}, bf16[4,64,512]{2,1,0:T(8,128)(2,1)S(1)}, u32[]{:S(2)}, u32[]{:S(2)}) %collective-permute-start.15) | collective-permute-done | bytes 262176 | tf_op jit(solution)/shard_map/ppermute | solution.py:42
  133.5 15.3 %collective-permute-done.16.p2 = bf16[4,64,512]{2,1,0:T(8,128)(2,1)S(1)} collective-permute-done((bf16[4,64,512]{2,1,0:T(8,128)(2,1)S(1)}, bf16[4,64,512]{2,1,0:T(8,128)(2,1)S(1)}, u32[]{:S(2)}, u32[]{:S(2)}) %collective-permute-start.16) | collective-permute-done | bytes 262176 | tf_op jit(solution)/shard_map/ppermute | solution.py:42
  148.7 6.2 %collective-permute-done.17.p3 = bf16[4,64,512]{2,1,0:T(8,128)(2,1)S(1)} collective-permute-done((bf16[4,64,512]{2,1,0:T(8,128)(2,1)S(1)}, bf16[4,64,512]{2,1,0:T(8,128)(2,1)S(1)}, u32[]{:S(2)}, u32[]{:S(2)}) %collective-permute-start.17) | collective-permute-done | bytes 262176 | tf_op jit(solution)/shard_map/ppermute | solution.py:42
  162.4 8.1 %convolution_convert_fusion = bf16[64,4096]{1,0:T(8,128)(2,1)} fusion(bf16[1,512,4096]{2,1,0:T(8,128)(2,1)} %param.24, bf16[64,8192]{1,0:T(8,128)(2,1)} %normalize.1, bf16[1,8192,512]{2,1,0:T(8,128)(2,1)} %param.22, f32[512]{0:T(512)S(1)} %bitcast.124), kind=kOutput, calls=%fused_computation.4 | convolution fusion | flops 805765120 | bytes 14157824 | tf_op jit(solution)/shard_map/dot_general | solution.py:282
  170.5 4.1 %all-to-all-start = ((bf16[4,16,4096]{2,1,0:T(8,128)(2,1)}), bf16[4,16,4096]{2,1,0:T(8,128)(2,1)}, u32[]{:S(2)}, u32[]{:S(2)}) async-start(bf16[4,16,4096]{2,1,0:T(8,128)(2,1)} %bitcast.103), calls=%async_computation | async-start | bytes 1048576 | tf_op jit(solution)/shard_map/all_to_all | solution.py:287
  178.4 10.3 %trunk_part.3.refs_12_ = f32[512,1024]{1,0:T(8,128)S(1)} custom-call(s32[3]{0:T(128)S(1)} %add_add_fusion.1.place_ref, bf16[4,512,1024]{2,1,0:T(8,128)(2,1)} %all-gather.6.cloned.1.call-done.here_ref, bf16[4,512,1024]{2,1,0:T(8,128)(2,1)} %bitcast.98, bf16[2,512,512]{2,1,0:T(8,128)(2,1)S(1)} %pad_maximum_fusion.refs_0_.refs_1_, ...), custom_call_target="tpu_custom_call" | custom-call | flops 4294967296 | bytes 16777216 | tf_op jit(solution)/shard_map/trunk_part/pallas_call | solution.py:133
  199.2 8.9 %trunk_part.4.refs_4_ = f32[512,1024]{1,0:T(8,128)S(1)} custom-call(s32[3]{0:T(128)S(1)} %add_add_fusion.place_ref, bf16[4,512,1024]{2,1,0:T(8,128)(2,1)} %all-gather.6.cloned.1.call-done.here_ref, bf16[4,512,1024]{2,1,0:T(8,128)(2,1)} %bitcast.99, bf16[2,512,512]{2,1,0:T(8,128)(2,1)S(1)} %copy-done.8, bf16[2,512,512]{2,1,0:T(8,128)(2,1)S(1)} %copy-done.8, ...), custom_call_target="tpu_custom_call" | custom-call | flops 3221225472 | bytes 13631488 | tf_op jit(solution)/shard_map/trunk_part/pallas_call | solution.py:133
  211.0 2.9 %collective-permute-start.35 = (f32[16]{0:T(128)S(1)}, f32[16]{0:T(128)S(1)}, u32[]{:S(2)}, u32[]{:S(2)}) collective-permute-start(f32[16]{0:T(128)S(1)} %broadcast_add_fusion), channel_id=1, source_target_pairs={{0,6},{2,0},{4,2},{6,4},{1,7},{3,1},{5,3},{7,5},{8,14},{10,8},{12,... | collective-permute-start | bytes 200 | tf_op jit(solution)/shard_map/ppermute | solution.py:42
  215.6 3.3 %collective-permute-done.36 = f32[16]{0:T(128)S(1)} collective-permute-done((f32[16]{0:T(128)S(1)}, f32[16]{0:T(128)S(1)}, u32[]{:S(2)}, u32[]{:S(2)}) %collective-permute-start.36) | collective-permute-done | bytes 96 | tf_op jit(solution)/shard_map/ppermute | solution.py:42
  221.9 5.8 %trunk_part.5 = bf16[512,1024]{1,0:T(8,128)(2,1)} custom-call(s32[3]{0:T(128)S(1)} %add_add_fusion.place_ref, bf16[4,512,1024]{2,1,0:T(8,128)(2,1)} %all-gather.6.cloned.1.call-done.here_ref, bf16[4,512,1024]{2,1,0:T(8,128)(2,1)} %bitcast.100, bf16[512,512]{1,0:T(8,128)(2,1)} %collective-permute-done.29.refs_0_, ...), custom_call_target="tpu_custom_call" | custom-call | flops 1073741824 | bytes 7340032 | tf_op jit(solution)/shard_map/trunk_part/pallas_call | solution.py:133
  (157 shorter events, 58.6 us)
Async XLA Ops:
  7.2 167.5 %all-gather.6.cloned.1.call-start = ((), (), s32[]{:S(2)}) async-start(), calls=%async_computation.1 | async-start | bytes 5242880 | tf_op jit(solution)/shard_map/all_gather | solution.py:236
  13.6 161.1 %all-gather.8.cloned.1.call-start = ((), (), s32[]{:S(2)}) async-start(), calls=%async_computation.2 | async-start | bytes 5242880 | tf_op jit(solution)/shard_map/all_gather | solution.py:255
  14.7 19.5 %collective-permute-start = (bf16[512,512]{1,0:T(8,128)(2,1)}, bf16[512,512]{1,0:T(8,128)(2,1)}, u32[]{:S(2)}, u32[]{:S(2)}) collective-permute-start(bf16[512,512]{1,0:T(8,128)(2,1)} %get-tuple-element.68), channel_id=1, source_target_pairs={{0,0},{1,1},{2,98},{3,99},{4,68},{5,69},{6,38},{7,39},{8,8},{9,9},... | collective-permute-start | bytes 1572872 | tf_op jit(solution)/shard_map/ppermute | solution.py:232
  20.1 18.1 %collective-permute-start.1 = (bf16[512,512]{1,0:T(8,128)(2,1)}, bf16[512,512]{1,0:T(8,128)(2,1)}, u32[]{:S(2)}, u32[]{:S(2)}) collective-permute-start(bf16[512,512]{1,0:T(8,128)(2,1)} %get-tuple-element.67), channel_id=1, source_target_pairs={{0,64},{1,65},{2,34},{3,35},{4,4},{5,5},{6,102},{7,103},{8,72},{9,... | collective-permute-start | bytes 1572872 | tf_op jit(solution)/shard_map/ppermute | solution.py:232
  42.8 33.6 %collective-permute-start.6 = (bf16[512,1024]{1,0:T(8,128)(2,1)S(1)}, bf16[512,1024]{1,0:T(8,128)(2,1)S(1)}, u32[]{:S(2)}, u32[]{:S(2)}) collective-permute-start(bf16[512,1024]{1,0:T(8,128)(2,1)S(1)} %bitcast.105), channel_id=1, source_target_pairs={{0,1},{1,0},{2,3},{3,2},{4,5},{5,4},{6,7},{7,6},{8,9},{9,8},{10,11... | collective-permute-start | bytes 3145736 | tf_op jit(solution)/shard_map/ppermute | solution.py:42
  45.9 23.1 %collective-permute-start.7 = (bf16[512,512]{1,0:T(8,128)(2,1)}, bf16[512,512]{1,0:T(8,128)(2,1)S(1)}, u32[]{:S(2)}, u32[]{:S(2)}) collective-permute-start(bf16[512,512]{1,0:T(8,128)(2,1)} %collective-permute-done), channel_id=1, source_target_pairs={{0,0},{1,16},{2,2},{3,18},{4,4},{5,20},{6,6},{7,22},{8,8},{9,24},{... | collective-permute-start | bytes 1572872 | tf_op jit(solution)/shard_map/ppermute | solution.py:247
  47.6 28.0 %collective-permute-start.8 = (bf16[512,512]{1,0:T(8,128)(2,1)}, bf16[512,512]{1,0:T(8,128)(2,1)S(1)}, u32[]{:S(2)}, u32[]{:S(2)}) collective-permute-start(bf16[512,512]{1,0:T(8,128)(2,1)} %collective-permute-done.1), channel_id=1, source_target_pairs={{0,4},{1,20},{2,6},{3,22},{4,0},{5,16},{6,2},{7,18},{8,12},{9,28},... | collective-permute-start | bytes 1572872 | tf_op jit(solution)/shard_map/ppermute | solution.py:247
  49.9 19.1 %collective-permute-start.5 = (bf16[64,512]{1,0:T(8,128)(2,1)S(1)}, bf16[64,512]{1,0:T(8,128)(2,1)S(1)}, u32[]{:S(2)}, u32[]{:S(2)}) collective-permute-start(bf16[64,512]{1,0:T(8,128)(2,1)S(1)} %fusion.13), channel_id=1, source_target_pairs={{0,1},{1,0},{2,3},{3,2},{4,5},{5,4},{6,7},{7,6},{8,9},{9,8},{10,11... | collective-permute-start | bytes 196616 | tf_op jit(solution)/shard_map/ppermute | solution.py:42
  78.7 43.4 %collective-permute-start.12 = (bf16[2,512,512]{2,1,0:T(8,128)(2,1)S(1)}, bf16[2,512,512]{2,1,0:T(8,128)(2,1)S(1)}, u32[]{:S(2)}, u32[]{:S(2)}) collective-permute-start(bf16[2,512,512]{2,1,0:T(8,128)(2,1)S(1)} %pad_maximum_fusion.refs_0_.refs_1_), channel_id=1, source_target_pairs={{0,96},{32,0},{64,32},{96,64},{1,97},{33,1},{65,33},{97,65},{2,98}... | collective-permute-start | bytes 3145736 | tf_op jit(solution)/shard_map/ppermute | solution.py:42
  81.3 40.8 %collective-permute-start.13 = (bf16[2,512,512]{2,1,0:T(8,128)(2,1)S(1)}, bf16[2,512,512]{2,1,0:T(8,128)(2,1)S(1)}, u32[]{:S(2)}, u32[]{:S(2)}) collective-permute-start(bf16[2,512,512]{2,1,0:T(8,128)(2,1)S(1)} %pad_maximum_fusion.refs_0_.refs_1_), channel_id=1, source_target_pairs={{0,32},{32,64},{64,96},{96,0},{1,33},{33,65},{65,97},{97,1},{2,34}... | collective-permute-start | bytes 3145736 | tf_op jit(solution)/shard_map/ppermute | solution.py:42
  81.3 40.8 %collective-permute-start.14 = (bf16[2,512,512]{2,1,0:T(8,128)(2,1)S(1)}, bf16[2,512,512]{2,1,0:T(8,128)(2,1)S(1)}, u32[]{:S(2)}, u32[]{:S(2)}) collective-permute-start(bf16[2,512,512]{2,1,0:T(8,128)(2,1)S(1)} %pad_maximum_fusion.refs_0_.refs_1_), channel_id=1, source_target_pairs={{0,16},{16,0},{1,17},{17,1},{2,18},{18,2},{3,19},{19,3},{4,20},{20... | collective-permute-start | bytes 3145736 | tf_op jit(solution)/shard_map/ppermute | solution.py:42
  108.4 50.0 %collective-permute-start.20 = (bf16[2,512,512]{2,1,0:T(8,128)(2,1)S(1)}, bf16[2,512,512]{2,1,0:T(8,128)(2,1)}, u32[]{:S(2)}, u32[]{:S(2)}) collective-permute-start(bf16[2,512,512]{2,1,0:T(8,128)(2,1)S(1)} %pad_maximum_fusion.refs_0_.refs_1_), channel_id=1, source_target_pairs={{0,8},{8,0},{1,9},{9,1},{2,10},{10,2},{3,11},{11,3},{4,12},{12,4},... | collective-permute-start | bytes 3145736 | tf_op jit(solution)/shard_map/ppermute | solution.py:42
  127.5 30.9 %collective-permute-start.18 = (bf16[512,512]{1,0:T(8,128)(2,1)}, bf16[512,512]{1,0:T(8,128)(2,1)}, u32[]{:S(2)}, u32[]{:S(2)}) collective-permute-start(bf16[512,512]{1,0:T(8,128)(2,1)} %slice_bitcast_fusion.3), channel_id=1, source_target_pairs={{0,96},{32,0},{64,32},{96,64},{1,97},{33,1},{65,33},{97,65},{2,98}... | collective-permute-start | bytes 1572872 | tf_op jit(solution)/shard_map/ppermute | solution.py:42
  128.3 30.1 %collective-permute-start.19 = (bf16[512,512]{1,0:T(8,128)(2,1)}, bf16[512,512]{1,0:T(8,128)(2,1)}, u32[]{:S(2)}, u32[]{:S(2)}) collective-permute-start(bf16[512,512]{1,0:T(8,128)(2,1)} %slice_bitcast_fusion.2), channel_id=1, source_target_pairs={{0,32},{32,64},{64,96},{96,0},{1,33},{33,65},{65,97},{97,1},{2,34}... | collective-permute-start | bytes 1572872 | tf_op jit(solution)/shard_map/ppermute | solution.py:42
  130.4 18.4 %collective-permute-start.16 = (bf16[4,64,512]{2,1,0:T(8,128)(2,1)S(1)}, bf16[4,64,512]{2,1,0:T(8,128)(2,1)S(1)}, u32[]{:S(2)}, u32[]{:S(2)}) collective-permute-start(bf16[4,64,512]{2,1,0:T(8,128)(2,1)S(1)} %bitcast.107), channel_id=1, source_target_pairs={{0,64},{32,96},{64,0},{96,32},{1,65},{33,97},{65,1},{97,33},{2,66}... | collective-permute-start | bytes 786440 | tf_op jit(solution)/shard_map/ppermute | solution.py:42
  133.3 21.6 %collective-permute-start.17 = (bf16[4,64,512]{2,1,0:T(8,128)(2,1)S(1)}, bf16[4,64,512]{2,1,0:T(8,128)(2,1)S(1)}, u32[]{:S(2)}, u32[]{:S(2)}) collective-permute-start(bf16[4,64,512]{2,1,0:T(8,128)(2,1)S(1)} %bitcast.108), channel_id=1, source_target_pairs={{0,32},{32,64},{64,96},{96,0},{1,33},{33,65},{65,97},{97,1},{2,34}... | collective-permute-start | bytes 786440 | tf_op jit(solution)/shard_map/ppermute | solution.py:42
  159.0 11.4 %collective-permute-start.21 = (bf16[2,512,512]{2,1,0:T(8,128)(2,1)S(1)}, bf16[2,512,512]{2,1,0:T(8,128)(2,1)}, u32[]{:S(2)}, u32[]{:S(2)}) collective-permute-start(bf16[2,512,512]{2,1,0:T(8,128)(2,1)S(1)} %collective-permute-done.12.refs_2_.refs_3_), channel_id=1, source_target_pairs={{0,8},{8,0},{1,9},{9,1},{2,10},{10,2},{3,11},{11,3},{4,12},{12,4},... | collective-permute-start | bytes 3145736 | tf_op jit(solution)/shard_map/ppermute | solution.py:42
  159.6 29.1 %collective-permute-start.25 = (bf16[2,512,512]{2,1,0:T(8,128)(2,1)}, bf16[2,512,512]{2,1,0:T(8,128)(2,1)}, u32[]{:S(2)}, u32[]{:S(2)}) collective-permute-start(bf16[2,512,512]{2,1,0:T(8,128)(2,1)} %copy-done.7), channel_id=1, source_target_pairs={{0,96},{32,0},{64,32},{96,64},{1,97},{33,1},{65,33},{97,65},{2,98}... | collective-permute-start | bytes 3145736 | tf_op jit(solution)/shard_map/ppermute | solution.py:42
  160.8 27.9 %collective-permute-start.26 = (bf16[2,512,512]{2,1,0:T(8,128)(2,1)}, bf16[2,512,512]{2,1,0:T(8,128)(2,1)}, u32[]{:S(2)}, u32[]{:S(2)}) collective-permute-start(bf16[2,512,512]{2,1,0:T(8,128)(2,1)} %copy-done.7), channel_id=1, source_target_pairs={{0,32},{32,64},{64,96},{96,0},{1,33},{33,65},{65,97},{97,1},{2,34}... | collective-permute-start | bytes 3145736 | tf_op jit(solution)/shard_map/ppermute | solution.py:42
  162.3 26.4 %collective-permute-start.27 = (bf16[2,512,512]{2,1,0:T(8,128)(2,1)}, bf16[2,512,512]{2,1,0:T(8,128)(2,1)}, u32[]{:S(2)}, u32[]{:S(2)}) collective-permute-start(bf16[2,512,512]{2,1,0:T(8,128)(2,1)} %copy-done.7), channel_id=1, source_target_pairs={{0,8},{8,0},{1,9},{9,1},{2,10},{10,2},{3,11},{11,3},{4,12},{12,4},... | collective-permute-start | bytes 3145736 | tf_op jit(solution)/shard_map/ppermute | solution.py:42
  170.5 18.2 %all-to-all-start = ((bf16[4,16,4096]{2,1,0:T(8,128)(2,1)}), bf16[4,16,4096]{2,1,0:T(8,128)(2,1)}, u32[]{:S(2)}, u32[]{:S(2)}) async-start(bf16[4,16,4096]{2,1,0:T(8,128)(2,1)} %bitcast.103), calls=%async_computation | async-start | bytes 1048576 | tf_op jit(solution)/shard_map/all_to_all | solution.py:287
  193.0 16.4 %collective-permute-start.29 = (bf16[512,512]{1,0:T(8,128)(2,1)}, bf16[512,512]{1,0:T(8,128)(2,1)}, u32[]{:S(2)}, u32[]{:S(2)}) collective-permute-start(bf16[512,512]{1,0:T(8,128)(2,1)} %slice_bitcast_fusion.1), channel_id=1, source_target_pairs={{0,96},{32,0},{64,32},{96,64},{1,97},{33,1},{65,33},{97,65},{2,98}... | collective-permute-start | bytes 1572872 | tf_op jit(solution)/shard_map/ppermute | solution.py:42
  194.7 15.5 %collective-permute-start.30 = (bf16[512,512]{1,0:T(8,128)(2,1)}, bf16[512,512]{1,0:T(8,128)(2,1)}, u32[]{:S(2)}, u32[]{:S(2)}) collective-permute-start(bf16[512,512]{1,0:T(8,128)(2,1)} %slice_bitcast_fusion), channel_id=1, source_target_pairs={{0,32},{32,64},{64,96},{96,0},{1,33},{33,65},{65,97},{97,1},{2,34}... | collective-permute-start | bytes 1572872 | tf_op jit(solution)/shard_map/ppermute | solution.py:42
  197.0 12.4 %collective-permute-start.28 = (bf16[16,4096]{1,0:T(8,128)(2,1)S(1)}, bf16[16,4096]{1,0:T(8,128)(2,1)S(1)}, u32[]{:S(2)}, u32[]{:S(2)}) collective-permute-start(bf16[16,4096]{1,0:T(8,128)(2,1)S(1)} %reduce_sum.71), channel_id=1, source_target_pairs={{0,1},{1,0},{2,3},{3,2},{4,5},{5,4},{6,7},{7,6},{8,9},{9,8},{10,11... | collective-permute-start | bytes 393224 | tf_op jit(solution)/shard_map/ppermute | solution.py:42
  (40 other events, 366.9 us)
Sparse Core Ops, SparseCore 0:
  13.7 61.5 all-gather.5
  77.5 65.5 all-gather.7

commit v7 on v1

--- a/solution.py
+++ b/solution.py
@@ -1,4 +1,5 @@
 import functools
+import itertools
 
 import jax
 import jax.numpy as jnp
@@ -19,14 +20,21 @@
     return (((z % Z) * XL + xl % XL) * CORE + core) * Y * XH + (y % Y) * XH + xh % XH
 
 
-def weight_moves():
+def places():
+    return itertools.product(range(Z), range(XL), range(CORE), range(Y), range(XH))
+
+
+def spread_moves(v):
     return [
-        (flat(z, xl, core, y, xh), flat(y - z, xh - xl, core, z, xl))
-        for z in range(Z)
-        for xl in range(XL)
-        for core in range(CORE)
-        for y in range(Y)
-        for xh in range(XH)
+        (flat(z, xl, core, y, xh), flat(z - y - 2 * v, xl, core, y, xh))
+        for z, xl, core, y, xh in places()
+    ]
+
+
+def column_moves(v):
+    return [
+        (flat(z, xl, core, y, xh), flat(z, xh, core, y + z + 2 * v, xl))
+        for z, xl, core, y, xh in places()
     ]
 
 
@@ -62,38 +70,84 @@
     return attn_out.astype(jnp.bfloat16).reshape(row_count, heads_here * HEAD_WIDTH)
 
 
-def trunk_kernel(*refs):
-    acts, w_ref, residual_ref, out_ref = refs[:8], refs[8], refs[9], refs[10]
-    total = residual_ref[...].astype(jnp.float32)
-    for slot in range(8):
-        total = total + jnp.dot(
-            acts[slot][...], w_ref[slot, 0], preferred_element_type=jnp.float32
-        )
-    out_ref[...] = total.astype(jnp.bfloat16)
-
-
-def trunk_matmul(acts, weights, residual):
-    rows, depth = acts[0].shape
-    half = weights.shape[-1]
-    width = 256
-    per = half // width
-    whole = pl.BlockSpec((rows, depth), lambda j: (0, 0), pipeline_mode=pl.Buffered(1))
-    tile = pl.BlockSpec((rows, width), lambda j: (0, j))
+def trunk_kernel(picks, has_base, place_ref, *refs):
+    count = len(picks)
+    sources, blocks = refs[:4], refs[4 : 4 + count]
+    base_ref = refs[4 + count] if has_base else None
+    out_ref, acts, sems = refs[-3:]
+    j = pl.program_id(0)
+
+    def copies(which):
+        for r in range(CORE):
+            for i, (s, v) in enumerate(picks):
+                depth = acts.shape[3]
+                group = lax.rem(place_ref[0] + 2 * Y - s - 2 * v, Y)
+                yield pltpu.make_async_copy(
+                    sources[2 * which + r].at[group, :, pl.ds(v * depth, depth)],
+                    acts.at[r, i],
+                    sems.at[r, i],
+                )
+
+    @pl.when(j == 0)
+    def _():
+        for which in range(2):
+
+            @pl.when(place_ref[1] == which)
+            def _():
+                for copy in copies(which):
+                    copy.start()
+
+        for copy in copies(0):
+            copy.wait()
+
+    if has_base:
+        total = base_ref[...]
+    else:
+        total = jnp.zeros(out_ref.shape, jnp.float32)
+    r = j // 2
+    for i, block in enumerate(blocks):
+        total = total + jnp.dot(acts[r, i], block[...], preferred_element_type=jnp.float32)
+    out_ref[...] = total.astype(out_ref.dtype)
+
+
+def trunk_part(place, sources, terms, base, dtype):
+    rows = sources[0].shape[1]
+    depth = sources[0].shape[2] // 2
+    width = terms[0][2].shape[-1]
+    count = len(terms)
+
+    def weight_spec(v):
+        return pl.BlockSpec((None, depth, width // 2), lambda j, p: (v, 0, lax.rem(j, 2)))
+
+    tile = pl.BlockSpec((rows, width // 2), lambda j, p: (j // 2, lax.rem(j, 2)))
     return pl.pallas_call(
-        trunk_kernel,
-        grid=(CORE * per,),
-        in_specs=[whole] * 8
-        + [pl.BlockSpec((8, 1, depth, width), lambda j: (0, j // per, 0, j % per)), tile],
-        out_specs=tile,
-        out_shape=jax.ShapeDtypeStruct(residual.shape, jnp.bfloat16),
-        compiler_params=pltpu.CompilerParams(vmem_limit_bytes=40 * 2**20),
+        functools.partial(trunk_kernel, [(s, v) for s, v, _ in terms], base is not None),
+        grid_spec=pltpu.PrefetchScalarGridSpec(
+            num_scalar_prefetch=1,
+            grid=(2 * CORE,),
+            in_specs=[pl.BlockSpec(memory_space=pltpu.HBM)] * 4
+            + [weight_spec(v) for _, v, _ in terms]
+            + ([] if base is None else [tile]),
+            out_specs=tile,
+            scratch_shapes=[
+                pltpu.VMEM((CORE, count, rows, depth), sources[0].dtype),
+                pltpu.SemaphoreType.DMA((CORE, count)),
+            ],
+        ),
+        out_shape=jax.ShapeDtypeStruct((CORE * rows, width), dtype),
+        compiler_params=pltpu.CompilerParams(vmem_limit_bytes=32 * 2**20),
         cost_estimate=pl.CostEstimate(
-            flops=2 * rows * 8 * depth * CORE * half,
-            bytes_accessed=2 * (8 * rows * depth + 8 * depth * CORE * half),
+            flops=2 * CORE * rows * count * depth * width,
+            bytes_accessed=2 * count * depth * (CORE * rows + width) + 8 * CORE * rows * width,
             transcendentals=0,
         ),
-        name="trunk_matmul",
-    )(*acts, weights, residual)
+        name="trunk_part",
+    )(
+        place,
+        *[pltpu.with_memory_space_constraint(x, pltpu.HBM) for x in sources],
+        *[t[2] for t in terms],
+        *([] if base is None else [base]),
+    )
 
 
 def norm_kernel(place_ref, p0, p1, p2, p3, gain_ref, out_ref):
@@ -159,52 +213,84 @@
     xh = lax.axis_index("xh")
     cand_count = cand_len.shape[0]
 
-    moved = lax.ppermute(out_weight, ALL, weight_moves())
+    lock = lax.optimization_barrier
+    rows_half = out_weight.shape[0] // 2
+    moved = [
+        lax.ppermute(out_weight[v * rows_half : (v + 1) * rows_half], ALL, spread_moves(v))
+        for v in range(2)
+    ]
     attn_out = attention(query, keys, values, cand_len)
+    here = lax.all_gather(attn_out, "y", axis=0, tiled=False)
 
     last_rows = jnp.arange(cand_count, dtype=jnp.int32) * SEQUENCE_SLOTS + cand_len - 1
     picked = jnp.concatenate(
         [jnp.take(attn_out, last_rows, axis=0), jnp.take(residual, last_rows, axis=0)], axis=1
     )
+    depth = attn_out.shape[1]
+    width = out_weight.shape[1]
     near = lax.all_gather(picked, ("xl", "core"), axis=0, tiled=True)
+    near, *moved = lock((near, *moved))
+    moved = [lax.ppermute(m, ALL, column_moves(v)) for v, m in enumerate(moved)]
     rows = jnp.concatenate([near] + [from_ahead(near, "z", Z, s) for s in (1, 2, 3)], axis=0)
-    width = out_weight.shape[1]
-    own = jnp.dot(rows[:, : attn_out.shape[1]], out_weight, preferred_element_type=jnp.float32)
-    res = rows[:, attn_out.shape[1] :]
+    own = jnp.dot(rows[:, :depth], out_weight, preferred_element_type=jnp.float32)
+    res = rows[:, depth:]
     res = jnp.where(core == 0, res[:, :width], res[:, width:]).astype(jnp.float32)
     own = jnp.where((y == z) & (xh == xl), own + res, own).astype(jnp.bfloat16)
     pair = jnp.stack([own, from_ahead(own, "xh", XH, 1)])
+    pair, held, *moved = lock((pair, attn_out, *moved))
+    w = {(0, 0): jnp.stack(moved)}
+    w[1, 0] = from_ahead(w[0, 0], "z", Z, 1)
+    w[3, 0] = from_ahead(w[0, 0], "z", Z, 3)
+    across = from_ahead(held, "xh", XH, 1)
     parts = [pair] + [from_ahead(pair, "y", Y, s) for s in (1, 2, 3)]
     pooled = sum(jnp.sum(p.astype(jnp.float32), axis=0) for p in parts).astype(jnp.bfloat16)
-    moved, bulk, _ = lax.optimization_barrier((moved, attn_out, pooled))
     near = lax.all_gather(pooled, ("xl", "core"), axis=0, tiled=False)
+    near, w[1, 0], w[3, 0], w[0, 0], across, here = lock(
+        (near, w[1, 0], w[3, 0], w[0, 0], across, here)
+    )
+    there = lax.all_gather(across, "y", axis=0, tiled=False)
     pieces = [near] + [from_ahead(near, "z", Z, s) for s in (1, 2, 3)]
+    w[0, 1] = from_ahead(w[0, 0], "xl", XL, 1)
     features = normalize(pieces, norm_gain, z)
+    features, w[0, 0], here = lock((features, w[0, 0], here))
+    w[2, 0] = from_ahead(w[0, 0], "z", Z, 2)
+    here_other = from_ahead(here, "core", CORE, 1)
     first = jax.nn.silu(
         jnp.dot(features, head_w1[0], preferred_element_type=jnp.float32) + head_b1[0]
     ).astype(jnp.bfloat16)
     terms = jnp.dot(first, head_w2[0], preferred_element_type=jnp.float32).astype(jnp.bfloat16)
+    terms, w[0, 1] = lock((terms, w[0, 1]))
+    w[1, 1] = from_ahead(w[0, 1], "z", Z, 1)
+    w[3, 1] = from_ahead(w[0, 1], "z", Z, 3)
     count = terms.shape[0] // Y
     terms = lax.all_to_all(
         terms.reshape(Y, count, terms.shape[1]), "y", split_axis=0, concat_axis=0, tiled=True
     )
+    terms, w[2, 0], w[0, 1], here_other = lock((terms, w[2, 0], w[0, 1], here_other))
+    w[2, 1] = from_ahead(w[0, 1], "z", Z, 2)
     half = jnp.sum(terms.astype(jnp.float32), axis=0).astype(jnp.bfloat16)
     other = from_ahead(half, "xh", XH, 1)
     second = jax.nn.silu(half.astype(jnp.float32) + other.astype(jnp.float32) + head_b2[0])
     mine = jnp.sum(second * head_w3[0].astype(jnp.float32), axis=-1) + head_b3[0]
-    scores = lax.all_gather(mine, "y", axis=0, tiled=False)
-    scores = jnp.roll(scores, z, axis=0).reshape(1, Y * count)
-
-    weights = lax.all_gather(moved, MEMBER, axis=0, tiled=False)
-    weights = weights.reshape((Z * XL, CORE) + out_weight.shape)
-    acts = {}
-    for e in range(XH):
-        base = bulk if e == 0 else from_ahead(bulk, "xh", XH, 1)
-        acts[0, e] = base
-        for s in (1, 3, 2):
-            acts[s, e] = from_ahead(base, "y", Y, s)
-    ordered = [acts[s, e] for s in range(Y) for e in range(XH)]
-    trunk_out = trunk_matmul(ordered, weights, residual)
+    scores = jnp.stack([mine] + [from_ahead(mine, "y", Y, s) for s in (1, 2, 3)])
+    scores = jnp.roll(scores, lax.rem(y + z, Y), axis=0).reshape(1, Y * count)
+
+    scores, w[1, 1], w[3, 1], there = lock((scores, w[1, 1], w[3, 1], there))
+    sources = (here, here_other, there, from_ahead(there, "core", CORE, 1))
+
+    def product(e, trunk, dtype):
+        items = [(s, v, w[s, e]) for s in range(Z) for v in range(2)]
+        place = jnp.stack([lax.rem(y - z + Y, Y), lax.rem(xl + e + xh, XH)])
+        return trunk_part(place, sources, items, trunk, dtype)
+
+    trunk = product(0, None, jnp.float32)
+    trunk = product(1, trunk, jnp.bfloat16)
+    row_count = residual.shape[0]
+    mine = trunk[:row_count]
+    other = from_ahead(trunk[row_count:], "core", CORE, 1)
+    left, right = jnp.where(core == 0, mine, other), jnp.where(core == 0, other, mine)
+    trunk = jnp.concatenate([left, right], axis=1).astype(jnp.float32)
+    trunk_out = (trunk + residual.astype(jnp.float32)).astype(jnp.bfloat16)
     return (trunk_out, scores)
 
 

time: 287 us -> 231 us (0.80)
  blocking collectives: 113 us -> 20.3 us
  waiting for transfers between devices: 47.9 us -> 99 us
  starting transfers between devices: 67.3 us -> 45.6 us
  Pallas kernels: 17.2 us -> 24.8 us
    unnamed x1 -> x0, blocking collectives: 69.2 us -> none
    ppermute x18 -> x25, starting transfers between devices: 57.8 us -> 26.5 us  [from_ahead(): return lax.ppermute(x, axis, [(i, (i - step) % size) for i in range(size)])]
    ppermute x1 -> x4, waiting for transfers between devices: 0.01 us -> 23.1 us  [the longest x2 19.2 us: local(): moved = [lax.ppermute(m, ALL, column_moves(v)) for v, m in enumerate(moved)]]
    ppermute x18 -> x25, waiting for transfers between devices: 47.9 us -> 68.2 us  [from_ahead(): return lax.ppermute(x, axis, [(i, (i - step) % size) for i in range(size)])]
    all_to_all x1 -> x0, blocking collectives: 19.1 us -> none  [local(): lax.all_to_all(terms.reshape(Y, count, terms.shape[1]), 'y', split_axis=0...]
    all_gather x1, blocking collectives: 16.7 us -> 5.25 us  [local(): near = lax.all_gather(picked, ('xl', 'core'), axis=0, tiled=True)]
    pallas_call x1 -> x2, Pallas kernels: 14.3 us -> 22 us  [trunk_part(): pl.pallas_call(functools.partial(trunk_kernel, [(s, v) for s, v, _ in ter...]
    all_to_all x0 -> x1, waiting for transfers between devices: none -> 7.61 us  [local(): lax.all_to_all(terms.reshape(Y, count, terms.shape[1]), 'y', split_axis=0...]
  transfers between devices with their start and end apart: 20 -> 32, of which waited for: 10 -> 20; matrix products, arithmetic and copies ran while one was open for 8% -> 7% of each run, Pallas kernels for 1% -> 6%
where the time goes in v7:
time: 231 us; the launch traced here: 229 us
  waiting for transfers between devices  99 us (43%)
  starting transfers between devices  45.6 us (20%)
  Pallas kernels  24.8 us (11%)
  blocking collectives  20.3 us (9%)
  between operations  15.1 us (7%)
  matrix products  9.83 us (4%)
  local copies, waits for them, and re-layouts  8.75 us (4%)
  other arithmetic  6.12 us (3%)
    ppermute x25, waiting for transfers between devices, from_ahead(): return lax.ppermute(x, axis, [(i, (i - step) % size) for i in range(size)])  68.2 us
    ppermute x25, starting transfers between devices, from_ahead(): return lax.ppermute(x, axis, [(i, (i - step) % size) for i in range(size)])  26.5 us
    pallas_call x2, Pallas kernels, trunk_part(): pl.pallas_call(functools.partial(trunk_kernel, [(s, v) for s, v, _ in ter...  22 us
    ppermute x2, waiting for transfers between devices, local(): moved = [lax.ppermute(m, ALL, column_moves(v)) for v, m in enumerate(moved)]  19.2 us
    all_gather x1, blocking collectives, local(): near = lax.all_gather(pooled, ('xl', 'core'), axis=0, tiled=False)  15.1 us
    ppermute x2, starting transfers between devices, local(): lax.ppermute(out_weight[v * rows_half:(v + 1) * rows_half], ALL, spread_m...  11.2 us
    dot_general x1, matrix products, local(): jnp.dot(first, head_w2[0], preferred_element_type=jnp.float32)  8.18 us
    all_to_all x1, waiting for transfers between devices, local(): lax.all_to_all(terms.reshape(Y, count, terms.shape[1]), 'y', split_axis=0...  7.61 us
  transfers between devices with their start and end apart: 32, of which 20 were waited for; matrix products, arithmetic and copies ran while one was open for 7% of the time, Pallas kernels for 6%

profile of v7, /device:TPU:0, one launch (start us, length us, event | category | flops | bytes accessed | tf_op | source)
XLA Modules:
  0.0 229.5 jit_solution(16787421694574119584)
XLA Ops:
  14.7 5.3 %collective-permute-start = (bf16[512,512]{1,0:T(8,128)(2,1)}, bf16[512,512]{1,0:T(8,128)(2,1)}, u32[]{:S(2)}, u32[]{:S(2)}) collective-permute-start(bf16[512,512]{1,0:T(8,128)(2,1)} %get-tuple-element.60), channel_id=1, source_target_pairs={{0,0},{1,1},{2,98},{3,99},{4,68},{5,69},{6,38},{7,39},{8,8},{9,9},... | collective-permute-start | bytes 1572872 | tf_op jit(solution)/shard_map/ppermute | solution.py:219
  20.0 5.9 %collective-permute-start.1 = (bf16[512,512]{1,0:T(8,128)(2,1)}, bf16[512,512]{1,0:T(8,128)(2,1)}, u32[]{:S(2)}, u32[]{:S(2)}) collective-permute-start(bf16[512,512]{1,0:T(8,128)(2,1)} %get-tuple-element.59), channel_id=1, source_target_pairs={{0,64},{1,65},{2,34},{3,35},{4,4},{5,5},{6,102},{7,103},{8,72},{9,... | collective-permute-start | bytes 1572872 | tf_op jit(solution)/shard_map/ppermute | solution.py:219
  28.9 5.2 %all-gather.2 = bf16[4,4,2048]{2,1,0:T(4,128)(2,1)S(1)} all-gather(bf16[1,4,2048]{2,1,0:T(4,128)(2,1)S(1)} %maximum_bitcast_fusion), channel_id=1, replica_groups=mesh['z'=4,'xl'=2,'core'=2,'y'=4,'xh'=2] {'xl','core'}, dimensions={0}, use_global_device_ids=true | all-gather | bytes 81920 | tf_op jit(solution)/shard_map/all_gather | solution.py:231
  34.2 4.0 %collective-permute-done.1 = bf16[512,512]{1,0:T(8,128)(2,1)} collective-permute-done((bf16[512,512]{1,0:T(8,128)(2,1)}, bf16[512,512]{1,0:T(8,128)(2,1)}, u32[]{:S(2)}, u32[]{:S(2)}) %collective-permute-start.1) | collective-permute-done | bytes 524320 | tf_op jit(solution)/shard_map/ppermute | solution.py:219
  38.1 3.4 %collective-permute-start.2 = (bf16[16,2048]{1,0:T(8,128)(2,1)S(1)}, bf16[16,2048]{1,0:T(8,128)(2,1)S(1)}, u32[]{:S(2)}, u32[]{:S(2)}) collective-permute-start(bf16[16,2048]{1,0:T(8,128)(2,1)S(1)} %reshape.160), channel_id=1, source_target_pairs={{0,96},{32,0},{64,32},{96,64},{1,97},{33,1},{65,33},{97,65},{2,98}... | collective-permute-start | bytes 196616 | tf_op jit(solution)/shard_map/ppermute | solution.py:42
  48.1 3.1 %collective-permute-start.5 = (bf16[64,512]{1,0:T(8,128)(2,1)S(1)}, bf16[64,512]{1,0:T(8,128)(2,1)S(1)}, u32[]{:S(2)}, u32[]{:S(2)}) collective-permute-start(bf16[64,512]{1,0:T(8,128)(2,1)S(1)} %fusion.13), channel_id=1, source_target_pairs={{0,1},{1,0},{2,3},{3,2},{4,5},{5,4},{6,7},{7,6},{8,9},{9,8},{10,11... | collective-permute-start | bytes 196616 | tf_op jit(solution)/shard_map/ppermute | solution.py:42
  51.2 2.7 %collective-permute-done.5 = bf16[64,512]{1,0:T(8,128)(2,1)S(1)} collective-permute-done((bf16[64,512]{1,0:T(8,128)(2,1)S(1)}, bf16[64,512]{1,0:T(8,128)(2,1)S(1)}, u32[]{:S(2)}, u32[]{:S(2)}) %collective-permute-start.5) | collective-permute-done | bytes 65568 | tf_op jit(solution)/shard_map/ppermute | solution.py:42
  54.0 19.2 %collective-permute-done.7 = bf16[512,512]{1,0:T(8,128)(2,1)S(1)} collective-permute-done((bf16[512,512]{1,0:T(8,128)(2,1)}, bf16[512,512]{1,0:T(8,128)(2,1)S(1)}, u32[]{:S(2)}, u32[]{:S(2)}) %collective-permute-start.7) | collective-permute-done | bytes 524320 | tf_op jit(solution)/shard_map/ppermute | solution.py:233
  76.1 3.6 %collective-permute-start.9 = (bf16[2,64,512]{2,1,0:T(8,128)(2,1)S(1)}, bf16[2,64,512]{2,1,0:T(8,128)(2,1)S(1)}, u32[]{:S(2)}, u32[]{:S(2)}) collective-permute-start(bf16[2,64,512]{2,1,0:T(8,128)(2,1)S(1)} %pad_maximum_fusion.1), channel_id=1, source_target_pairs={{0,4},{2,6},{4,0},{6,2},{1,5},{3,7},{5,1},{7,3},{8,12},{10,14},{12... | collective-permute-start | bytes 393224 | tf_op jit(solution)/shard_map/ppermute | solution.py:42
  86.8 15.1 %all-gather = bf16[256,512]{1,0:T(8,128)(2,1)S(1)} all-gather(bf16[64,512]{1,0:T(8,128)(2,1)S(1)} %add_convert_fusion.1), channel_id=2, replica_groups=mesh['z'=4,'xl'=2,'core'=2,'y'=4,'xh'=2] {'xl','core'}, dimensions={0}, use_global_device_ids=true | all-gather | bytes 327680 | tf_op jit(solution)/shard_map/all_gather | solution.py:247
  102.0 3.0 %collective-permute-start.14 = (bf16[4,64,512]{2,1,0:T(8,128)(2,1)S(1)}, bf16[4,64,512]{2,1,0:T(8,128)(2,1)S(1)}, u32[]{:S(2)}, u32[]{:S(2)}) collective-permute-start(bf16[4,64,512]{2,1,0:T(8,128)(2,1)S(1)} %bitcast.97), channel_id=1, source_target_pairs={{0,96},{32,0},{64,32},{96,64},{1,97},{33,1},{65,33},{97,65},{2,98}... | collective-permute-start | bytes 786440 | tf_op jit(solution)/shard_map/ppermute | solution.py:42
  105.9 10.7 %collective-permute-done.14.p1 = bf16[4,64,512]{2,1,0:T(8,128)(2,1)S(1)} collective-permute-done((bf16[4,64,512]{2,1,0:T(8,128)(2,1)S(1)}, bf16[4,64,512]{2,1,0:T(8,128)(2,1)S(1)}, u32[]{:S(2)}, u32[]{:S(2)}) %collective-permute-start.14) | collective-permute-done | bytes 262176 | tf_op jit(solution)/shard_map/ppermute | solution.py:42
  116.7 3.4 %collective-permute-done.16.p3 = bf16[4,64,512]{2,1,0:T(8,128)(2,1)S(1)} collective-permute-done((bf16[4,64,512]{2,1,0:T(8,128)(2,1)S(1)}, bf16[4,64,512]{2,1,0:T(8,128)(2,1)S(1)}, u32[]{:S(2)}, u32[]{:S(2)}) %collective-permute-start.16) | collective-permute-done | bytes 262176 | tf_op jit(solution)/shard_map/ppermute | solution.py:42
  120.8 2.8 %normalize.1 = bf16[64,8192]{1,0:T(8,128)(2,1)} custom-call(s32[1]{0:T(128)} %bitcast.2.place_ref, bf16[4,64,512]{2,1,0:T(8,128)(2,1)} %bitcast.100, bf16[4,64,512]{2,1,0:T(8,128)(2,1)} %copy-done.5, bf16[4,64,512]{2,1,0:T(8,128)(2,1)} %copy-done.6, bf16[4,64,512]{2,1,0:T(8,128)(2,1)} %copy-done.7, f32[1,8192]{1,0:T(1,128)} %bitcast.107), custom_call_target="tpu_custom_call" | custom-call | flops 4194304 | bytes 2097152 | tf_op jit(solution)/shard_map/normalize/pallas_call | solution.py:181
  124.5 8.2 %convolution_convert_fusion = bf16[64,4096]{1,0:T(8,128)(2,1)} fusion(bf16[1,512,4096]{2,1,0:T(8,128)(2,1)} %param.24, bf16[64,8192]{1,0:T(8,128)(2,1)} %normalize.1, bf16[1,8192,512]{2,1,0:T(8,128)(2,1)} %param.22, f32[512]{0:T(512)S(1)} %bitcast.115), kind=kOutput, calls=%fused_computation.4 | convolution fusion | flops 805765120 | bytes 14157824 | tf_op jit(solution)/shard_map/dot_general | solution.py:261
  132.7 16.7 %collective-permute-done.17.refs_4_.refs_5_ = bf16[2,512,512]{2,1,0:T(8,128)(2,1)} collective-permute-done((bf16[2,512,512]{2,1,0:T(8,128)(2,1)S(1)}, bf16[2,512,512]{2,1,0:T(8,128)(2,1)}, u32[]{:S(2)}, u32[]{:S(2)}) %collective-permute-start.17) | collective-permute-done | bytes 1048608 | tf_op jit(solution)/shard_map/ppermute | solution.py:42
  149.3 4.1 %all-to-all-start = ((bf16[4,16,4096]{2,1,0:T(8,128)(2,1)}), bf16[4,16,4096]{2,1,0:T(8,128)(2,1)}, u32[]{:S(2)}, u32[]{:S(2)}) async-start(bf16[4,16,4096]{2,1,0:T(8,128)(2,1)} %bitcast.94), calls=%async_computation | async-start | bytes 1048576 | tf_op jit(solution)/shard_map/all_to_all | solution.py:266
  155.6 7.6 %all-to-all-done = bf16[4,16,4096]{2,1,0:T(8,128)(2,1)} async-done(((bf16[4,16,4096]{2,1,0:T(8,128)(2,1)}), bf16[4,16,4096]{2,1,0:T(8,128)(2,1)}, u32[]{:S(2)}, u32[]{:S(2)}) %all-to-all-start) | async-done | bytes 524320 | tf_op jit(solution)/shard_map/all_to_all | solution.py:266
  166.7 4.2 %collective-permute-done.20 = bf16[16,4096]{1,0:T(8,128)(2,1)S(1)} collective-permute-done((bf16[16,4096]{1,0:T(8,128)(2,1)S(1)}, bf16[16,4096]{1,0:T(8,128)(2,1)S(1)}, u32[]{:S(2)}, u32[]{:S(2)}) %collective-permute-start.20) | collective-permute-done | bytes 131104 | tf_op jit(solution)/shard_map/ppermute | solution.py:42
  175.4 2.7 %collective-permute-done.22 = f32[16]{0:T(128)S(1)} collective-permute-done((f32[16]{0:T(128)S(1)}, f32[16]{0:T(128)S(1)}, u32[]{:S(2)}, u32[]{:S(2)}) %collective-permute-start.22) | collective-permute-done | bytes 96 | tf_op jit(solution)/shard_map/ppermute | solution.py:42
  180.9 7.2 %collective-permute-done.26.refs_3_ = bf16[4,512,1024]{2,1,0:T(8,128)(2,1)} collective-permute-done((bf16[4,512,1024]{2,1,0:T(8,128)(2,1)}, bf16[4,512,1024]{2,1,0:T(8,128)(2,1)}, u32[]{:S(2)}, u32[]{:S(2)}) %collective-permute-start.26) | collective-permute-done | bytes 4194336 | tf_op jit(solution)/shard_map/ppermute | solution.py:42
  188.1 10.8 %trunk_part.2.refs_12_ = f32[1024,512]{1,0:T(8,128)S(1)} custom-call(s32[2]{0:T(128)S(1)} %pad_add_fusion.1.place_ref, bf16[4,512,1024]{2,1,0:T(8,128)(2,1)} %all-gather.6.cloned.1.call-done.refs_0_, bf16[4,512,1024]{2,1,0:T(8,128)(2,1)} %collective-permute-done.19.refs_1_, bf16[4,512,1024]{2,1,0:T(8,128)(2,1)} %bitcast.90, ...), custom_call_target="tpu_custom_call" | custom-call | flops 4294967296 | bytes 16777216 | tf_op jit(solution)/shard_map/trunk_part/pallas_call | solution.py:123
  198.9 9.1 %collective-permute-done.27.refs_8_.refs_9_ = bf16[2,512,512]{2,1,0:T(8,128)(2,1)} collective-permute-done((bf16[2,512,512]{2,1,0:T(8,128)(2,1)}, bf16[2,512,512]{2,1,0:T(8,128)(2,1)}, u32[]{:S(2)}, u32[]{:S(2)}) %collective-permute-start.27) | collective-permute-done | bytes 1048608 | tf_op jit(solution)/shard_map/ppermute | solution.py:42
  208.0 11.2 %trunk_part.3 = bf16[1024,512]{1,0:T(8,128)(2,1)S(1)} custom-call(s32[2]{0:T(128)S(1)} %pad_add_fusion.place_ref, bf16[4,512,1024]{2,1,0:T(8,128)(2,1)} %all-gather.6.cloned.1.call-done.refs_0_, bf16[4,512,1024]{2,1,0:T(8,128)(2,1)} %collective-permute-done.19.refs_1_, bf16[4,512,1024]{2,1,0:T(8,128)(2,1)} %bitcast.91, ...), custom_call_target="tpu_custom_call" | custom-call | flops 4294967296 | bytes 16777216 | tf_op jit(solution)/shard_map/trunk_part/pallas_call | solution.py:123
  (113 shorter events, 45.2 us)
Async XLA Ops:
  7.2 94.7 %all-gather.6.cloned.1.call-start = ((), (), s32[]{:S(2)}) async-start(), calls=%async_computation.1 | async-start | bytes 5242880 | tf_op jit(solution)/shard_map/all_gather | solution.py:223
  13.6 167.0 %all-gather.8.cloned.1.call-start = ((), (), s32[]{:S(2)}) async-start(), calls=%async_computation.2 | async-start | bytes 5242880 | tf_op jit(solution)/shard_map/all_gather | solution.py:251
  14.7 19.4 %collective-permute-start = (bf16[512,512]{1,0:T(8,128)(2,1)}, bf16[512,512]{1,0:T(8,128)(2,1)}, u32[]{:S(2)}, u32[]{:S(2)}) collective-permute-start(bf16[512,512]{1,0:T(8,128)(2,1)} %get-tuple-element.60), channel_id=1, source_target_pairs={{0,0},{1,1},{2,98},{3,99},{4,68},{5,69},{6,38},{7,39},{8,8},{9,9},... | collective-permute-start | bytes 1572872 | tf_op jit(solution)/shard_map/ppermute | solution.py:219
  20.0 18.1 %collective-permute-start.1 = (bf16[512,512]{1,0:T(8,128)(2,1)}, bf16[512,512]{1,0:T(8,128)(2,1)}, u32[]{:S(2)}, u32[]{:S(2)}) collective-permute-start(bf16[512,512]{1,0:T(8,128)(2,1)} %get-tuple-element.59), channel_id=1, source_target_pairs={{0,64},{1,65},{2,34},{3,35},{4,4},{5,5},{6,102},{7,103},{8,72},{9,... | collective-permute-start | bytes 1572872 | tf_op jit(solution)/shard_map/ppermute | solution.py:219
  38.1 8.3 %collective-permute-start.2 = (bf16[16,2048]{1,0:T(8,128)(2,1)S(1)}, bf16[16,2048]{1,0:T(8,128)(2,1)S(1)}, u32[]{:S(2)}, u32[]{:S(2)}) collective-permute-start(bf16[16,2048]{1,0:T(8,128)(2,1)S(1)} %reshape.160), channel_id=1, source_target_pairs={{0,96},{32,0},{64,32},{96,64},{1,97},{33,1},{65,33},{97,65},{2,98}... | collective-permute-start | bytes 196616 | tf_op jit(solution)/shard_map/ppermute | solution.py:42
  42.8 11.2 %collective-permute-start.6 = (bf16[512,512]{1,0:T(8,128)(2,1)}, bf16[512,512]{1,0:T(8,128)(2,1)S(1)}, u32[]{:S(2)}, u32[]{:S(2)}) collective-permute-start(bf16[512,512]{1,0:T(8,128)(2,1)} %collective-permute-done), channel_id=1, source_target_pairs={{0,0},{1,16},{2,2},{3,18},{4,4},{5,20},{6,6},{7,22},{8,8},{9,24},{... | collective-permute-start | bytes 1572872 | tf_op jit(solution)/shard_map/ppermute | solution.py:233
  44.5 28.6 %collective-permute-start.7 = (bf16[512,512]{1,0:T(8,128)(2,1)}, bf16[512,512]{1,0:T(8,128)(2,1)S(1)}, u32[]{:S(2)}, u32[]{:S(2)}) collective-permute-start(bf16[512,512]{1,0:T(8,128)(2,1)} %collective-permute-done.1), channel_id=1, source_target_pairs={{0,4},{1,20},{2,6},{3,22},{4,0},{5,16},{6,2},{7,18},{8,12},{9,28},... | collective-permute-start | bytes 1572872 | tf_op jit(solution)/shard_map/ppermute | solution.py:233
  73.2 28.6 %collective-permute-start.11 = (bf16[2,512,512]{2,1,0:T(8,128)(2,1)S(1)}, bf16[2,512,512]{2,1,0:T(8,128)(2,1)S(1)}, u32[]{:S(2)}, u32[]{:S(2)}) collective-permute-start(bf16[2,512,512]{2,1,0:T(8,128)(2,1)S(1)} %pad_maximum_fusion.refs_4_.refs_5_), channel_id=1, source_target_pairs={{0,96},{32,0},{64,32},{96,64},{1,97},{33,1},{65,33},{97,65},{2,98}... | collective-permute-start | bytes 3145736 | tf_op jit(solution)/shard_map/ppermute | solution.py:42
  75.4 26.5 %collective-permute-start.12 = (bf16[2,512,512]{2,1,0:T(8,128)(2,1)S(1)}, bf16[2,512,512]{2,1,0:T(8,128)(2,1)S(1)}, u32[]{:S(2)}, u32[]{:S(2)}) collective-permute-start(bf16[2,512,512]{2,1,0:T(8,128)(2,1)S(1)} %pad_maximum_fusion.refs_4_.refs_5_), channel_id=1, source_target_pairs={{0,32},{32,64},{64,96},{96,0},{1,33},{33,65},{65,97},{97,1},{2,34}... | collective-permute-start | bytes 3145736 | tf_op jit(solution)/shard_map/ppermute | solution.py:42
  75.4 26.5 %collective-permute-start.13 = (bf16[512,1024]{1,0:T(8,128)(2,1)}, bf16[512,1024]{1,0:T(8,128)(2,1)}, u32[]{:S(2)}, u32[]{:S(2)}) collective-permute-start(bf16[512,1024]{1,0:T(8,128)(2,1)} %bitcast.96), channel_id=1, source_target_pairs={{0,1},{1,0},{2,3},{3,2},{4,5},{5,4},{6,7},{7,6},{8,9},{9,8},{10,11... | collective-permute-start | bytes 3145736 | tf_op jit(solution)/shard_map/ppermute | solution.py:42
  75.4 6.4 %collective-permute-start.10 = (bf16[2,64,512]{2,1,0:T(8,128)(2,1)S(1)}, bf16[2,64,512]{2,1,0:T(8,128)(2,1)S(1)}, u32[]{:S(2)}, u32[]{:S(2)}) collective-permute-start(bf16[2,64,512]{2,1,0:T(8,128)(2,1)S(1)} %pad_maximum_fusion.1), channel_id=1, source_target_pairs={{0,2},{2,4},{4,6},{6,0},{1,3},{3,5},{5,7},{7,1},{8,10},{10,12},{12... | collective-permute-start | bytes 393224 | tf_op jit(solution)/shard_map/ppermute | solution.py:42
  76.1 8.0 %collective-permute-start.9 = (bf16[2,64,512]{2,1,0:T(8,128)(2,1)S(1)}, bf16[2,64,512]{2,1,0:T(8,128)(2,1)S(1)}, u32[]{:S(2)}, u32[]{:S(2)}) collective-permute-start(bf16[2,64,512]{2,1,0:T(8,128)(2,1)S(1)} %pad_maximum_fusion.1), channel_id=1, source_target_pairs={{0,4},{2,6},{4,0},{6,2},{1,5},{3,7},{5,1},{7,3},{8,12},{10,14},{12... | collective-permute-start | bytes 393224 | tf_op jit(solution)/shard_map/ppermute | solution.py:42
  102.0 14.7 %collective-permute-start.14 = (bf16[4,64,512]{2,1,0:T(8,128)(2,1)S(1)}, bf16[4,64,512]{2,1,0:T(8,128)(2,1)S(1)}, u32[]{:S(2)}, u32[]{:S(2)}) collective-permute-start(bf16[4,64,512]{2,1,0:T(8,128)(2,1)S(1)} %bitcast.97), channel_id=1, source_target_pairs={{0,96},{32,0},{64,32},{96,64},{1,97},{33,1},{65,33},{97,65},{2,98}... | collective-permute-start | bytes 786440 | tf_op jit(solution)/shard_map/ppermute | solution.py:42
  105.0 11.7 %collective-permute-start.15 = (bf16[4,64,512]{2,1,0:T(8,128)(2,1)S(1)}, bf16[4,64,512]{2,1,0:T(8,128)(2,1)S(1)}, u32[]{:S(2)}, u32[]{:S(2)}) collective-permute-start(bf16[4,64,512]{2,1,0:T(8,128)(2,1)S(1)} %bitcast.98), channel_id=1, source_target_pairs={{0,64},{32,96},{64,0},{96,32},{1,65},{33,97},{65,1},{97,33},{2,66}... | collective-permute-start | bytes 786440 | tf_op jit(solution)/shard_map/ppermute | solution.py:42
  105.0 15.1 %collective-permute-start.16 = (bf16[4,64,512]{2,1,0:T(8,128)(2,1)S(1)}, bf16[4,64,512]{2,1,0:T(8,128)(2,1)S(1)}, u32[]{:S(2)}, u32[]{:S(2)}) collective-permute-start(bf16[4,64,512]{2,1,0:T(8,128)(2,1)S(1)} %bitcast.99), channel_id=1, source_target_pairs={{0,32},{32,64},{64,96},{96,0},{1,33},{33,65},{65,97},{97,1},{2,34}... | collective-permute-start | bytes 786440 | tf_op jit(solution)/shard_map/ppermute | solution.py:42
  123.6 39.5 %collective-permute-start.19 = (bf16[4,512,1024]{2,1,0:T(8,128)(2,1)}, bf16[4,512,1024]{2,1,0:T(8,128)(2,1)}, u32[]{:S(2)}, u32[]{:S(2)}) collective-permute-start(bf16[4,512,1024]{2,1,0:T(8,128)(2,1)} %all-gather.6.cloned.1.call-done.refs_0_), channel_id=1, source_target_pairs={{0,8},{8,0},{1,9},{9,1},{2,10},{10,2},{3,11},{11,3},{4,12},{12,4},... | collective-permute-start | bytes 12582920 | tf_op jit(solution)/shard_map/ppermute | solution.py:42
  123.7 25.7 %collective-permute-start.17 = (bf16[2,512,512]{2,1,0:T(8,128)(2,1)S(1)}, bf16[2,512,512]{2,1,0:T(8,128)(2,1)}, u32[]{:S(2)}, u32[]{:S(2)}) collective-permute-start(bf16[2,512,512]{2,1,0:T(8,128)(2,1)S(1)} %pad_maximum_fusion.refs_4_.refs_5_), channel_id=1, source_target_pairs={{0,16},{16,0},{1,17},{17,1},{2,18},{18,2},{3,19},{19,3},{4,20},{20... | collective-permute-start | bytes 3145736 | tf_op jit(solution)/shard_map/ppermute | solution.py:42
  123.7 31.9 %collective-permute-start.18 = (bf16[2,512,512]{2,1,0:T(8,128)(2,1)S(1)}, bf16[2,512,512]{2,1,0:T(8,128)(2,1)}, u32[]{:S(2)}, u32[]{:S(2)}) collective-permute-start(bf16[2,512,512]{2,1,0:T(8,128)(2,1)S(1)} %pad_maximum_fusion.refs_4_.refs_5_), channel_id=1, source_target_pairs={{0,64},{32,96},{64,0},{96,32},{1,65},{33,97},{65,1},{97,33},{2,66}... | collective-permute-start | bytes 3145736 | tf_op jit(solution)/shard_map/ppermute | solution.py:42
  149.3 13.8 %all-to-all-start = ((bf16[4,16,4096]{2,1,0:T(8,128)(2,1)}), bf16[4,16,4096]{2,1,0:T(8,128)(2,1)}, u32[]{:S(2)}, u32[]{:S(2)}) async-start(bf16[4,16,4096]{2,1,0:T(8,128)(2,1)} %bitcast.94), calls=%async_computation | async-start | bytes 1048576 | tf_op jit(solution)/shard_map/all_to_all | solution.py:266
  153.5 26.4 %collective-permute-start.24 = (bf16[2,512,512]{2,1,0:T(8,128)(2,1)}, bf16[2,512,512]{2,1,0:T(8,128)(2,1)}, u32[]{:S(2)}, u32[]{:S(2)}) collective-permute-start(bf16[2,512,512]{2,1,0:T(8,128)(2,1)} %collective-permute-done.17.refs_4_.refs_5_), channel_id=1, source_target_pairs={{0,96},{32,0},{64,32},{96,64},{1,97},{33,1},{65,33},{97,65},{2,98}... | collective-permute-start | bytes 3145736 | tf_op jit(solution)/shard_map/ppermute | solution.py:42
  154.5 26.0 %collective-permute-start.25 = (bf16[2,512,512]{2,1,0:T(8,128)(2,1)}, bf16[2,512,512]{2,1,0:T(8,128)(2,1)}, u32[]{:S(2)}, u32[]{:S(2)}) collective-permute-start(bf16[2,512,512]{2,1,0:T(8,128)(2,1)} %collective-permute-done.17.refs_4_.refs_5_), channel_id=1, source_target_pairs={{0,32},{32,64},{64,96},{96,0},{1,33},{33,65},{65,97},{97,1},{2,34}... | collective-permute-start | bytes 3145736 | tf_op jit(solution)/shard_map/ppermute | solution.py:42
  164.3 6.6 %collective-permute-start.20 = (bf16[16,4096]{1,0:T(8,128)(2,1)S(1)}, bf16[16,4096]{1,0:T(8,128)(2,1)S(1)}, u32[]{:S(2)}, u32[]{:S(2)}) collective-permute-start(bf16[16,4096]{1,0:T(8,128)(2,1)S(1)} %reduce_sum.71), channel_id=1, source_target_pairs={{0,1},{1,0},{2,3},{3,2},{4,5},{5,4},{6,7},{7,6},{8,9},{9,8},{10,11... | collective-permute-start | bytes 393224 | tf_op jit(solution)/shard_map/ppermute | solution.py:42
  180.6 7.5 %collective-permute-start.26 = (bf16[4,512,1024]{2,1,0:T(8,128)(2,1)}, bf16[4,512,1024]{2,1,0:T(8,128)(2,1)}, u32[]{:S(2)}, u32[]{:S(2)}) collective-permute-start(bf16[4,512,1024]{2,1,0:T(8,128)(2,1)} %bitcast.89), channel_id=1, source_target_pairs={{0,8},{8,0},{1,9},{9,1},{2,10},{10,2},{3,11},{11,3},{4,12},{12,4},... | collective-permute-start | bytes 12582920 | tf_op jit(solution)/shard_map/ppermute | solution.py:42
  180.6 27.4 %collective-permute-start.27 = (bf16[2,512,512]{2,1,0:T(8,128)(2,1)}, bf16[2,512,512]{2,1,0:T(8,128)(2,1)}, u32[]{:S(2)}, u32[]{:S(2)}) collective-permute-start(bf16[2,512,512]{2,1,0:T(8,128)(2,1)} %collective-permute-done.17.refs_4_.refs_5_), channel_id=1, source_target_pairs={{0,64},{32,96},{64,0},{96,32},{1,65},{33,97},{65,1},{97,33},{2,66}... | collective-permute-start | bytes 3145736 | tf_op jit(solution)/shard_map/ppermute | solution.py:42
  (19 other events, 168.9 us)
Sparse Core Ops, SparseCore 0:
  13.7 61.9 all-gather.5
  102.1 46.3 all-gather.7

commit v8 on v7

--- a/solution.py
+++ b/solution.py
@@ -137,9 +137,7 @@
         out_shape=jax.ShapeDtypeStruct((CORE * rows, width), dtype),
         compiler_params=pltpu.CompilerParams(vmem_limit_bytes=32 * 2**20),
         cost_estimate=pl.CostEstimate(
-            flops=2 * CORE * rows * count * depth * width,
-            bytes_accessed=2 * count * depth * (CORE * rows + width) + 8 * CORE * rows * width,
-            transcendentals=0,
+            flops=CORE * rows * width, bytes_accessed=CORE * rows * width, transcendentals=0
         ),
         name="trunk_part",
     )(
@@ -241,32 +239,35 @@
     w = {(0, 0): jnp.stack(moved)}
     w[1, 0] = from_ahead(w[0, 0], "z", Z, 1)
     w[3, 0] = from_ahead(w[0, 0], "z", Z, 3)
+    w[2, 0] = from_ahead(w[0, 0], "z", Z, 2)
     across = from_ahead(held, "xh", XH, 1)
     parts = [pair] + [from_ahead(pair, "y", Y, s) for s in (1, 2, 3)]
     pooled = sum(jnp.sum(p.astype(jnp.float32), axis=0) for p in parts).astype(jnp.bfloat16)
+    pooled, across = lock((pooled, across))
+    there = lax.all_gather(across, "y", axis=0, tiled=False)
     near = lax.all_gather(pooled, ("xl", "core"), axis=0, tiled=False)
-    near, w[1, 0], w[3, 0], w[0, 0], across, here = lock(
-        (near, w[1, 0], w[3, 0], w[0, 0], across, here)
-    )
-    there = lax.all_gather(across, "y", axis=0, tiled=False)
+    near, w[1, 0], w[3, 0], w[2, 0], w[0, 0], here = lock(
+        (near, w[1, 0], w[3, 0], w[2, 0], w[0, 0], here)
+    )
     pieces = [near] + [from_ahead(near, "z", Z, s) for s in (1, 2, 3)]
     w[0, 1] = from_ahead(w[0, 0], "xl", XL, 1)
     features = normalize(pieces, norm_gain, z)
-    features, w[0, 0], here = lock((features, w[0, 0], here))
-    w[2, 0] = from_ahead(w[0, 0], "z", Z, 2)
+    features, w[0, 1], here = lock((features, w[0, 1], here))
+    w[1, 1] = from_ahead(w[0, 1], "z", Z, 1)
+    w[3, 1] = from_ahead(w[0, 1], "z", Z, 3)
     here_other = from_ahead(here, "core", CORE, 1)
     first = jax.nn.silu(
         jnp.dot(features, head_w1[0], preferred_element_type=jnp.float32) + head_b1[0]
     ).astype(jnp.bfloat16)
     terms = jnp.dot(first, head_w2[0], preferred_element_type=jnp.float32).astype(jnp.bfloat16)
-    terms, w[0, 1] = lock((terms, w[0, 1]))
-    w[1, 1] = from_ahead(w[0, 1], "z", Z, 1)
-    w[3, 1] = from_ahead(w[0, 1], "z", Z, 3)
     count = terms.shape[0] // Y
     terms = lax.all_to_all(
         terms.reshape(Y, count, terms.shape[1]), "y", split_axis=0, concat_axis=0, tiled=True
     )
-    terms, w[2, 0], w[0, 1], here_other = lock((terms, w[2, 0], w[0, 1], here_other))
+    terms, there, w[0, 1], w[1, 1], w[3, 1], here_other = lock(
+        (terms, there, w[0, 1], w[1, 1], w[3, 1], here_other)
+    )
+    there_other = from_ahead(there, "core", CORE, 1)
     w[2, 1] = from_ahead(w[0, 1], "z", Z, 2)
     half = jnp.sum(terms.astype(jnp.float32), axis=0).astype(jnp.bfloat16)
     other = from_ahead(half, "xh", XH, 1)
@@ -275,14 +276,14 @@
     scores = jnp.stack([mine] + [from_ahead(mine, "y", Y, s) for s in (1, 2, 3)])
     scores = jnp.roll(scores, lax.rem(y + z, Y), axis=0).reshape(1, Y * count)
 
-    scores, w[1, 1], w[3, 1], there = lock((scores, w[1, 1], w[3, 1], there))
-    sources = (here, here_other, there, from_ahead(there, "core", CORE, 1))
 
     def product(e, trunk, dtype):
         items = [(s, v, w[s, e]) for s in range(Z) for v in range(2)]
         place = jnp.stack([lax.rem(y - z + Y, Y), lax.rem(xl + e + xh, XH)])
         return trunk_part(place, sources, items, trunk, dtype)
 
+    scores, there_other = lock((scores, there_other))
+    sources = (here, here_other, there, there_other)
     trunk = product(0, None, jnp.float32)
     trunk = product(1, trunk, jnp.bfloat16)
     row_count = residual.shape[0]

time: 231 us -> 221 us (0.957)
  waiting for transfers between devices: 99 us -> 75.6 us
  starting transfers between devices: 45.6 us -> 51.4 us
  blocking collectives: 20.3 us -> 25.3 us
    all_to_all x0 -> x1, blocking collectives: none -> 14 us  [local(): lax.all_to_all(terms.reshape(Y, count, terms.shape[1]), 'y', split_axis=0...]
    ppermute x25, starting transfers between devices: 26.5 us -> 38.7 us  [from_ahead(): return lax.ppermute(x, axis, [(i, (i - step) % size) for i in range(size)])]
    ppermute x25, waiting for transfers between devices: 68.2 us -> 56.6 us  [from_ahead(): return lax.ppermute(x, axis, [(i, (i - step) % size) for i in range(size)])]
    all_gather x1, blocking collectives: 15.1 us -> 6 us  [local(): near = lax.all_gather(pooled, ('xl', 'core'), axis=0, tiled=False)]
    all_to_all x1 -> x0, waiting for transfers between devices: 7.61 us -> none  [local(): lax.all_to_all(terms.reshape(Y, count, terms.shape[1]), 'y', split_axis=0...]
    all_to_all x1 -> x0, starting transfers between devices: 4.13 us -> none  [local(): lax.all_to_all(terms.reshape(Y, count, terms.shape[1]), 'y', split_axis=0...]
    ppermute x2, starting transfers between devices: 11.2 us -> 7.32 us  [local(): lax.ppermute(out_weight[v * rows_half:(v + 1) * rows_half], ALL, spread_m...]
    ppermute x2, waiting for transfers between devices: 3.98 us -> 1.35 us  [local(): lax.ppermute(out_weight[v * rows_half:(v + 1) * rows_half], ALL, spread_m...]
  transfers between devices with their start and end apart: 32 -> 31, of which waited for: 20 -> 17; matrix products, arithmetic and copies ran while one was open for 7% -> 9% of each run, Pallas kernels for 6% -> 6%
where the time goes in v8:
time: 221 us; the launch traced here: 220 us
  waiting for transfers between devices  75.6 us (34%)
  starting transfers between devices  51.4 us (23%)
  blocking collectives  25.3 us (11%)
  Pallas kernels  24.8 us (11%)
  between operations  15.1 us (7%)
  local copies, waits for them, and re-layouts  10.2 us (5%)
  matrix products  9.71 us (4%)
  other arithmetic  7.38 us (3%)
    ppermute x25, waiting for transfers between devices, from_ahead(): return lax.ppermute(x, axis, [(i, (i - step) % size) for i in range(size)])  56.6 us
    ppermute x25, starting transfers between devices, from_ahead(): return lax.ppermute(x, axis, [(i, (i - step) % size) for i in range(size)])  38.7 us
    pallas_call x2, Pallas kernels, trunk_part(): pl.pallas_call(functools.partial(trunk_kernel, [(s, v) for s, v, _ in ter...  22 us
    ppermute x2, waiting for transfers between devices, local(): moved = [lax.ppermute(m, ALL, column_moves(v)) for v, m in enumerate(moved)]  17.5 us
    all_to_all x1, blocking collectives, local(): lax.all_to_all(terms.reshape(Y, count, terms.shape[1]), 'y', split_axis=0...  14 us
    dot_general x1, matrix products, local(): jnp.dot(first, head_w2[0], preferred_element_type=jnp.float32)  8.06 us
    ppermute x2, starting transfers between devices, local(): lax.ppermute(out_weight[v * rows_half:(v + 1) * rows_half], ALL, spread_m...  7.32 us
    all_gather x1, blocking collectives, local(): near = lax.all_gather(pooled, ('xl', 'core'), axis=0, tiled=False)  6 us
  transfers between devices with their start and end apart: 31, of which 17 were waited for; matrix products, arithmetic and copies ran while one was open for 9% of the time, Pallas kernels for 6%

profile of v8, /device:TPU:0, one launch (start us, length us, event | category | flops | bytes accessed | tf_op | source)
XLA Modules:
  0.0 219.5 jit_solution(17300680280239877162)
XLA Ops:
  15.2 5.9 %collective-permute-start.1 = (bf16[512,512]{1,0:T(8,128)(2,1)S(1)}, bf16[512,512]{1,0:T(8,128)(2,1)}, u32[]{:S(2)}, u32[]{:S(2)}) collective-permute-start(bf16[512,512]{1,0:T(8,128)(2,1)S(1)} %get-tuple-element.59), channel_id=1, source_target_pairs={{0,64},{1,65},{2,34},{3,35},{4,4},{5,5},{6,102},{7,103},{8,72},{9,... | collective-permute-start | bytes 1572872 | tf_op jit(solution)/shard_map/ppermute | solution.py:217
  26.4 5.2 %all-gather.2 = bf16[4,4,2048]{2,1,0:T(4,128)(2,1)S(1)} all-gather(bf16[1,4,2048]{2,1,0:T(4,128)(2,1)S(1)} %maximum_bitcast_fusion), channel_id=1, replica_groups=mesh['z'=4,'xl'=2,'core'=2,'y'=4,'xh'=2] {'xl','core'}, dimensions={0}, use_global_device_ids=true | all-gather | bytes 81920 | tf_op jit(solution)/shard_map/all_gather | solution.py:229
  33.1 3.4 %collective-permute-start.2 = (bf16[16,2048]{1,0:T(8,128)(2,1)S(1)}, bf16[16,2048]{1,0:T(8,128)(2,1)S(1)}, u32[]{:S(2)}, u32[]{:S(2)}) collective-permute-start(bf16[16,2048]{1,0:T(8,128)(2,1)S(1)} %reshape.128), channel_id=1, source_target_pairs={{0,96},{32,0},{64,32},{96,64},{1,97},{33,1},{65,33},{97,65},{2,98}... | collective-permute-start | bytes 196616 | tf_op jit(solution)/shard_map/ppermute | solution.py:42
  39.4 3.6 %collective-permute-start.7 = (bf16[512,512]{1,0:T(8,128)(2,1)}, bf16[512,512]{1,0:T(8,128)(2,1)S(1)}, u32[]{:S(2)}, u32[]{:S(2)}) collective-permute-start(bf16[512,512]{1,0:T(8,128)(2,1)} %collective-permute-done.1), channel_id=1, source_target_pairs={{0,4},{1,20},{2,6},{3,22},{4,0},{5,16},{6,2},{7,18},{8,12},{9,28},... | collective-permute-start | bytes 1572872 | tf_op jit(solution)/shard_map/ppermute | solution.py:231
  43.5 4.8 %collective-permute-start.5 = (bf16[64,512]{1,0:T(8,128)(2,1)S(1)}, bf16[64,512]{1,0:T(8,128)(2,1)S(1)}, u32[]{:S(2)}, u32[]{:S(2)}) collective-permute-start(bf16[64,512]{1,0:T(8,128)(2,1)S(1)} %fusion.13), channel_id=1, source_target_pairs={{0,1},{1,0},{2,3},{3,2},{4,5},{5,4},{6,7},{7,6},{8,9},{9,8},{10,11... | collective-permute-start | bytes 196616 | tf_op jit(solution)/shard_map/ppermute | solution.py:42
  50.5 17.5 %collective-permute-done.7 = bf16[512,512]{1,0:T(8,128)(2,1)S(1)} collective-permute-done((bf16[512,512]{1,0:T(8,128)(2,1)}, bf16[512,512]{1,0:T(8,128)(2,1)S(1)}, u32[]{:S(2)}, u32[]{:S(2)}) %collective-permute-start.7) | collective-permute-done | bytes 524320 | tf_op jit(solution)/shard_map/ppermute | solution.py:231
  71.2 3.0 %collective-permute-start.12 = (bf16[2,512,512]{2,1,0:T(8,128)(2,1)S(1)}, bf16[2,512,512]{2,1,0:T(8,128)(2,1)S(1)}, u32[]{:S(2)}, u32[]{:S(2)}) collective-permute-start(bf16[2,512,512]{2,1,0:T(8,128)(2,1)S(1)} %pad_maximum_fusion.refs_4_.refs_5_), channel_id=1, source_target_pairs={{0,96},{32,0},{64,32},{96,64},{1,97},{33,1},{65,33},{97,65},{2,98}... | collective-permute-start | bytes 3145736 | tf_op jit(solution)/shard_map/ppermute | solution.py:42
  75.9 3.2 %collective-permute-done.10 = bf16[2,64,512]{2,1,0:T(8,128)(2,1)S(1)} collective-permute-done((bf16[2,64,512]{2,1,0:T(8,128)(2,1)S(1)}, bf16[2,64,512]{2,1,0:T(8,128)(2,1)S(1)}, u32[]{:S(2)}, u32[]{:S(2)}) %collective-permute-start.10) | collective-permute-done | bytes 131104 | tf_op jit(solution)/shard_map/ppermute | solution.py:42
  81.2 3.1 %collective-permute-start.14 = (bf16[2,512,512]{2,1,0:T(8,128)(2,1)S(1)}, bf16[2,512,512]{2,1,0:T(8,128)(2,1)}, u32[]{:S(2)}, u32[]{:S(2)}) collective-permute-start(bf16[2,512,512]{2,1,0:T(8,128)(2,1)S(1)} %pad_maximum_fusion.refs_4_.refs_5_), channel_id=1, source_target_pairs={{0,64},{32,96},{64,0},{96,32},{1,65},{33,97},{65,1},{97,33},{2,66}... | collective-permute-start | bytes 3145736 | tf_op jit(solution)/shard_map/ppermute | solution.py:42
  85.1 7.1 %collective-permute-done.11 = bf16[512,1024]{1,0:T(8,128)(2,1)} collective-permute-done((bf16[512,1024]{1,0:T(8,128)(2,1)}, bf16[512,1024]{1,0:T(8,128)(2,1)}, u32[]{:S(2)}, u32[]{:S(2)}) %collective-permute-start.11) | collective-permute-done | bytes 1048608 | tf_op jit(solution)/shard_map/ppermute | solution.py:42
  92.3 6.0 %all-gather = bf16[256,512]{1,0:T(8,128)(2,1)S(1)} all-gather(bf16[64,512]{1,0:T(8,128)(2,1)} %add_convert_fusion.1), channel_id=2, replica_groups=mesh['z'=4,'xl'=2,'core'=2,'y'=4,'xh'=2] {'xl','core'}, dimensions={0}, use_global_device_ids=true | all-gather | bytes 327680 | tf_op jit(solution)/shard_map/all_gather | solution.py:248
  98.3 17.6 %collective-permute-done.12.refs_6_.refs_7_ = bf16[2,512,512]{2,1,0:T(8,128)(2,1)S(1)} collective-permute-done((bf16[2,512,512]{2,1,0:T(8,128)(2,1)S(1)}, bf16[2,512,512]{2,1,0:T(8,128)(2,1)S(1)}, u32[]{:S(2)}, u32[]{:S(2)}) %collective-permute-start.12) | collective-permute-done | bytes 1048608 | tf_op jit(solution)/shard_map/ppermute | solution.py:42
  115.9 3.4 %collective-permute-done.13.refs_10_.refs_11_ = bf16[2,512,512]{2,1,0:T(8,128)(2,1)S(1)} collective-permute-done((bf16[2,512,512]{2,1,0:T(8,128)(2,1)S(1)}, bf16[2,512,512]{2,1,0:T(8,128)(2,1)S(1)}, u32[]{:S(2)}, u32[]{:S(2)}) %collective-permute-start.13) | collective-permute-done | bytes 1048608 | tf_op jit(solution)/shard_map/ppermute | solution.py:42
  119.3 7.1 %collective-permute-start.18 = (bf16[2,512,512]{2,1,0:T(8,128)(2,1)S(1)}, bf16[2,512,512]{2,1,0:T(8,128)(2,1)}, u32[]{:S(2)}, u32[]{:S(2)}) collective-permute-start(bf16[2,512,512]{2,1,0:T(8,128)(2,1)S(1)} %pad_maximum_fusion.refs_4_.refs_5_), channel_id=1, source_target_pairs={{0,16},{16,0},{1,17},{17,1},{2,18},{18,2},{3,19},{19,3},{4,20},{20... | collective-permute-start | bytes 3145736 | tf_op jit(solution)/shard_map/ppermute | solution.py:42
  128.4 4.3 %collective-permute-done.15.p1 = bf16[4,64,512]{2,1,0:T(8,128)(2,1)S(1)} collective-permute-done((bf16[4,64,512]{2,1,0:T(8,128)(2,1)S(1)}, bf16[4,64,512]{2,1,0:T(8,128)(2,1)S(1)}, u32[]{:S(2)}, u32[]{:S(2)}) %collective-permute-start.15) | collective-permute-done | bytes 262176 | tf_op jit(solution)/shard_map/ppermute | solution.py:42
  134.4 2.7 %collective-permute-done.17.p3 = bf16[4,64,512]{2,1,0:T(8,128)(2,1)S(1)} collective-permute-done((bf16[4,64,512]{2,1,0:T(8,128)(2,1)S(1)}, bf16[4,64,512]{2,1,0:T(8,128)(2,1)S(1)}, u32[]{:S(2)}, u32[]{:S(2)}) %collective-permute-start.17) | collective-permute-done | bytes 262176 | tf_op jit(solution)/shard_map/ppermute | solution.py:42
  137.8 2.8 %normalize.1 = bf16[64,8192]{1,0:T(8,128)(2,1)} custom-call(s32[1]{0:T(128)} %bitcast.2.place_ref, bf16[4,64,512]{2,1,0:T(8,128)(2,1)} %bitcast.98, bf16[4,64,512]{2,1,0:T(8,128)(2,1)} %copy-done.4, bf16[4,64,512]{2,1,0:T(8,128)(2,1)} %copy-done.5, bf16[4,64,512]{2,1,0:T(8,128)(2,1)} %copy-done.6, f32[1,8192]{1,0:T(1,128)} %bitcast.105), custom_call_target="tpu_custom_call" | custom-call | flops 4194304 | bytes 2097152 | tf_op jit(solution)/shard_map/normalize/pallas_call | solution.py:179
  142.7 8.1 %convolution_convert_fusion = bf16[64,4096]{1,0:T(8,128)(2,1)} fusion(bf16[1,512,4096]{2,1,0:T(8,128)(2,1)} %param.24, bf16[64,8192]{1,0:T(8,128)(2,1)} %normalize.1, bf16[1,8192,512]{2,1,0:T(8,128)(2,1)} %param.22, f32[512]{0:T(512)S(1)} %bitcast.113), kind=kOutput, calls=%fused_computation.4 | convolution fusion | flops 805765120 | bytes 14157824 | tf_op jit(solution)/shard_map/dot_general | solution.py:262
  150.8 14.0 %all_to_all.5 = bf16[4,16,4096]{2,1,0:T(8,128)(2,1)} all-to-all(bf16[4,16,4096]{2,1,0:T(8,128)(2,1)} %bitcast.94), channel_id=1, replica_groups=mesh['z'=4,'xl'=2,'core'=2,'y'=4,'xh'=2] {'y'}, dimensions={0} | all-to-all | bytes 1048576 | tf_op jit(solution)/shard_map/all_to_all | solution.py:264
  173.7 3.7 %collective-permute-done.22 = bf16[16,4096]{1,0:T(8,128)(2,1)S(1)} collective-permute-done((bf16[16,4096]{1,0:T(8,128)(2,1)S(1)}, bf16[16,4096]{1,0:T(8,128)(2,1)S(1)}, u32[]{:S(2)}, u32[]{:S(2)}) %collective-permute-start.22) | collective-permute-done | bytes 131104 | tf_op jit(solution)/shard_map/ppermute | solution.py:42
  178.3 3.2 %collective-permute-start.23 = (f32[16]{0:T(128)S(1)}, f32[16]{0:T(128)S(1)}, u32[]{:S(2)}, u32[]{:S(2)}) collective-permute-start(f32[16]{0:T(128)S(1)} %broadcast_add_fusion), channel_id=1, source_target_pairs={{0,6},{2,0},{4,2},{6,4},{1,7},{3,1},{5,3},{7,5},{8,14},{10,8},{12,... | collective-permute-start | bytes 200 | tf_op jit(solution)/shard_map/ppermute | solution.py:42
  182.8 3.7 %collective-permute-done.24 = f32[16]{0:T(128)S(1)} collective-permute-done((f32[16]{0:T(128)S(1)}, f32[16]{0:T(128)S(1)}, u32[]{:S(2)}, u32[]{:S(2)}) %collective-permute-start.24) | collective-permute-done | bytes 96 | tf_op jit(solution)/shard_map/ppermute | solution.py:42
  187.2 10.8 %trunk_part.2.refs_12_ = f32[1024,512]{1,0:T(8,128)S(1)} custom-call(s32[2]{0:T(128)S(1)} %pad_add_fusion.1.place_ref, bf16[4,512,1024]{2,1,0:T(8,128)(2,1)} %all-gather.6.cloned.1.call-done.refs_0_, bf16[4,512,1024]{2,1,0:T(8,128)(2,1)} %collective-permute-done.21.refs_1_, bf16[4,512,1024]{2,1,0:T(8,128)(2,1)} %bitcast.90, ...), custom_call_target="tpu_custom_call" | custom-call | flops 524288 | bytes 524288 | tf_op jit(solution)/shard_map/trunk_part/pallas_call | solution.py:123
  198.0 11.2 %trunk_part.3 = bf16[1024,512]{1,0:T(8,128)(2,1)S(1)} custom-call(s32[2]{0:T(128)S(1)} %pad_add_fusion.place_ref, bf16[4,512,1024]{2,1,0:T(8,128)(2,1)} %all-gather.6.cloned.1.call-done.refs_0_, bf16[4,512,1024]{2,1,0:T(8,128)(2,1)} %collective-permute-done.21.refs_1_, bf16[4,512,1024]{2,1,0:T(8,128)(2,1)} %bitcast.91, ...), custom_call_target="tpu_custom_call" | custom-call | flops 524288 | bytes 524288 | tf_op jit(solution)/shard_map/trunk_part/pallas_call | solution.py:123
  (110 shorter events, 48.7 us)
Async XLA Ops:
  7.2 112.1 %all-gather.6.cloned.1.call-start = ((), (), s32[]{:S(2)}) async-start(), calls=%async_computation.1 | async-start | bytes 5242880 | tf_op jit(solution)/shard_map/all_gather | solution.py:221
  13.6 155.1 %all-gather.8.cloned.1.call-start = ((), (), s32[]{:S(2)}) async-start(), calls=%async_computation.2 | async-start | bytes 5242880 | tf_op jit(solution)/shard_map/all_gather | solution.py:247
  13.7 18.0 %collective-permute-start = (bf16[512,512]{1,0:T(8,128)(2,1)S(1)}, bf16[512,512]{1,0:T(8,128)(2,1)}, u32[]{:S(2)}, u32[]{:S(2)}) collective-permute-start(bf16[512,512]{1,0:T(8,128)(2,1)S(1)} %get-tuple-element.60), channel_id=1, source_target_pairs={{0,0},{1,1},{2,98},{3,99},{4,68},{5,69},{6,38},{7,39},{8,8},{9,9},... | collective-permute-start | bytes 1572872 | tf_op jit(solution)/shard_map/ppermute | solution.py:217
  15.2 17.9 %collective-permute-start.1 = (bf16[512,512]{1,0:T(8,128)(2,1)S(1)}, bf16[512,512]{1,0:T(8,128)(2,1)}, u32[]{:S(2)}, u32[]{:S(2)}) collective-permute-start(bf16[512,512]{1,0:T(8,128)(2,1)S(1)} %get-tuple-element.59), channel_id=1, source_target_pairs={{0,64},{1,65},{2,34},{3,35},{4,4},{5,5},{6,102},{7,103},{8,72},{9,... | collective-permute-start | bytes 1572872 | tf_op jit(solution)/shard_map/ppermute | solution.py:217
  33.1 10.0 %collective-permute-start.2 = (bf16[16,2048]{1,0:T(8,128)(2,1)S(1)}, bf16[16,2048]{1,0:T(8,128)(2,1)S(1)}, u32[]{:S(2)}, u32[]{:S(2)}) collective-permute-start(bf16[16,2048]{1,0:T(8,128)(2,1)S(1)} %reshape.128), channel_id=1, source_target_pairs={{0,96},{32,0},{64,32},{96,64},{1,97},{33,1},{65,33},{97,65},{2,98}... | collective-permute-start | bytes 196616 | tf_op jit(solution)/shard_map/ppermute | solution.py:42
  36.5 6.6 %collective-permute-start.4 = (bf16[16,2048]{1,0:T(8,128)(2,1)S(1)}, bf16[16,2048]{1,0:T(8,128)(2,1)S(1)}, u32[]{:S(2)}, u32[]{:S(2)}) collective-permute-start(bf16[16,2048]{1,0:T(8,128)(2,1)S(1)} %reshape.128), channel_id=1, source_target_pairs={{0,32},{32,64},{64,96},{96,0},{1,33},{33,65},{65,97},{97,1},{2,34}... | collective-permute-start | bytes 196616 | tf_op jit(solution)/shard_map/ppermute | solution.py:42
  37.7 12.8 %collective-permute-start.6 = (bf16[512,512]{1,0:T(8,128)(2,1)}, bf16[512,512]{1,0:T(8,128)(2,1)S(1)}, u32[]{:S(2)}, u32[]{:S(2)}) collective-permute-start(bf16[512,512]{1,0:T(8,128)(2,1)} %collective-permute-done), channel_id=1, source_target_pairs={{0,0},{1,16},{2,2},{3,18},{4,4},{5,20},{6,6},{7,22},{8,8},{9,24},{... | collective-permute-start | bytes 1572872 | tf_op jit(solution)/shard_map/ppermute | solution.py:231
  39.4 28.6 %collective-permute-start.7 = (bf16[512,512]{1,0:T(8,128)(2,1)}, bf16[512,512]{1,0:T(8,128)(2,1)S(1)}, u32[]{:S(2)}, u32[]{:S(2)}) collective-permute-start(bf16[512,512]{1,0:T(8,128)(2,1)} %collective-permute-done.1), channel_id=1, source_target_pairs={{0,4},{1,20},{2,6},{3,22},{4,0},{5,16},{6,2},{7,18},{8,12},{9,28},... | collective-permute-start | bytes 1572872 | tf_op jit(solution)/shard_map/ppermute | solution.py:231
  43.5 7.0 %collective-permute-start.5 = (bf16[64,512]{1,0:T(8,128)(2,1)S(1)}, bf16[64,512]{1,0:T(8,128)(2,1)S(1)}, u32[]{:S(2)}, u32[]{:S(2)}) collective-permute-start(bf16[64,512]{1,0:T(8,128)(2,1)S(1)} %fusion.13), channel_id=1, source_target_pairs={{0,1},{1,0},{2,3},{3,2},{4,5},{5,4},{6,7},{7,6},{8,9},{9,8},{10,11... | collective-permute-start | bytes 196616 | tf_op jit(solution)/shard_map/ppermute | solution.py:42
  68.1 24.2 %collective-permute-start.11 = (bf16[512,1024]{1,0:T(8,128)(2,1)}, bf16[512,1024]{1,0:T(8,128)(2,1)}, u32[]{:S(2)}, u32[]{:S(2)}) collective-permute-start(bf16[512,1024]{1,0:T(8,128)(2,1)} %bitcast.85), channel_id=1, source_target_pairs={{0,1},{1,0},{2,3},{3,2},{4,5},{5,4},{6,7},{7,6},{8,9},{9,8},{10,11... | collective-permute-start | bytes 3145736 | tf_op jit(solution)/shard_map/ppermute | solution.py:42
  69.0 10.0 %collective-permute-start.10 = (bf16[2,64,512]{2,1,0:T(8,128)(2,1)S(1)}, bf16[2,64,512]{2,1,0:T(8,128)(2,1)S(1)}, u32[]{:S(2)}, u32[]{:S(2)}) collective-permute-start(bf16[2,64,512]{2,1,0:T(8,128)(2,1)S(1)} %pad_maximum_fusion.1), channel_id=1, source_target_pairs={{0,2},{2,4},{4,6},{6,0},{1,3},{3,5},{5,7},{7,1},{8,10},{10,12},{12... | collective-permute-start | bytes 393224 | tf_op jit(solution)/shard_map/ppermute | solution.py:42
  71.2 44.7 %collective-permute-start.12 = (bf16[2,512,512]{2,1,0:T(8,128)(2,1)S(1)}, bf16[2,512,512]{2,1,0:T(8,128)(2,1)S(1)}, u32[]{:S(2)}, u32[]{:S(2)}) collective-permute-start(bf16[2,512,512]{2,1,0:T(8,128)(2,1)S(1)} %pad_maximum_fusion.refs_4_.refs_5_), channel_id=1, source_target_pairs={{0,96},{32,0},{64,32},{96,64},{1,97},{33,1},{65,33},{97,65},{2,98}... | collective-permute-start | bytes 3145736 | tf_op jit(solution)/shard_map/ppermute | solution.py:42
  74.2 45.1 %collective-permute-start.13 = (bf16[2,512,512]{2,1,0:T(8,128)(2,1)S(1)}, bf16[2,512,512]{2,1,0:T(8,128)(2,1)S(1)}, u32[]{:S(2)}, u32[]{:S(2)}) collective-permute-start(bf16[2,512,512]{2,1,0:T(8,128)(2,1)S(1)} %pad_maximum_fusion.refs_4_.refs_5_), channel_id=1, source_target_pairs={{0,32},{32,64},{64,96},{96,0},{1,33},{33,65},{65,97},{97,1},{2,34}... | collective-permute-start | bytes 3145736 | tf_op jit(solution)/shard_map/ppermute | solution.py:42
  74.2 7.0 %collective-permute-start.9 = (bf16[2,64,512]{2,1,0:T(8,128)(2,1)S(1)}, bf16[2,64,512]{2,1,0:T(8,128)(2,1)S(1)}, u32[]{:S(2)}, u32[]{:S(2)}) collective-permute-start(bf16[2,64,512]{2,1,0:T(8,128)(2,1)S(1)} %pad_maximum_fusion.1), channel_id=1, source_target_pairs={{0,4},{2,6},{4,0},{6,2},{1,5},{3,7},{5,1},{7,3},{8,12},{10,14},{12... | collective-permute-start | bytes 393224 | tf_op jit(solution)/shard_map/ppermute | solution.py:42
  81.2 38.1 %collective-permute-start.14 = (bf16[2,512,512]{2,1,0:T(8,128)(2,1)S(1)}, bf16[2,512,512]{2,1,0:T(8,128)(2,1)}, u32[]{:S(2)}, u32[]{:S(2)}) collective-permute-start(bf16[2,512,512]{2,1,0:T(8,128)(2,1)S(1)} %pad_maximum_fusion.refs_4_.refs_5_), channel_id=1, source_target_pairs={{0,64},{32,96},{64,0},{96,32},{1,65},{33,97},{65,1},{97,33},{2,66}... | collective-permute-start | bytes 3145736 | tf_op jit(solution)/shard_map/ppermute | solution.py:42
  119.3 21.3 %collective-permute-start.18 = (bf16[2,512,512]{2,1,0:T(8,128)(2,1)S(1)}, bf16[2,512,512]{2,1,0:T(8,128)(2,1)}, u32[]{:S(2)}, u32[]{:S(2)}) collective-permute-start(bf16[2,512,512]{2,1,0:T(8,128)(2,1)S(1)} %pad_maximum_fusion.refs_4_.refs_5_), channel_id=1, source_target_pairs={{0,16},{16,0},{1,17},{17,1},{2,18},{18,2},{3,19},{19,3},{4,20},{20... | collective-permute-start | bytes 3145736 | tf_op jit(solution)/shard_map/ppermute | solution.py:42
  126.4 8.0 %collective-permute-start.16 = (bf16[4,64,512]{2,1,0:T(8,128)(2,1)S(1)}, bf16[4,64,512]{2,1,0:T(8,128)(2,1)S(1)}, u32[]{:S(2)}, u32[]{:S(2)}) collective-permute-start(bf16[4,64,512]{2,1,0:T(8,128)(2,1)S(1)} %bitcast.96), channel_id=1, source_target_pairs={{0,64},{32,96},{64,0},{96,32},{1,65},{33,97},{65,1},{97,33},{2,66}... | collective-permute-start | bytes 786440 | tf_op jit(solution)/shard_map/ppermute | solution.py:42
  126.4 10.7 %collective-permute-start.17 = (bf16[4,64,512]{2,1,0:T(8,128)(2,1)S(1)}, bf16[4,64,512]{2,1,0:T(8,128)(2,1)S(1)}, u32[]{:S(2)}, u32[]{:S(2)}) collective-permute-start(bf16[4,64,512]{2,1,0:T(8,128)(2,1)S(1)} %bitcast.97), channel_id=1, source_target_pairs={{0,32},{32,64},{64,96},{96,0},{1,33},{33,65},{65,97},{97,1},{2,34}... | collective-permute-start | bytes 786440 | tf_op jit(solution)/shard_map/ppermute | solution.py:42
  140.6 28.1 %collective-permute-start.21 = (bf16[4,512,1024]{2,1,0:T(8,128)(2,1)}, bf16[4,512,1024]{2,1,0:T(8,128)(2,1)}, u32[]{:S(2)}, u32[]{:S(2)}) collective-permute-start(bf16[4,512,1024]{2,1,0:T(8,128)(2,1)} %all-gather.6.cloned.1.call-done.refs_0_), channel_id=1, source_target_pairs={{0,8},{8,0},{1,9},{9,1},{2,10},{10,2},{3,11},{11,3},{4,12},{12,4},... | collective-permute-start | bytes 12582920 | tf_op jit(solution)/shard_map/ppermute | solution.py:42
  140.6 25.9 %collective-permute-start.19 = (bf16[2,512,512]{2,1,0:T(8,128)(2,1)}, bf16[2,512,512]{2,1,0:T(8,128)(2,1)}, u32[]{:S(2)}, u32[]{:S(2)}) collective-permute-start(bf16[2,512,512]{2,1,0:T(8,128)(2,1)} %collective-permute-done.18.refs_4_.refs_5_), channel_id=1, source_target_pairs={{0,96},{32,0},{64,32},{96,64},{1,97},{33,1},{65,33},{97,65},{2,98}... | collective-permute-start | bytes 3145736 | tf_op jit(solution)/shard_map/ppermute | solution.py:42
  141.9 26.8 %collective-permute-start.20 = (bf16[2,512,512]{2,1,0:T(8,128)(2,1)}, bf16[2,512,512]{2,1,0:T(8,128)(2,1)}, u32[]{:S(2)}, u32[]{:S(2)}) collective-permute-start(bf16[2,512,512]{2,1,0:T(8,128)(2,1)} %collective-permute-done.18.refs_4_.refs_5_), channel_id=1, source_target_pairs={{0,32},{32,64},{64,96},{96,0},{1,33},{33,65},{65,97},{97,1},{2,34}... | collective-permute-start | bytes 3145736 | tf_op jit(solution)/shard_map/ppermute | solution.py:42
  168.7 18.5 %collective-permute-start.26 = (bf16[4,512,1024]{2,1,0:T(8,128)(2,1)}, bf16[4,512,1024]{2,1,0:T(8,128)(2,1)}, u32[]{:S(2)}, u32[]{:S(2)}) collective-permute-start(bf16[4,512,1024]{2,1,0:T(8,128)(2,1)} %bitcast.89), channel_id=1, source_target_pairs={{0,8},{8,0},{1,9},{9,1},{2,10},{10,2},{3,11},{11,3},{4,12},{12,4},... | collective-permute-start | bytes 12582920 | tf_op jit(solution)/shard_map/ppermute | solution.py:42
  168.7 29.3 %collective-permute-start.27 = (bf16[2,512,512]{2,1,0:T(8,128)(2,1)}, bf16[2,512,512]{2,1,0:T(8,128)(2,1)}, u32[]{:S(2)}, u32[]{:S(2)}) collective-permute-start(bf16[2,512,512]{2,1,0:T(8,128)(2,1)} %collective-permute-done.18.refs_4_.refs_5_), channel_id=1, source_target_pairs={{0,64},{32,96},{64,0},{96,32},{1,65},{33,97},{65,1},{97,33},{2,66}... | collective-permute-start | bytes 3145736 | tf_op jit(solution)/shard_map/ppermute | solution.py:42
  169.9 7.4 %collective-permute-start.22 = (bf16[16,4096]{1,0:T(8,128)(2,1)S(1)}, bf16[16,4096]{1,0:T(8,128)(2,1)S(1)}, u32[]{:S(2)}, u32[]{:S(2)}) collective-permute-start(bf16[16,4096]{1,0:T(8,128)(2,1)S(1)} %reduce_sum.71), channel_id=1, source_target_pairs={{0,1},{1,0},{2,3},{3,2},{4,5},{5,4},{6,7},{7,6},{8,9},{9,8},{10,11... | collective-permute-start | bytes 393224 | tf_op jit(solution)/shard_map/ppermute | solution.py:42
  (17 other events, 155.0 us)
Sparse Core Ops, SparseCore 0:
  13.7 65.8 all-gather.5
  92.4 48.9 all-gather.7

commit v9 on v8

--- a/solution.py
+++ b/solution.py
@@ -116,7 +116,9 @@
     width = terms[0][2].shape[-1]
     count = len(terms)
 
-    def weight_spec(v):
+    def weight_spec(v, w):
+        if w.ndim == 2:
+            return pl.BlockSpec((depth, width // 2), lambda j, p: (0, lax.rem(j, 2)))
         return pl.BlockSpec((None, depth, width // 2), lambda j, p: (v, 0, lax.rem(j, 2)))
 
     tile = pl.BlockSpec((rows, width // 2), lambda j, p: (j // 2, lax.rem(j, 2)))
@@ -126,7 +128,7 @@
             num_scalar_prefetch=1,
             grid=(2 * CORE,),
             in_specs=[pl.BlockSpec(memory_space=pltpu.HBM)] * 4
-            + [weight_spec(v) for _, v, _ in terms]
+            + [weight_spec(v, w) for _, v, w in terms]
             + ([] if base is None else [tile]),
             out_specs=tile,
             scratch_shapes=[
@@ -239,20 +241,19 @@
     w = {(0, 0): jnp.stack(moved)}
     w[1, 0] = from_ahead(w[0, 0], "z", Z, 1)
     w[3, 0] = from_ahead(w[0, 0], "z", Z, 3)
-    w[2, 0] = from_ahead(w[0, 0], "z", Z, 2)
     across = from_ahead(held, "xh", XH, 1)
     parts = [pair] + [from_ahead(pair, "y", Y, s) for s in (1, 2, 3)]
     pooled = sum(jnp.sum(p.astype(jnp.float32), axis=0) for p in parts).astype(jnp.bfloat16)
     pooled, across = lock((pooled, across))
     there = lax.all_gather(across, "y", axis=0, tiled=False)
     near = lax.all_gather(pooled, ("xl", "core"), axis=0, tiled=False)
-    near, w[1, 0], w[3, 0], w[2, 0], w[0, 0], here = lock(
-        (near, w[1, 0], w[3, 0], w[2, 0], w[0, 0], here)
-    )
+    near, w[1, 0], w[3, 0], w[0, 0], here = lock((near, w[1, 0], w[3, 0], w[0, 0], here))
     pieces = [near] + [from_ahead(near, "z", Z, s) for s in (1, 2, 3)]
     w[0, 1] = from_ahead(w[0, 0], "xl", XL, 1)
+    pieces[1], w[1, 0], w[3, 0] = lock((pieces[1], w[1, 0], w[3, 0]))
+    w[2, 0] = [from_ahead(w[1, 0][0], "z", Z, 1), from_ahead(w[3, 0][1], "z", Z, 3)]
     features = normalize(pieces, norm_gain, z)
-    features, w[0, 1], here = lock((features, w[0, 1], here))
+    features, w[0, 1], here, *w[2, 0] = lock((features, w[0, 1], here, *w[2, 0]))
     w[1, 1] = from_ahead(w[0, 1], "z", Z, 1)
     w[3, 1] = from_ahead(w[0, 1], "z", Z, 3)
     here_other = from_ahead(here, "core", CORE, 1)
@@ -264,21 +265,26 @@
     terms = lax.all_to_all(
         terms.reshape(Y, count, terms.shape[1]), "y", split_axis=0, concat_axis=0, tiled=True
     )
-    terms, there, w[0, 1], w[1, 1], w[3, 1], here_other = lock(
-        (terms, there, w[0, 1], w[1, 1], w[3, 1], here_other)
-    )
-    there_other = from_ahead(there, "core", CORE, 1)
+    terms, w[0, 1], w[1, 1], w[3, 1], here_other = lock(
+        (terms, w[0, 1], w[1, 1], w[3, 1], here_other)
+    )
     w[2, 1] = from_ahead(w[0, 1], "z", Z, 2)
     half = jnp.sum(terms.astype(jnp.float32), axis=0).astype(jnp.bfloat16)
     other = from_ahead(half, "xh", XH, 1)
     second = jax.nn.silu(half.astype(jnp.float32) + other.astype(jnp.float32) + head_b2[0])
+    second, there = lock((second, there))
+    there_other = from_ahead(there, "core", CORE, 1)
     mine = jnp.sum(second * head_w3[0].astype(jnp.float32), axis=-1) + head_b3[0]
     scores = jnp.stack([mine] + [from_ahead(mine, "y", Y, s) for s in (1, 2, 3)])
     scores = jnp.roll(scores, lax.rem(y + z, Y), axis=0).reshape(1, Y * count)
 
 
     def product(e, trunk, dtype):
-        items = [(s, v, w[s, e]) for s in range(Z) for v in range(2)]
+        items = [
+            (s, v, w[s, e][v] if isinstance(w[s, e], list) else w[s, e])
+            for s in range(Z)
+            for v in range(2)
+        ]
         place = jnp.stack([lax.rem(y - z + Y, Y), lax.rem(xl + e + xh, XH)])
         return trunk_part(place, sources, items, trunk, dtype)
 

time: 221 us -> 231 us (1.045)
  waiting for transfers between devices: 75.6 us -> 82.3 us
    ppermute x25 -> x26, waiting for transfers between devices: 56.6 us -> 63.4 us  [from_ahead(): return lax.ppermute(x, axis, [(i, (i - step) % size) for i in range(size)])]
    ppermute x25 -> x26, starting transfers between devices: 38.7 us -> 39.3 us  [from_ahead(): return lax.ppermute(x, axis, [(i, (i - step) % size) for i in range(size)])]
  transfers between devices with their start and end apart: 31 -> 32, of which waited for: 17 -> 17; matrix products, arithmetic and copies ran while one was open for 9% -> 9% of each run, Pallas kernels for 6% -> 6%
where the time goes in v9:
time: 231 us; the launch traced here: 229 us
  waiting for transfers between devices  82.3 us (36%)
  starting transfers between devices  52 us (23%)
  blocking collectives  25.2 us (11%)
  Pallas kernels  24.8 us (11%)
  between operations  15.1 us (7%)
  local copies, waits for them, and re-layouts  11.9 us (5%)
  matrix products  9.7 us (4%)
  other arithmetic  8.28 us (4%)
    ppermute x26, waiting for transfers between devices, from_ahead(): return lax.ppermute(x, axis, [(i, (i - step) % size) for i in range(size)])  63.4 us
    ppermute x26, starting transfers between devices, from_ahead(): return lax.ppermute(x, axis, [(i, (i - step) % size) for i in range(size)])  39.3 us
    pallas_call x2, Pallas kernels, trunk_part(): pl.pallas_call(functools.partial(trunk_kernel, [(s, v) for s, v, _ in ter...  22 us
    ppermute x2, waiting for transfers between devices, local(): moved = [lax.ppermute(m, ALL, column_moves(v)) for v, m in enumerate(moved)]  17.5 us
    all_to_all x1, blocking collectives, local(): lax.all_to_all(terms.reshape(Y, count, terms.shape[1]), 'y', split_axis=0...  14 us
    dot_general x1, matrix products, local(): jnp.dot(first, head_w2[0], preferred_element_type=jnp.float32)  8.06 us
    ppermute x2, starting transfers between devices, local(): lax.ppermute(out_weight[v * rows_half:(v + 1) * rows_half], ALL, spread_m...  7.31 us
    all_gather x1, blocking collectives, local(): near = lax.all_gather(pooled, ('xl', 'core'), axis=0, tiled=False)  5.98 us
  transfers between devices with their start and end apart: 32, of which 17 were waited for; matrix products, arithmetic and copies ran while one was open for 9% of the time, Pallas kernels for 6%

profile of v9, /device:TPU:0, one launch (start us, length us, event | category | flops | bytes accessed | tf_op | source)
XLA Modules:
  0.0 229.4 jit_solution(7142413578720792546)
XLA Ops:
  15.2 5.9 %collective-permute-start.1 = (bf16[512,512]{1,0:T(8,128)(2,1)S(1)}, bf16[512,512]{1,0:T(8,128)(2,1)}, u32[]{:S(2)}, u32[]{:S(2)}) collective-permute-start(bf16[512,512]{1,0:T(8,128)(2,1)S(1)} %get-tuple-element.69), channel_id=1, source_target_pairs={{0,64},{1,65},{2,34},{3,35},{4,4},{5,5},{6,102},{7,103},{8,72},{9,... | collective-permute-start | bytes 1572872 | tf_op jit(solution)/shard_map/ppermute | solution.py:219
  26.4 5.2 %all-gather.2 = bf16[4,4,2048]{2,1,0:T(4,128)(2,1)S(1)} all-gather(bf16[1,4,2048]{2,1,0:T(4,128)(2,1)S(1)} %maximum_bitcast_fusion), channel_id=1, replica_groups=mesh['z'=4,'xl'=2,'core'=2,'y'=4,'xh'=2] {'xl','core'}, dimensions={0}, use_global_device_ids=true | all-gather | bytes 81920 | tf_op jit(solution)/shard_map/all_gather | solution.py:231
  33.1 3.4 %collective-permute-start.2 = (bf16[16,2048]{1,0:T(8,128)(2,1)S(1)}, bf16[16,2048]{1,0:T(8,128)(2,1)S(1)}, u32[]{:S(2)}, u32[]{:S(2)}) collective-permute-start(bf16[16,2048]{1,0:T(8,128)(2,1)S(1)} %reshape.128), channel_id=1, source_target_pairs={{0,96},{32,0},{64,32},{96,64},{1,97},{33,1},{65,33},{97,65},{2,98}... | collective-permute-start | bytes 196616 | tf_op jit(solution)/shard_map/ppermute | solution.py:42
  39.4 3.6 %collective-permute-start.7 = (bf16[512,512]{1,0:T(8,128)(2,1)}, bf16[512,512]{1,0:T(8,128)(2,1)S(1)}, u32[]{:S(2)}, u32[]{:S(2)}) collective-permute-start(bf16[512,512]{1,0:T(8,128)(2,1)} %collective-permute-done.1), channel_id=1, source_target_pairs={{0,4},{1,20},{2,6},{3,22},{4,0},{5,16},{6,2},{7,18},{8,12},{9,28},... | collective-permute-start | bytes 1572872 | tf_op jit(solution)/shard_map/ppermute | solution.py:233
  43.5 4.8 %collective-permute-start.5 = (bf16[64,512]{1,0:T(8,128)(2,1)S(1)}, bf16[64,512]{1,0:T(8,128)(2,1)S(1)}, u32[]{:S(2)}, u32[]{:S(2)}) collective-permute-start(bf16[64,512]{1,0:T(8,128)(2,1)S(1)} %fusion.13), channel_id=1, source_target_pairs={{0,1},{1,0},{2,3},{3,2},{4,5},{5,4},{6,7},{7,6},{8,9},{9,8},{10,11... | collective-permute-start | bytes 196616 | tf_op jit(solution)/shard_map/ppermute | solution.py:42
  50.5 17.5 %collective-permute-done.7 = bf16[512,512]{1,0:T(8,128)(2,1)S(1)} collective-permute-done((bf16[512,512]{1,0:T(8,128)(2,1)}, bf16[512,512]{1,0:T(8,128)(2,1)S(1)}, u32[]{:S(2)}, u32[]{:S(2)}) %collective-permute-start.7) | collective-permute-done | bytes 524320 | tf_op jit(solution)/shard_map/ppermute | solution.py:233
  69.2 4.4 %collective-permute-start.12 = (bf16[2,512,512]{2,1,0:T(8,128)(2,1)S(1)}, bf16[2,512,512]{2,1,0:T(8,128)(2,1)S(1)}, u32[]{:S(2)}, u32[]{:S(2)}) collective-permute-start(bf16[2,512,512]{2,1,0:T(8,128)(2,1)S(1)} %pad_maximum_fusion.refs_4_.refs_5_), channel_id=1, source_target_pairs={{0,96},{32,0},{64,32},{96,64},{1,97},{33,1},{65,33},{97,65},{2,98}... | collective-permute-start | bytes 3145736 | tf_op jit(solution)/shard_map/ppermute | solution.py:42
  75.9 5.8 %collective-permute-done.10 = bf16[2,64,512]{2,1,0:T(8,128)(2,1)S(1)} collective-permute-done((bf16[2,64,512]{2,1,0:T(8,128)(2,1)S(1)}, bf16[2,64,512]{2,1,0:T(8,128)(2,1)S(1)}, u32[]{:S(2)}, u32[]{:S(2)}) %collective-permute-start.10) | collective-permute-done | bytes 131104 | tf_op jit(solution)/shard_map/ppermute | solution.py:42
  81.7 4.9 %collective-permute-done.8 = bf16[2,64,512]{2,1,0:T(8,128)(2,1)S(1)} collective-permute-done((bf16[2,64,512]{2,1,0:T(8,128)(2,1)S(1)}, bf16[2,64,512]{2,1,0:T(8,128)(2,1)S(1)}, u32[]{:S(2)}, u32[]{:S(2)}) %collective-permute-start.8) | collective-permute-done | bytes 131104 | tf_op jit(solution)/shard_map/ppermute | solution.py:42
  87.3 4.9 %collective-permute-done.11 = bf16[512,1024]{1,0:T(8,128)(2,1)} collective-permute-done((bf16[512,1024]{1,0:T(8,128)(2,1)}, bf16[512,1024]{1,0:T(8,128)(2,1)}, u32[]{:S(2)}, u32[]{:S(2)}) %collective-permute-start.11) | collective-permute-done | bytes 1048608 | tf_op jit(solution)/shard_map/ppermute | solution.py:42
  92.2 6.0 %all-gather = bf16[256,512]{1,0:T(8,128)(2,1)S(1)} all-gather(bf16[64,512]{1,0:T(8,128)(2,1)} %add_convert_fusion.1), channel_id=2, replica_groups=mesh['z'=4,'xl'=2,'core'=2,'y'=4,'xh'=2] {'xl','core'}, dimensions={0}, use_global_device_ids=true | all-gather | bytes 327680 | tf_op jit(solution)/shard_map/all_gather | solution.py:249
  98.3 5.3 %collective-permute-start.14 = (bf16[4,64,512]{2,1,0:T(8,128)(2,1)S(1)}, bf16[4,64,512]{2,1,0:T(8,128)(2,1)}, u32[]{:S(2)}, u32[]{:S(2)}) collective-permute-start(bf16[4,64,512]{2,1,0:T(8,128)(2,1)S(1)} %bitcast.99), channel_id=1, source_target_pairs={{0,96},{32,0},{64,32},{96,64},{1,97},{33,1},{65,33},{97,65},{2,98}... | collective-permute-start | bytes 786440 | tf_op jit(solution)/shard_map/ppermute | solution.py:42
  104.1 5.5 %collective-permute-done.14.p1 = bf16[4,64,512]{2,1,0:T(8,128)(2,1)} collective-permute-done((bf16[4,64,512]{2,1,0:T(8,128)(2,1)S(1)}, bf16[4,64,512]{2,1,0:T(8,128)(2,1)}, u32[]{:S(2)}, u32[]{:S(2)}) %collective-permute-start.14) | collective-permute-done | bytes 262176 | tf_op jit(solution)/shard_map/ppermute | solution.py:42
  110.4 3.8 %collective-permute-start.18 = (bf16[512,512]{1,0:T(8,128)(2,1)}, bf16[512,512]{1,0:T(8,128)(2,1)}, u32[]{:S(2)}, u32[]{:S(2)}) collective-permute-start(bf16[512,512]{1,0:T(8,128)(2,1)} %slice_bitcast_fusion.1), channel_id=1, source_target_pairs={{0,96},{32,0},{64,32},{96,64},{1,97},{33,1},{65,33},{97,65},{2,98}... | collective-permute-start | bytes 1572872 | tf_op jit(solution)/shard_map/ppermute | solution.py:42
  119.2 16.1 %collective-permute-done.15.p2 = bf16[4,64,512]{2,1,0:T(8,128)(2,1)S(1)} collective-permute-done((bf16[4,64,512]{2,1,0:T(8,128)(2,1)S(1)}, bf16[4,64,512]{2,1,0:T(8,128)(2,1)S(1)}, u32[]{:S(2)}, u32[]{:S(2)}) %collective-permute-start.15) | collective-permute-done | bytes 262176 | tf_op jit(solution)/shard_map/ppermute | solution.py:42
  135.2 5.6 %collective-permute-done.16.p3 = bf16[4,64,512]{2,1,0:T(8,128)(2,1)S(1)} collective-permute-done((bf16[4,64,512]{2,1,0:T(8,128)(2,1)S(1)}, bf16[4,64,512]{2,1,0:T(8,128)(2,1)S(1)}, u32[]{:S(2)}, u32[]{:S(2)}) %collective-permute-start.16) | collective-permute-done | bytes 262176 | tf_op jit(solution)/shard_map/ppermute | solution.py:42
  141.5 2.8 %normalize.1 = bf16[64,8192]{1,0:T(8,128)(2,1)} custom-call(s32[1]{0:T(128)} %bitcast.2.place_ref, bf16[4,64,512]{2,1,0:T(8,128)(2,1)} %bitcast.102, bf16[4,64,512]{2,1,0:T(8,128)(2,1)} %collective-permute-done.14.p1, bf16[4,64,512]{2,1,0:T(8,128)(2,1)} %copy-done.5, bf16[4,64,512]{2,1,0:T(8,128)(2,1)} %copy-done.6, f32[1,8192]{1,0:T(1,128)} %bitcast.109), custom_call_target="tpu_custom_call" | custom-call | flops 4194304 | bytes 2097152 | tf_op jit(solution)/shard_map/normalize/pallas_call | solution.py:181
  146.7 8.1 %convolution_convert_fusion = bf16[64,4096]{1,0:T(8,128)(2,1)} fusion(bf16[1,512,4096]{2,1,0:T(8,128)(2,1)} %param.24, bf16[64,8192]{1,0:T(8,128)(2,1)} %normalize.1, bf16[1,8192,512]{2,1,0:T(8,128)(2,1)} %param.22, f32[512]{0:T(512)S(1)} %bitcast.117), kind=kOutput, calls=%fused_computation.4 | convolution fusion | flops 805765120 | bytes 14157824 | tf_op jit(solution)/shard_map/dot_general | solution.py:263
  154.8 14.0 %all_to_all.5 = bf16[4,16,4096]{2,1,0:T(8,128)(2,1)} all-to-all(bf16[4,16,4096]{2,1,0:T(8,128)(2,1)} %bitcast.98), channel_id=1, replica_groups=mesh['z'=4,'xl'=2,'core'=2,'y'=4,'xh'=2] {'y'}, dimensions={0} | all-to-all | bytes 1048576 | tf_op jit(solution)/shard_map/all_to_all | solution.py:265
  172.9 2.8 %collective-permute-start.23 = (bf16[16,4096]{1,0:T(8,128)(2,1)S(1)}, bf16[16,4096]{1,0:T(8,128)(2,1)S(1)}, u32[]{:S(2)}, u32[]{:S(2)}) collective-permute-start(bf16[16,4096]{1,0:T(8,128)(2,1)S(1)} %reduce_sum.71), channel_id=1, source_target_pairs={{0,1},{1,0},{2,3},{3,2},{4,5},{5,4},{6,7},{7,6},{8,9},{9,8},{10,11... | collective-permute-start | bytes 393224 | tf_op jit(solution)/shard_map/ppermute | solution.py:42
  175.6 3.8 %collective-permute-done.23 = bf16[16,4096]{1,0:T(8,128)(2,1)S(1)} collective-permute-done((bf16[16,4096]{1,0:T(8,128)(2,1)S(1)}, bf16[16,4096]{1,0:T(8,128)(2,1)S(1)}, u32[]{:S(2)}, u32[]{:S(2)}) %collective-permute-start.23) | collective-permute-done | bytes 131104 | tf_op jit(solution)/shard_map/ppermute | solution.py:42
  191.6 10.8 %trunk_part.2.refs_12_ = f32[1024,512]{1,0:T(8,128)S(1)} custom-call(s32[2]{0:T(128)S(1)} %pad_add_fusion.1.place_ref, bf16[4,512,1024]{2,1,0:T(8,128)(2,1)} %all-gather.6.cloned.1.call-done.refs_0_, bf16[4,512,1024]{2,1,0:T(8,128)(2,1)} %collective-permute-done.22.refs_1_, bf16[4,512,1024]{2,1,0:T(8,128)(2,1)} %bitcast.94, ...), custom_call_target="tpu_custom_call" | custom-call | flops 524288 | bytes 524288 | tf_op jit(solution)/shard_map/trunk_part/pallas_call | solution.py:125
  202.4 5.6 %collective-permute-done.28.refs_8_.refs_9_ = bf16[2,512,512]{2,1,0:T(8,128)(2,1)} collective-permute-done((bf16[2,512,512]{2,1,0:T(8,128)(2,1)}, bf16[2,512,512]{2,1,0:T(8,128)(2,1)}, u32[]{:S(2)}, u32[]{:S(2)}) %collective-permute-start.28) | collective-permute-done | bytes 1048608 | tf_op jit(solution)/shard_map/ppermute | solution.py:42
  207.9 11.2 %trunk_part.3 = bf16[1024,512]{1,0:T(8,128)(2,1)S(1)} custom-call(s32[2]{0:T(128)S(1)} %pad_add_fusion.place_ref, bf16[4,512,1024]{2,1,0:T(8,128)(2,1)} %all-gather.6.cloned.1.call-done.refs_0_, bf16[4,512,1024]{2,1,0:T(8,128)(2,1)} %collective-permute-done.22.refs_1_, bf16[4,512,1024]{2,1,0:T(8,128)(2,1)} %bitcast.95, ...), custom_call_target="tpu_custom_call" | custom-call | flops 524288 | bytes 524288 | tf_op jit(solution)/shard_map/trunk_part/pallas_call | solution.py:125
  (115 shorter events, 52.6 us)
Async XLA Ops:
  7.2 91.1 %all-gather.6.cloned.1.call-start = ((), (), s32[]{:S(2)}) async-start(), calls=%async_computation.1 | async-start | bytes 5242880 | tf_op jit(solution)/shard_map/all_gather | solution.py:223
  13.6 166.9 %all-gather.8.cloned.1.call-start = ((), (), s32[]{:S(2)}) async-start(), calls=%async_computation.2 | async-start | bytes 5242880 | tf_op jit(solution)/shard_map/all_gather | solution.py:248
  13.7 18.0 %collective-permute-start = (bf16[512,512]{1,0:T(8,128)(2,1)S(1)}, bf16[512,512]{1,0:T(8,128)(2,1)}, u32[]{:S(2)}, u32[]{:S(2)}) collective-permute-start(bf16[512,512]{1,0:T(8,128)(2,1)S(1)} %get-tuple-element.70), channel_id=1, source_target_pairs={{0,0},{1,1},{2,98},{3,99},{4,68},{5,69},{6,38},{7,39},{8,8},{9,9},... | collective-permute-start | bytes 1572872 | tf_op jit(solution)/shard_map/ppermute | solution.py:219
  15.2 17.9 %collective-permute-start.1 = (bf16[512,512]{1,0:T(8,128)(2,1)S(1)}, bf16[512,512]{1,0:T(8,128)(2,1)}, u32[]{:S(2)}, u32[]{:S(2)}) collective-permute-start(bf16[512,512]{1,0:T(8,128)(2,1)S(1)} %get-tuple-element.69), channel_id=1, source_target_pairs={{0,64},{1,65},{2,34},{3,35},{4,4},{5,5},{6,102},{7,103},{8,72},{9,... | collective-permute-start | bytes 1572872 | tf_op jit(solution)/shard_map/ppermute | solution.py:219
  33.1 10.0 %collective-permute-start.2 = (bf16[16,2048]{1,0:T(8,128)(2,1)S(1)}, bf16[16,2048]{1,0:T(8,128)(2,1)S(1)}, u32[]{:S(2)}, u32[]{:S(2)}) collective-permute-start(bf16[16,2048]{1,0:T(8,128)(2,1)S(1)} %reshape.128), channel_id=1, source_target_pairs={{0,96},{32,0},{64,32},{96,64},{1,97},{33,1},{65,33},{97,65},{2,98}... | collective-permute-start | bytes 196616 | tf_op jit(solution)/shard_map/ppermute | solution.py:42
  37.7 12.8 %collective-permute-start.6 = (bf16[512,512]{1,0:T(8,128)(2,1)}, bf16[512,512]{1,0:T(8,128)(2,1)S(1)}, u32[]{:S(2)}, u32[]{:S(2)}) collective-permute-start(bf16[512,512]{1,0:T(8,128)(2,1)} %collective-permute-done), channel_id=1, source_target_pairs={{0,0},{1,16},{2,2},{3,18},{4,4},{5,20},{6,6},{7,22},{8,8},{9,24},{... | collective-permute-start | bytes 1572872 | tf_op jit(solution)/shard_map/ppermute | solution.py:233
  39.4 28.6 %collective-permute-start.7 = (bf16[512,512]{1,0:T(8,128)(2,1)}, bf16[512,512]{1,0:T(8,128)(2,1)S(1)}, u32[]{:S(2)}, u32[]{:S(2)}) collective-permute-start(bf16[512,512]{1,0:T(8,128)(2,1)} %collective-permute-done.1), channel_id=1, source_target_pairs={{0,4},{1,20},{2,6},{3,22},{4,0},{5,16},{6,2},{7,18},{8,12},{9,28},... | collective-permute-start | bytes 1572872 | tf_op jit(solution)/shard_map/ppermute | solution.py:233
  43.5 7.0 %collective-permute-start.5 = (bf16[64,512]{1,0:T(8,128)(2,1)S(1)}, bf16[64,512]{1,0:T(8,128)(2,1)S(1)}, u32[]{:S(2)}, u32[]{:S(2)}) collective-permute-start(bf16[64,512]{1,0:T(8,128)(2,1)S(1)} %fusion.13), channel_id=1, source_target_pairs={{0,1},{1,0},{2,3},{3,2},{4,5},{5,4},{6,7},{7,6},{8,9},{9,8},{10,11... | collective-permute-start | bytes 196616 | tf_op jit(solution)/shard_map/ppermute | solution.py:42
  68.1 24.2 %collective-permute-start.11 = (bf16[512,1024]{1,0:T(8,128)(2,1)}, bf16[512,1024]{1,0:T(8,128)(2,1)}, u32[]{:S(2)}, u32[]{:S(2)}) collective-permute-start(bf16[512,1024]{1,0:T(8,128)(2,1)} %bitcast.89), channel_id=1, source_target_pairs={{0,1},{1,0},{2,3},{3,2},{4,5},{5,4},{6,7},{7,6},{8,9},{9,8},{10,11... | collective-permute-start | bytes 3145736 | tf_op jit(solution)/shard_map/ppermute | solution.py:42
  69.2 29.0 %collective-permute-start.12 = (bf16[2,512,512]{2,1,0:T(8,128)(2,1)S(1)}, bf16[2,512,512]{2,1,0:T(8,128)(2,1)S(1)}, u32[]{:S(2)}, u32[]{:S(2)}) collective-permute-start(bf16[2,512,512]{2,1,0:T(8,128)(2,1)S(1)} %pad_maximum_fusion.refs_4_.refs_5_), channel_id=1, source_target_pairs={{0,96},{32,0},{64,32},{96,64},{1,97},{33,1},{65,33},{97,65},{2,98}... | collective-permute-start | bytes 3145736 | tf_op jit(solution)/shard_map/ppermute | solution.py:42
  73.6 24.6 %collective-permute-start.13 = (bf16[2,512,512]{2,1,0:T(8,128)(2,1)S(1)}, bf16[2,512,512]{2,1,0:T(8,128)(2,1)S(1)}, u32[]{:S(2)}, u32[]{:S(2)}) collective-permute-start(bf16[2,512,512]{2,1,0:T(8,128)(2,1)S(1)} %pad_maximum_fusion.refs_4_.refs_5_), channel_id=1, source_target_pairs={{0,32},{32,64},{64,96},{96,0},{1,33},{33,65},{65,97},{97,1},{2,34}... | collective-permute-start | bytes 3145736 | tf_op jit(solution)/shard_map/ppermute | solution.py:42
  73.6 8.1 %collective-permute-start.10 = (bf16[2,64,512]{2,1,0:T(8,128)(2,1)S(1)}, bf16[2,64,512]{2,1,0:T(8,128)(2,1)S(1)}, u32[]{:S(2)}, u32[]{:S(2)}) collective-permute-start(bf16[2,64,512]{2,1,0:T(8,128)(2,1)S(1)} %pad_maximum_fusion.1), channel_id=1, source_target_pairs={{0,2},{2,4},{4,6},{6,0},{1,3},{3,5},{5,7},{7,1},{8,10},{10,12},{12... | collective-permute-start | bytes 393224 | tf_op jit(solution)/shard_map/ppermute | solution.py:42
  74.2 7.5 %collective-permute-start.9 = (bf16[2,64,512]{2,1,0:T(8,128)(2,1)S(1)}, bf16[2,64,512]{2,1,0:T(8,128)(2,1)S(1)}, u32[]{:S(2)}, u32[]{:S(2)}) collective-permute-start(bf16[2,64,512]{2,1,0:T(8,128)(2,1)S(1)} %pad_maximum_fusion.1), channel_id=1, source_target_pairs={{0,4},{2,6},{4,0},{6,2},{1,5},{3,7},{5,1},{7,3},{8,12},{10,14},{12... | collective-permute-start | bytes 393224 | tf_op jit(solution)/shard_map/ppermute | solution.py:42
  98.3 11.3 %collective-permute-start.14 = (bf16[4,64,512]{2,1,0:T(8,128)(2,1)S(1)}, bf16[4,64,512]{2,1,0:T(8,128)(2,1)}, u32[]{:S(2)}, u32[]{:S(2)}) collective-permute-start(bf16[4,64,512]{2,1,0:T(8,128)(2,1)S(1)} %bitcast.99), channel_id=1, source_target_pairs={{0,96},{32,0},{64,32},{96,64},{1,97},{33,1},{65,33},{97,65},{2,98}... | collective-permute-start | bytes 786440 | tf_op jit(solution)/shard_map/ppermute | solution.py:42
  103.6 40.8 %collective-permute-start.17 = (bf16[2,512,512]{2,1,0:T(8,128)(2,1)S(1)}, bf16[2,512,512]{2,1,0:T(8,128)(2,1)}, u32[]{:S(2)}, u32[]{:S(2)}) collective-permute-start(bf16[2,512,512]{2,1,0:T(8,128)(2,1)S(1)} %pad_maximum_fusion.refs_4_.refs_5_), channel_id=1, source_target_pairs={{0,16},{16,0},{1,17},{17,1},{2,18},{18,2},{3,19},{19,3},{4,20},{20... | collective-permute-start | bytes 3145736 | tf_op jit(solution)/shard_map/ppermute | solution.py:42
  110.4 33.9 %collective-permute-start.18 = (bf16[512,512]{1,0:T(8,128)(2,1)}, bf16[512,512]{1,0:T(8,128)(2,1)}, u32[]{:S(2)}, u32[]{:S(2)}) collective-permute-start(bf16[512,512]{1,0:T(8,128)(2,1)} %slice_bitcast_fusion.1), channel_id=1, source_target_pairs={{0,96},{32,0},{64,32},{96,64},{1,97},{33,1},{65,33},{97,65},{2,98}... | collective-permute-start | bytes 1572872 | tf_op jit(solution)/shard_map/ppermute | solution.py:42
  115.1 29.3 %collective-permute-start.19 = (bf16[512,512]{1,0:T(8,128)(2,1)}, bf16[512,512]{1,0:T(8,128)(2,1)}, u32[]{:S(2)}, u32[]{:S(2)}) collective-permute-start(bf16[512,512]{1,0:T(8,128)(2,1)} %slice_bitcast_fusion), channel_id=1, source_target_pairs={{0,32},{32,64},{64,96},{96,0},{1,33},{33,65},{65,97},{97,1},{2,34}... | collective-permute-start | bytes 1572872 | tf_op jit(solution)/shard_map/ppermute | solution.py:42
  115.1 20.2 %collective-permute-start.15 = (bf16[4,64,512]{2,1,0:T(8,128)(2,1)S(1)}, bf16[4,64,512]{2,1,0:T(8,128)(2,1)S(1)}, u32[]{:S(2)}, u32[]{:S(2)}) collective-permute-start(bf16[4,64,512]{2,1,0:T(8,128)(2,1)S(1)} %bitcast.100), channel_id=1, source_target_pairs={{0,64},{32,96},{64,0},{96,32},{1,65},{33,97},{65,1},{97,33},{2,66}... | collective-permute-start | bytes 786440 | tf_op jit(solution)/shard_map/ppermute | solution.py:42
  116.5 24.3 %collective-permute-start.16 = (bf16[4,64,512]{2,1,0:T(8,128)(2,1)S(1)}, bf16[4,64,512]{2,1,0:T(8,128)(2,1)S(1)}, u32[]{:S(2)}, u32[]{:S(2)}) collective-permute-start(bf16[4,64,512]{2,1,0:T(8,128)(2,1)S(1)} %bitcast.101), channel_id=1, source_target_pairs={{0,32},{32,64},{64,96},{96,0},{1,33},{33,65},{65,97},{97,1},{2,34}... | collective-permute-start | bytes 786440 | tf_op jit(solution)/shard_map/ppermute | solution.py:42
  144.4 27.4 %collective-permute-start.22 = (bf16[4,512,1024]{2,1,0:T(8,128)(2,1)}, bf16[4,512,1024]{2,1,0:T(8,128)(2,1)}, u32[]{:S(2)}, u32[]{:S(2)}) collective-permute-start(bf16[4,512,1024]{2,1,0:T(8,128)(2,1)} %all-gather.6.cloned.1.call-done.refs_0_), channel_id=1, source_target_pairs={{0,8},{8,0},{1,9},{9,1},{2,10},{10,2},{3,11},{11,3},{4,12},{12,4},... | collective-permute-start | bytes 12582920 | tf_op jit(solution)/shard_map/ppermute | solution.py:42
  144.6 25.9 %collective-permute-start.20 = (bf16[2,512,512]{2,1,0:T(8,128)(2,1)}, bf16[2,512,512]{2,1,0:T(8,128)(2,1)}, u32[]{:S(2)}, u32[]{:S(2)}) collective-permute-start(bf16[2,512,512]{2,1,0:T(8,128)(2,1)} %collective-permute-done.17.refs_4_.refs_5_), channel_id=1, source_target_pairs={{0,96},{32,0},{64,32},{96,64},{1,97},{33,1},{65,33},{97,65},{2,98}... | collective-permute-start | bytes 3145736 | tf_op jit(solution)/shard_map/ppermute | solution.py:42
  144.7 27.0 %collective-permute-start.21 = (bf16[2,512,512]{2,1,0:T(8,128)(2,1)}, bf16[2,512,512]{2,1,0:T(8,128)(2,1)}, u32[]{:S(2)}, u32[]{:S(2)}) collective-permute-start(bf16[2,512,512]{2,1,0:T(8,128)(2,1)} %collective-permute-done.17.refs_4_.refs_5_), channel_id=1, source_target_pairs={{0,32},{32,64},{64,96},{96,0},{1,33},{33,65},{65,97},{97,1},{2,34}... | collective-permute-start | bytes 3145736 | tf_op jit(solution)/shard_map/ppermute | solution.py:42
  180.5 11.1 %collective-permute-start.27 = (bf16[4,512,1024]{2,1,0:T(8,128)(2,1)}, bf16[4,512,1024]{2,1,0:T(8,128)(2,1)}, u32[]{:S(2)}, u32[]{:S(2)}) collective-permute-start(bf16[4,512,1024]{2,1,0:T(8,128)(2,1)} %bitcast.93), channel_id=1, source_target_pairs={{0,8},{8,0},{1,9},{9,1},{2,10},{10,2},{3,11},{11,3},{4,12},{12,4},... | collective-permute-start | bytes 12582920 | tf_op jit(solution)/shard_map/ppermute | solution.py:42
  180.5 27.4 %collective-permute-start.28 = (bf16[2,512,512]{2,1,0:T(8,128)(2,1)}, bf16[2,512,512]{2,1,0:T(8,128)(2,1)}, u32[]{:S(2)}, u32[]{:S(2)}) collective-permute-start(bf16[2,512,512]{2,1,0:T(8,128)(2,1)} %collective-permute-done.17.refs_4_.refs_5_), channel_id=1, source_target_pairs={{0,64},{32,96},{64,0},{96,32},{1,65},{33,97},{65,1},{97,33},{2,66}... | collective-permute-start | bytes 3145736 | tf_op jit(solution)/shard_map/ppermute | solution.py:42
  (18 other events, 154.4 us)
Sparse Core Ops, SparseCore 0:
  13.7 62.5 all-gather.5
  103.7 45.4 all-gather.7

commit v10 on v9

--- a/solution.py
+++ b/solution.py
@@ -9,7 +9,6 @@
 from jax.sharding import Mesh, PartitionSpec as P
 
 HEAD_WIDTH = 128
-SEQUENCE_SLOTS = 128
 Z, XL, CORE, Y, XH = 4, 2, 2, 4, 2
 MEMBER = ("z", "xl", "core")
 TENSOR = ("y", "xh")
@@ -42,32 +41,64 @@
     return lax.ppermute(x, axis, [(i, (i - step) % size) for i in range(size)])
 
 
-def attention(query, keys, values, cand_len):
-    row_count = query.shape[0]
-    cand_count = row_count // SEQUENCE_SLOTS
-    heads_here = query.shape[1] // HEAD_WIDTH
-    kv_here = keys.shape[1] // HEAD_WIDTH
-    group_width = heads_here // kv_here
-    query_tiles = query.reshape(cand_count, SEQUENCE_SLOTS, kv_here, group_width, HEAD_WIDTH)
-    key_tiles = keys.reshape(cand_count, SEQUENCE_SLOTS, kv_here, HEAD_WIDTH)
-    value_tiles = values.reshape(cand_count, SEQUENCE_SLOTS, kv_here, HEAD_WIDTH)
-    logits = jnp.einsum(
-        "cskgd,ctkd->ckgst", query_tiles, key_tiles, preferred_element_type=jnp.float32
+def attention_kernel(len_ref, query_ref, keys_ref, values_ref, residual_ref, out_ref, picked_ref):
+    length = len_ref[pl.program_id(0)]
+    slots, width = query_ref.shape
+    heads = width // HEAD_WIDTH
+    queries = jnp.concatenate(
+        [query_ref[:, h * HEAD_WIDTH : (h + 1) * HEAD_WIDTH] for h in range(heads)], axis=0
+    )
+    logits = lax.dot_general(
+        queries, keys_ref[...], (((1,), (1,)), ((), ())), preferred_element_type=jnp.float32
     ) * HEAD_WIDTH ** (-0.5)
-    places = jnp.arange(SEQUENCE_SLOTS, dtype=jnp.int32)
-    allowed = (places[None, :, None] >= places[None, None, :]) & (
-        places[None, None, :] < cand_len[:, None, None]
-    )
-    allowed = allowed[:, None, None]
+    row = lax.rem(lax.broadcasted_iota(jnp.int32, logits.shape, 0), slots)
+    column = lax.broadcasted_iota(jnp.int32, logits.shape, 1)
+    allowed = (row >= column) & (column < length)
     logits = jnp.where(allowed, logits, jnp.float32(-1e30))
     row_max = jnp.max(logits, axis=-1, keepdims=True)
     probs = jnp.where(allowed, jnp.exp(logits - row_max), jnp.float32(0.0))
     totals = jnp.sum(probs, axis=-1, keepdims=True)
-    attn_weights = (probs / totals).astype(jnp.bfloat16)
-    attn_out = jnp.einsum(
-        "ckgst,ctkd->cskgd", attn_weights, value_tiles, preferred_element_type=jnp.float32
-    )
-    return attn_out.astype(jnp.bfloat16).reshape(row_count, heads_here * HEAD_WIDTH)
+    weights = (probs / totals).astype(jnp.bfloat16)
+    result = jnp.dot(weights, values_ref[...], preferred_element_type=jnp.float32)
+    result = result.astype(jnp.bfloat16)
+    scored = lax.broadcasted_iota(jnp.int32, (slots, 1), 0) == length - 1
+    for h in range(heads):
+        part = result[h * slots : (h + 1) * slots]
+        out_ref[:, h * HEAD_WIDTH : (h + 1) * HEAD_WIDTH] = part
+        picked_ref[0, :, h * HEAD_WIDTH : (h + 1) * HEAD_WIDTH] = jnp.sum(
+            jnp.where(scored, part.astype(jnp.float32), 0.0), axis=0, keepdims=True
+        ).astype(jnp.bfloat16)
+    picked_ref[0, :, width:] = jnp.sum(
+        jnp.where(scored, residual_ref[...].astype(jnp.float32), 0.0), axis=0, keepdims=True
+    ).astype(jnp.bfloat16)
+
+
+def attention(query, keys, values, residual, cand_len):
+    count = cand_len.shape[0]
+    slots = query.shape[0] // count
+    wide = pl.BlockSpec((slots, query.shape[1]), lambda c, n: (c, 0))
+    narrow = pl.BlockSpec((slots, keys.shape[1]), lambda c, n: (c, 0))
+    picked_width = query.shape[1] + residual.shape[1]
+    out, picked = pl.pallas_call(
+        attention_kernel,
+        grid_spec=pltpu.PrefetchScalarGridSpec(
+            num_scalar_prefetch=1,
+            grid=(count,),
+            in_specs=[wide, narrow, narrow, wide],
+            out_specs=[wide, pl.BlockSpec((1, 1, picked_width), lambda c, n: (c, 0, 0))],
+        ),
+        out_shape=[
+            jax.ShapeDtypeStruct(query.shape, jnp.bfloat16),
+            jax.ShapeDtypeStruct((count, 1, picked_width), jnp.bfloat16),
+        ],
+        cost_estimate=pl.CostEstimate(
+            flops=4 * query.size * slots,
+            bytes_accessed=6 * query.size,
+            transcendentals=query.size,
+        ),
+        name="attention",
+    )(cand_len, query, keys, values, residual)
+    return out, picked.reshape(count, picked_width)
 
 
 def trunk_kernel(picks, has_base, place_ref, *refs):
@@ -211,7 +242,6 @@
     core = lax.axis_index("core")
     y = lax.axis_index("y")
     xh = lax.axis_index("xh")
-    cand_count = cand_len.shape[0]
 
     lock = lax.optimization_barrier
     rows_half = out_weight.shape[0] // 2
@@ -219,13 +249,9 @@
         lax.ppermute(out_weight[v * rows_half : (v + 1) * rows_half], ALL, spread_moves(v))
         for v in range(2)
     ]
-    attn_out = attention(query, keys, values, cand_len)
+    attn_out, picked = attention(query, keys, values, residual, cand_len)
     here = lax.all_gather(attn_out, "y", axis=0, tiled=False)
 
-    last_rows = jnp.arange(cand_count, dtype=jnp.int32) * SEQUENCE_SLOTS + cand_len - 1
-    picked = jnp.concatenate(
-        [jnp.take(attn_out, last_rows, axis=0), jnp.take(residual, last_rows, axis=0)], axis=1
-    )
     depth = attn_out.shape[1]
     width = out_weight.shape[1]
     near = lax.all_gather(picked, ("xl", "core"), axis=0, tiled=True)
@@ -250,7 +276,7 @@
     near, w[1, 0], w[3, 0], w[0, 0], here = lock((near, w[1, 0], w[3, 0], w[0, 0], here))
     pieces = [near] + [from_ahead(near, "z", Z, s) for s in (1, 2, 3)]
     w[0, 1] = from_ahead(w[0, 0], "xl", XL, 1)
-    pieces[1], w[1, 0], w[3, 0] = lock((pieces[1], w[1, 0], w[3, 0]))
+    *pieces, w[1, 0], w[3, 0] = lock((*pieces, w[1, 0], w[3, 0]))
     w[2, 0] = [from_ahead(w[1, 0][0], "z", Z, 1), from_ahead(w[3, 0][1], "z", Z, 3)]
     features = normalize(pieces, norm_gain, z)
     features, w[0, 1], here, *w[2, 0] = lock((features, w[0, 1], here, *w[2, 0]))
@@ -265,15 +291,14 @@
     terms = lax.all_to_all(
         terms.reshape(Y, count, terms.shape[1]), "y", split_axis=0, concat_axis=0, tiled=True
     )
-    terms, w[0, 1], w[1, 1], w[3, 1], here_other = lock(
-        (terms, w[0, 1], w[1, 1], w[3, 1], here_other)
-    )
+    terms, there, w[0, 1], w[1, 1], w[3, 1], here_other = lock(
+        (terms, there, w[0, 1], w[1, 1], w[3, 1], here_other)
+    )
+    there_other = from_ahead(there, "core", CORE, 1)
     w[2, 1] = from_ahead(w[0, 1], "z", Z, 2)
     half = jnp.sum(terms.astype(jnp.float32), axis=0).astype(jnp.bfloat16)
     other = from_ahead(half, "xh", XH, 1)
     second = jax.nn.silu(half.astype(jnp.float32) + other.astype(jnp.float32) + head_b2[0])
-    second, there = lock((second, there))
-    there_other = from_ahead(there, "core", CORE, 1)
     mine = jnp.sum(second * head_w3[0].astype(jnp.float32), axis=-1) + head_b3[0]
     scores = jnp.stack([mine] + [from_ahead(mine, "y", Y, s) for s in (1, 2, 3)])
     scores = jnp.roll(scores, lax.rem(y + z, Y), axis=0).reshape(1, Y * count)

time: 231 us -> 215 us (0.931)
  waiting for transfers between devices: 82.3 us -> 74.7 us
  local copies, waits for them, and re-layouts: 11.9 us -> 5.1 us
  Pallas kernels: 24.8 us -> 30.7 us
  other arithmetic: 8.28 us -> 3.12 us
    ppermute x26, waiting for transfers between devices: 63.4 us -> 52.9 us  [from_ahead(): return lax.ppermute(x, axis, [(i, (i - step) % size) for i in range(size)])]
    pallas_call x0 -> x1, Pallas kernels: none -> 5.82 us  [attention(): pl.pallas_call(attention_kernel, grid_spec=pltpu.PrefetchScalarGridSpec(n...]
    ppermute x2, waiting for transfers between devices: 1.33 us -> 6.19 us  [local(): lax.ppermute(out_weight[v * rows_half:(v + 1) * rows_half], ALL, spread_m...]
    gather x2 -> x0, local copies, waits for them, and re-layouts: 3.96 us -> none  [the longest x1 2.03 us: local(): jnp.take(residual, last_rows, axis=0)]
  transfers between devices with their start and end apart: 32 -> 32, of which waited for: 17 -> 20; matrix products, arithmetic and copies ran while one was open for 9% -> 6% of each run, Pallas kernels for 6% -> 6%
where the time goes in v10:
time: 215 us; the launch traced here: 213 us
  waiting for transfers between devices  74.7 us (35%)
  starting transfers between devices  50.5 us (23%)
  Pallas kernels  30.7 us (14%)
  blocking collectives  25.5 us (12%)
  between operations  15 us (7%)
  matrix products  8.38 us (4%)
  local copies, waits for them, and re-layouts  5.1 us (2%)
  other arithmetic  3.12 us (1%)
    ppermute x26, waiting for transfers between devices, from_ahead(): return lax.ppermute(x, axis, [(i, (i - step) % size) for i in range(size)])  52.9 us
    ppermute x26, starting transfers between devices, from_ahead(): return lax.ppermute(x, axis, [(i, (i - step) % size) for i in range(size)])  38.8 us
    pallas_call x2, Pallas kernels, trunk_part(): pl.pallas_call(functools.partial(trunk_kernel, [(s, v) for s, v, _ in ter...  22 us
    ppermute x2, waiting for transfers between devices, local(): moved = [lax.ppermute(m, ALL, column_moves(v)) for v, m in enumerate(moved)]  15.6 us
    all_to_all x1, blocking collectives, local(): lax.all_to_all(terms.reshape(Y, count, terms.shape[1]), 'y', split_axis=0...  14.1 us
    dot_general x1, matrix products, local(): jnp.dot(first, head_w2[0], preferred_element_type=jnp.float32)  8.08 us
    ppermute x2, starting transfers between devices, local(): lax.ppermute(out_weight[v * rows_half:(v + 1) * rows_half], ALL, spread_m...  6.56 us
    ppermute x2, waiting for transfers between devices, local(): lax.ppermute(out_weight[v * rows_half:(v + 1) * rows_half], ALL, spread_m...  6.19 us
  transfers between devices with their start and end apart: 32, of which 20 were waited for; matrix products, arithmetic and copies ran while one was open for 6% of the time, Pallas kernels for 6%

profile of v10, /device:TPU:0, one launch (start us, length us, event | category | flops | bytes accessed | tf_op | source)
XLA Modules:
  0.0 213.0 jit_solution(13171024089038937542)
XLA Ops:
  7.2 5.8 %attention.1 = (bf16[512,1024]{1,0:T(8,128)(2,1)}, bf16[4,1,2048]{2,1,0:T(2,128)(2,1)}) custom-call(s32[4]{0:T(128)} %len_ref.1, bf16[512,1024]{1,0:T(8,128)(2,1)} %query_ref.1, bf16[512,128]{1,0:T(8,128)(2,1)} %keys_ref.1, bf16[512,128]{1,0:T(8,128)(2,1)} %values_ref.1, bf16[512,1024]{1,0:T(8,128)(2,1)} %residual_ref.1), custom_call_target="tpu_custom_call" | custom-call | flops 268435456 | bytes 3145728 | tf_op jit(solution)/shard_map/attention/pallas_call | solution.py:82
  15.1 5.9 %collective-permute-start.1 = (bf16[512,512]{1,0:T(8,128)(2,1)S(1)}, bf16[512,512]{1,0:T(8,128)(2,1)S(1)}, u32[]{:S(2)}, u32[]{:S(2)}) collective-permute-start(bf16[512,512]{1,0:T(8,128)(2,1)S(1)} %get-tuple-element.74), channel_id=1, source_target_pairs={{0,64},{1,65},{2,34},{3,35},{4,4},{5,5},{6,102},{7,103},{8,72},{9,... | collective-permute-start | bytes 1572872 | tf_op jit(solution)/shard_map/ppermute | solution.py:249
  21.0 5.6 %all-gather = bf16[16,1,2048]{2,1,0:T(2,128)(2,1)S(1)} all-gather(bf16[4,1,2048]{2,1,0:T(2,128)(2,1)} %get-tuple-element.37), channel_id=2, replica_groups=mesh['z'=4,'xl'=2,'core'=2,'y'=4,'xh'=2] {'xl','core'}, dimensions={0}, use_global_device_ids=true | all-gather | bytes 81920 | tf_op jit(solution)/shard_map/all_gather | solution.py:257
  26.7 6.2 %collective-permute-done.1 = bf16[512,512]{1,0:T(8,128)(2,1)S(1)} collective-permute-done((bf16[512,512]{1,0:T(8,128)(2,1)S(1)}, bf16[512,512]{1,0:T(8,128)(2,1)S(1)}, u32[]{:S(2)}, u32[]{:S(2)}) %collective-permute-start.1) | collective-permute-done | bytes 524320 | tf_op jit(solution)/shard_map/ppermute | solution.py:249
  32.9 3.4 %collective-permute-start.2 = (bf16[16,2048]{1,0:T(8,128)(2,1)S(1)}, bf16[16,2048]{1,0:T(8,128)(2,1)S(1)}, u32[]{:S(2)}, u32[]{:S(2)}) collective-permute-start(bf16[16,2048]{1,0:T(8,128)(2,1)S(1)} %bitcast.58), channel_id=1, source_target_pairs={{0,96},{32,0},{64,32},{96,64},{1,97},{33,1},{65,33},{97,65},{2,98}... | collective-permute-start | bytes 196616 | tf_op jit(solution)/shard_map/ppermute | solution.py:41
  38.2 4.4 %collective-permute-start.7 = (bf16[512,512]{1,0:T(8,128)(2,1)S(1)}, bf16[512,512]{1,0:T(8,128)(2,1)S(1)}, u32[]{:S(2)}, u32[]{:S(2)}) collective-permute-start(bf16[512,512]{1,0:T(8,128)(2,1)S(1)} %collective-permute-done.1), channel_id=1, source_target_pairs={{0,4},{1,20},{2,6},{3,22},{4,0},{5,16},{6,2},{7,18},{8,12},{9,28},... | collective-permute-start | bytes 1572872 | tf_op jit(solution)/shard_map/ppermute | solution.py:259
  43.0 5.8 %collective-permute-start.5 = (bf16[64,512]{1,0:T(8,128)(2,1)S(1)}, bf16[64,512]{1,0:T(8,128)(2,1)S(1)}, u32[]{:S(2)}, u32[]{:S(2)}) collective-permute-start(bf16[64,512]{1,0:T(8,128)(2,1)S(1)} %fusion.6), channel_id=1, source_target_pairs={{0,1},{1,0},{2,3},{3,2},{4,5},{5,4},{6,7},{7,6},{8,9},{9,8},{10,11... | collective-permute-start | bytes 196616 | tf_op jit(solution)/shard_map/ppermute | solution.py:41
  51.1 15.6 %collective-permute-done.7 = bf16[512,512]{1,0:T(8,128)(2,1)S(1)} collective-permute-done((bf16[512,512]{1,0:T(8,128)(2,1)S(1)}, bf16[512,512]{1,0:T(8,128)(2,1)S(1)}, u32[]{:S(2)}, u32[]{:S(2)}) %collective-permute-start.7) | collective-permute-done | bytes 524320 | tf_op jit(solution)/shard_map/ppermute | solution.py:259
  71.6 3.0 %collective-permute-start.12 = (bf16[2,512,512]{2,1,0:T(8,128)(2,1)S(1)}, bf16[2,512,512]{2,1,0:T(8,128)(2,1)S(1)}, u32[]{:S(2)}, u32[]{:S(2)}) collective-permute-start(bf16[2,512,512]{2,1,0:T(8,128)(2,1)S(1)} %pad_maximum_fusion.refs_4_.refs_5_), channel_id=1, source_target_pairs={{0,96},{32,0},{64,32},{96,64},{1,97},{33,1},{65,33},{97,65},{2,98}... | collective-permute-start | bytes 3145736 | tf_op jit(solution)/shard_map/ppermute | solution.py:41
  76.1 2.7 %collective-permute-done.10 = bf16[2,64,512]{2,1,0:T(8,128)(2,1)S(1)} collective-permute-done((bf16[2,64,512]{2,1,0:T(8,128)(2,1)S(1)}, bf16[2,64,512]{2,1,0:T(8,128)(2,1)S(1)}, u32[]{:S(2)}, u32[]{:S(2)}) %collective-permute-start.10) | collective-permute-done | bytes 131104 | tf_op jit(solution)/shard_map/ppermute | solution.py:41
  81.1 2.6 %collective-permute-done.8 = bf16[2,64,512]{2,1,0:T(8,128)(2,1)S(1)} collective-permute-done((bf16[2,64,512]{2,1,0:T(8,128)(2,1)S(1)}, bf16[2,64,512]{2,1,0:T(8,128)(2,1)S(1)}, u32[]{:S(2)}, u32[]{:S(2)}) %collective-permute-start.8) | collective-permute-done | bytes 131104 | tf_op jit(solution)/shard_map/ppermute | solution.py:41
  83.8 7.2 %collective-permute-done.11 = bf16[512,1024]{1,0:T(8,128)(2,1)} collective-permute-done((bf16[512,1024]{1,0:T(8,128)(2,1)}, bf16[512,1024]{1,0:T(8,128)(2,1)}, u32[]{:S(2)}, u32[]{:S(2)}) %collective-permute-start.11) | collective-permute-done | bytes 1048608 | tf_op jit(solution)/shard_map/ppermute | solution.py:41
  91.0 5.8 %all-gather.1 = bf16[256,512]{1,0:T(8,128)(2,1)S(1)} all-gather(bf16[64,512]{1,0:T(8,128)(2,1)S(1)} %add_convert_fusion.1), channel_id=3, replica_groups=mesh['z'=4,'xl'=2,'core'=2,'y'=4,'xh'=2] {'xl','core'}, dimensions={0}, use_global_device_ids=true | all-gather | bytes 327680 | tf_op jit(solution)/shard_map/all_gather | solution.py:275
  97.4 6.5 %collective-permute-start.14 = (bf16[4,64,512]{2,1,0:T(8,128)(2,1)S(1)}, bf16[4,64,512]{2,1,0:T(8,128)(2,1)S(1)}, u32[]{:S(2)}, u32[]{:S(2)}) collective-permute-start(bf16[4,64,512]{2,1,0:T(8,128)(2,1)S(1)} %bitcast.52), channel_id=1, source_target_pairs={{0,96},{32,0},{64,32},{96,64},{1,97},{33,1},{65,33},{97,65},{2,98}... | collective-permute-start | bytes 786440 | tf_op jit(solution)/shard_map/ppermute | solution.py:41
  105.3 10.3 %collective-permute-done.14.p1 = bf16[4,64,512]{2,1,0:T(8,128)(2,1)S(1)} collective-permute-done((bf16[4,64,512]{2,1,0:T(8,128)(2,1)S(1)}, bf16[4,64,512]{2,1,0:T(8,128)(2,1)S(1)}, u32[]{:S(2)}, u32[]{:S(2)}) %collective-permute-start.14) | collective-permute-done | bytes 262176 | tf_op jit(solution)/shard_map/ppermute | solution.py:41
  122.7 2.8 %normalize.1 = bf16[64,8192]{1,0:T(8,128)(2,1)} custom-call(s32[1]{0:T(128)} %bitcast.2.place_ref, bf16[4,64,512]{2,1,0:T(8,128)(2,1)} %bitcast.55, bf16[4,64,512]{2,1,0:T(8,128)(2,1)} %copy-done.3, bf16[4,64,512]{2,1,0:T(8,128)(2,1)} %copy-done.4, bf16[4,64,512]{2,1,0:T(8,128)(2,1)} %collective-permute-done.16.p3, f32[1,8192]{1,0:T(1,128)} %bitcast.65), custom_call_target="tpu_custom_call" | custom-call | flops 4194304 | bytes 2097152 | tf_op jit(solution)/shard_map/normalize/pallas_call | solution.py:212
  125.6 8.2 %collective-permute-done.18.refs_8_ = bf16[512,512]{1,0:T(8,128)(2,1)} collective-permute-done((bf16[512,512]{1,0:T(8,128)(2,1)}, bf16[512,512]{1,0:T(8,128)(2,1)}, u32[]{:S(2)}, u32[]{:S(2)}) %collective-permute-start.18) | collective-permute-done | bytes 524320 | tf_op jit(solution)/shard_map/ppermute | solution.py:41
  133.8 3.3 %collective-permute-done.19.refs_9_ = bf16[512,512]{1,0:T(8,128)(2,1)} collective-permute-done((bf16[512,512]{1,0:T(8,128)(2,1)}, bf16[512,512]{1,0:T(8,128)(2,1)}, u32[]{:S(2)}, u32[]{:S(2)}) %collective-permute-start.19) | collective-permute-done | bytes 524320 | tf_op jit(solution)/shard_map/ppermute | solution.py:41
  139.1 8.1 %convolution_convert_fusion = bf16[64,4096]{1,0:T(8,128)(2,1)} fusion(bf16[1,512,4096]{2,1,0:T(8,128)(2,1)} %param.22, bf16[64,8192]{1,0:T(8,128)(2,1)} %normalize.1, bf16[1,8192,512]{2,1,0:T(8,128)(2,1)} %param.20, f32[512]{0:T(512)S(1)} %bitcast.73), kind=kOutput, calls=%fused_computation.2 | convolution fusion | flops 805765120 | bytes 14157824 | tf_op jit(solution)/shard_map/dot_general | solution.py:289
  147.1 14.1 %all_to_all.5 = bf16[4,16,4096]{2,1,0:T(8,128)(2,1)} all-to-all(bf16[4,16,4096]{2,1,0:T(8,128)(2,1)} %bitcast.51), channel_id=1, replica_groups=mesh['z'=4,'xl'=2,'core'=2,'y'=4,'xh'=2] {'y'}, dimensions={0} | all-to-all | bytes 1048576 | tf_op jit(solution)/shard_map/all_to_all | solution.py:291
  166.4 2.8 %collective-permute-start.23 = (bf16[16,4096]{1,0:T(8,128)(2,1)S(1)}, bf16[16,4096]{1,0:T(8,128)(2,1)S(1)}, u32[]{:S(2)}, u32[]{:S(2)}) collective-permute-start(bf16[16,4096]{1,0:T(8,128)(2,1)S(1)} %reduce_sum.61), channel_id=1, source_target_pairs={{0,1},{1,0},{2,3},{3,2},{4,5},{5,4},{6,7},{7,6},{8,9},{9,8},{10,11... | collective-permute-start | bytes 393224 | tf_op jit(solution)/shard_map/ppermute | solution.py:41
  170.0 3.3 %collective-permute-done.23 = bf16[16,4096]{1,0:T(8,128)(2,1)S(1)} collective-permute-done((bf16[16,4096]{1,0:T(8,128)(2,1)S(1)}, bf16[16,4096]{1,0:T(8,128)(2,1)S(1)}, u32[]{:S(2)}, u32[]{:S(2)}) %collective-permute-start.23) | collective-permute-done | bytes 131104 | tf_op jit(solution)/shard_map/ppermute | solution.py:41
  180.5 10.8 %trunk_part.2.refs_12_ = f32[1024,512]{1,0:T(8,128)S(1)} custom-call(s32[2]{0:T(128)S(1)} %pad_add_fusion.1.place_ref, bf16[4,512,1024]{2,1,0:T(8,128)(2,1)} %bitcast.46, bf16[4,512,1024]{2,1,0:T(8,128)(2,1)} %collective-permute-done.22.refs_1_, bf16[4,512,1024]{2,1,0:T(8,128)(2,1)} %bitcast.49, bf16[4,512,1024]{2,1,0:T(8,128)(2,1)} %collective-permute-done.27.refs_3_, ...), custom_call_target="tpu_custom_call" | custom-call | flops 524288 | bytes 524288 | tf_op jit(solution)/shard_map/trunk_part/pallas_call | solution.py:156
  191.5 11.2 %trunk_part.3 = bf16[1024,512]{1,0:T(8,128)(2,1)S(1)} custom-call(s32[2]{0:T(128)S(1)} %pad_add_fusion.place_ref, bf16[4,512,1024]{2,1,0:T(8,128)(2,1)} %bitcast.47, bf16[4,512,1024]{2,1,0:T(8,128)(2,1)} %collective-permute-done.22.refs_1_, bf16[4,512,1024]{2,1,0:T(8,128)(2,1)} %bitcast.50, bf16[4,512,1024]{2,1,0:T(8,128)(2,1)} %collective-permute-done.27.refs_3_, ...), custom_call_target="tpu_custom_call" | custom-call | flops 524288 | bytes 524288 | tf_op jit(solution)/shard_map/trunk_part/pallas_call | solution.py:156
  (95 shorter events, 42.8 us)
Async XLA Ops:
  7.2 90.2 %all-gather.7.cloned.1.call-start = ((), (), s32[]{:S(2)}) async-start(), calls=%async_computation.1 | async-start | bytes 5242880 | tf_op jit(solution)/shard_map/all_gather | solution.py:253
  13.1 151.1 %all-gather.9.cloned.1.call-start = ((), (), s32[]{:S(2)}) async-start(), calls=%async_computation.2 | async-start | bytes 5242880 | tf_op jit(solution)/shard_map/all_gather | solution.py:274
  14.4 12.3 %collective-permute-start = (bf16[512,512]{1,0:T(8,128)(2,1)S(1)}, bf16[512,512]{1,0:T(8,128)(2,1)S(1)}, u32[]{:S(2)}, u32[]{:S(2)}) collective-permute-start(bf16[512,512]{1,0:T(8,128)(2,1)S(1)} %get-tuple-element.75), channel_id=1, source_target_pairs={{0,0},{1,1},{2,98},{3,99},{4,68},{5,69},{6,38},{7,39},{8,8},{9,9},... | collective-permute-start | bytes 1572872 | tf_op jit(solution)/shard_map/ppermute | solution.py:249
  15.1 17.8 %collective-permute-start.1 = (bf16[512,512]{1,0:T(8,128)(2,1)S(1)}, bf16[512,512]{1,0:T(8,128)(2,1)S(1)}, u32[]{:S(2)}, u32[]{:S(2)}) collective-permute-start(bf16[512,512]{1,0:T(8,128)(2,1)S(1)} %get-tuple-element.74), channel_id=1, source_target_pairs={{0,64},{1,65},{2,34},{3,35},{4,4},{5,5},{6,102},{7,103},{8,72},{9,... | collective-permute-start | bytes 1572872 | tf_op jit(solution)/shard_map/ppermute | solution.py:249
  32.9 9.8 %collective-permute-start.2 = (bf16[16,2048]{1,0:T(8,128)(2,1)S(1)}, bf16[16,2048]{1,0:T(8,128)(2,1)S(1)}, u32[]{:S(2)}, u32[]{:S(2)}) collective-permute-start(bf16[16,2048]{1,0:T(8,128)(2,1)S(1)} %bitcast.58), channel_id=1, source_target_pairs={{0,96},{32,0},{64,32},{96,64},{1,97},{33,1},{65,33},{97,65},{2,98}... | collective-permute-start | bytes 196616 | tf_op jit(solution)/shard_map/ppermute | solution.py:41
  37.5 13.5 %collective-permute-start.6 = (bf16[512,512]{1,0:T(8,128)(2,1)S(1)}, bf16[512,512]{1,0:T(8,128)(2,1)S(1)}, u32[]{:S(2)}, u32[]{:S(2)}) collective-permute-start(bf16[512,512]{1,0:T(8,128)(2,1)S(1)} %collective-permute-done), channel_id=1, source_target_pairs={{0,0},{1,16},{2,2},{3,18},{4,4},{5,20},{6,6},{7,22},{8,8},{9,24},{... | collective-permute-start | bytes 1572872 | tf_op jit(solution)/shard_map/ppermute | solution.py:259
  38.2 28.5 %collective-permute-start.7 = (bf16[512,512]{1,0:T(8,128)(2,1)S(1)}, bf16[512,512]{1,0:T(8,128)(2,1)S(1)}, u32[]{:S(2)}, u32[]{:S(2)}) collective-permute-start(bf16[512,512]{1,0:T(8,128)(2,1)S(1)} %collective-permute-done.1), channel_id=1, source_target_pairs={{0,4},{1,20},{2,6},{3,22},{4,0},{5,16},{6,2},{7,18},{8,12},{9,28},... | collective-permute-start | bytes 1572872 | tf_op jit(solution)/shard_map/ppermute | solution.py:259
  43.0 8.0 %collective-permute-start.5 = (bf16[64,512]{1,0:T(8,128)(2,1)S(1)}, bf16[64,512]{1,0:T(8,128)(2,1)S(1)}, u32[]{:S(2)}, u32[]{:S(2)}) collective-permute-start(bf16[64,512]{1,0:T(8,128)(2,1)S(1)} %fusion.6), channel_id=1, source_target_pairs={{0,1},{1,0},{2,3},{3,2},{4,5},{5,4},{6,7},{7,6},{8,9},{9,8},{10,11... | collective-permute-start | bytes 196616 | tf_op jit(solution)/shard_map/ppermute | solution.py:41
  66.7 24.3 %collective-permute-start.11 = (bf16[512,1024]{1,0:T(8,128)(2,1)}, bf16[512,1024]{1,0:T(8,128)(2,1)}, u32[]{:S(2)}, u32[]{:S(2)}) collective-permute-start(bf16[512,1024]{1,0:T(8,128)(2,1)} %get-tuple-element.43), channel_id=1, source_target_pairs={{0,1},{1,0},{2,3},{3,2},{4,5},{5,4},{6,7},{7,6},{8,9},{9,8},{10,11... | collective-permute-start | bytes 3145736 | tf_op jit(solution)/shard_map/ppermute | solution.py:41
  69.1 9.6 %collective-permute-start.10 = (bf16[2,64,512]{2,1,0:T(8,128)(2,1)S(1)}, bf16[2,64,512]{2,1,0:T(8,128)(2,1)S(1)}, u32[]{:S(2)}, u32[]{:S(2)}) collective-permute-start(bf16[2,64,512]{2,1,0:T(8,128)(2,1)S(1)} %pad_maximum_fusion.1), channel_id=1, source_target_pairs={{0,2},{2,4},{4,6},{6,0},{1,3},{3,5},{5,7},{7,1},{8,10},{10,12},{12... | collective-permute-start | bytes 393224 | tf_op jit(solution)/shard_map/ppermute | solution.py:41
  71.6 25.2 %collective-permute-start.12 = (bf16[2,512,512]{2,1,0:T(8,128)(2,1)S(1)}, bf16[2,512,512]{2,1,0:T(8,128)(2,1)S(1)}, u32[]{:S(2)}, u32[]{:S(2)}) collective-permute-start(bf16[2,512,512]{2,1,0:T(8,128)(2,1)S(1)} %pad_maximum_fusion.refs_4_.refs_5_), channel_id=1, source_target_pairs={{0,96},{32,0},{64,32},{96,64},{1,97},{33,1},{65,33},{97,65},{2,98}... | collective-permute-start | bytes 3145736 | tf_op jit(solution)/shard_map/ppermute | solution.py:41
  74.6 22.7 %collective-permute-start.13 = (bf16[2,512,512]{2,1,0:T(8,128)(2,1)S(1)}, bf16[2,512,512]{2,1,0:T(8,128)(2,1)S(1)}, u32[]{:S(2)}, u32[]{:S(2)}) collective-permute-start(bf16[2,512,512]{2,1,0:T(8,128)(2,1)S(1)} %pad_maximum_fusion.refs_4_.refs_5_), channel_id=1, source_target_pairs={{0,32},{32,64},{64,96},{96,0},{1,33},{33,65},{65,97},{97,1},{2,34}... | collective-permute-start | bytes 3145736 | tf_op jit(solution)/shard_map/ppermute | solution.py:41
  97.4 18.2 %collective-permute-start.14 = (bf16[4,64,512]{2,1,0:T(8,128)(2,1)S(1)}, bf16[4,64,512]{2,1,0:T(8,128)(2,1)S(1)}, u32[]{:S(2)}, u32[]{:S(2)}) collective-permute-start(bf16[4,64,512]{2,1,0:T(8,128)(2,1)S(1)} %bitcast.52), channel_id=1, source_target_pairs={{0,96},{32,0},{64,32},{96,64},{1,97},{33,1},{65,33},{97,65},{2,98}... | collective-permute-start | bytes 786440 | tf_op jit(solution)/shard_map/ppermute | solution.py:41
  103.8 11.7 %collective-permute-start.15 = (bf16[4,64,512]{2,1,0:T(8,128)(2,1)S(1)}, bf16[4,64,512]{2,1,0:T(8,128)(2,1)S(1)}, u32[]{:S(2)}, u32[]{:S(2)}) collective-permute-start(bf16[4,64,512]{2,1,0:T(8,128)(2,1)S(1)} %bitcast.53), channel_id=1, source_target_pairs={{0,64},{32,96},{64,0},{96,32},{1,65},{33,97},{65,1},{97,33},{2,66}... | collective-permute-start | bytes 786440 | tf_op jit(solution)/shard_map/ppermute | solution.py:41
  103.8 15.2 %collective-permute-start.16 = (bf16[4,64,512]{2,1,0:T(8,128)(2,1)S(1)}, bf16[4,64,512]{2,1,0:T(8,128)(2,1)}, u32[]{:S(2)}, u32[]{:S(2)}) collective-permute-start(bf16[4,64,512]{2,1,0:T(8,128)(2,1)S(1)} %bitcast.54), channel_id=1, source_target_pairs={{0,32},{32,64},{64,96},{96,0},{1,33},{33,65},{65,97},{97,1},{2,34}... | collective-permute-start | bytes 786440 | tf_op jit(solution)/shard_map/ppermute | solution.py:41
  104.8 32.3 %collective-permute-start.17 = (bf16[2,512,512]{2,1,0:T(8,128)(2,1)S(1)}, bf16[2,512,512]{2,1,0:T(8,128)(2,1)}, u32[]{:S(2)}, u32[]{:S(2)}) collective-permute-start(bf16[2,512,512]{2,1,0:T(8,128)(2,1)S(1)} %pad_maximum_fusion.refs_4_.refs_5_), channel_id=1, source_target_pairs={{0,16},{16,0},{1,17},{17,1},{2,18},{18,2},{3,19},{19,3},{4,20},{20... | collective-permute-start | bytes 3145736 | tf_op jit(solution)/shard_map/ppermute | solution.py:41
  119.9 13.9 %collective-permute-start.18 = (bf16[512,512]{1,0:T(8,128)(2,1)}, bf16[512,512]{1,0:T(8,128)(2,1)}, u32[]{:S(2)}, u32[]{:S(2)}) collective-permute-start(bf16[512,512]{1,0:T(8,128)(2,1)} %slice_bitcast_fusion.1), channel_id=1, source_target_pairs={{0,96},{32,0},{64,32},{96,64},{1,97},{33,1},{65,33},{97,65},{2,98}... | collective-permute-start | bytes 1572872 | tf_op jit(solution)/shard_map/ppermute | solution.py:41
  122.3 14.7 %collective-permute-start.19 = (bf16[512,512]{1,0:T(8,128)(2,1)}, bf16[512,512]{1,0:T(8,128)(2,1)}, u32[]{:S(2)}, u32[]{:S(2)}) collective-permute-start(bf16[512,512]{1,0:T(8,128)(2,1)} %slice_bitcast_fusion), channel_id=1, source_target_pairs={{0,32},{32,64},{64,96},{96,0},{1,33},{33,65},{65,97},{97,1},{2,34}... | collective-permute-start | bytes 1572872 | tf_op jit(solution)/shard_map/ppermute | solution.py:41
  137.0 27.1 %collective-permute-start.22 = (bf16[4,512,1024]{2,1,0:T(8,128)(2,1)}, bf16[4,512,1024]{2,1,0:T(8,128)(2,1)}, u32[]{:S(2)}, u32[]{:S(2)}) collective-permute-start(bf16[4,512,1024]{2,1,0:T(8,128)(2,1)} %bitcast.45), channel_id=1, source_target_pairs={{0,8},{8,0},{1,9},{9,1},{2,10},{10,2},{3,11},{11,3},{4,12},{12,4},... | collective-permute-start | bytes 12582920 | tf_op jit(solution)/shard_map/ppermute | solution.py:41
  137.0 25.9 %collective-permute-start.20 = (bf16[2,512,512]{2,1,0:T(8,128)(2,1)}, bf16[2,512,512]{2,1,0:T(8,128)(2,1)}, u32[]{:S(2)}, u32[]{:S(2)}) collective-permute-start(bf16[2,512,512]{2,1,0:T(8,128)(2,1)} %collective-permute-done.17.refs_4_.refs_5_), channel_id=1, source_target_pairs={{0,96},{32,0},{64,32},{96,64},{1,97},{33,1},{65,33},{97,65},{2,98}... | collective-permute-start | bytes 3145736 | tf_op jit(solution)/shard_map/ppermute | solution.py:41
  137.0 27.1 %collective-permute-start.21 = (bf16[2,512,512]{2,1,0:T(8,128)(2,1)}, bf16[2,512,512]{2,1,0:T(8,128)(2,1)}, u32[]{:S(2)}, u32[]{:S(2)}) collective-permute-start(bf16[2,512,512]{2,1,0:T(8,128)(2,1)} %collective-permute-done.17.refs_4_.refs_5_), channel_id=1, source_target_pairs={{0,32},{32,64},{64,96},{96,0},{1,33},{33,65},{65,97},{97,1},{2,34}... | collective-permute-start | bytes 3145736 | tf_op jit(solution)/shard_map/ppermute | solution.py:41
  164.1 16.4 %collective-permute-start.27 = (bf16[4,512,1024]{2,1,0:T(8,128)(2,1)}, bf16[4,512,1024]{2,1,0:T(8,128)(2,1)}, u32[]{:S(2)}, u32[]{:S(2)}) collective-permute-start(bf16[4,512,1024]{2,1,0:T(8,128)(2,1)} %bitcast.48), channel_id=1, source_target_pairs={{0,8},{8,0},{1,9},{9,1},{2,10},{10,2},{3,11},{11,3},{4,12},{12,4},... | collective-permute-start | bytes 12582920 | tf_op jit(solution)/shard_map/ppermute | solution.py:41
  164.2 27.4 %collective-permute-start.28 = (bf16[2,512,512]{2,1,0:T(8,128)(2,1)}, bf16[2,512,512]{2,1,0:T(8,128)(2,1)}, u32[]{:S(2)}, u32[]{:S(2)}) collective-permute-start(bf16[2,512,512]{2,1,0:T(8,128)(2,1)} %collective-permute-done.17.refs_4_.refs_5_), channel_id=1, source_target_pairs={{0,64},{32,96},{64,0},{96,32},{1,65},{33,97},{65,1},{97,33},{2,66}... | collective-permute-start | bytes 3145736 | tf_op jit(solution)/shard_map/ppermute | solution.py:41
  166.4 7.0 %collective-permute-start.23 = (bf16[16,4096]{1,0:T(8,128)(2,1)S(1)}, bf16[16,4096]{1,0:T(8,128)(2,1)S(1)}, u32[]{:S(2)}, u32[]{:S(2)}) collective-permute-start(bf16[16,4096]{1,0:T(8,128)(2,1)S(1)} %reduce_sum.61), channel_id=1, source_target_pairs={{0,1},{1,0},{2,3},{3,2},{4,5},{5,4},{6,7},{7,6},{8,9},{9,8},{10,11... | collective-permute-start | bytes 393224 | tf_op jit(solution)/shard_map/ppermute | solution.py:41
  (16 other events, 248.6 us)
Sparse Core Ops, SparseCore 0:
  13.2 65.5 all-gather.6
  91.1 50.6 all-gather.8

commit v11 on v10

--- a/solution.py
+++ b/solution.py
@@ -258,15 +258,16 @@
     near, *moved = lock((near, *moved))
     moved = [lax.ppermute(m, ALL, column_moves(v)) for v, m in enumerate(moved)]
     rows = jnp.concatenate([near] + [from_ahead(near, "z", Z, s) for s in (1, 2, 3)], axis=0)
+    rows, *moved = lock((rows, *moved))
+    w = {(0, 0): jnp.stack(moved)}
+    w[1, 0] = from_ahead(w[0, 0], "z", Z, 1)
+    w[3, 0] = from_ahead(w[0, 0], "z", Z, 3)
     own = jnp.dot(rows[:, :depth], out_weight, preferred_element_type=jnp.float32)
     res = rows[:, depth:]
     res = jnp.where(core == 0, res[:, :width], res[:, width:]).astype(jnp.float32)
     own = jnp.where((y == z) & (xh == xl), own + res, own).astype(jnp.bfloat16)
     pair = jnp.stack([own, from_ahead(own, "xh", XH, 1)])
-    pair, held, *moved = lock((pair, attn_out, *moved))
-    w = {(0, 0): jnp.stack(moved)}
-    w[1, 0] = from_ahead(w[0, 0], "z", Z, 1)
-    w[3, 0] = from_ahead(w[0, 0], "z", Z, 3)
+    pair, held = lock((pair, attn_out))
     across = from_ahead(held, "xh", XH, 1)
     parts = [pair] + [from_ahead(pair, "y", Y, s) for s in (1, 2, 3)]
     pooled = sum(jnp.sum(p.astype(jnp.float32), axis=0) for p in parts).astype(jnp.bfloat16)
@@ -279,7 +280,7 @@
     *pieces, w[1, 0], w[3, 0] = lock((*pieces, w[1, 0], w[3, 0]))
     w[2, 0] = [from_ahead(w[1, 0][0], "z", Z, 1), from_ahead(w[3, 0][1], "z", Z, 3)]
     features = normalize(pieces, norm_gain, z)
-    features, w[0, 1], here, *w[2, 0] = lock((features, w[0, 1], here, *w[2, 0]))
+    features, w[0, 1], here = lock((features, w[0, 1], here))
     w[1, 1] = from_ahead(w[0, 1], "z", Z, 1)
     w[3, 1] = from_ahead(w[0, 1], "z", Z, 3)
     here_other = from_ahead(here, "core", CORE, 1)
@@ -291,8 +292,8 @@
     terms = lax.all_to_all(
         terms.reshape(Y, count, terms.shape[1]), "y", split_axis=0, concat_axis=0, tiled=True
     )
-    terms, there, w[0, 1], w[1, 1], w[3, 1], here_other = lock(
-        (terms, there, w[0, 1], w[1, 1], w[3, 1], here_other)
+    terms, there, w[0, 1], w[1, 1], w[3, 1], here_other, *w[2, 0] = lock(
+        (terms, there, w[0, 1], w[1, 1], w[3, 1], here_other, *w[2, 0])
     )
     there_other = from_ahead(there, "core", CORE, 1)
     w[2, 1] = from_ahead(w[0, 1], "z", Z, 2)
@@ -300,9 +301,6 @@
     other = from_ahead(half, "xh", XH, 1)
     second = jax.nn.silu(half.astype(jnp.float32) + other.astype(jnp.float32) + head_b2[0])
     mine = jnp.sum(second * head_w3[0].astype(jnp.float32), axis=-1) + head_b3[0]
-    scores = jnp.stack([mine] + [from_ahead(mine, "y", Y, s) for s in (1, 2, 3)])
-    scores = jnp.roll(scores, lax.rem(y + z, Y), axis=0).reshape(1, Y * count)
-
 
     def product(e, trunk, dtype):
         items = [
@@ -313,9 +311,11 @@
         place = jnp.stack([lax.rem(y - z + Y, Y), lax.rem(xl + e + xh, XH)])
         return trunk_part(place, sources, items, trunk, dtype)
 
-    scores, there_other = lock((scores, there_other))
     sources = (here, here_other, there, there_other)
     trunk = product(0, None, jnp.float32)
+    scores = [mine] + [from_ahead(mine, "y", Y, s) for s in (1, 2, 3)]
+    *scores, trunk = lock((*scores, trunk))
+    scores = jnp.roll(jnp.stack(scores), lax.rem(y + z, Y), axis=0).reshape(1, Y * count)
     trunk = product(1, trunk, jnp.bfloat16)
     row_count = residual.shape[0]
     mine = trunk[:row_count]

time: 215 us -> 222 us (1.033)
  blocking collectives: 25.5 us -> 11.4 us
  waiting for transfers between devices: 74.7 us -> 87.6 us
  starting transfers between devices: 50.5 us -> 60 us
    all_to_all x1 -> x0, blocking collectives: 14.1 us -> none  [local(): lax.all_to_all(terms.reshape(Y, count, terms.shape[1]), 'y', split_axis=0...]
    all_to_all x0 -> x1, waiting for transfers between devices: none -> 8.85 us  [local(): lax.all_to_all(terms.reshape(Y, count, terms.shape[1]), 'y', split_axis=0...]
    ppermute x26, waiting for transfers between devices: 52.9 us -> 60.8 us  [from_ahead(): return lax.ppermute(x, axis, [(i, (i - step) % size) for i in range(size)])]
    ppermute x26, starting transfers between devices: 38.8 us -> 44.1 us  [from_ahead(): return lax.ppermute(x, axis, [(i, (i - step) % size) for i in range(size)])]
    all_to_all x0 -> x1, starting transfers between devices: none -> 4.15 us  [local(): lax.all_to_all(terms.reshape(Y, count, terms.shape[1]), 'y', split_axis=0...]
    ppermute x2, waiting for transfers between devices: 15.6 us -> 11.8 us  [local(): moved = [lax.ppermute(m, ALL, column_moves(v)) for v, m in enumerate(moved)]]
  transfers between devices with their start and end apart: 32 -> 33, of which waited for: 20 -> 20; matrix products, arithmetic and copies ran while one was open for 6% -> 6% of each run, Pallas kernels for 6% -> 6%
where the time goes in v11:
time: 222 us; the launch traced here: 221 us
  waiting for transfers between devices  87.6 us (39%)
  starting transfers between devices  60 us (27%)
  Pallas kernels  30.7 us (14%)
  between operations  15 us (7%)
  blocking collectives  11.4 us (5%)
  matrix products  8.38 us (4%)
  local copies, waits for them, and re-layouts  4.42 us (2%)
  other arithmetic  3.14 us (1%)
    ppermute x26, waiting for transfers between devices, from_ahead(): return lax.ppermute(x, axis, [(i, (i - step) % size) for i in range(size)])  60.8 us
    ppermute x26, starting transfers between devices, from_ahead(): return lax.ppermute(x, axis, [(i, (i - step) % size) for i in range(size)])  44.1 us
    pallas_call x2, Pallas kernels, trunk_part(): pl.pallas_call(functools.partial(trunk_kernel, [(s, v) for s, v, _ in ter...  22 us
    ppermute x2, waiting for transfers between devices, local(): moved = [lax.ppermute(m, ALL, column_moves(v)) for v, m in enumerate(moved)]  11.8 us
    all_to_all x1, waiting for transfers between devices, local(): lax.all_to_all(terms.reshape(Y, count, terms.shape[1]), 'y', split_axis=0...  8.85 us
    dot_general x1, matrix products, local(): jnp.dot(first, head_w2[0], preferred_element_type=jnp.float32)  8.08 us
    ppermute x2, starting transfers between devices, local(): lax.ppermute(out_weight[v * rows_half:(v + 1) * rows_half], ALL, spread_m...  6.56 us
    ppermute x2, waiting for transfers between devices, local(): lax.ppermute(out_weight[v * rows_half:(v + 1) * rows_half], ALL, spread_m...  6.22 us
  transfers between devices with their start and end apart: 33, of which 20 were waited for; matrix products, arithmetic and copies ran while one was open for 6% of the time, Pallas kernels for 6%

profile of v11, /device:TPU:0, one launch (start us, length us, event | category | flops | bytes accessed | tf_op | source)
XLA Modules:
  0.0 220.6 jit_solution(2311881956068487148)
XLA Ops:
  7.2 5.8 %attention.1 = (bf16[512,1024]{1,0:T(8,128)(2,1)}, bf16[4,1,2048]{2,1,0:T(2,128)(2,1)}) custom-call(s32[4]{0:T(128)} %len_ref.1, bf16[512,1024]{1,0:T(8,128)(2,1)} %query_ref.1, bf16[512,128]{1,0:T(8,128)(2,1)} %keys_ref.1, bf16[512,128]{1,0:T(8,128)(2,1)} %values_ref.1, bf16[512,1024]{1,0:T(8,128)(2,1)} %residual_ref.1), custom_call_target="tpu_custom_call" | custom-call | flops 268435456 | bytes 3145728 | tf_op jit(solution)/shard_map/attention/pallas_call | solution.py:82
  15.1 5.9 %collective-permute-start.1 = (bf16[512,512]{1,0:T(8,128)(2,1)S(1)}, bf16[512,512]{1,0:T(8,128)(2,1)S(1)}, u32[]{:S(2)}, u32[]{:S(2)}) collective-permute-start(bf16[512,512]{1,0:T(8,128)(2,1)S(1)} %get-tuple-element.82), channel_id=1, source_target_pairs={{0,64},{1,65},{2,34},{3,35},{4,4},{5,5},{6,102},{7,103},{8,72},{9,... | collective-permute-start | bytes 1572872 | tf_op jit(solution)/shard_map/ppermute | solution.py:249
  21.0 5.6 %all-gather = bf16[16,1,2048]{2,1,0:T(2,128)(2,1)S(1)} all-gather(bf16[4,1,2048]{2,1,0:T(2,128)(2,1)} %get-tuple-element.41), channel_id=2, replica_groups=mesh['z'=4,'xl'=2,'core'=2,'y'=4,'xh'=2] {'xl','core'}, dimensions={0}, use_global_device_ids=true | all-gather | bytes 81920 | tf_op jit(solution)/shard_map/all_gather | solution.py:257
  26.7 6.2 %collective-permute-done.1 = bf16[512,512]{1,0:T(8,128)(2,1)S(1)} collective-permute-done((bf16[512,512]{1,0:T(8,128)(2,1)S(1)}, bf16[512,512]{1,0:T(8,128)(2,1)S(1)}, u32[]{:S(2)}, u32[]{:S(2)}) %collective-permute-start.1) | collective-permute-done | bytes 524320 | tf_op jit(solution)/shard_map/ppermute | solution.py:249
  33.6 4.4 %collective-permute-start.6 = (bf16[512,512]{1,0:T(8,128)(2,1)S(1)}, bf16[512,512]{1,0:T(8,128)(2,1)S(1)}, u32[]{:S(2)}, u32[]{:S(2)}) collective-permute-start(bf16[512,512]{1,0:T(8,128)(2,1)S(1)} %collective-permute-done.1), channel_id=1, source_target_pairs={{0,4},{1,20},{2,6},{3,22},{4,0},{5,16},{6,2},{7,18},{8,12},{9,28},... | collective-permute-start | bytes 1572872 | tf_op jit(solution)/shard_map/ppermute | solution.py:259
  38.0 6.1 %collective-permute-start.2 = (bf16[16,2048]{1,0:T(8,128)(2,1)S(1)}, bf16[16,2048]{1,0:T(8,128)(2,1)S(1)}, u32[]{:S(2)}, u32[]{:S(2)}) collective-permute-start(bf16[16,2048]{1,0:T(8,128)(2,1)S(1)} %bitcast.57), channel_id=1, source_target_pairs={{0,96},{32,0},{64,32},{96,64},{1,97},{33,1},{65,33},{97,65},{2,98}... | collective-permute-start | bytes 196616 | tf_op jit(solution)/shard_map/ppermute | solution.py:41
  50.6 11.8 %collective-permute-done.6 = bf16[512,512]{1,0:T(8,128)(2,1)S(1)} collective-permute-done((bf16[512,512]{1,0:T(8,128)(2,1)S(1)}, bf16[512,512]{1,0:T(8,128)(2,1)S(1)}, u32[]{:S(2)}, u32[]{:S(2)}) %collective-permute-start.6) | collective-permute-done | bytes 524320 | tf_op jit(solution)/shard_map/ppermute | solution.py:259
  64.6 4.0 %collective-permute-done.7 = bf16[64,512]{1,0:T(8,128)(2,1)S(1)} collective-permute-done((bf16[64,512]{1,0:T(8,128)(2,1)S(1)}, bf16[64,512]{1,0:T(8,128)(2,1)S(1)}, u32[]{:S(2)}, u32[]{:S(2)}) %collective-permute-start.7) | collective-permute-done | bytes 65568 | tf_op jit(solution)/shard_map/ppermute | solution.py:41
  70.5 3.7 %collective-permute-start.10 = (bf16[2,64,512]{2,1,0:T(8,128)(2,1)S(1)}, bf16[2,64,512]{2,1,0:T(8,128)(2,1)S(1)}, u32[]{:S(2)}, u32[]{:S(2)}) collective-permute-start(bf16[2,64,512]{2,1,0:T(8,128)(2,1)S(1)} %pad_maximum_fusion.2), channel_id=1, source_target_pairs={{0,2},{2,4},{4,6},{6,0},{1,3},{3,5},{5,7},{7,1},{8,10},{10,12},{12... | collective-permute-start | bytes 393224 | tf_op jit(solution)/shard_map/ppermute | solution.py:41
  85.5 7.3 %collective-permute-done.11 = bf16[512,1024]{1,0:T(8,128)(2,1)} collective-permute-done((bf16[512,1024]{1,0:T(8,128)(2,1)}, bf16[512,1024]{1,0:T(8,128)(2,1)}, u32[]{:S(2)}, u32[]{:S(2)}) %collective-permute-start.11) | collective-permute-done | bytes 1048608 | tf_op jit(solution)/shard_map/ppermute | solution.py:41
  92.9 5.8 %all-gather.1 = bf16[256,512]{1,0:T(8,128)(2,1)S(1)} all-gather(bf16[64,512]{1,0:T(8,128)(2,1)S(1)} %add_convert_fusion.1), channel_id=3, replica_groups=mesh['z'=4,'xl'=2,'core'=2,'y'=4,'xh'=2] {'xl','core'}, dimensions={0}, use_global_device_ids=true | all-gather | bytes 327680 | tf_op jit(solution)/shard_map/all_gather | solution.py:276
  103.2 4.1 %collective-permute-start.14 = (bf16[4,64,512]{2,1,0:T(8,128)(2,1)S(1)}, bf16[4,64,512]{2,1,0:T(8,128)(2,1)S(1)}, u32[]{:S(2)}, u32[]{:S(2)}) collective-permute-start(bf16[4,64,512]{2,1,0:T(8,128)(2,1)S(1)} %bitcast.50), channel_id=1, source_target_pairs={{0,96},{32,0},{64,32},{96,64},{1,97},{33,1},{65,33},{97,65},{2,98}... | collective-permute-start | bytes 786440 | tf_op jit(solution)/shard_map/ppermute | solution.py:41
  108.1 10.6 %collective-permute-done.14.p1 = bf16[4,64,512]{2,1,0:T(8,128)(2,1)S(1)} collective-permute-done((bf16[4,64,512]{2,1,0:T(8,128)(2,1)S(1)}, bf16[4,64,512]{2,1,0:T(8,128)(2,1)S(1)}, u32[]{:S(2)}, u32[]{:S(2)}) %collective-permute-start.14) | collective-permute-done | bytes 262176 | tf_op jit(solution)/shard_map/ppermute | solution.py:41
  118.7 3.4 %collective-permute-done.16.p3 = bf16[4,64,512]{2,1,0:T(8,128)(2,1)S(1)} collective-permute-done((bf16[4,64,512]{2,1,0:T(8,128)(2,1)S(1)}, bf16[4,64,512]{2,1,0:T(8,128)(2,1)S(1)}, u32[]{:S(2)}, u32[]{:S(2)}) %collective-permute-start.16) | collective-permute-done | bytes 262176 | tf_op jit(solution)/shard_map/ppermute | solution.py:41
  126.5 6.3 %collective-permute-start.21 = (bf16[512,512]{1,0:T(8,128)(2,1)}, bf16[512,512]{1,0:T(8,128)(2,1)}, u32[]{:S(2)}, u32[]{:S(2)}) collective-permute-start(bf16[512,512]{1,0:T(8,128)(2,1)} %slice_bitcast_fusion.1), channel_id=1, source_target_pairs={{0,96},{32,0},{64,32},{96,64},{1,97},{33,1},{65,33},{97,65},{2,98}... | collective-permute-start | bytes 1572872 | tf_op jit(solution)/shard_map/ppermute | solution.py:41
  136.9 8.1 %convolution_convert_fusion = bf16[64,4096]{1,0:T(8,128)(2,1)} fusion(bf16[1,512,4096]{2,1,0:T(8,128)(2,1)} %param.22, bf16[64,8192]{1,0:T(8,128)(2,1)} %normalize.1, bf16[1,8192,512]{2,1,0:T(8,128)(2,1)} %param.20, f32[512]{0:T(512)S(1)} %bitcast.73), kind=kOutput, calls=%fused_computation.2 | convolution fusion | flops 805765120 | bytes 14157824 | tf_op jit(solution)/shard_map/dot_general | solution.py:290
  145.0 4.2 %all-to-all-start = ((bf16[4,16,4096]{2,1,0:T(8,128)(2,1)}), bf16[4,16,4096]{2,1,0:T(8,128)(2,1)}, u32[]{:S(2)}, u32[]{:S(2)}) async-start(bf16[4,16,4096]{2,1,0:T(8,128)(2,1)} %bitcast.49), calls=%async_computation | async-start | bytes 1048576 | tf_op jit(solution)/shard_map/all_to_all | solution.py:292
  150.0 8.9 %all-to-all-done = bf16[4,16,4096]{2,1,0:T(8,128)(2,1)} async-done(((bf16[4,16,4096]{2,1,0:T(8,128)(2,1)}), bf16[4,16,4096]{2,1,0:T(8,128)(2,1)}, u32[]{:S(2)}, u32[]{:S(2)}) %all-to-all-start) | async-done | bytes 524320 | tf_op jit(solution)/shard_map/all_to_all | solution.py:292
  158.8 8.7 %collective-permute-done.18.refs_6_.refs_7_ = bf16[2,512,512]{2,1,0:T(8,128)(2,1)} collective-permute-done((bf16[2,512,512]{2,1,0:T(8,128)(2,1)}, bf16[2,512,512]{2,1,0:T(8,128)(2,1)}, u32[]{:S(2)}, u32[]{:S(2)}) %collective-permute-start.18) | collective-permute-done | bytes 1048608 | tf_op jit(solution)/shard_map/ppermute | solution.py:41
  167.5 4.2 %collective-permute-done.19.refs_10_.refs_11_ = bf16[2,512,512]{2,1,0:T(8,128)(2,1)} collective-permute-done((bf16[2,512,512]{2,1,0:T(8,128)(2,1)}, bf16[2,512,512]{2,1,0:T(8,128)(2,1)}, u32[]{:S(2)}, u32[]{:S(2)}) %collective-permute-start.19) | collective-permute-done | bytes 1048608 | tf_op jit(solution)/shard_map/ppermute | solution.py:41
  176.7 3.6 %collective-permute-done.25 = bf16[16,4096]{1,0:T(8,128)(2,1)S(1)} collective-permute-done((bf16[16,4096]{1,0:T(8,128)(2,1)S(1)}, bf16[16,4096]{1,0:T(8,128)(2,1)S(1)}, u32[]{:S(2)}, u32[]{:S(2)}) %collective-permute-start.25) | collective-permute-done | bytes 131104 | tf_op jit(solution)/shard_map/ppermute | solution.py:41
  182.7 10.8 %trunk_part.2.refs_12_ = f32[1024,512]{1,0:T(8,128)S(1)} custom-call(s32[2]{0:T(128)S(1)} %pad_add_fusion.1.place_ref, bf16[4,512,1024]{2,1,0:T(8,128)(2,1)} %bitcast.44, bf16[4,512,1024]{2,1,0:T(8,128)(2,1)} %collective-permute-done.20.refs_1_, bf16[4,512,1024]{2,1,0:T(8,128)(2,1)} %bitcast.47, bf16[4,512,1024]{2,1,0:T(8,128)(2,1)} %collective-permute-done.23.refs_3_, ...), custom_call_target="tpu_custom_call" | custom-call | flops 524288 | bytes 524288 | tf_op jit(solution)/shard_map/trunk_part/pallas_call | solution.py:156
  193.5 5.6 %collective-permute-done.24.refs_8_.refs_9_ = bf16[2,512,512]{2,1,0:T(8,128)(2,1)} collective-permute-done((bf16[2,512,512]{2,1,0:T(8,128)(2,1)}, bf16[2,512,512]{2,1,0:T(8,128)(2,1)}, u32[]{:S(2)}, u32[]{:S(2)}) %collective-permute-start.24) | collective-permute-done | bytes 1048608 | tf_op jit(solution)/shard_map/ppermute | solution.py:41
  199.1 11.2 %trunk_part.3 = bf16[1024,512]{1,0:T(8,128)(2,1)S(1)} custom-call(s32[2]{0:T(128)S(1)} %pad_add_fusion.place_ref, bf16[4,512,1024]{2,1,0:T(8,128)(2,1)} %bitcast.45, bf16[4,512,1024]{2,1,0:T(8,128)(2,1)} %collective-permute-done.20.refs_1_, bf16[4,512,1024]{2,1,0:T(8,128)(2,1)} %bitcast.48, bf16[4,512,1024]{2,1,0:T(8,128)(2,1)} %collective-permute-done.23.refs_3_, ...), custom_call_target="tpu_custom_call" | custom-call | flops 524288 | bytes 524288 | tf_op jit(solution)/shard_map/trunk_part/pallas_call | solution.py:156
  (94 shorter events, 49.5 us)
Async XLA Ops:
  7.2 93.1 %all-gather.7.cloned.1.call-start = ((), (), s32[]{:S(2)}) async-start(), calls=%async_computation.1 | async-start | bytes 5242880 | tf_op jit(solution)/shard_map/all_gather | solution.py:253
  13.1 158.7 %all-gather.9.cloned.1.call-start = ((), (), s32[]{:S(2)}) async-start(), calls=%async_computation.2 | async-start | bytes 5242880 | tf_op jit(solution)/shard_map/all_gather | solution.py:275
  14.4 12.3 %collective-permute-start = (bf16[512,512]{1,0:T(8,128)(2,1)S(1)}, bf16[512,512]{1,0:T(8,128)(2,1)S(1)}, u32[]{:S(2)}, u32[]{:S(2)}) collective-permute-start(bf16[512,512]{1,0:T(8,128)(2,1)S(1)} %get-tuple-element.83), channel_id=1, source_target_pairs={{0,0},{1,1},{2,98},{3,99},{4,68},{5,69},{6,38},{7,39},{8,8},{9,9},... | collective-permute-start | bytes 1572872 | tf_op jit(solution)/shard_map/ppermute | solution.py:249
  15.1 17.8 %collective-permute-start.1 = (bf16[512,512]{1,0:T(8,128)(2,1)S(1)}, bf16[512,512]{1,0:T(8,128)(2,1)S(1)}, u32[]{:S(2)}, u32[]{:S(2)}) collective-permute-start(bf16[512,512]{1,0:T(8,128)(2,1)S(1)} %get-tuple-element.82), channel_id=1, source_target_pairs={{0,64},{1,65},{2,34},{3,35},{4,4},{5,5},{6,102},{7,103},{8,72},{9,... | collective-permute-start | bytes 1572872 | tf_op jit(solution)/shard_map/ppermute | solution.py:249
  32.9 17.7 %collective-permute-start.5 = (bf16[512,512]{1,0:T(8,128)(2,1)S(1)}, bf16[512,512]{1,0:T(8,128)(2,1)S(1)}, u32[]{:S(2)}, u32[]{:S(2)}) collective-permute-start(bf16[512,512]{1,0:T(8,128)(2,1)S(1)} %collective-permute-done), channel_id=1, source_target_pairs={{0,0},{1,16},{2,2},{3,18},{4,4},{5,20},{6,6},{7,22},{8,8},{9,24},{... | collective-permute-start | bytes 1572872 | tf_op jit(solution)/shard_map/ppermute | solution.py:259
  33.6 28.8 %collective-permute-start.6 = (bf16[512,512]{1,0:T(8,128)(2,1)S(1)}, bf16[512,512]{1,0:T(8,128)(2,1)S(1)}, u32[]{:S(2)}, u32[]{:S(2)}) collective-permute-start(bf16[512,512]{1,0:T(8,128)(2,1)S(1)} %collective-permute-done.1), channel_id=1, source_target_pairs={{0,4},{1,20},{2,6},{3,22},{4,0},{5,16},{6,2},{7,18},{8,12},{9,28},... | collective-permute-start | bytes 1572872 | tf_op jit(solution)/shard_map/ppermute | solution.py:259
  68.6 24.2 %collective-permute-start.11 = (bf16[512,1024]{1,0:T(8,128)(2,1)}, bf16[512,1024]{1,0:T(8,128)(2,1)}, u32[]{:S(2)}, u32[]{:S(2)}) collective-permute-start(bf16[512,1024]{1,0:T(8,128)(2,1)} %get-tuple-element.48), channel_id=1, source_target_pairs={{0,1},{1,0},{2,3},{3,2},{4,5},{5,4},{6,7},{7,6},{8,9},{9,8},{10,11... | collective-permute-start | bytes 3145736 | tf_op jit(solution)/shard_map/ppermute | solution.py:41
  74.2 24.4 %collective-permute-start.12 = (bf16[2,512,512]{2,1,0:T(8,128)(2,1)S(1)}, bf16[2,512,512]{2,1,0:T(8,128)(2,1)S(1)}, u32[]{:S(2)}, u32[]{:S(2)}) collective-permute-start(bf16[2,512,512]{2,1,0:T(8,128)(2,1)S(1)} %pad_maximum_fusion.refs_4_.refs_5_), channel_id=1, source_target_pairs={{0,96},{32,0},{64,32},{96,64},{1,97},{33,1},{65,33},{97,65},{2,98}... | collective-permute-start | bytes 3145736 | tf_op jit(solution)/shard_map/ppermute | solution.py:41
  77.0 23.2 %collective-permute-start.13 = (bf16[2,512,512]{2,1,0:T(8,128)(2,1)S(1)}, bf16[2,512,512]{2,1,0:T(8,128)(2,1)S(1)}, u32[]{:S(2)}, u32[]{:S(2)}) collective-permute-start(bf16[2,512,512]{2,1,0:T(8,128)(2,1)S(1)} %pad_maximum_fusion.refs_4_.refs_5_), channel_id=1, source_target_pairs={{0,32},{32,64},{64,96},{96,0},{1,33},{33,65},{65,97},{97,1},{2,34}... | collective-permute-start | bytes 3145736 | tf_op jit(solution)/shard_map/ppermute | solution.py:41
  100.2 25.4 %collective-permute-start.17 = (bf16[2,512,512]{2,1,0:T(8,128)(2,1)S(1)}, bf16[2,512,512]{2,1,0:T(8,128)(2,1)}, u32[]{:S(2)}, u32[]{:S(2)}) collective-permute-start(bf16[2,512,512]{2,1,0:T(8,128)(2,1)S(1)} %pad_maximum_fusion.refs_4_.refs_5_), channel_id=1, source_target_pairs={{0,16},{16,0},{1,17},{17,1},{2,18},{18,2},{3,19},{19,3},{4,20},{20... | collective-permute-start | bytes 3145736 | tf_op jit(solution)/shard_map/ppermute | solution.py:41
  103.2 15.5 %collective-permute-start.14 = (bf16[4,64,512]{2,1,0:T(8,128)(2,1)S(1)}, bf16[4,64,512]{2,1,0:T(8,128)(2,1)S(1)}, u32[]{:S(2)}, u32[]{:S(2)}) collective-permute-start(bf16[4,64,512]{2,1,0:T(8,128)(2,1)S(1)} %bitcast.50), channel_id=1, source_target_pairs={{0,96},{32,0},{64,32},{96,64},{1,97},{33,1},{65,33},{97,65},{2,98}... | collective-permute-start | bytes 786440 | tf_op jit(solution)/shard_map/ppermute | solution.py:41
  107.2 11.4 %collective-permute-start.15 = (bf16[4,64,512]{2,1,0:T(8,128)(2,1)S(1)}, bf16[4,64,512]{2,1,0:T(8,128)(2,1)S(1)}, u32[]{:S(2)}, u32[]{:S(2)}) collective-permute-start(bf16[4,64,512]{2,1,0:T(8,128)(2,1)S(1)} %bitcast.51), channel_id=1, source_target_pairs={{0,64},{32,96},{64,0},{96,32},{1,65},{33,97},{65,1},{97,33},{2,66}... | collective-permute-start | bytes 786440 | tf_op jit(solution)/shard_map/ppermute | solution.py:41
  107.2 14.8 %collective-permute-start.16 = (bf16[4,64,512]{2,1,0:T(8,128)(2,1)S(1)}, bf16[4,64,512]{2,1,0:T(8,128)(2,1)S(1)}, u32[]{:S(2)}, u32[]{:S(2)}) collective-permute-start(bf16[4,64,512]{2,1,0:T(8,128)(2,1)S(1)} %bitcast.52), channel_id=1, source_target_pairs={{0,32},{32,64},{64,96},{96,0},{1,33},{33,65},{65,97},{97,1},{2,34}... | collective-permute-start | bytes 786440 | tf_op jit(solution)/shard_map/ppermute | solution.py:41
  125.6 46.1 %collective-permute-start.20 = (bf16[4,512,1024]{2,1,0:T(8,128)(2,1)}, bf16[4,512,1024]{2,1,0:T(8,128)(2,1)}, u32[]{:S(2)}, u32[]{:S(2)}) collective-permute-start(bf16[4,512,1024]{2,1,0:T(8,128)(2,1)} %bitcast.43), channel_id=1, source_target_pairs={{0,8},{8,0},{1,9},{9,1},{2,10},{10,2},{3,11},{11,3},{4,12},{12,4},... | collective-permute-start | bytes 12582920 | tf_op jit(solution)/shard_map/ppermute | solution.py:41
  126.5 22.7 %collective-permute-start.21 = (bf16[512,512]{1,0:T(8,128)(2,1)}, bf16[512,512]{1,0:T(8,128)(2,1)}, u32[]{:S(2)}, u32[]{:S(2)}) collective-permute-start(bf16[512,512]{1,0:T(8,128)(2,1)} %slice_bitcast_fusion.1), channel_id=1, source_target_pairs={{0,96},{32,0},{64,32},{96,64},{1,97},{33,1},{65,33},{97,65},{2,98}... | collective-permute-start | bytes 1572872 | tf_op jit(solution)/shard_map/ppermute | solution.py:41
  133.7 16.3 %collective-permute-start.22 = (bf16[512,512]{1,0:T(8,128)(2,1)}, bf16[512,512]{1,0:T(8,128)(2,1)}, u32[]{:S(2)}, u32[]{:S(2)}) collective-permute-start(bf16[512,512]{1,0:T(8,128)(2,1)} %slice_bitcast_fusion), channel_id=1, source_target_pairs={{0,32},{32,64},{64,96},{96,0},{1,33},{33,65},{65,97},{97,1},{2,34}... | collective-permute-start | bytes 1572872 | tf_op jit(solution)/shard_map/ppermute | solution.py:41
  133.7 33.8 %collective-permute-start.18 = (bf16[2,512,512]{2,1,0:T(8,128)(2,1)}, bf16[2,512,512]{2,1,0:T(8,128)(2,1)}, u32[]{:S(2)}, u32[]{:S(2)}) collective-permute-start(bf16[2,512,512]{2,1,0:T(8,128)(2,1)} %collective-permute-done.17.refs_4_.refs_5_), channel_id=1, source_target_pairs={{0,96},{32,0},{64,32},{96,64},{1,97},{33,1},{65,33},{97,65},{2,98}... | collective-permute-start | bytes 3145736 | tf_op jit(solution)/shard_map/ppermute | solution.py:41
  136.9 34.8 %collective-permute-start.19 = (bf16[2,512,512]{2,1,0:T(8,128)(2,1)}, bf16[2,512,512]{2,1,0:T(8,128)(2,1)}, u32[]{:S(2)}, u32[]{:S(2)}) collective-permute-start(bf16[2,512,512]{2,1,0:T(8,128)(2,1)} %collective-permute-done.17.refs_4_.refs_5_), channel_id=1, source_target_pairs={{0,32},{32,64},{64,96},{96,0},{1,33},{33,65},{65,97},{97,1},{2,34}... | collective-permute-start | bytes 3145736 | tf_op jit(solution)/shard_map/ppermute | solution.py:41
  145.0 13.8 %all-to-all-start = ((bf16[4,16,4096]{2,1,0:T(8,128)(2,1)}), bf16[4,16,4096]{2,1,0:T(8,128)(2,1)}, u32[]{:S(2)}, u32[]{:S(2)}) async-start(bf16[4,16,4096]{2,1,0:T(8,128)(2,1)} %bitcast.49), calls=%async_computation | async-start | bytes 1048576 | tf_op jit(solution)/shard_map/all_to_all | solution.py:292
  171.7 11.0 %collective-permute-start.23 = (bf16[4,512,1024]{2,1,0:T(8,128)(2,1)}, bf16[4,512,1024]{2,1,0:T(8,128)(2,1)}, u32[]{:S(2)}, u32[]{:S(2)}) collective-permute-start(bf16[4,512,1024]{2,1,0:T(8,128)(2,1)} %bitcast.46), channel_id=1, source_target_pairs={{0,8},{8,0},{1,9},{9,1},{2,10},{10,2},{3,11},{11,3},{4,12},{12,4},... | collective-permute-start | bytes 12582920 | tf_op jit(solution)/shard_map/ppermute | solution.py:41
  171.7 27.4 %collective-permute-start.24 = (bf16[2,512,512]{2,1,0:T(8,128)(2,1)}, bf16[2,512,512]{2,1,0:T(8,128)(2,1)}, u32[]{:S(2)}, u32[]{:S(2)}) collective-permute-start(bf16[2,512,512]{2,1,0:T(8,128)(2,1)} %collective-permute-done.17.refs_4_.refs_5_), channel_id=1, source_target_pairs={{0,64},{32,96},{64,0},{96,32},{1,65},{33,97},{65,1},{97,33},{2,66}... | collective-permute-start | bytes 3145736 | tf_op jit(solution)/shard_map/ppermute | solution.py:41
  180.6 12.9 %collective-permute-start.26 = (f32[16]{0:T(128)S(1)}, f32[16]{0:T(128)S(1)}, u32[]{:S(2)}, u32[]{:S(2)}) collective-permute-start(f32[16]{0:T(128)S(1)} %broadcast_add_fusion), channel_id=1, source_target_pairs={{0,6},{2,0},{4,2},{6,4},{1,7},{3,1},{5,3},{7,5},{8,14},{10,8},{12,... | collective-permute-start | bytes 200 | tf_op jit(solution)/shard_map/ppermute | solution.py:41
  180.7 12.9 %collective-permute-start.27 = (f32[16]{0:T(128)S(1)}, f32[16]{0:T(128)S(1)}, u32[]{:S(2)}, u32[]{:S(2)}) collective-permute-start(f32[16]{0:T(128)S(1)} %broadcast_add_fusion), channel_id=1, source_target_pairs={{0,4},{2,6},{4,0},{6,2},{1,5},{3,7},{5,1},{7,3},{8,12},{10,14},{12... | collective-permute-start | bytes 200 | tf_op jit(solution)/shard_map/ppermute | solution.py:41
  181.9 11.7 %collective-permute-start.28 = (f32[16]{0:T(128)S(1)}, f32[16]{0:T(128)S(1)}, u32[]{:S(2)}, u32[]{:S(2)}) collective-permute-start(f32[16]{0:T(128)S(1)} %broadcast_add_fusion), channel_id=1, source_target_pairs={{0,2},{2,4},{4,6},{6,0},{1,3},{3,5},{5,7},{7,1},{8,10},{10,12},{12... | collective-permute-start | bytes 200 | tf_op jit(solution)/shard_map/ppermute | solution.py:41
  (18 other events, 308.3 us)
Sparse Core Ops, SparseCore 0:
  13.2 62.9 all-gather.6
  93.0 51.4 all-gather.8

commit v12 on v10

--- a/solution.py
+++ b/solution.py
@@ -108,16 +108,16 @@
     out_ref, acts, sems = refs[-3:]
     j = pl.program_id(0)
 
-    def copies(which):
-        for r in range(CORE):
-            for i, (s, v) in enumerate(picks):
-                depth = acts.shape[3]
-                group = lax.rem(place_ref[0] + 2 * Y - s - 2 * v, Y)
-                yield pltpu.make_async_copy(
-                    sources[2 * which + r].at[group, :, pl.ds(v * depth, depth)],
-                    acts.at[r, i],
-                    sems.at[r, i],
-                )
+    depth = acts.shape[2] // count
+
+    def copies(which, r):
+        for i, (s, v) in enumerate(picks):
+            group = lax.rem(place_ref[0] + 2 * Y - s - 2 * v, Y)
+            yield pltpu.make_async_copy(
+                sources[2 * which + r].at[group, :, pl.ds(v * depth, depth)],
+                acts.at[r, :, pl.ds(i * depth, depth)],
+                sems.at[r, i],
+            )
 
     @pl.when(j == 0)
     def _():
@@ -125,19 +125,24 @@
 
             @pl.when(place_ref[1] == which)
             def _():
-                for copy in copies(which):
-                    copy.start()
-
-        for copy in copies(0):
-            copy.wait()
-
+                for r in range(CORE):
+                    for copy in copies(which, r):
+                        copy.start()
+
+    for r in range(CORE):
+
+        @pl.when(j == 2 * r)
+        def _():
+            for copy in copies(0, r):
+                copy.wait()
+
+    total = jnp.dot(
+        acts[j // 2],
+        jnp.concatenate([block[...] for block in blocks], axis=0),
+        preferred_element_type=jnp.float32,
+    )
     if has_base:
-        total = base_ref[...]
-    else:
-        total = jnp.zeros(out_ref.shape, jnp.float32)
-    r = j // 2
-    for i, block in enumerate(blocks):
-        total = total + jnp.dot(acts[r, i], block[...], preferred_element_type=jnp.float32)
+        total = total + base_ref[...]
     out_ref[...] = total.astype(out_ref.dtype)
 
 
@@ -163,7 +168,7 @@
             + ([] if base is None else [tile]),
             out_specs=tile,
             scratch_shapes=[
-                pltpu.VMEM((CORE, count, rows, depth), sources[0].dtype),
+                pltpu.VMEM((CORE, rows, count * depth), sources[0].dtype),
                 pltpu.SemaphoreType.DMA((CORE, count)),
             ],
         ),
@@ -300,23 +305,23 @@
     other = from_ahead(half, "xh", XH, 1)
     second = jax.nn.silu(half.astype(jnp.float32) + other.astype(jnp.float32) + head_b2[0])
     mine = jnp.sum(second * head_w3[0].astype(jnp.float32), axis=-1) + head_b3[0]
-    scores = jnp.stack([mine] + [from_ahead(mine, "y", Y, s) for s in (1, 2, 3)])
-    scores = jnp.roll(scores, lax.rem(y + z, Y), axis=0).reshape(1, Y * count)
-
-
-    def product(e, trunk, dtype):
+
+    def product(e, steps, trunk, dtype):
         items = [
             (s, v, w[s, e][v] if isinstance(w[s, e], list) else w[s, e])
-            for s in range(Z)
+            for s in steps
             for v in range(2)
         ]
         place = jnp.stack([lax.rem(y - z + Y, Y), lax.rem(xl + e + xh, XH)])
         return trunk_part(place, sources, items, trunk, dtype)
 
-    scores, there_other = lock((scores, there_other))
     sources = (here, here_other, there, there_other)
-    trunk = product(0, None, jnp.float32)
-    trunk = product(1, trunk, jnp.bfloat16)
+    trunk = product(0, range(Z), None, jnp.float32)
+    scores = [mine] + [from_ahead(mine, "y", Y, s) for s in (1, 2, 3)]
+    *scores, trunk = lock((*scores, trunk))
+    scores = jnp.roll(jnp.stack(scores), lax.rem(y + z, Y), axis=0).reshape(1, Y * count)
+    trunk = product(1, (0, 1, 3), trunk, jnp.float32)
+    trunk = product(1, (2,), trunk, jnp.bfloat16)
     row_count = residual.shape[0]
     mine = trunk[:row_count]
     other = from_ahead(trunk[row_count:], "core", CORE, 1)

time: 215 us -> 211 us (0.981)
  waiting for transfers between devices: 74.7 us -> 69.7 us
    ppermute x26, waiting for transfers between devices: 52.9 us -> 47.9 us  [from_ahead(): return lax.ppermute(x, axis, [(i, (i - step) % size) for i in range(size)])]
    pallas_call x2 -> x3, Pallas kernels: 22 us -> 23.7 us  [trunk_part(): pl.pallas_call(functools.partial(trunk_kernel, [(s, v) for s, v, _ in ter...]
  transfers between devices with their start and end apart: 32 -> 32, of which waited for: 20 -> 16; matrix products, arithmetic and copies ran while one was open for 6% -> 7% of each run, Pallas kernels for 6% -> 10%
where the time goes in v12:
time: 211 us; the launch traced here: 210 us
  waiting for transfers between devices  69.7 us (33%)
  starting transfers between devices  50.5 us (24%)
  Pallas kernels  32.3 us (15%)
  blocking collectives  25.5 us (12%)
  between operations  15.1 us (7%)
  matrix products  8.38 us (4%)
  local copies, waits for them, and re-layouts  5.1 us (2%)
  other arithmetic  3.11 us (1%)
    ppermute x26, waiting for transfers between devices, from_ahead(): return lax.ppermute(x, axis, [(i, (i - step) % size) for i in range(size)])  47.9 us
    ppermute x26, starting transfers between devices, from_ahead(): return lax.ppermute(x, axis, [(i, (i - step) % size) for i in range(size)])  38.8 us
    pallas_call x3, Pallas kernels, trunk_part(): pl.pallas_call(functools.partial(trunk_kernel, [(s, v) for s, v, _ in ter...  23.7 us
    ppermute x2, waiting for transfers between devices, local(): moved = [lax.ppermute(m, ALL, column_moves(v)) for v, m in enumerate(moved)]  15.6 us
    all_to_all x1, blocking collectives, local(): lax.all_to_all(terms.reshape(Y, count, terms.shape[1]), 'y', split_axis=0...  14.1 us
    dot_general x1, matrix products, local(): jnp.dot(first, head_w2[0], preferred_element_type=jnp.float32)  8.08 us
    ppermute x2, starting transfers between devices, local(): lax.ppermute(out_weight[v * rows_half:(v + 1) * rows_half], ALL, spread_m...  6.56 us
    ppermute x2, waiting for transfers between devices, local(): lax.ppermute(out_weight[v * rows_half:(v + 1) * rows_half], ALL, spread_m...  6.19 us
  transfers between devices with their start and end apart: 32, of which 16 were waited for; matrix products, arithmetic and copies ran while one was open for 7% of the time, Pallas kernels for 10%

profile of v12, /device:TPU:0, one launch (start us, length us, event | category | flops | bytes accessed | tf_op | source)
XLA Modules:
  0.0 209.7 jit_solution(9946553973423938109)
XLA Ops:
  7.2 5.8 %attention.1 = (bf16[512,1024]{1,0:T(8,128)(2,1)}, bf16[4,1,2048]{2,1,0:T(2,128)(2,1)}) custom-call(s32[4]{0:T(128)} %len_ref.1, bf16[512,1024]{1,0:T(8,128)(2,1)} %query_ref.1, bf16[512,128]{1,0:T(8,128)(2,1)} %keys_ref.1, bf16[512,128]{1,0:T(8,128)(2,1)} %values_ref.1, bf16[512,1024]{1,0:T(8,128)(2,1)} %residual_ref.1), custom_call_target="tpu_custom_call" | custom-call | flops 268435456 | bytes 3145728 | tf_op jit(solution)/shard_map/attention/pallas_call | solution.py:82
  15.1 5.9 %collective-permute-start.1 = (bf16[512,512]{1,0:T(8,128)(2,1)S(1)}, bf16[512,512]{1,0:T(8,128)(2,1)S(1)}, u32[]{:S(2)}, u32[]{:S(2)}) collective-permute-start(bf16[512,512]{1,0:T(8,128)(2,1)S(1)} %get-tuple-element.80), channel_id=1, source_target_pairs={{0,64},{1,65},{2,34},{3,35},{4,4},{5,5},{6,102},{7,103},{8,72},{9,... | collective-permute-start | bytes 1572872 | tf_op jit(solution)/shard_map/ppermute | solution.py:254
  21.0 5.6 %all-gather = bf16[16,1,2048]{2,1,0:T(2,128)(2,1)S(1)} all-gather(bf16[4,1,2048]{2,1,0:T(2,128)(2,1)} %get-tuple-element.40), channel_id=2, replica_groups=mesh['z'=4,'xl'=2,'core'=2,'y'=4,'xh'=2] {'xl','core'}, dimensions={0}, use_global_device_ids=true | all-gather | bytes 81920 | tf_op jit(solution)/shard_map/all_gather | solution.py:262
  26.7 6.2 %collective-permute-done.1 = bf16[512,512]{1,0:T(8,128)(2,1)S(1)} collective-permute-done((bf16[512,512]{1,0:T(8,128)(2,1)S(1)}, bf16[512,512]{1,0:T(8,128)(2,1)S(1)}, u32[]{:S(2)}, u32[]{:S(2)}) %collective-permute-start.1) | collective-permute-done | bytes 524320 | tf_op jit(solution)/shard_map/ppermute | solution.py:254
  32.9 3.4 %collective-permute-start.2 = (bf16[16,2048]{1,0:T(8,128)(2,1)S(1)}, bf16[16,2048]{1,0:T(8,128)(2,1)S(1)}, u32[]{:S(2)}, u32[]{:S(2)}) collective-permute-start(bf16[16,2048]{1,0:T(8,128)(2,1)S(1)} %bitcast.58), channel_id=1, source_target_pairs={{0,96},{32,0},{64,32},{96,64},{1,97},{33,1},{65,33},{97,65},{2,98}... | collective-permute-start | bytes 196616 | tf_op jit(solution)/shard_map/ppermute | solution.py:41
  38.2 4.4 %collective-permute-start.7 = (bf16[512,512]{1,0:T(8,128)(2,1)S(1)}, bf16[512,512]{1,0:T(8,128)(2,1)S(1)}, u32[]{:S(2)}, u32[]{:S(2)}) collective-permute-start(bf16[512,512]{1,0:T(8,128)(2,1)S(1)} %collective-permute-done.1), channel_id=1, source_target_pairs={{0,4},{1,20},{2,6},{3,22},{4,0},{5,16},{6,2},{7,18},{8,12},{9,28},... | collective-permute-start | bytes 1572872 | tf_op jit(solution)/shard_map/ppermute | solution.py:264
  43.0 5.8 %collective-permute-start.5 = (bf16[64,512]{1,0:T(8,128)(2,1)S(1)}, bf16[64,512]{1,0:T(8,128)(2,1)S(1)}, u32[]{:S(2)}, u32[]{:S(2)}) collective-permute-start(bf16[64,512]{1,0:T(8,128)(2,1)S(1)} %fusion.6), channel_id=1, source_target_pairs={{0,1},{1,0},{2,3},{3,2},{4,5},{5,4},{6,7},{7,6},{8,9},{9,8},{10,11... | collective-permute-start | bytes 196616 | tf_op jit(solution)/shard_map/ppermute | solution.py:41
  51.1 15.6 %collective-permute-done.7 = bf16[512,512]{1,0:T(8,128)(2,1)S(1)} collective-permute-done((bf16[512,512]{1,0:T(8,128)(2,1)S(1)}, bf16[512,512]{1,0:T(8,128)(2,1)S(1)}, u32[]{:S(2)}, u32[]{:S(2)}) %collective-permute-start.7) | collective-permute-done | bytes 524320 | tf_op jit(solution)/shard_map/ppermute | solution.py:264
  71.6 3.0 %collective-permute-start.12 = (bf16[2,512,512]{2,1,0:T(8,128)(2,1)S(1)}, bf16[2,512,512]{2,1,0:T(8,128)(2,1)S(1)}, u32[]{:S(2)}, u32[]{:S(2)}) collective-permute-start(bf16[2,512,512]{2,1,0:T(8,128)(2,1)S(1)} %pad_maximum_fusion.refs_4_.refs_5_), channel_id=1, source_target_pairs={{0,96},{32,0},{64,32},{96,64},{1,97},{33,1},{65,33},{97,65},{2,98}... | collective-permute-start | bytes 3145736 | tf_op jit(solution)/shard_map/ppermute | solution.py:41
  76.1 2.7 %collective-permute-done.10 = bf16[2,64,512]{2,1,0:T(8,128)(2,1)S(1)} collective-permute-done((bf16[2,64,512]{2,1,0:T(8,128)(2,1)S(1)}, bf16[2,64,512]{2,1,0:T(8,128)(2,1)S(1)}, u32[]{:S(2)}, u32[]{:S(2)}) %collective-permute-start.10) | collective-permute-done | bytes 131104 | tf_op jit(solution)/shard_map/ppermute | solution.py:41
  83.8 7.2 %collective-permute-done.11 = bf16[512,1024]{1,0:T(8,128)(2,1)} collective-permute-done((bf16[512,1024]{1,0:T(8,128)(2,1)}, bf16[512,1024]{1,0:T(8,128)(2,1)}, u32[]{:S(2)}, u32[]{:S(2)}) %collective-permute-start.11) | collective-permute-done | bytes 1048608 | tf_op jit(solution)/shard_map/ppermute | solution.py:41
  91.0 5.8 %all-gather.1 = bf16[256,512]{1,0:T(8,128)(2,1)S(1)} all-gather(bf16[64,512]{1,0:T(8,128)(2,1)S(1)} %add_convert_fusion.1), channel_id=3, replica_groups=mesh['z'=4,'xl'=2,'core'=2,'y'=4,'xh'=2] {'xl','core'}, dimensions={0}, use_global_device_ids=true | all-gather | bytes 327680 | tf_op jit(solution)/shard_map/all_gather | solution.py:280
  97.4 6.5 %collective-permute-start.14 = (bf16[4,64,512]{2,1,0:T(8,128)(2,1)S(1)}, bf16[4,64,512]{2,1,0:T(8,128)(2,1)S(1)}, u32[]{:S(2)}, u32[]{:S(2)}) collective-permute-start(bf16[4,64,512]{2,1,0:T(8,128)(2,1)S(1)} %bitcast.52), channel_id=1, source_target_pairs={{0,96},{32,0},{64,32},{96,64},{1,97},{33,1},{65,33},{97,65},{2,98}... | collective-permute-start | bytes 786440 | tf_op jit(solution)/shard_map/ppermute | solution.py:41
  105.3 10.3 %collective-permute-done.14.p1 = bf16[4,64,512]{2,1,0:T(8,128)(2,1)S(1)} collective-permute-done((bf16[4,64,512]{2,1,0:T(8,128)(2,1)S(1)}, bf16[4,64,512]{2,1,0:T(8,128)(2,1)S(1)}, u32[]{:S(2)}, u32[]{:S(2)}) %collective-permute-start.14) | collective-permute-done | bytes 262176 | tf_op jit(solution)/shard_map/ppermute | solution.py:41
  122.7 2.8 %normalize.1 = bf16[64,8192]{1,0:T(8,128)(2,1)} custom-call(s32[1]{0:T(128)} %bitcast.2.place_ref, bf16[4,64,512]{2,1,0:T(8,128)(2,1)} %bitcast.55, bf16[4,64,512]{2,1,0:T(8,128)(2,1)} %copy-done.3, bf16[4,64,512]{2,1,0:T(8,128)(2,1)} %copy-done.4, bf16[4,64,512]{2,1,0:T(8,128)(2,1)} %collective-permute-done.16.p3, f32[1,8192]{1,0:T(1,128)} %bitcast.65), custom_call_target="tpu_custom_call" | custom-call | flops 4194304 | bytes 2097152 | tf_op jit(solution)/shard_map/normalize/pallas_call | solution.py:217
  125.6 8.2 %collective-permute-done.18.refs_8_ = bf16[512,512]{1,0:T(8,128)(2,1)} collective-permute-done((bf16[512,512]{1,0:T(8,128)(2,1)}, bf16[512,512]{1,0:T(8,128)(2,1)}, u32[]{:S(2)}, u32[]{:S(2)}) %collective-permute-start.18) | collective-permute-done | bytes 524320 | tf_op jit(solution)/shard_map/ppermute | solution.py:41
  133.8 3.3 %collective-permute-done.19.refs_9_ = bf16[512,512]{1,0:T(8,128)(2,1)} collective-permute-done((bf16[512,512]{1,0:T(8,128)(2,1)}, bf16[512,512]{1,0:T(8,128)(2,1)}, u32[]{:S(2)}, u32[]{:S(2)}) %collective-permute-start.19) | collective-permute-done | bytes 524320 | tf_op jit(solution)/shard_map/ppermute | solution.py:41
  139.1 8.1 %convolution_convert_fusion = bf16[64,4096]{1,0:T(8,128)(2,1)} fusion(bf16[1,512,4096]{2,1,0:T(8,128)(2,1)} %param.22, bf16[64,8192]{1,0:T(8,128)(2,1)} %normalize.1, bf16[1,8192,512]{2,1,0:T(8,128)(2,1)} %param.20, f32[512]{0:T(512)S(1)} %bitcast.75), kind=kOutput, calls=%fused_computation.2 | convolution fusion | flops 805765120 | bytes 14157824 | tf_op jit(solution)/shard_map/dot_general | solution.py:294
  147.1 14.1 %all_to_all.5 = bf16[4,16,4096]{2,1,0:T(8,128)(2,1)} all-to-all(bf16[4,16,4096]{2,1,0:T(8,128)(2,1)} %bitcast.51), channel_id=1, replica_groups=mesh['z'=4,'xl'=2,'core'=2,'y'=4,'xh'=2] {'y'}, dimensions={0} | all-to-all | bytes 1048576 | tf_op jit(solution)/shard_map/all_to_all | solution.py:296
  166.4 2.8 %collective-permute-start.25 = (bf16[16,4096]{1,0:T(8,128)(2,1)S(1)}, bf16[16,4096]{1,0:T(8,128)(2,1)S(1)}, u32[]{:S(2)}, u32[]{:S(2)}) collective-permute-start(bf16[16,4096]{1,0:T(8,128)(2,1)S(1)} %reduce_sum.61), channel_id=1, source_target_pairs={{0,1},{1,0},{2,3},{3,2},{4,5},{5,4},{6,7},{7,6},{8,9},{9,8},{10,11... | collective-permute-start | bytes 393224 | tf_op jit(solution)/shard_map/ppermute | solution.py:41
  170.0 3.4 %collective-permute-done.25 = bf16[16,4096]{1,0:T(8,128)(2,1)S(1)} collective-permute-done((bf16[16,4096]{1,0:T(8,128)(2,1)S(1)}, bf16[16,4096]{1,0:T(8,128)(2,1)S(1)}, u32[]{:S(2)}, u32[]{:S(2)}) %collective-permute-start.25) | collective-permute-done | bytes 131104 | tf_op jit(solution)/shard_map/ppermute | solution.py:41
  175.7 9.6 %trunk_part.3.refs_10_ = f32[1024,512]{1,0:T(8,128)S(1)} custom-call(s32[2]{0:T(128)S(1)} %pad_add_fusion.1.place_ref, bf16[4,512,1024]{2,1,0:T(8,128)(2,1)} %bitcast.44, bf16[4,512,1024]{2,1,0:T(8,128)(2,1)} %collective-permute-done.22.refs_1_, bf16[4,512,1024]{2,1,0:T(8,128)(2,1)} %bitcast.48, bf16[4,512,1024]{2,1,0:T(8,128)(2,1)} %collective-permute-done.23.refs_3_, ...), custom_call_target="tpu_custom_call" | custom-call | flops 524288 | bytes 524288 | tf_op jit(solution)/shard_map/trunk_part/pallas_call | solution.py:161
  185.4 8.6 %trunk_part.4.refs_6_ = f32[1024,512]{1,0:T(8,128)S(1)} custom-call(s32[2]{0:T(128)S(1)} %pad_add_fusion.place_ref, bf16[4,512,1024]{2,1,0:T(8,128)(2,1)} %bitcast.45, bf16[4,512,1024]{2,1,0:T(8,128)(2,1)} %collective-permute-done.22.refs_1_, bf16[4,512,1024]{2,1,0:T(8,128)(2,1)} %bitcast.49, bf16[4,512,1024]{2,1,0:T(8,128)(2,1)} %collective-permute-done.23.refs_3_, ...), custom_call_target="tpu_custom_call" | custom-call | flops 524288 | bytes 524288 | tf_op jit(solution)/shard_map/trunk_part/pallas_call | solution.py:161
  194.0 5.4 %trunk_part.5 = bf16[1024,512]{1,0:T(8,128)(2,1)S(1)} custom-call(s32[2]{0:T(128)S(1)} %pad_add_fusion.place_ref, bf16[4,512,1024]{2,1,0:T(8,128)(2,1)} %bitcast.46, bf16[4,512,1024]{2,1,0:T(8,128)(2,1)} %collective-permute-done.22.refs_1_, bf16[4,512,1024]{2,1,0:T(8,128)(2,1)} %bitcast.50, bf16[4,512,1024]{2,1,0:T(8,128)(2,1)} %collective-permute-done.23.refs_3_, ...), custom_call_target="tpu_custom_call" | custom-call | flops 524288 | bytes 524288 | tf_op jit(solution)/shard_map/trunk_part/pallas_call | solution.py:161
  (95 shorter events, 40.3 us)
Async XLA Ops:
  7.2 90.2 %all-gather.7.cloned.1.call-start = ((), (), s32[]{:S(2)}) async-start(), calls=%async_computation.1 | async-start | bytes 5242880 | tf_op jit(solution)/shard_map/all_gather | solution.py:258
  13.1 151.1 %all-gather.9.cloned.1.call-start = ((), (), s32[]{:S(2)}) async-start(), calls=%async_computation.2 | async-start | bytes 5242880 | tf_op jit(solution)/shard_map/all_gather | solution.py:279
  14.4 12.3 %collective-permute-start = (bf16[512,512]{1,0:T(8,128)(2,1)S(1)}, bf16[512,512]{1,0:T(8,128)(2,1)S(1)}, u32[]{:S(2)}, u32[]{:S(2)}) collective-permute-start(bf16[512,512]{1,0:T(8,128)(2,1)S(1)} %get-tuple-element.81), channel_id=1, source_target_pairs={{0,0},{1,1},{2,98},{3,99},{4,68},{5,69},{6,38},{7,39},{8,8},{9,9},... | collective-permute-start | bytes 1572872 | tf_op jit(solution)/shard_map/ppermute | solution.py:254
  15.1 17.8 %collective-permute-start.1 = (bf16[512,512]{1,0:T(8,128)(2,1)S(1)}, bf16[512,512]{1,0:T(8,128)(2,1)S(1)}, u32[]{:S(2)}, u32[]{:S(2)}) collective-permute-start(bf16[512,512]{1,0:T(8,128)(2,1)S(1)} %get-tuple-element.80), channel_id=1, source_target_pairs={{0,64},{1,65},{2,34},{3,35},{4,4},{5,5},{6,102},{7,103},{8,72},{9,... | collective-permute-start | bytes 1572872 | tf_op jit(solution)/shard_map/ppermute | solution.py:254
  32.9 9.8 %collective-permute-start.2 = (bf16[16,2048]{1,0:T(8,128)(2,1)S(1)}, bf16[16,2048]{1,0:T(8,128)(2,1)S(1)}, u32[]{:S(2)}, u32[]{:S(2)}) collective-permute-start(bf16[16,2048]{1,0:T(8,128)(2,1)S(1)} %bitcast.58), channel_id=1, source_target_pairs={{0,96},{32,0},{64,32},{96,64},{1,97},{33,1},{65,33},{97,65},{2,98}... | collective-permute-start | bytes 196616 | tf_op jit(solution)/shard_map/ppermute | solution.py:41
  37.5 13.5 %collective-permute-start.6 = (bf16[512,512]{1,0:T(8,128)(2,1)S(1)}, bf16[512,512]{1,0:T(8,128)(2,1)S(1)}, u32[]{:S(2)}, u32[]{:S(2)}) collective-permute-start(bf16[512,512]{1,0:T(8,128)(2,1)S(1)} %collective-permute-done), channel_id=1, source_target_pairs={{0,0},{1,16},{2,2},{3,18},{4,4},{5,20},{6,6},{7,22},{8,8},{9,24},{... | collective-permute-start | bytes 1572872 | tf_op jit(solution)/shard_map/ppermute | solution.py:264
  38.2 28.5 %collective-permute-start.7 = (bf16[512,512]{1,0:T(8,128)(2,1)S(1)}, bf16[512,512]{1,0:T(8,128)(2,1)S(1)}, u32[]{:S(2)}, u32[]{:S(2)}) collective-permute-start(bf16[512,512]{1,0:T(8,128)(2,1)S(1)} %collective-permute-done.1), channel_id=1, source_target_pairs={{0,4},{1,20},{2,6},{3,22},{4,0},{5,16},{6,2},{7,18},{8,12},{9,28},... | collective-permute-start | bytes 1572872 | tf_op jit(solution)/shard_map/ppermute | solution.py:264
  66.7 24.3 %collective-permute-start.11 = (bf16[512,1024]{1,0:T(8,128)(2,1)}, bf16[512,1024]{1,0:T(8,128)(2,1)}, u32[]{:S(2)}, u32[]{:S(2)}) collective-permute-start(bf16[512,1024]{1,0:T(8,128)(2,1)} %get-tuple-element.46), channel_id=1, source_target_pairs={{0,1},{1,0},{2,3},{3,2},{4,5},{5,4},{6,7},{7,6},{8,9},{9,8},{10,11... | collective-permute-start | bytes 3145736 | tf_op jit(solution)/shard_map/ppermute | solution.py:41
  71.6 25.2 %collective-permute-start.12 = (bf16[2,512,512]{2,1,0:T(8,128)(2,1)S(1)}, bf16[2,512,512]{2,1,0:T(8,128)(2,1)S(1)}, u32[]{:S(2)}, u32[]{:S(2)}) collective-permute-start(bf16[2,512,512]{2,1,0:T(8,128)(2,1)S(1)} %pad_maximum_fusion.refs_4_.refs_5_), channel_id=1, source_target_pairs={{0,96},{32,0},{64,32},{96,64},{1,97},{33,1},{65,33},{97,65},{2,98}... | collective-permute-start | bytes 3145736 | tf_op jit(solution)/shard_map/ppermute | solution.py:41
  74.6 22.7 %collective-permute-start.13 = (bf16[2,512,512]{2,1,0:T(8,128)(2,1)S(1)}, bf16[2,512,512]{2,1,0:T(8,128)(2,1)S(1)}, u32[]{:S(2)}, u32[]{:S(2)}) collective-permute-start(bf16[2,512,512]{2,1,0:T(8,128)(2,1)S(1)} %pad_maximum_fusion.refs_4_.refs_5_), channel_id=1, source_target_pairs={{0,32},{32,64},{64,96},{96,0},{1,33},{33,65},{65,97},{97,1},{2,34}... | collective-permute-start | bytes 3145736 | tf_op jit(solution)/shard_map/ppermute | solution.py:41
  97.4 18.2 %collective-permute-start.14 = (bf16[4,64,512]{2,1,0:T(8,128)(2,1)S(1)}, bf16[4,64,512]{2,1,0:T(8,128)(2,1)S(1)}, u32[]{:S(2)}, u32[]{:S(2)}) collective-permute-start(bf16[4,64,512]{2,1,0:T(8,128)(2,1)S(1)} %bitcast.52), channel_id=1, source_target_pairs={{0,96},{32,0},{64,32},{96,64},{1,97},{33,1},{65,33},{97,65},{2,98}... | collective-permute-start | bytes 786440 | tf_op jit(solution)/shard_map/ppermute | solution.py:41
  103.8 11.7 %collective-permute-start.15 = (bf16[4,64,512]{2,1,0:T(8,128)(2,1)S(1)}, bf16[4,64,512]{2,1,0:T(8,128)(2,1)S(1)}, u32[]{:S(2)}, u32[]{:S(2)}) collective-permute-start(bf16[4,64,512]{2,1,0:T(8,128)(2,1)S(1)} %bitcast.53), channel_id=1, source_target_pairs={{0,64},{32,96},{64,0},{96,32},{1,65},{33,97},{65,1},{97,33},{2,66}... | collective-permute-start | bytes 786440 | tf_op jit(solution)/shard_map/ppermute | solution.py:41
  103.8 15.2 %collective-permute-start.16 = (bf16[4,64,512]{2,1,0:T(8,128)(2,1)S(1)}, bf16[4,64,512]{2,1,0:T(8,128)(2,1)}, u32[]{:S(2)}, u32[]{:S(2)}) collective-permute-start(bf16[4,64,512]{2,1,0:T(8,128)(2,1)S(1)} %bitcast.54), channel_id=1, source_target_pairs={{0,32},{32,64},{64,96},{96,0},{1,33},{33,65},{65,97},{97,1},{2,34}... | collective-permute-start | bytes 786440 | tf_op jit(solution)/shard_map/ppermute | solution.py:41
  104.8 32.3 %collective-permute-start.17 = (bf16[2,512,512]{2,1,0:T(8,128)(2,1)S(1)}, bf16[2,512,512]{2,1,0:T(8,128)(2,1)}, u32[]{:S(2)}, u32[]{:S(2)}) collective-permute-start(bf16[2,512,512]{2,1,0:T(8,128)(2,1)S(1)} %pad_maximum_fusion.refs_4_.refs_5_), channel_id=1, source_target_pairs={{0,16},{16,0},{1,17},{17,1},{2,18},{18,2},{3,19},{19,3},{4,20},{20... | collective-permute-start | bytes 3145736 | tf_op jit(solution)/shard_map/ppermute | solution.py:41
  119.9 13.9 %collective-permute-start.18 = (bf16[512,512]{1,0:T(8,128)(2,1)}, bf16[512,512]{1,0:T(8,128)(2,1)}, u32[]{:S(2)}, u32[]{:S(2)}) collective-permute-start(bf16[512,512]{1,0:T(8,128)(2,1)} %slice_bitcast_fusion.1), channel_id=1, source_target_pairs={{0,96},{32,0},{64,32},{96,64},{1,97},{33,1},{65,33},{97,65},{2,98}... | collective-permute-start | bytes 1572872 | tf_op jit(solution)/shard_map/ppermute | solution.py:41
  122.3 14.7 %collective-permute-start.19 = (bf16[512,512]{1,0:T(8,128)(2,1)}, bf16[512,512]{1,0:T(8,128)(2,1)}, u32[]{:S(2)}, u32[]{:S(2)}) collective-permute-start(bf16[512,512]{1,0:T(8,128)(2,1)} %slice_bitcast_fusion), channel_id=1, source_target_pairs={{0,32},{32,64},{64,96},{96,0},{1,33},{33,65},{65,97},{97,1},{2,34}... | collective-permute-start | bytes 1572872 | tf_op jit(solution)/shard_map/ppermute | solution.py:41
  137.0 27.1 %collective-permute-start.22 = (bf16[4,512,1024]{2,1,0:T(8,128)(2,1)}, bf16[4,512,1024]{2,1,0:T(8,128)(2,1)}, u32[]{:S(2)}, u32[]{:S(2)}) collective-permute-start(bf16[4,512,1024]{2,1,0:T(8,128)(2,1)} %bitcast.43), channel_id=1, source_target_pairs={{0,8},{8,0},{1,9},{9,1},{2,10},{10,2},{3,11},{11,3},{4,12},{12,4},... | collective-permute-start | bytes 12582920 | tf_op jit(solution)/shard_map/ppermute | solution.py:41
  137.0 25.9 %collective-permute-start.20 = (bf16[2,512,512]{2,1,0:T(8,128)(2,1)}, bf16[2,512,512]{2,1,0:T(8,128)(2,1)}, u32[]{:S(2)}, u32[]{:S(2)}) collective-permute-start(bf16[2,512,512]{2,1,0:T(8,128)(2,1)} %collective-permute-done.17.refs_4_.refs_5_), channel_id=1, source_target_pairs={{0,96},{32,0},{64,32},{96,64},{1,97},{33,1},{65,33},{97,65},{2,98}... | collective-permute-start | bytes 3145736 | tf_op jit(solution)/shard_map/ppermute | solution.py:41
  137.0 27.1 %collective-permute-start.21 = (bf16[2,512,512]{2,1,0:T(8,128)(2,1)}, bf16[2,512,512]{2,1,0:T(8,128)(2,1)}, u32[]{:S(2)}, u32[]{:S(2)}) collective-permute-start(bf16[2,512,512]{2,1,0:T(8,128)(2,1)} %collective-permute-done.17.refs_4_.refs_5_), channel_id=1, source_target_pairs={{0,32},{32,64},{64,96},{96,0},{1,33},{33,65},{65,97},{97,1},{2,34}... | collective-permute-start | bytes 3145736 | tf_op jit(solution)/shard_map/ppermute | solution.py:41
  164.1 11.5 %collective-permute-start.23 = (bf16[4,512,1024]{2,1,0:T(8,128)(2,1)}, bf16[4,512,1024]{2,1,0:T(8,128)(2,1)}, u32[]{:S(2)}, u32[]{:S(2)}) collective-permute-start(bf16[4,512,1024]{2,1,0:T(8,128)(2,1)} %bitcast.47), channel_id=1, source_target_pairs={{0,8},{8,0},{1,9},{9,1},{2,10},{10,2},{3,11},{11,3},{4,12},{12,4},... | collective-permute-start | bytes 12582920 | tf_op jit(solution)/shard_map/ppermute | solution.py:41
  164.2 29.8 %collective-permute-start.24 = (bf16[2,512,512]{2,1,0:T(8,128)(2,1)}, bf16[2,512,512]{2,1,0:T(8,128)(2,1)}, u32[]{:S(2)}, u32[]{:S(2)}) collective-permute-start(bf16[2,512,512]{2,1,0:T(8,128)(2,1)} %collective-permute-done.17.refs_4_.refs_5_), channel_id=1, source_target_pairs={{0,64},{32,96},{64,0},{96,32},{1,65},{33,97},{65,1},{97,33},{2,66}... | collective-permute-start | bytes 3145736 | tf_op jit(solution)/shard_map/ppermute | solution.py:41
  173.6 11.7 %collective-permute-start.26 = (f32[16]{0:T(128)S(1)}, f32[16]{0:T(128)S(1)}, u32[]{:S(2)}, u32[]{:S(2)}) collective-permute-start(f32[16]{0:T(128)S(1)} %broadcast_add_fusion), channel_id=1, source_target_pairs={{0,6},{2,0},{4,2},{6,4},{1,7},{3,1},{5,3},{7,5},{8,14},{10,8},{12,... | collective-permute-start | bytes 200 | tf_op jit(solution)/shard_map/ppermute | solution.py:41
  173.7 11.7 %collective-permute-start.27 = (f32[16]{0:T(128)S(1)}, f32[16]{0:T(128)S(1)}, u32[]{:S(2)}, u32[]{:S(2)}) collective-permute-start(f32[16]{0:T(128)S(1)} %broadcast_add_fusion), channel_id=1, source_target_pairs={{0,4},{2,6},{4,0},{6,2},{1,5},{3,7},{5,1},{7,3},{8,12},{10,14},{12... | collective-permute-start | bytes 200 | tf_op jit(solution)/shard_map/ppermute | solution.py:41
  174.8 10.6 %collective-permute-start.28 = (f32[16]{0:T(128)S(1)}, f32[16]{0:T(128)S(1)}, u32[]{:S(2)}, u32[]{:S(2)}) collective-permute-start(f32[16]{0:T(128)S(1)} %broadcast_add_fusion), channel_id=1, source_target_pairs={{0,2},{2,4},{4,6},{6,0},{1,3},{3,5},{5,7},{7,1},{8,10},{10,12},{12... | collective-permute-start | bytes 200 | tf_op jit(solution)/shard_map/ppermute | solution.py:41
  (16 other events, 253.4 us)
Sparse Core Ops, SparseCore 0:
  13.2 65.5 all-gather.6
  91.1 50.6 all-gather.8

commit v13 on v12

--- a/solution.py
+++ b/solution.py
@@ -300,11 +300,11 @@
         (terms, there, w[0, 1], w[1, 1], w[3, 1], here_other)
     )
     there_other = from_ahead(there, "core", CORE, 1)
-    w[2, 1] = from_ahead(w[0, 1], "z", Z, 2)
+    w[2, 1] = [from_ahead(w[1, 1][0], "z", Z, 1), from_ahead(w[3, 1][1], "z", Z, 3)]
     half = jnp.sum(terms.astype(jnp.float32), axis=0).astype(jnp.bfloat16)
     other = from_ahead(half, "xh", XH, 1)
-    second = jax.nn.silu(half.astype(jnp.float32) + other.astype(jnp.float32) + head_b2[0])
-    mine = jnp.sum(second * head_w3[0].astype(jnp.float32), axis=-1) + head_b3[0]
+
+    sources = (here, here_other, there, there_other)
 
     def product(e, steps, trunk, dtype):
         items = [
@@ -315,13 +315,14 @@
         place = jnp.stack([lax.rem(y - z + Y, Y), lax.rem(xl + e + xh, XH)])
         return trunk_part(place, sources, items, trunk, dtype)
 
-    sources = (here, here_other, there, there_other)
     trunk = product(0, range(Z), None, jnp.float32)
+    other, trunk = lock((other, trunk))
+    second = jax.nn.silu(half.astype(jnp.float32) + other.astype(jnp.float32) + head_b2[0])
+    mine = jnp.sum(second * head_w3[0].astype(jnp.float32), axis=-1) + head_b3[0]
     scores = [mine] + [from_ahead(mine, "y", Y, s) for s in (1, 2, 3)]
+    trunk = product(1, range(Z), trunk, jnp.bfloat16)
     *scores, trunk = lock((*scores, trunk))
     scores = jnp.roll(jnp.stack(scores), lax.rem(y + z, Y), axis=0).reshape(1, Y * count)
-    trunk = product(1, (0, 1, 3), trunk, jnp.float32)
-    trunk = product(1, (2,), trunk, jnp.bfloat16)
     row_count = residual.shape[0]
     mine = trunk[:row_count]
     other = from_ahead(trunk[row_count:], "core", CORE, 1)

time: 211 us -> 208 us (0.986)
  Pallas kernels: 32.3 us -> 28.3 us
  local copies, waits for them, and re-layouts: 5.1 us -> 8.65 us
  starting transfers between devices: 50.5 us -> 47.9 us
    pallas_call x3 -> x2, Pallas kernels: 23.7 us -> 19.7 us  [trunk_part(): pl.pallas_call(functools.partial(trunk_kernel, [(s, v) for s, v, _ in ter...]
    squeeze x0 -> x2, local copies, waits for them, and re-layouts: none -> 3.75 us  [the longest x1 1.88 us: local(): w[3, 1][1]]
    ppermute x26 -> x27, starting transfers between devices: 38.8 us -> 36.2 us  [from_ahead(): return lax.ppermute(x, axis, [(i, (i - step) % size) for i in range(size)])]
    ppermute x26 -> x27, waiting for transfers between devices: 47.9 us -> 47.8 us  [from_ahead(): return lax.ppermute(x, axis, [(i, (i - step) % size) for i in range(size)])]
  transfers between devices with their start and end apart: 32 -> 33, of which waited for: 16 -> 16; matrix products, arithmetic and copies ran while one was open for 7% -> 8% of each run, Pallas kernels for 10% -> 11%
where the time goes in v13:
time: 208 us; the launch traced here: 207 us
  waiting for transfers between devices  69.7 us (34%)
  starting transfers between devices  47.9 us (23%)
  Pallas kernels  28.3 us (14%)
  blocking collectives  25.5 us (12%)
  between operations  15.1 us (7%)
  local copies, waits for them, and re-layouts  8.65 us (4%)
  matrix products  8.35 us (4%)
  other arithmetic  3.13 us (2%)
    ppermute x27, waiting for transfers between devices, from_ahead(): return lax.ppermute(x, axis, [(i, (i - step) % size) for i in range(size)])  47.8 us
    ppermute x27, starting transfers between devices, from_ahead(): return lax.ppermute(x, axis, [(i, (i - step) % size) for i in range(size)])  36.2 us
    pallas_call x2, Pallas kernels, trunk_part(): pl.pallas_call(functools.partial(trunk_kernel, [(s, v) for s, v, _ in ter...  19.7 us
    ppermute x2, waiting for transfers between devices, local(): moved = [lax.ppermute(m, ALL, column_moves(v)) for v, m in enumerate(moved)]  15.6 us
    all_to_all x1, blocking collectives, local(): lax.all_to_all(terms.reshape(Y, count, terms.shape[1]), 'y', split_axis=0...  14.1 us
    dot_general x1, matrix products, local(): jnp.dot(first, head_w2[0], preferred_element_type=jnp.float32)  8.05 us
    ppermute x2, starting transfers between devices, local(): lax.ppermute(out_weight[v * rows_half:(v + 1) * rows_half], ALL, spread_m...  6.56 us
    ppermute x2, waiting for transfers between devices, local(): lax.ppermute(out_weight[v * rows_half:(v + 1) * rows_half], ALL, spread_m...  6.19 us
  transfers between devices with their start and end apart: 33, of which 16 were waited for; matrix products, arithmetic and copies ran while one was open for 8% of the time, Pallas kernels for 11%

profile of v13, /device:TPU:0, one launch (start us, length us, event | category | flops | bytes accessed | tf_op | source)
XLA Modules:
  0.0 206.6 jit_solution(1697659843362428369)
XLA Ops:
  7.2 5.8 %attention.1 = (bf16[512,1024]{1,0:T(8,128)(2,1)}, bf16[4,1,2048]{2,1,0:T(2,128)(2,1)}) custom-call(s32[4]{0:T(128)} %len_ref.1, bf16[512,1024]{1,0:T(8,128)(2,1)} %query_ref.1, bf16[512,128]{1,0:T(8,128)(2,1)} %keys_ref.1, bf16[512,128]{1,0:T(8,128)(2,1)} %values_ref.1, bf16[512,1024]{1,0:T(8,128)(2,1)} %residual_ref.1), custom_call_target="tpu_custom_call" | custom-call | flops 268435456 | bytes 3145728 | tf_op jit(solution)/shard_map/attention/pallas_call | solution.py:82
  15.1 5.9 %collective-permute-start.1 = (bf16[512,512]{1,0:T(8,128)(2,1)S(1)}, bf16[512,512]{1,0:T(8,128)(2,1)S(1)}, u32[]{:S(2)}, u32[]{:S(2)}) collective-permute-start(bf16[512,512]{1,0:T(8,128)(2,1)S(1)} %get-tuple-element.84), channel_id=1, source_target_pairs={{0,64},{1,65},{2,34},{3,35},{4,4},{5,5},{6,102},{7,103},{8,72},{9,... | collective-permute-start | bytes 1572872 | tf_op jit(solution)/shard_map/ppermute | solution.py:254
  21.0 5.6 %all-gather = bf16[16,1,2048]{2,1,0:T(2,128)(2,1)S(1)} all-gather(bf16[4,1,2048]{2,1,0:T(2,128)(2,1)} %get-tuple-element.42), channel_id=2, replica_groups=mesh['z'=4,'xl'=2,'core'=2,'y'=4,'xh'=2] {'xl','core'}, dimensions={0}, use_global_device_ids=true | all-gather | bytes 81920 | tf_op jit(solution)/shard_map/all_gather | solution.py:262
  26.7 6.2 %collective-permute-done.1 = bf16[512,512]{1,0:T(8,128)(2,1)S(1)} collective-permute-done((bf16[512,512]{1,0:T(8,128)(2,1)S(1)}, bf16[512,512]{1,0:T(8,128)(2,1)S(1)}, u32[]{:S(2)}, u32[]{:S(2)}) %collective-permute-start.1) | collective-permute-done | bytes 524320 | tf_op jit(solution)/shard_map/ppermute | solution.py:254
  32.9 3.4 %collective-permute-start.2 = (bf16[16,2048]{1,0:T(8,128)(2,1)S(1)}, bf16[16,2048]{1,0:T(8,128)(2,1)S(1)}, u32[]{:S(2)}, u32[]{:S(2)}) collective-permute-start(bf16[16,2048]{1,0:T(8,128)(2,1)S(1)} %bitcast.60), channel_id=1, source_target_pairs={{0,96},{32,0},{64,32},{96,64},{1,97},{33,1},{65,33},{97,65},{2,98}... | collective-permute-start | bytes 196616 | tf_op jit(solution)/shard_map/ppermute | solution.py:41
  38.2 4.4 %collective-permute-start.7 = (bf16[512,512]{1,0:T(8,128)(2,1)S(1)}, bf16[512,512]{1,0:T(8,128)(2,1)S(1)}, u32[]{:S(2)}, u32[]{:S(2)}) collective-permute-start(bf16[512,512]{1,0:T(8,128)(2,1)S(1)} %collective-permute-done.1), channel_id=1, source_target_pairs={{0,4},{1,20},{2,6},{3,22},{4,0},{5,16},{6,2},{7,18},{8,12},{9,28},... | collective-permute-start | bytes 1572872 | tf_op jit(solution)/shard_map/ppermute | solution.py:264
  43.0 5.8 %collective-permute-start.5 = (bf16[64,512]{1,0:T(8,128)(2,1)S(1)}, bf16[64,512]{1,0:T(8,128)(2,1)S(1)}, u32[]{:S(2)}, u32[]{:S(2)}) collective-permute-start(bf16[64,512]{1,0:T(8,128)(2,1)S(1)} %fusion.6), channel_id=1, source_target_pairs={{0,1},{1,0},{2,3},{3,2},{4,5},{5,4},{6,7},{7,6},{8,9},{9,8},{10,11... | collective-permute-start | bytes 196616 | tf_op jit(solution)/shard_map/ppermute | solution.py:41
  48.8 2.2 %collective-permute-done.5 = bf16[64,512]{1,0:T(8,128)(2,1)S(1)} collective-permute-done((bf16[64,512]{1,0:T(8,128)(2,1)S(1)}, bf16[64,512]{1,0:T(8,128)(2,1)S(1)}, u32[]{:S(2)}, u32[]{:S(2)}) %collective-permute-start.5) | collective-permute-done | bytes 65568 | tf_op jit(solution)/shard_map/ppermute | solution.py:41
  51.1 15.6 %collective-permute-done.7 = bf16[512,512]{1,0:T(8,128)(2,1)S(1)} collective-permute-done((bf16[512,512]{1,0:T(8,128)(2,1)S(1)}, bf16[512,512]{1,0:T(8,128)(2,1)S(1)}, u32[]{:S(2)}, u32[]{:S(2)}) %collective-permute-start.7) | collective-permute-done | bytes 524320 | tf_op jit(solution)/shard_map/ppermute | solution.py:264
  66.7 2.4 %collective-permute-start.11 = (bf16[512,1024]{1,0:T(8,128)(2,1)}, bf16[512,1024]{1,0:T(8,128)(2,1)}, u32[]{:S(2)}, u32[]{:S(2)}) collective-permute-start(bf16[512,1024]{1,0:T(8,128)(2,1)} %get-tuple-element.48), channel_id=1, source_target_pairs={{0,1},{1,0},{2,3},{3,2},{4,5},{5,4},{6,7},{7,6},{8,9},{9,8},{10,11... | collective-permute-start | bytes 3145736 | tf_op jit(solution)/shard_map/ppermute | solution.py:41
  69.1 2.4 %collective-permute-start.10 = (bf16[2,64,512]{2,1,0:T(8,128)(2,1)S(1)}, bf16[2,64,512]{2,1,0:T(8,128)(2,1)S(1)}, u32[]{:S(2)}, u32[]{:S(2)}) collective-permute-start(bf16[2,64,512]{2,1,0:T(8,128)(2,1)S(1)} %pad_maximum_fusion.1), channel_id=1, source_target_pairs={{0,2},{2,4},{4,6},{6,0},{1,3},{3,5},{5,7},{7,1},{8,10},{10,12},{12... | collective-permute-start | bytes 393224 | tf_op jit(solution)/shard_map/ppermute | solution.py:41
  71.5 2.3 %collective-permute-start.9 = (bf16[2,64,512]{2,1,0:T(8,128)(2,1)S(1)}, bf16[2,64,512]{2,1,0:T(8,128)(2,1)S(1)}, u32[]{:S(2)}, u32[]{:S(2)}) collective-permute-start(bf16[2,64,512]{2,1,0:T(8,128)(2,1)S(1)} %pad_maximum_fusion.1), channel_id=1, source_target_pairs={{0,4},{2,6},{4,0},{6,2},{1,5},{3,7},{5,1},{7,3},{8,12},{10,14},{12... | collective-permute-start | bytes 393224 | tf_op jit(solution)/shard_map/ppermute | solution.py:41
  74.3 3.0 %collective-permute-start.12 = (bf16[2,512,512]{2,1,0:T(8,128)(2,1)S(1)}, bf16[2,512,512]{2,1,0:T(8,128)(2,1)S(1)}, u32[]{:S(2)}, u32[]{:S(2)}) collective-permute-start(bf16[2,512,512]{2,1,0:T(8,128)(2,1)S(1)} %pad_maximum_fusion.refs_4_.refs_5_), channel_id=1, source_target_pairs={{0,96},{32,0},{64,32},{96,64},{1,97},{33,1},{65,33},{97,65},{2,98}... | collective-permute-start | bytes 3145736 | tf_op jit(solution)/shard_map/ppermute | solution.py:41
  80.8 10.2 %collective-permute-done.11 = bf16[512,1024]{1,0:T(8,128)(2,1)} collective-permute-done((bf16[512,1024]{1,0:T(8,128)(2,1)}, bf16[512,1024]{1,0:T(8,128)(2,1)}, u32[]{:S(2)}, u32[]{:S(2)}) %collective-permute-start.11) | collective-permute-done | bytes 1048608 | tf_op jit(solution)/shard_map/ppermute | solution.py:41
  91.0 5.8 %all-gather.1 = bf16[256,512]{1,0:T(8,128)(2,1)S(1)} all-gather(bf16[64,512]{1,0:T(8,128)(2,1)S(1)} %add_convert_fusion.1), channel_id=3, replica_groups=mesh['z'=4,'xl'=2,'core'=2,'y'=4,'xh'=2] {'xl','core'}, dimensions={0}, use_global_device_ids=true | all-gather | bytes 327680 | tf_op jit(solution)/shard_map/all_gather | solution.py:280
  96.8 6.5 %collective-permute-done.13.refs_10_.refs_11_ = bf16[2,512,512]{2,1,0:T(8,128)(2,1)S(1)} collective-permute-done((bf16[2,512,512]{2,1,0:T(8,128)(2,1)S(1)}, bf16[2,512,512]{2,1,0:T(8,128)(2,1)S(1)}, u32[]{:S(2)}, u32[]{:S(2)}) %collective-permute-start.13) | collective-permute-done | bytes 1048608 | tf_op jit(solution)/shard_map/ppermute | solution.py:41
  106.8 8.7 %collective-permute-done.14.p1 = bf16[4,64,512]{2,1,0:T(8,128)(2,1)S(1)} collective-permute-done((bf16[4,64,512]{2,1,0:T(8,128)(2,1)S(1)}, bf16[4,64,512]{2,1,0:T(8,128)(2,1)S(1)}, u32[]{:S(2)}, u32[]{:S(2)}) %collective-permute-start.14) | collective-permute-done | bytes 262176 | tf_op jit(solution)/shard_map/ppermute | solution.py:41
  122.8 2.8 %normalize.1 = bf16[64,8192]{1,0:T(8,128)(2,1)} custom-call(s32[1]{0:T(128)} %bitcast.place_ref, bf16[4,64,512]{2,1,0:T(8,128)(2,1)} %bitcast.57, bf16[4,64,512]{2,1,0:T(8,128)(2,1)} %copy-done.3, bf16[4,64,512]{2,1,0:T(8,128)(2,1)} %copy-done.4, bf16[4,64,512]{2,1,0:T(8,128)(2,1)} %collective-permute-done.16.p3, f32[1,8192]{1,0:T(1,128)} %bitcast.67), custom_call_target="tpu_custom_call" | custom-call | flops 4194304 | bytes 2097152 | tf_op jit(solution)/shard_map/normalize/pallas_call | solution.py:217
  125.6 8.1 %collective-permute-done.18.refs_8_ = bf16[512,512]{1,0:T(8,128)(2,1)} collective-permute-done((bf16[512,512]{1,0:T(8,128)(2,1)}, bf16[512,512]{1,0:T(8,128)(2,1)}, u32[]{:S(2)}, u32[]{:S(2)}) %collective-permute-start.18) | collective-permute-done | bytes 524320 | tf_op jit(solution)/shard_map/ppermute | solution.py:41
  133.7 3.1 %collective-permute-done.19.refs_9_ = bf16[512,512]{1,0:T(8,128)(2,1)} collective-permute-done((bf16[512,512]{1,0:T(8,128)(2,1)}, bf16[512,512]{1,0:T(8,128)(2,1)}, u32[]{:S(2)}, u32[]{:S(2)}) %collective-permute-start.19) | collective-permute-done | bytes 524320 | tf_op jit(solution)/shard_map/ppermute | solution.py:41
  138.8 8.1 %convolution_convert_fusion = bf16[64,4096]{1,0:T(8,128)(2,1)} fusion(bf16[1,512,4096]{2,1,0:T(8,128)(2,1)} %param.22, bf16[64,8192]{1,0:T(8,128)(2,1)} %normalize.1, bf16[1,8192,512]{2,1,0:T(8,128)(2,1)} %param.20, f32[512]{0:T(512)S(1)} %bitcast.77), kind=kOutput, calls=%fused_computation.2 | convolution fusion | flops 805765120 | bytes 14157824 | tf_op jit(solution)/shard_map/dot_general | solution.py:294
  146.9 14.1 %all_to_all.5 = bf16[4,16,4096]{2,1,0:T(8,128)(2,1)} all-to-all(bf16[4,16,4096]{2,1,0:T(8,128)(2,1)} %bitcast.53), channel_id=1, replica_groups=mesh['z'=4,'xl'=2,'core'=2,'y'=4,'xh'=2] {'y'}, dimensions={0} | all-to-all | bytes 1048576 | tf_op jit(solution)/shard_map/all_to_all | solution.py:296
  173.6 9.6 %trunk_part.2.refs_12_ = f32[1024,512]{1,0:T(8,128)S(1)} custom-call(s32[2]{0:T(128)S(1)} %pad_add_fusion.place_ref, bf16[4,512,1024]{2,1,0:T(8,128)(2,1)} %bitcast.48, bf16[4,512,1024]{2,1,0:T(8,128)(2,1)} %collective-permute-done.22.refs_1_, bf16[4,512,1024]{2,1,0:T(8,128)(2,1)} %bitcast.51, bf16[4,512,1024]{2,1,0:T(8,128)(2,1)} %collective-permute-done.24.refs_3_, ...), custom_call_target="tpu_custom_call" | custom-call | flops 524288 | bytes 524288 | tf_op jit(solution)/shard_map/trunk_part/pallas_call | solution.py:161
  186.3 10.0 %trunk_part.3 = bf16[1024,512]{1,0:T(8,128)(2,1)S(1)} custom-call(s32[2]{0:T(128)S(1)} %pad_add_fusion.1.place_ref, bf16[4,512,1024]{2,1,0:T(8,128)(2,1)} %bitcast.49, bf16[4,512,1024]{2,1,0:T(8,128)(2,1)} %collective-permute-done.22.refs_1_, bf16[4,512,1024]{2,1,0:T(8,128)(2,1)} %bitcast.52, bf16[4,512,1024]{2,1,0:T(8,128)(2,1)} %collective-permute-done.24.refs_3_, ...), custom_call_target="tpu_custom_call" | custom-call | flops 524288 | bytes 524288 | tf_op jit(solution)/shard_map/trunk_part/pallas_call | solution.py:161
  (98 shorter events, 39.6 us)
Async XLA Ops:
  7.2 96.1 %all-gather.7.cloned.1.call-start = ((), (), s32[]{:S(2)}) async-start(), calls=%async_computation.1 | async-start | bytes 5242880 | tf_op jit(solution)/shard_map/all_gather | solution.py:258
  13.1 147.9 %all-gather.9.cloned.1.call-start = ((), (), s32[]{:S(2)}) async-start(), calls=%async_computation.2 | async-start | bytes 5242880 | tf_op jit(solution)/shard_map/all_gather | solution.py:279
  14.4 12.3 %collective-permute-start = (bf16[512,512]{1,0:T(8,128)(2,1)S(1)}, bf16[512,512]{1,0:T(8,128)(2,1)S(1)}, u32[]{:S(2)}, u32[]{:S(2)}) collective-permute-start(bf16[512,512]{1,0:T(8,128)(2,1)S(1)} %get-tuple-element.85), channel_id=1, source_target_pairs={{0,0},{1,1},{2,98},{3,99},{4,68},{5,69},{6,38},{7,39},{8,8},{9,9},... | collective-permute-start | bytes 1572872 | tf_op jit(solution)/shard_map/ppermute | solution.py:254
  15.1 17.8 %collective-permute-start.1 = (bf16[512,512]{1,0:T(8,128)(2,1)S(1)}, bf16[512,512]{1,0:T(8,128)(2,1)S(1)}, u32[]{:S(2)}, u32[]{:S(2)}) collective-permute-start(bf16[512,512]{1,0:T(8,128)(2,1)S(1)} %get-tuple-element.84), channel_id=1, source_target_pairs={{0,64},{1,65},{2,34},{3,35},{4,4},{5,5},{6,102},{7,103},{8,72},{9,... | collective-permute-start | bytes 1572872 | tf_op jit(solution)/shard_map/ppermute | solution.py:254
  37.5 13.5 %collective-permute-start.6 = (bf16[512,512]{1,0:T(8,128)(2,1)S(1)}, bf16[512,512]{1,0:T(8,128)(2,1)S(1)}, u32[]{:S(2)}, u32[]{:S(2)}) collective-permute-start(bf16[512,512]{1,0:T(8,128)(2,1)S(1)} %collective-permute-done), channel_id=1, source_target_pairs={{0,0},{1,16},{2,2},{3,18},{4,4},{5,20},{6,6},{7,22},{8,8},{9,24},{... | collective-permute-start | bytes 1572872 | tf_op jit(solution)/shard_map/ppermute | solution.py:264
  38.2 28.5 %collective-permute-start.7 = (bf16[512,512]{1,0:T(8,128)(2,1)S(1)}, bf16[512,512]{1,0:T(8,128)(2,1)S(1)}, u32[]{:S(2)}, u32[]{:S(2)}) collective-permute-start(bf16[512,512]{1,0:T(8,128)(2,1)S(1)} %collective-permute-done.1), channel_id=1, source_target_pairs={{0,4},{1,20},{2,6},{3,22},{4,0},{5,16},{6,2},{7,18},{8,12},{9,28},... | collective-permute-start | bytes 1572872 | tf_op jit(solution)/shard_map/ppermute | solution.py:264
  66.7 24.3 %collective-permute-start.11 = (bf16[512,1024]{1,0:T(8,128)(2,1)}, bf16[512,1024]{1,0:T(8,128)(2,1)}, u32[]{:S(2)}, u32[]{:S(2)}) collective-permute-start(bf16[512,1024]{1,0:T(8,128)(2,1)} %get-tuple-element.48), channel_id=1, source_target_pairs={{0,1},{1,0},{2,3},{3,2},{4,5},{5,4},{6,7},{7,6},{8,9},{9,8},{10,11... | collective-permute-start | bytes 3145736 | tf_op jit(solution)/shard_map/ppermute | solution.py:41
  74.3 22.5 %collective-permute-start.12 = (bf16[2,512,512]{2,1,0:T(8,128)(2,1)S(1)}, bf16[2,512,512]{2,1,0:T(8,128)(2,1)S(1)}, u32[]{:S(2)}, u32[]{:S(2)}) collective-permute-start(bf16[2,512,512]{2,1,0:T(8,128)(2,1)S(1)} %pad_maximum_fusion.refs_4_.refs_5_), channel_id=1, source_target_pairs={{0,96},{32,0},{64,32},{96,64},{1,97},{33,1},{65,33},{97,65},{2,98}... | collective-permute-start | bytes 3145736 | tf_op jit(solution)/shard_map/ppermute | solution.py:41
  78.7 24.5 %collective-permute-start.13 = (bf16[2,512,512]{2,1,0:T(8,128)(2,1)S(1)}, bf16[2,512,512]{2,1,0:T(8,128)(2,1)S(1)}, u32[]{:S(2)}, u32[]{:S(2)}) collective-permute-start(bf16[2,512,512]{2,1,0:T(8,128)(2,1)S(1)} %pad_maximum_fusion.refs_4_.refs_5_), channel_id=1, source_target_pairs={{0,32},{32,64},{64,96},{96,0},{1,33},{33,65},{65,97},{97,1},{2,34}... | collective-permute-start | bytes 3145736 | tf_op jit(solution)/shard_map/ppermute | solution.py:41
  103.2 12.3 %collective-permute-start.14 = (bf16[4,64,512]{2,1,0:T(8,128)(2,1)S(1)}, bf16[4,64,512]{2,1,0:T(8,128)(2,1)S(1)}, u32[]{:S(2)}, u32[]{:S(2)}) collective-permute-start(bf16[4,64,512]{2,1,0:T(8,128)(2,1)S(1)} %bitcast.54), channel_id=1, source_target_pairs={{0,96},{32,0},{64,32},{96,64},{1,97},{33,1},{65,33},{97,65},{2,98}... | collective-permute-start | bytes 786440 | tf_op jit(solution)/shard_map/ppermute | solution.py:41
  105.0 10.7 %collective-permute-start.15 = (bf16[4,64,512]{2,1,0:T(8,128)(2,1)S(1)}, bf16[4,64,512]{2,1,0:T(8,128)(2,1)S(1)}, u32[]{:S(2)}, u32[]{:S(2)}) collective-permute-start(bf16[4,64,512]{2,1,0:T(8,128)(2,1)S(1)} %bitcast.55), channel_id=1, source_target_pairs={{0,64},{32,96},{64,0},{96,32},{1,65},{33,97},{65,1},{97,33},{2,66}... | collective-permute-start | bytes 786440 | tf_op jit(solution)/shard_map/ppermute | solution.py:41
  105.0 14.0 %collective-permute-start.16 = (bf16[4,64,512]{2,1,0:T(8,128)(2,1)S(1)}, bf16[4,64,512]{2,1,0:T(8,128)(2,1)}, u32[]{:S(2)}, u32[]{:S(2)}) collective-permute-start(bf16[4,64,512]{2,1,0:T(8,128)(2,1)S(1)} %bitcast.56), channel_id=1, source_target_pairs={{0,32},{32,64},{64,96},{96,0},{1,33},{33,65},{65,97},{97,1},{2,34}... | collective-permute-start | bytes 786440 | tf_op jit(solution)/shard_map/ppermute | solution.py:41
  105.9 30.9 %collective-permute-start.17 = (bf16[2,512,512]{2,1,0:T(8,128)(2,1)S(1)}, bf16[2,512,512]{2,1,0:T(8,128)(2,1)}, u32[]{:S(2)}, u32[]{:S(2)}) collective-permute-start(bf16[2,512,512]{2,1,0:T(8,128)(2,1)S(1)} %pad_maximum_fusion.refs_4_.refs_5_), channel_id=1, source_target_pairs={{0,16},{16,0},{1,17},{17,1},{2,18},{18,2},{3,19},{19,3},{4,20},{20... | collective-permute-start | bytes 3145736 | tf_op jit(solution)/shard_map/ppermute | solution.py:41
  119.9 13.8 %collective-permute-start.18 = (bf16[512,512]{1,0:T(8,128)(2,1)}, bf16[512,512]{1,0:T(8,128)(2,1)}, u32[]{:S(2)}, u32[]{:S(2)}) collective-permute-start(bf16[512,512]{1,0:T(8,128)(2,1)} %slice_bitcast_fusion.3), channel_id=1, source_target_pairs={{0,96},{32,0},{64,32},{96,64},{1,97},{33,1},{65,33},{97,65},{2,98}... | collective-permute-start | bytes 1572872 | tf_op jit(solution)/shard_map/ppermute | solution.py:41
  122.3 14.5 %collective-permute-start.19 = (bf16[512,512]{1,0:T(8,128)(2,1)}, bf16[512,512]{1,0:T(8,128)(2,1)}, u32[]{:S(2)}, u32[]{:S(2)}) collective-permute-start(bf16[512,512]{1,0:T(8,128)(2,1)} %slice_bitcast_fusion.2), channel_id=1, source_target_pairs={{0,32},{32,64},{64,96},{96,0},{1,33},{33,65},{65,97},{97,1},{2,34}... | collective-permute-start | bytes 1572872 | tf_op jit(solution)/shard_map/ppermute | solution.py:41
  136.8 27.1 %collective-permute-start.22 = (bf16[4,512,1024]{2,1,0:T(8,128)(2,1)}, bf16[4,512,1024]{2,1,0:T(8,128)(2,1)}, u32[]{:S(2)}, u32[]{:S(2)}) collective-permute-start(bf16[4,512,1024]{2,1,0:T(8,128)(2,1)} %bitcast.47), channel_id=1, source_target_pairs={{0,8},{8,0},{1,9},{9,1},{2,10},{10,2},{3,11},{11,3},{4,12},{12,4},... | collective-permute-start | bytes 12582920 | tf_op jit(solution)/shard_map/ppermute | solution.py:41
  136.8 25.9 %collective-permute-start.20 = (bf16[2,512,512]{2,1,0:T(8,128)(2,1)}, bf16[2,512,512]{2,1,0:T(8,128)(2,1)}, u32[]{:S(2)}, u32[]{:S(2)}) collective-permute-start(bf16[2,512,512]{2,1,0:T(8,128)(2,1)} %collective-permute-done.17.refs_4_.refs_5_), channel_id=1, source_target_pairs={{0,96},{32,0},{64,32},{96,64},{1,97},{33,1},{65,33},{97,65},{2,98}... | collective-permute-start | bytes 3145736 | tf_op jit(solution)/shard_map/ppermute | solution.py:41
  136.8 27.1 %collective-permute-start.21 = (bf16[2,512,512]{2,1,0:T(8,128)(2,1)}, bf16[2,512,512]{2,1,0:T(8,128)(2,1)}, u32[]{:S(2)}, u32[]{:S(2)}) collective-permute-start(bf16[2,512,512]{2,1,0:T(8,128)(2,1)} %collective-permute-done.17.refs_4_.refs_5_), channel_id=1, source_target_pairs={{0,32},{32,64},{64,96},{96,0},{1,33},{33,65},{65,97},{97,1},{2,34}... | collective-permute-start | bytes 3145736 | tf_op jit(solution)/shard_map/ppermute | solution.py:41
  165.0 18.2 %collective-permute-start.23 = (bf16[16,4096]{1,0:T(8,128)(2,1)S(1)}, bf16[16,4096]{1,0:T(8,128)(2,1)S(1)}, u32[]{:S(2)}, u32[]{:S(2)}) collective-permute-start(bf16[16,4096]{1,0:T(8,128)(2,1)S(1)} %reduce_sum.61), channel_id=1, source_target_pairs={{0,1},{1,0},{2,3},{3,2},{4,5},{5,4},{6,7},{7,6},{8,9},{9,8},{10,11... | collective-permute-start | bytes 393224 | tf_op jit(solution)/shard_map/ppermute | solution.py:41
  168.8 16.9 %collective-permute-start.28 = (bf16[512,512]{1,0:T(8,128)(2,1)}, bf16[512,512]{1,0:T(8,128)(2,1)}, u32[]{:S(2)}, u32[]{:S(2)}) collective-permute-start(bf16[512,512]{1,0:T(8,128)(2,1)} %slice_bitcast_fusion.1), channel_id=1, source_target_pairs={{0,96},{32,0},{64,32},{96,64},{1,97},{33,1},{65,33},{97,65},{2,98}... | collective-permute-start | bytes 1572872 | tf_op jit(solution)/shard_map/ppermute | solution.py:41
  171.0 15.3 %collective-permute-start.29 = (bf16[512,512]{1,0:T(8,128)(2,1)}, bf16[512,512]{1,0:T(8,128)(2,1)}, u32[]{:S(2)}, u32[]{:S(2)}) collective-permute-start(bf16[512,512]{1,0:T(8,128)(2,1)} %slice_bitcast_fusion), channel_id=1, source_target_pairs={{0,32},{32,64},{64,96},{96,0},{1,33},{33,65},{65,97},{97,1},{2,34}... | collective-permute-start | bytes 1572872 | tf_op jit(solution)/shard_map/ppermute | solution.py:41
  183.5 12.9 %collective-permute-start.25 = (f32[16]{0:T(128)S(1)}, f32[16]{0:T(128)S(1)}, u32[]{:S(2)}, u32[]{:S(2)}) collective-permute-start(f32[16]{0:T(128)S(1)} %broadcast_add_fusion), channel_id=1, source_target_pairs={{0,6},{2,0},{4,2},{6,4},{1,7},{3,1},{5,3},{7,5},{8,14},{10,8},{12,... | collective-permute-start | bytes 200 | tf_op jit(solution)/shard_map/ppermute | solution.py:41
  183.6 12.8 %collective-permute-start.26 = (f32[16]{0:T(128)S(1)}, f32[16]{0:T(128)S(1)}, u32[]{:S(2)}, u32[]{:S(2)}) collective-permute-start(f32[16]{0:T(128)S(1)} %broadcast_add_fusion), channel_id=1, source_target_pairs={{0,4},{2,6},{4,0},{6,2},{1,5},{3,7},{5,1},{7,3},{8,12},{10,14},{12... | collective-permute-start | bytes 200 | tf_op jit(solution)/shard_map/ppermute | solution.py:41
  185.6 10.8 %collective-permute-start.27 = (f32[16]{0:T(128)S(1)}, f32[16]{0:T(128)S(1)}, u32[]{:S(2)}, u32[]{:S(2)}) collective-permute-start(f32[16]{0:T(128)S(1)} %broadcast_add_fusion), channel_id=1, source_target_pairs={{0,2},{2,4},{4,6},{6,0},{1,3},{3,5},{5,7},{7,1},{8,10},{10,12},{12... | collective-permute-start | bytes 200 | tf_op jit(solution)/shard_map/ppermute | solution.py:41
  (17 other events, 254.2 us)
Sparse Core Ops, SparseCore 0:
  13.2 65.5 all-gather.6
  91.1 50.6 all-gather.8

commit v14 on v13

--- a/solution.py
+++ b/solution.py
@@ -281,13 +281,15 @@
     near, w[1, 0], w[3, 0], w[0, 0], here = lock((near, w[1, 0], w[3, 0], w[0, 0], here))
     pieces = [near] + [from_ahead(near, "z", Z, s) for s in (1, 2, 3)]
     w[0, 1] = from_ahead(w[0, 0], "xl", XL, 1)
+    here_other = from_ahead(here, "core", CORE, 1)
     *pieces, w[1, 0], w[3, 0] = lock((*pieces, w[1, 0], w[3, 0]))
     w[2, 0] = [from_ahead(w[1, 0][0], "z", Z, 1), from_ahead(w[3, 0][1], "z", Z, 3)]
     features = normalize(pieces, norm_gain, z)
-    features, w[0, 1], here, *w[2, 0] = lock((features, w[0, 1], here, *w[2, 0]))
+    features, w[0, 1], here_other, *w[2, 0] = lock(
+        (features, w[0, 1], here_other, *w[2, 0])
+    )
     w[1, 1] = from_ahead(w[0, 1], "z", Z, 1)
     w[3, 1] = from_ahead(w[0, 1], "z", Z, 3)
-    here_other = from_ahead(here, "core", CORE, 1)
     first = jax.nn.silu(
         jnp.dot(features, head_w1[0], preferred_element_type=jnp.float32) + head_b1[0]
     ).astype(jnp.bfloat16)
@@ -296,9 +298,7 @@
     terms = lax.all_to_all(
         terms.reshape(Y, count, terms.shape[1]), "y", split_axis=0, concat_axis=0, tiled=True
     )
-    terms, there, w[0, 1], w[1, 1], w[3, 1], here_other = lock(
-        (terms, there, w[0, 1], w[1, 1], w[3, 1], here_other)
-    )
+    terms, there, w[1, 1], w[3, 1] = lock((terms, there, w[1, 1], w[3, 1]))
     there_other = from_ahead(there, "core", CORE, 1)
     w[2, 1] = [from_ahead(w[1, 1][0], "z", Z, 1), from_ahead(w[3, 1][1], "z", Z, 3)]
     half = jnp.sum(terms.astype(jnp.float32), axis=0).astype(jnp.bfloat16)

time: 208 us -> 208 us (level)
  blocking collectives: 25.5 us -> 11.4 us
  waiting for transfers between devices: 69.7 us -> 77.9 us
  starting transfers between devices: 47.9 us -> 53.7 us
    all_to_all x1 -> x0, blocking collectives: 14.1 us -> none  [local(): lax.all_to_all(terms.reshape(Y, count, terms.shape[1]), 'y', split_axis=0...]
    all_to_all x0 -> x1, waiting for transfers between devices: none -> 8.11 us  [local(): lax.all_to_all(terms.reshape(Y, count, terms.shape[1]), 'y', split_axis=0...]
    all_to_all x0 -> x1, starting transfers between devices: none -> 4.16 us  [local(): lax.all_to_all(terms.reshape(Y, count, terms.shape[1]), 'y', split_axis=0...]
  transfers between devices with their start and end apart: 33 -> 34, of which waited for: 16 -> 16; matrix products, arithmetic and copies ran while one was open for 8% -> 8% of each run, Pallas kernels for 11% -> 11%
where the time goes in v14:
time: 208 us; the launch traced here: 207 us
  waiting for transfers between devices  77.9 us (37%)
  starting transfers between devices  53.7 us (26%)
  Pallas kernels  28.3 us (14%)
  between operations  15.1 us (7%)
  blocking collectives  11.4 us (5%)
  local copies, waits for them, and re-layouts  8.89 us (4%)
  matrix products  8.37 us (4%)
  other arithmetic  3.13 us (2%)
    ppermute x27, waiting for transfers between devices, from_ahead(): return lax.ppermute(x, axis, [(i, (i - step) % size) for i in range(size)])  47.9 us
    ppermute x27, starting transfers between devices, from_ahead(): return lax.ppermute(x, axis, [(i, (i - step) % size) for i in range(size)])  37.8 us
    pallas_call x2, Pallas kernels, trunk_part(): pl.pallas_call(functools.partial(trunk_kernel, [(s, v) for s, v, _ in ter...  19.7 us
    ppermute x2, waiting for transfers between devices, local(): moved = [lax.ppermute(m, ALL, column_moves(v)) for v, m in enumerate(moved)]  15.6 us
    all_to_all x1, waiting for transfers between devices, local(): lax.all_to_all(terms.reshape(Y, count, terms.shape[1]), 'y', split_axis=0...  8.11 us
    dot_general x1, matrix products, local(): jnp.dot(first, head_w2[0], preferred_element_type=jnp.float32)  8.07 us
    ppermute x2, starting transfers between devices, local(): lax.ppermute(out_weight[v * rows_half:(v + 1) * rows_half], ALL, spread_m...  6.56 us
    ppermute x2, waiting for transfers between devices, local(): lax.ppermute(out_weight[v * rows_half:(v + 1) * rows_half], ALL, spread_m...  6.19 us
  transfers between devices with their start and end apart: 34, of which 16 were waited for; matrix products, arithmetic and copies ran while one was open for 8% of the time, Pallas kernels for 11%

profile of v14, /device:TPU:0, one launch (start us, length us, event | category | flops | bytes accessed | tf_op | source)
XLA Modules:
  0.0 206.8 jit_solution(13946506375554312850)
XLA Ops:
  7.2 5.8 %attention.1 = (bf16[512,1024]{1,0:T(8,128)(2,1)}, bf16[4,1,2048]{2,1,0:T(2,128)(2,1)}) custom-call(s32[4]{0:T(128)} %len_ref.1, bf16[512,1024]{1,0:T(8,128)(2,1)} %query_ref.1, bf16[512,128]{1,0:T(8,128)(2,1)} %keys_ref.1, bf16[512,128]{1,0:T(8,128)(2,1)} %values_ref.1, bf16[512,1024]{1,0:T(8,128)(2,1)} %residual_ref.1), custom_call_target="tpu_custom_call" | custom-call | flops 268435456 | bytes 3145728 | tf_op jit(solution)/shard_map/attention/pallas_call | solution.py:82
  15.1 5.9 %collective-permute-start.1 = (bf16[512,512]{1,0:T(8,128)(2,1)S(1)}, bf16[512,512]{1,0:T(8,128)(2,1)S(1)}, u32[]{:S(2)}, u32[]{:S(2)}) collective-permute-start(bf16[512,512]{1,0:T(8,128)(2,1)S(1)} %get-tuple-element.80), channel_id=1, source_target_pairs={{0,64},{1,65},{2,34},{3,35},{4,4},{5,5},{6,102},{7,103},{8,72},{9,... | collective-permute-start | bytes 1572872 | tf_op jit(solution)/shard_map/ppermute | solution.py:254
  21.0 5.6 %all-gather = bf16[16,1,2048]{2,1,0:T(2,128)(2,1)S(1)} all-gather(bf16[4,1,2048]{2,1,0:T(2,128)(2,1)} %get-tuple-element.40), channel_id=2, replica_groups=mesh['z'=4,'xl'=2,'core'=2,'y'=4,'xh'=2] {'xl','core'}, dimensions={0}, use_global_device_ids=true | all-gather | bytes 81920 | tf_op jit(solution)/shard_map/all_gather | solution.py:262
  26.7 6.2 %collective-permute-done.1 = bf16[512,512]{1,0:T(8,128)(2,1)S(1)} collective-permute-done((bf16[512,512]{1,0:T(8,128)(2,1)S(1)}, bf16[512,512]{1,0:T(8,128)(2,1)S(1)}, u32[]{:S(2)}, u32[]{:S(2)}) %collective-permute-start.1) | collective-permute-done | bytes 524320 | tf_op jit(solution)/shard_map/ppermute | solution.py:254
  32.9 3.4 %collective-permute-start.2 = (bf16[16,2048]{1,0:T(8,128)(2,1)S(1)}, bf16[16,2048]{1,0:T(8,128)(2,1)S(1)}, u32[]{:S(2)}, u32[]{:S(2)}) collective-permute-start(bf16[16,2048]{1,0:T(8,128)(2,1)S(1)} %bitcast.60), channel_id=1, source_target_pairs={{0,96},{32,0},{64,32},{96,64},{1,97},{33,1},{65,33},{97,65},{2,98}... | collective-permute-start | bytes 196616 | tf_op jit(solution)/shard_map/ppermute | solution.py:41
  38.2 4.4 %collective-permute-start.7 = (bf16[512,512]{1,0:T(8,128)(2,1)S(1)}, bf16[512,512]{1,0:T(8,128)(2,1)S(1)}, u32[]{:S(2)}, u32[]{:S(2)}) collective-permute-start(bf16[512,512]{1,0:T(8,128)(2,1)S(1)} %collective-permute-done.1), channel_id=1, source_target_pairs={{0,4},{1,20},{2,6},{3,22},{4,0},{5,16},{6,2},{7,18},{8,12},{9,28},... | collective-permute-start | bytes 1572872 | tf_op jit(solution)/shard_map/ppermute | solution.py:264
  43.0 5.8 %collective-permute-start.5 = (bf16[64,512]{1,0:T(8,128)(2,1)S(1)}, bf16[64,512]{1,0:T(8,128)(2,1)S(1)}, u32[]{:S(2)}, u32[]{:S(2)}) collective-permute-start(bf16[64,512]{1,0:T(8,128)(2,1)S(1)} %fusion.6), channel_id=1, source_target_pairs={{0,1},{1,0},{2,3},{3,2},{4,5},{5,4},{6,7},{7,6},{8,9},{9,8},{10,11... | collective-permute-start | bytes 196616 | tf_op jit(solution)/shard_map/ppermute | solution.py:41
  51.1 15.6 %collective-permute-done.7 = bf16[512,512]{1,0:T(8,128)(2,1)S(1)} collective-permute-done((bf16[512,512]{1,0:T(8,128)(2,1)S(1)}, bf16[512,512]{1,0:T(8,128)(2,1)S(1)}, u32[]{:S(2)}, u32[]{:S(2)}) %collective-permute-start.7) | collective-permute-done | bytes 524320 | tf_op jit(solution)/shard_map/ppermute | solution.py:264
  66.7 2.4 %collective-permute-start.11 = (bf16[512,1024]{1,0:T(8,128)(2,1)}, bf16[512,1024]{1,0:T(8,128)(2,1)}, u32[]{:S(2)}, u32[]{:S(2)}) collective-permute-start(bf16[512,1024]{1,0:T(8,128)(2,1)} %get-tuple-element.46), channel_id=1, source_target_pairs={{0,1},{1,0},{2,3},{3,2},{4,5},{5,4},{6,7},{7,6},{8,9},{9,8},{10,11... | collective-permute-start | bytes 3145736 | tf_op jit(solution)/shard_map/ppermute | solution.py:41
  69.1 2.4 %collective-permute-start.10 = (bf16[2,64,512]{2,1,0:T(8,128)(2,1)S(1)}, bf16[2,64,512]{2,1,0:T(8,128)(2,1)S(1)}, u32[]{:S(2)}, u32[]{:S(2)}) collective-permute-start(bf16[2,64,512]{2,1,0:T(8,128)(2,1)S(1)} %pad_maximum_fusion.1), channel_id=1, source_target_pairs={{0,2},{2,4},{4,6},{6,0},{1,3},{3,5},{5,7},{7,1},{8,10},{10,12},{12... | collective-permute-start | bytes 393224 | tf_op jit(solution)/shard_map/ppermute | solution.py:41
  74.3 3.0 %collective-permute-start.12 = (bf16[2,512,512]{2,1,0:T(8,128)(2,1)S(1)}, bf16[2,512,512]{2,1,0:T(8,128)(2,1)S(1)}, u32[]{:S(2)}, u32[]{:S(2)}) collective-permute-start(bf16[2,512,512]{2,1,0:T(8,128)(2,1)S(1)} %pad_maximum_fusion.refs_4_.refs_5_), channel_id=1, source_target_pairs={{0,96},{32,0},{64,32},{96,64},{1,97},{33,1},{65,33},{97,65},{2,98}... | collective-permute-start | bytes 3145736 | tf_op jit(solution)/shard_map/ppermute | solution.py:41
  80.8 10.2 %collective-permute-done.11 = bf16[512,1024]{1,0:T(8,128)(2,1)} collective-permute-done((bf16[512,1024]{1,0:T(8,128)(2,1)}, bf16[512,1024]{1,0:T(8,128)(2,1)}, u32[]{:S(2)}, u32[]{:S(2)}) %collective-permute-start.11) | collective-permute-done | bytes 1048608 | tf_op jit(solution)/shard_map/ppermute | solution.py:41
  91.0 5.8 %all-gather.1 = bf16[256,512]{1,0:T(8,128)(2,1)S(1)} all-gather(bf16[64,512]{1,0:T(8,128)(2,1)S(1)} %add_convert_fusion.1), channel_id=3, replica_groups=mesh['z'=4,'xl'=2,'core'=2,'y'=4,'xh'=2] {'xl','core'}, dimensions={0}, use_global_device_ids=true | all-gather | bytes 327680 | tf_op jit(solution)/shard_map/all_gather | solution.py:280
  96.8 6.5 %collective-permute-done.13.refs_10_.refs_11_ = bf16[2,512,512]{2,1,0:T(8,128)(2,1)S(1)} collective-permute-done((bf16[2,512,512]{2,1,0:T(8,128)(2,1)S(1)}, bf16[2,512,512]{2,1,0:T(8,128)(2,1)S(1)}, u32[]{:S(2)}, u32[]{:S(2)}) %collective-permute-start.13) | collective-permute-done | bytes 1048608 | tf_op jit(solution)/shard_map/ppermute | solution.py:41
  106.9 10.0 %collective-permute-done.14.p1 = bf16[4,64,512]{2,1,0:T(8,128)(2,1)S(1)} collective-permute-done((bf16[4,64,512]{2,1,0:T(8,128)(2,1)S(1)}, bf16[4,64,512]{2,1,0:T(8,128)(2,1)S(1)}, u32[]{:S(2)}, u32[]{:S(2)}) %collective-permute-start.14) | collective-permute-done | bytes 262176 | tf_op jit(solution)/shard_map/ppermute | solution.py:41
  124.1 2.8 %normalize.1 = bf16[64,8192]{1,0:T(8,128)(2,1)} custom-call(s32[1]{0:T(128)} %bitcast.place_ref, bf16[4,64,512]{2,1,0:T(8,128)(2,1)} %bitcast.57, bf16[4,64,512]{2,1,0:T(8,128)(2,1)} %copy-done.3, bf16[4,64,512]{2,1,0:T(8,128)(2,1)} %copy-done.4, bf16[4,64,512]{2,1,0:T(8,128)(2,1)} %collective-permute-done.16.p3, f32[1,8192]{1,0:T(1,128)} %bitcast.67), custom_call_target="tpu_custom_call" | custom-call | flops 4194304 | bytes 2097152 | tf_op jit(solution)/shard_map/normalize/pallas_call | solution.py:217
  126.9 8.2 %collective-permute-done.19.refs_8_ = bf16[512,512]{1,0:T(8,128)(2,1)} collective-permute-done((bf16[512,512]{1,0:T(8,128)(2,1)}, bf16[512,512]{1,0:T(8,128)(2,1)}, u32[]{:S(2)}, u32[]{:S(2)}) %collective-permute-start.19) | collective-permute-done | bytes 524320 | tf_op jit(solution)/shard_map/ppermute | solution.py:41
  135.1 2.4 %collective-permute-done.20.refs_9_ = bf16[512,512]{1,0:T(8,128)(2,1)} collective-permute-done((bf16[512,512]{1,0:T(8,128)(2,1)}, bf16[512,512]{1,0:T(8,128)(2,1)}, u32[]{:S(2)}, u32[]{:S(2)}) %collective-permute-start.20) | collective-permute-done | bytes 524320 | tf_op jit(solution)/shard_map/ppermute | solution.py:41
  139.5 8.1 %convolution_convert_fusion = bf16[64,4096]{1,0:T(8,128)(2,1)} fusion(bf16[1,512,4096]{2,1,0:T(8,128)(2,1)} %param.22, bf16[64,8192]{1,0:T(8,128)(2,1)} %normalize.1, bf16[1,8192,512]{2,1,0:T(8,128)(2,1)} %param.20, f32[512]{0:T(512)S(1)} %bitcast.77), kind=kOutput, calls=%fused_computation.2 | convolution fusion | flops 805765120 | bytes 14157824 | tf_op jit(solution)/shard_map/dot_general | solution.py:296
  147.6 4.2 %all-to-all-start = ((bf16[4,16,4096]{2,1,0:T(8,128)(2,1)}), bf16[4,16,4096]{2,1,0:T(8,128)(2,1)}, u32[]{:S(2)}, u32[]{:S(2)}) async-start(bf16[4,16,4096]{2,1,0:T(8,128)(2,1)} %bitcast.53), calls=%async_computation | async-start | bytes 1048576 | tf_op jit(solution)/shard_map/all_to_all | solution.py:298
  151.8 8.1 %all-to-all-done = bf16[4,16,4096]{2,1,0:T(8,128)(2,1)} async-done(((bf16[4,16,4096]{2,1,0:T(8,128)(2,1)}), bf16[4,16,4096]{2,1,0:T(8,128)(2,1)}, u32[]{:S(2)}, u32[]{:S(2)}) %all-to-all-start) | async-done | bytes 524320 | tf_op jit(solution)/shard_map/all_to_all | solution.py:298
  162.9 3.7 %collective-permute-start.23 = (bf16[16,4096]{1,0:T(8,128)(2,1)S(1)}, bf16[16,4096]{1,0:T(8,128)(2,1)S(1)}, u32[]{:S(2)}, u32[]{:S(2)}) collective-permute-start(bf16[16,4096]{1,0:T(8,128)(2,1)S(1)} %reduce_sum.61), channel_id=1, source_target_pairs={{0,1},{1,0},{2,3},{3,2},{4,5},{5,4},{6,7},{7,6},{8,9},{9,8},{10,11... | collective-permute-start | bytes 393224 | tf_op jit(solution)/shard_map/ppermute | solution.py:41
  173.2 9.6 %trunk_part.2.refs_12_ = f32[1024,512]{1,0:T(8,128)S(1)} custom-call(s32[2]{0:T(128)S(1)} %pad_add_fusion.place_ref, bf16[4,512,1024]{2,1,0:T(8,128)(2,1)} %bitcast.48, bf16[4,512,1024]{2,1,0:T(8,128)(2,1)} %collective-permute-done.18.refs_1_, bf16[4,512,1024]{2,1,0:T(8,128)(2,1)} %bitcast.51, bf16[4,512,1024]{2,1,0:T(8,128)(2,1)} %collective-permute-done.24.refs_3_, ...), custom_call_target="tpu_custom_call" | custom-call | flops 524288 | bytes 524288 | tf_op jit(solution)/shard_map/trunk_part/pallas_call | solution.py:161
  186.4 10.0 %trunk_part.3 = bf16[1024,512]{1,0:T(8,128)(2,1)S(1)} custom-call(s32[2]{0:T(128)S(1)} %pad_add_fusion.1.place_ref, bf16[4,512,1024]{2,1,0:T(8,128)(2,1)} %bitcast.49, bf16[4,512,1024]{2,1,0:T(8,128)(2,1)} %collective-permute-done.18.refs_1_, bf16[4,512,1024]{2,1,0:T(8,128)(2,1)} %bitcast.52, bf16[4,512,1024]{2,1,0:T(8,128)(2,1)} %collective-permute-done.24.refs_3_, ...), custom_call_target="tpu_custom_call" | custom-call | flops 524288 | bytes 524288 | tf_op jit(solution)/shard_map/trunk_part/pallas_call | solution.py:161
  (99 shorter events, 41.7 us)
Async XLA Ops:
  7.2 96.1 %all-gather.7.cloned.1.call-start = ((), (), s32[]{:S(2)}) async-start(), calls=%async_computation.1 | async-start | bytes 5242880 | tf_op jit(solution)/shard_map/all_gather | solution.py:258
  13.1 138.7 %all-gather.9.cloned.1.call-start = ((), (), s32[]{:S(2)}) async-start(), calls=%async_computation.2 | async-start | bytes 5242880 | tf_op jit(solution)/shard_map/all_gather | solution.py:279
  14.4 12.3 %collective-permute-start = (bf16[512,512]{1,0:T(8,128)(2,1)S(1)}, bf16[512,512]{1,0:T(8,128)(2,1)S(1)}, u32[]{:S(2)}, u32[]{:S(2)}) collective-permute-start(bf16[512,512]{1,0:T(8,128)(2,1)S(1)} %get-tuple-element.81), channel_id=1, source_target_pairs={{0,0},{1,1},{2,98},{3,99},{4,68},{5,69},{6,38},{7,39},{8,8},{9,9},... | collective-permute-start | bytes 1572872 | tf_op jit(solution)/shard_map/ppermute | solution.py:254
  15.1 17.8 %collective-permute-start.1 = (bf16[512,512]{1,0:T(8,128)(2,1)S(1)}, bf16[512,512]{1,0:T(8,128)(2,1)S(1)}, u32[]{:S(2)}, u32[]{:S(2)}) collective-permute-start(bf16[512,512]{1,0:T(8,128)(2,1)S(1)} %get-tuple-element.80), channel_id=1, source_target_pairs={{0,64},{1,65},{2,34},{3,35},{4,4},{5,5},{6,102},{7,103},{8,72},{9,... | collective-permute-start | bytes 1572872 | tf_op jit(solution)/shard_map/ppermute | solution.py:254
  37.5 13.5 %collective-permute-start.6 = (bf16[512,512]{1,0:T(8,128)(2,1)S(1)}, bf16[512,512]{1,0:T(8,128)(2,1)S(1)}, u32[]{:S(2)}, u32[]{:S(2)}) collective-permute-start(bf16[512,512]{1,0:T(8,128)(2,1)S(1)} %collective-permute-done), channel_id=1, source_target_pairs={{0,0},{1,16},{2,2},{3,18},{4,4},{5,20},{6,6},{7,22},{8,8},{9,24},{... | collective-permute-start | bytes 1572872 | tf_op jit(solution)/shard_map/ppermute | solution.py:264
  38.2 28.5 %collective-permute-start.7 = (bf16[512,512]{1,0:T(8,128)(2,1)S(1)}, bf16[512,512]{1,0:T(8,128)(2,1)S(1)}, u32[]{:S(2)}, u32[]{:S(2)}) collective-permute-start(bf16[512,512]{1,0:T(8,128)(2,1)S(1)} %collective-permute-done.1), channel_id=1, source_target_pairs={{0,4},{1,20},{2,6},{3,22},{4,0},{5,16},{6,2},{7,18},{8,12},{9,28},... | collective-permute-start | bytes 1572872 | tf_op jit(solution)/shard_map/ppermute | solution.py:264
  66.7 24.3 %collective-permute-start.11 = (bf16[512,1024]{1,0:T(8,128)(2,1)}, bf16[512,1024]{1,0:T(8,128)(2,1)}, u32[]{:S(2)}, u32[]{:S(2)}) collective-permute-start(bf16[512,1024]{1,0:T(8,128)(2,1)} %get-tuple-element.46), channel_id=1, source_target_pairs={{0,1},{1,0},{2,3},{3,2},{4,5},{5,4},{6,7},{7,6},{8,9},{9,8},{10,11... | collective-permute-start | bytes 3145736 | tf_op jit(solution)/shard_map/ppermute | solution.py:41
  74.3 22.5 %collective-permute-start.12 = (bf16[2,512,512]{2,1,0:T(8,128)(2,1)S(1)}, bf16[2,512,512]{2,1,0:T(8,128)(2,1)S(1)}, u32[]{:S(2)}, u32[]{:S(2)}) collective-permute-start(bf16[2,512,512]{2,1,0:T(8,128)(2,1)S(1)} %pad_maximum_fusion.refs_4_.refs_5_), channel_id=1, source_target_pairs={{0,96},{32,0},{64,32},{96,64},{1,97},{33,1},{65,33},{97,65},{2,98}... | collective-permute-start | bytes 3145736 | tf_op jit(solution)/shard_map/ppermute | solution.py:41
  78.7 24.5 %collective-permute-start.13 = (bf16[2,512,512]{2,1,0:T(8,128)(2,1)S(1)}, bf16[2,512,512]{2,1,0:T(8,128)(2,1)S(1)}, u32[]{:S(2)}, u32[]{:S(2)}) collective-permute-start(bf16[2,512,512]{2,1,0:T(8,128)(2,1)S(1)} %pad_maximum_fusion.refs_4_.refs_5_), channel_id=1, source_target_pairs={{0,32},{32,64},{64,96},{96,0},{1,33},{33,65},{65,97},{97,1},{2,34}... | collective-permute-start | bytes 3145736 | tf_op jit(solution)/shard_map/ppermute | solution.py:41
  103.2 34.3 %collective-permute-start.18 = (bf16[4,512,1024]{2,1,0:T(8,128)(2,1)}, bf16[4,512,1024]{2,1,0:T(8,128)(2,1)}, u32[]{:S(2)}, u32[]{:S(2)}) collective-permute-start(bf16[4,512,1024]{2,1,0:T(8,128)(2,1)} %bitcast.47), channel_id=1, source_target_pairs={{0,8},{8,0},{1,9},{9,1},{2,10},{10,2},{3,11},{11,3},{4,12},{12,4},... | collective-permute-start | bytes 12582920 | tf_op jit(solution)/shard_map/ppermute | solution.py:41
  103.2 13.6 %collective-permute-start.14 = (bf16[4,64,512]{2,1,0:T(8,128)(2,1)S(1)}, bf16[4,64,512]{2,1,0:T(8,128)(2,1)S(1)}, u32[]{:S(2)}, u32[]{:S(2)}) collective-permute-start(bf16[4,64,512]{2,1,0:T(8,128)(2,1)S(1)} %bitcast.54), channel_id=1, source_target_pairs={{0,96},{32,0},{64,32},{96,64},{1,97},{33,1},{65,33},{97,65},{2,98}... | collective-permute-start | bytes 786440 | tf_op jit(solution)/shard_map/ppermute | solution.py:41
  105.0 15.4 %collective-permute-start.16 = (bf16[4,64,512]{2,1,0:T(8,128)(2,1)S(1)}, bf16[4,64,512]{2,1,0:T(8,128)(2,1)}, u32[]{:S(2)}, u32[]{:S(2)}) collective-permute-start(bf16[4,64,512]{2,1,0:T(8,128)(2,1)S(1)} %bitcast.56), channel_id=1, source_target_pairs={{0,32},{32,64},{64,96},{96,0},{1,33},{33,65},{65,97},{97,1},{2,34}... | collective-permute-start | bytes 786440 | tf_op jit(solution)/shard_map/ppermute | solution.py:41
  105.9 31.6 %collective-permute-start.17 = (bf16[2,512,512]{2,1,0:T(8,128)(2,1)S(1)}, bf16[2,512,512]{2,1,0:T(8,128)(2,1)}, u32[]{:S(2)}, u32[]{:S(2)}) collective-permute-start(bf16[2,512,512]{2,1,0:T(8,128)(2,1)S(1)} %pad_maximum_fusion.refs_4_.refs_5_), channel_id=1, source_target_pairs={{0,16},{16,0},{1,17},{17,1},{2,18},{18,2},{3,19},{19,3},{4,20},{20... | collective-permute-start | bytes 3145736 | tf_op jit(solution)/shard_map/ppermute | solution.py:41
  121.2 13.9 %collective-permute-start.19 = (bf16[512,512]{1,0:T(8,128)(2,1)}, bf16[512,512]{1,0:T(8,128)(2,1)}, u32[]{:S(2)}, u32[]{:S(2)}) collective-permute-start(bf16[512,512]{1,0:T(8,128)(2,1)} %slice_bitcast_fusion.3), channel_id=1, source_target_pairs={{0,96},{32,0},{64,32},{96,64},{1,97},{33,1},{65,33},{97,65},{2,98}... | collective-permute-start | bytes 1572872 | tf_op jit(solution)/shard_map/ppermute | solution.py:41
  123.7 13.9 %collective-permute-start.20 = (bf16[512,512]{1,0:T(8,128)(2,1)}, bf16[512,512]{1,0:T(8,128)(2,1)}, u32[]{:S(2)}, u32[]{:S(2)}) collective-permute-start(bf16[512,512]{1,0:T(8,128)(2,1)} %slice_bitcast_fusion.2), channel_id=1, source_target_pairs={{0,32},{32,64},{64,96},{96,0},{1,33},{33,65},{65,97},{97,1},{2,34}... | collective-permute-start | bytes 1572872 | tf_op jit(solution)/shard_map/ppermute | solution.py:41
  137.5 22.9 %collective-permute-start.21 = (bf16[2,512,512]{2,1,0:T(8,128)(2,1)}, bf16[2,512,512]{2,1,0:T(8,128)(2,1)}, u32[]{:S(2)}, u32[]{:S(2)}) collective-permute-start(bf16[2,512,512]{2,1,0:T(8,128)(2,1)} %collective-permute-done.17.refs_4_.refs_5_), channel_id=1, source_target_pairs={{0,96},{32,0},{64,32},{96,64},{1,97},{33,1},{65,33},{97,65},{2,98}... | collective-permute-start | bytes 3145736 | tf_op jit(solution)/shard_map/ppermute | solution.py:41
  137.5 24.2 %collective-permute-start.22 = (bf16[2,512,512]{2,1,0:T(8,128)(2,1)}, bf16[2,512,512]{2,1,0:T(8,128)(2,1)}, u32[]{:S(2)}, u32[]{:S(2)}) collective-permute-start(bf16[2,512,512]{2,1,0:T(8,128)(2,1)} %collective-permute-done.17.refs_4_.refs_5_), channel_id=1, source_target_pairs={{0,32},{32,64},{64,96},{96,0},{1,33},{33,65},{65,97},{97,1},{2,34}... | collective-permute-start | bytes 3145736 | tf_op jit(solution)/shard_map/ppermute | solution.py:41
  147.6 12.3 %all-to-all-start = ((bf16[4,16,4096]{2,1,0:T(8,128)(2,1)}), bf16[4,16,4096]{2,1,0:T(8,128)(2,1)}, u32[]{:S(2)}, u32[]{:S(2)}) async-start(bf16[4,16,4096]{2,1,0:T(8,128)(2,1)} %bitcast.53), calls=%async_computation | async-start | bytes 1048576 | tf_op jit(solution)/shard_map/all_to_all | solution.py:298
  162.9 19.9 %collective-permute-start.23 = (bf16[16,4096]{1,0:T(8,128)(2,1)S(1)}, bf16[16,4096]{1,0:T(8,128)(2,1)S(1)}, u32[]{:S(2)}, u32[]{:S(2)}) collective-permute-start(bf16[16,4096]{1,0:T(8,128)(2,1)S(1)} %reduce_sum.61), channel_id=1, source_target_pairs={{0,1},{1,0},{2,3},{3,2},{4,5},{5,4},{6,7},{7,6},{8,9},{9,8},{10,11... | collective-permute-start | bytes 393224 | tf_op jit(solution)/shard_map/ppermute | solution.py:41
  168.4 16.8 %collective-permute-start.28 = (bf16[512,512]{1,0:T(8,128)(2,1)}, bf16[512,512]{1,0:T(8,128)(2,1)}, u32[]{:S(2)}, u32[]{:S(2)}) collective-permute-start(bf16[512,512]{1,0:T(8,128)(2,1)} %slice_bitcast_fusion.1), channel_id=1, source_target_pairs={{0,96},{32,0},{64,32},{96,64},{1,97},{33,1},{65,33},{97,65},{2,98}... | collective-permute-start | bytes 1572872 | tf_op jit(solution)/shard_map/ppermute | solution.py:41
  171.1 15.3 %collective-permute-start.29 = (bf16[512,512]{1,0:T(8,128)(2,1)}, bf16[512,512]{1,0:T(8,128)(2,1)}, u32[]{:S(2)}, u32[]{:S(2)}) collective-permute-start(bf16[512,512]{1,0:T(8,128)(2,1)} %slice_bitcast_fusion), channel_id=1, source_target_pairs={{0,32},{32,64},{64,96},{96,0},{1,33},{33,65},{65,97},{97,1},{2,34}... | collective-permute-start | bytes 1572872 | tf_op jit(solution)/shard_map/ppermute | solution.py:41
  183.1 13.4 %collective-permute-start.25 = (f32[16]{0:T(128)S(1)}, f32[16]{0:T(128)S(1)}, u32[]{:S(2)}, u32[]{:S(2)}) collective-permute-start(f32[16]{0:T(128)S(1)} %broadcast_add_fusion), channel_id=1, source_target_pairs={{0,6},{2,0},{4,2},{6,4},{1,7},{3,1},{5,3},{7,5},{8,14},{10,8},{12,... | collective-permute-start | bytes 200 | tf_op jit(solution)/shard_map/ppermute | solution.py:41
  183.8 12.7 %collective-permute-start.26 = (f32[16]{0:T(128)S(1)}, f32[16]{0:T(128)S(1)}, u32[]{:S(2)}, u32[]{:S(2)}) collective-permute-start(f32[16]{0:T(128)S(1)} %broadcast_add_fusion), channel_id=1, source_target_pairs={{0,4},{2,6},{4,0},{6,2},{1,5},{3,7},{5,1},{7,3},{8,12},{10,14},{12... | collective-permute-start | bytes 200 | tf_op jit(solution)/shard_map/ppermute | solution.py:41
  184.0 12.5 %collective-permute-start.27 = (f32[16]{0:T(128)S(1)}, f32[16]{0:T(128)S(1)}, u32[]{:S(2)}, u32[]{:S(2)}) collective-permute-start(f32[16]{0:T(128)S(1)} %broadcast_add_fusion), channel_id=1, source_target_pairs={{0,2},{2,4},{4,6},{6,0},{1,3},{3,5},{5,7},{7,1},{8,10},{10,12},{12... | collective-permute-start | bytes 200 | tf_op jit(solution)/shard_map/ppermute | solution.py:41
  (18 other events, 269.3 us)
Sparse Core Ops, SparseCore 0:
  13.2 65.5 all-gather.6
  91.1 50.6 all-gather.8
